TPU v7x, 32 devices: a whole 2x2x4 slice. The times are simulated.
32 devices in a mesh: groups: 2 (over y), ctx: 4 (over z), enc: 2 (over x), tp: 2 (over core).
Axes of the slice: x: 2, y: 2, z: 4, core: 2. Of those that a mesh axis runs over, the one named last changes fastest.
Arguments:
- enc_rows: bfloat16 [4, 1024, 1280], P(('groups', 'enc'), 'ctx'), parts along dimension 0, may hold values from -6 to 6
- row_slot: int32 [4, 1024], P(('groups', 'enc'), 'ctx'), parts along dimension 0, may hold values from 0 to 1023, as said below
- row_kind: int32 [4, 1024], P(('groups', 'enc'), 'ctx'), parts along dimension 0, may hold values from 0 to 1, as said below
- audio_proj: bfloat16 [1280, 8192], P(None, ('ctx', 'tp')), may hold values from -0.15625 to 0.15625
- frame_proj: bfloat16 [1280, 8192], P(None, ('ctx', 'tp')), may hold values from -0.15625 to 0.15625
- audio_bias: bfloat16 [8192], P(('ctx', 'tp')), may hold values from -3 to 3
- frame_bias: bfloat16 [8192], P(('ctx', 'tp')), may hold values from -3 to 3
- norm_gain: bfloat16 [8192], replicated, may hold values from 0.5 to 1.5
Outputs:
- normed: bfloat16 [4, 1024, 8192], P(('groups', 'enc'), ('ctx', 'tp')), parts along dimension 0
There are 2 independent parts, one for each index of `groups`. A program takes and returns all parts, laid end to end along the dimension named above; an argument that names none is the same for every part. Nothing has to cross between parts.
Inputs may be any that keep to these rules, and one draw needn't show every extreme that they name: `row_slot`: in each conversation every value appears exactly once. A row with value s fills context shard s // 256. Of the 256 rows of one owner (one index of ctx, in one conversation), at most 128 fill any one context shard, and every owner sends exactly 128 rows to some context shard. Rows come in 2-second spans of at most 128 rows: one span's rows are consecutive at the owner and fill consecutive positions. `row_kind`: within a span the audio rows come before the frame rows.
All inputs are finite; a program needn't handle non-finite values.
Results may differ from a plain program's by a relative error of at most 0.005.
Values may be sent and summed in bfloat16 or wider, within the bound.
No kernel may reach another device: no remote copies, remote signals or barrier semaphores. Data moves between devices by JAX's collectives and lax.ppermute only.
A program may use at most 128 MiB of HBM per device.

v0:
```python
import jax
import jax.numpy as jnp
from jax import lax
from jax.sharding import PartitionSpec as P


def project(enc_part, kind_part, weights, bias_audio, bias_frame):
    is_audio = (kind_part == 0)[:, None]
    nothing = jnp.zeros((), enc_part.dtype)
    stacked = jnp.concatenate(
        [jnp.where(is_audio, enc_part, nothing), jnp.where(is_audio, nothing, enc_part)], axis=1
    )
    result = jnp.dot(stacked, weights, preferred_element_type=jnp.float32)
    return result + jnp.where(is_audio, bias_audio[None, :], bias_frame[None, :])


def body(enc_rows, row_slot, row_kind, audio_proj, frame_proj, audio_bias, frame_bias, norm_gain):
    owned_rows = enc_rows[0]
    owned_slot = row_slot[0]
    owned_kind = row_kind[0]
    seq_dev = owned_rows.shape[0]
    width_enc = owned_rows.shape[1]
    n_ctx = lax.axis_size("ctx")
    capacity = 2 * seq_dev // n_ctx
    target = owned_slot // seq_dev
    position = owned_slot % seq_dev
    onehot = (target[:, None] == jnp.arange(n_ctx, dtype=jnp.int32)[None, :]).astype(jnp.int32)
    before = jnp.cumsum(onehot, axis=0) - onehot
    ranking = jnp.sum(before * onehot, axis=1)
    send_index = target * capacity + ranking
    outgoing = n_ctx * capacity
    select_send = send_index[None, :] == jnp.arange(outgoing, dtype=jnp.int32)[:, None]
    parcel = jnp.dot(
        select_send.astype(jnp.bfloat16), owned_rows, preferred_element_type=jnp.float32
    )
    parcel = parcel.astype(jnp.bfloat16).reshape(n_ctx, capacity, width_enc)
    send_int = select_send.astype(jnp.int32)
    where_to = (jnp.sum(send_int * (position + 1)[None, :], axis=1) - 1).reshape(n_ctx, capacity)
    what_kind = jnp.sum(send_int * owned_kind[None, :], axis=1).reshape(n_ctx, capacity)
    arrived = (
        lax.all_to_all(parcel, "ctx", split_axis=0, concat_axis=0, tiled=True),
        lax.all_to_all(where_to, "ctx", split_axis=0, concat_axis=0, tiled=True),
        lax.all_to_all(what_kind, "ctx", split_axis=0, concat_axis=0, tiled=True),
    )
    rows_in = arrived[0].reshape(outgoing, width_enc)
    pos_in = arrived[1].reshape(outgoing)
    kind_in = arrived[2].reshape(outgoing)
    select_land = pos_in[None, :] == jnp.arange(seq_dev, dtype=jnp.int32)[:, None]
    shard_rows = jnp.dot(
        select_land.astype(jnp.bfloat16), rows_in, preferred_element_type=jnp.float32
    ).astype(jnp.bfloat16)
    shard_kind = jnp.sum(select_land.astype(jnp.int32) * kind_in[None, :], axis=1)
    weights = jnp.concatenate([audio_proj, frame_proj], axis=0)
    bias_audio = audio_bias.astype(jnp.float32)
    bias_frame = frame_bias.astype(jnp.float32)
    columns = project(
        lax.all_gather(shard_rows, "ctx", axis=0, tiled=True),
        lax.all_gather(shard_kind, "ctx", axis=0, tiled=True),
        weights,
        bias_audio,
        bias_frame,
    )
    embeds = lax.all_to_all(
        columns.astype(jnp.bfloat16), ("ctx", "tp"), split_axis=0, concat_axis=1, tiled=True
    )
    widened = embeds.astype(jnp.float32)
    mean_square = jnp.mean(widened * widened, axis=-1, keepdims=True)
    normed = (widened * lax.rsqrt(mean_square + 1e-06) * norm_gain.astype(jnp.float32)).astype(
        jnp.bfloat16
    )
    return normed[None]


def solution(mesh):
    return jax.shard_map(
        body,
        mesh=mesh,
        in_specs=(
            P(("groups", "enc"), "ctx", None),
            P(("groups", "enc"), "ctx"),
            P(("groups", "enc"), "ctx"),
            P(None, ("ctx", "tp")),
            P(None, ("ctx", "tp")),
            P(("ctx", "tp")),
            P(("ctx", "tp")),
            P(),
        ),
        out_specs=P(("groups", "enc"), ("ctx", "tp"), None),
        check_vma=False,
    )
```

profile of v0, /device:TPU:0, one launch (start us, length us, event | category | flops | bytes accessed | tf_op | source)
XLA Modules:
  0.0 195.7 jit_solution(15758488479154289342)
XLA Ops:
  6.5 0.0 copy-start
  6.5 0.8 and_select_fusion.3
  7.3 0.7 and_select_fusion.2
  8.0 1.2 reduce-window.6
  9.2 0.1 slice.8
  9.3 0.1 copy.18
  9.4 0.1 copy.19
  9.5 0.1 add_bitcast_fusion
  9.6 0.7 multiply_add_fusion
  10.3 1.5 select_reduce_fusion.2
  11.8 0.6 broadcast_add_fusion
  12.4 6.3 %all-to-all-start = ((s32[4,1,128]{2,1,0:T(1,128)}), s32[4,1,128]{2,1,0:T(1,128)S(1)}, u32[]{:S(2)}, u32[]{:S(2)}) async-start(s32[4,1,128]{2,1,0:T(1,128)} %bitcast.7), calls=%async_computation | async-start | bytes 4096 | tf_op jit(solution)/shard_map/all_to_all | solution.py:42
  18.7 0.0 all-gather.3.cloned.1.call-start
  18.7 0.0 copy-done
  18.7 0.5 convolution_convert_fusion
  19.2 4.9 %all-to-all-done = s32[4,1,128]{2,1,0:T(1,128)S(1)} async-done(((s32[4,1,128]{2,1,0:T(1,128)}), s32[4,1,128]{2,1,0:T(1,128)S(1)}, u32[]{:S(2)}, u32[]{:S(2)}) %all-to-all-start) | async-done | bytes 2080 | tf_op jit(solution)/shard_map/all_to_all | solution.py:42
  24.2 0.0 copy-start.2
  24.2 0.0 copy-start.3
  24.2 32.7 %all_to_all.33 = bf16[4,128,1280]{2,1,0:T(8,128)(2,1)S(1)} all-to-all(bf16[4,128,1280]{2,1,0:T(8,128)(2,1)S(1)} %bitcast.39), channel_id=1, replica_groups=mesh['groups'=2,'ctx'=4,'enc'=2,'tp'=2] {'ctx'}, dimensions={0} | all-to-all | bytes 2621440 | tf_op jit(solution)/shard_map/all_to_all | solution.py:41
  56.9 1.3 convolution_convert_fusion.1
  58.3 0.0 all-gather.3.cloned.1.call-update
  58.3 3.2 %all-to-all-start.1 = ((s32[4,1,128]{2,1,0:T(1,128)}), s32[4,1,128]{2,1,0:T(1,128)S(1)}, u32[]{:S(2)}, u32[]{:S(2)}) async-start(s32[4,1,128]{2,1,0:T(1,128)} %bitcast.10), calls=%async_computation.1 | async-start | bytes 4096 | tf_op jit(solution)/shard_map/all_to_all | solution.py:43
  61.5 0.0 copy-done.2
  61.5 0.0 copy-done.3
  61.6 5.5 %all-to-all-done.1 = s32[4,1,128]{2,1,0:T(1,128)S(1)} async-done(((s32[4,1,128]{2,1,0:T(1,128)}), s32[4,1,128]{2,1,0:T(1,128)S(1)}, u32[]{:S(2)}, u32[]{:S(2)}) %all-to-all-start.1) | async-done | bytes 2080 | tf_op jit(solution)/shard_map/all_to_all | solution.py:43
  67.0 0.1 select_reduce_fusion
  67.2 8.4 %all-gather = s32[4,1,256]{2,1,0:T(1,128)S(1)} all-gather(s32[1,1,256]{2,1,0:T(1,128)S(1)} %bitcast.50), channel_id=1, replica_groups=mesh['groups'=2,'ctx'=4,'enc'=2,'tp'=2] {'ctx'}, dimensions={0}, use_global_device_ids=true | all-gather | bytes 5120 | tf_op jit(solution)/shard_map/all_gather | solution.py:58
  75.5 0.0 copy-start.4
  75.6 36.9 %all-gather.3.cloned.1.call-done = bf16[1024,1280]{1,0:T(8,128)(2,1)} async-done(((bf16[256,1280]{1,0:T(8,128)(2,1)}), bf16[1024,1280]{1,0:T(8,128)(2,1)}) %all-gather.3.cloned.1.call-update) | async-done | bytes 2621456 | tf_op jit(solution)/shard_map/all_gather | solution.py:57
  112.4 0.0 copy-start.5
  112.4 2.4 %broadcast_select_fusion.1 = (bf16[1024,1280]{1,0:T(8,128)(2,1)S(1)}, bf16[1024,1280]{1,0:T(8,128)(2,1)S(1)}) fusion(bf16[1024,1280]{1,0:T(8,128)(2,1)} %all-gather.3.cloned.1.call-done, pred[1024]{0:T(1024)(128)(4,1)S(1)} %reshape.162), kind=kLoop, calls=%fused_computation.14 | loop fusion | flops 2621440 | bytes 7865344 | tf_op jit(solution)/shard_map/jit(_where)/select_n | solution.py:11
  114.8 0.0 copy-done.4
  114.8 0.1 copy-done.5
  114.9 6.9 %add_convert_fusion = bf16[1024,1024]{1,0:T(8,128)(2,1)} fusion(f32[1024]{0:T(1024)S(1)} %convert_element_type.64, f32[1024]{0:T(1024)S(1)} %convert_element_type.63, pred[1024]{0:T(1024)(128)(4,1)S(1)} %reshape.162, bf16[1280,1024]{1,0:T(8,128)(2,1)S(1)} %copy-done.4, bf16[1280,1024]{1,0:T(8,128)(2,1)S(1)} %copy-done.5, ...), kind=kOutput, calls=%fused_computation.11 | convolution fusion | flops 5392826368 | bytes 12592128 | tf_op jit(solution)/shard_map/dot_general | solution.py:13
  121.8 0.0 copy-start.1
  121.8 3.7 %all-to-all-start.3 = ((bf16[8,128,1024]{2,1,0:T(8,128)(2,1)}), bf16[8,128,1024]{2,1,0:T(8,128)(2,1)S(1)}, u32[]{:S(2)}, u32[]{:S(2)}) async-start(bf16[8,128,1024]{2,1,0:T(8,128)(2,1)} %bitcast.41), calls=%async_computation.3 | async-start | bytes 4194304 | tf_op jit(solution)/shard_map/all_to_all | solution.py:63
  125.6 0.0 copy-done.1
  125.6 49.0 %all-to-all-done.3 = bf16[8,128,1024]{2,1,0:T(8,128)(2,1)S(1)} async-done(((bf16[8,128,1024]{2,1,0:T(8,128)(2,1)}), bf16[8,128,1024]{2,1,0:T(8,128)(2,1)S(1)}, u32[]{:S(2)}, u32[]{:S(2)}) %all-to-all-start.3) | async-done | bytes 2097184 | tf_op jit(solution)/shard_map/all_to_all | solution.py:63
  174.6 0.5 fusion.7
  175.1 0.5 convert_bitcast_fusion
  175.5 4.4 %copy.20 = f32[128,8,1024]{2,1,0:T(8,128)} copy(f32[128,8,1024]{2,0,1:T(8,128)S(1)} %convert_bitcast_fusion) | data formatting | bytes 8388608 | tf_op jit(solution)/shard_map/convert_element_type | solution.py:66
  179.9 5.0 %reshape.158 = f32[1,128,8192]{2,1,0:T(8,128)} reshape(f32[128,8,1024]{2,1,0:T(8,128)} %copy.20) | data formatting | bytes 8388608 | tf_op jit(solution)/shard_map/convert_element_type | solution.py:66
  184.9 4.0 %multiply_convert_fusion = bf16[1,128,8192]{2,1,0:T(8,128)(2,1)} fusion(f32[1,128,8192]{2,1,0:T(8,128)} %reshape.158, f32[8192]{0:T(1024)S(1)} %convert_element_type.70, f32[128]{0:T(128)S(1)} %add_rsqrt_fusion), kind=kLoop, calls=%fused_computation.10 | loop fusion | flops 3145728 | bytes 6324736 | tf_op jit(solution)/shard_map/convert_element_type | solution.py:68
  (10 shorter events, 0.1 us)
Async XLA Ops:
  6.5 12.2 %copy-start = (bf16[1,256,1280]{2,1,0:T(8,128)(2,1)S(1)}, bf16[1,256,1280]{2,1,0:T(8,128)(2,1)}, u32[]{:S(2)}) copy-start(bf16[1,256,1280]{2,1,0:T(8,128)(2,1)} %param.8) | copy-start | bytes 1966084
  12.4 11.8 %all-to-all-start = ((s32[4,1,128]{2,1,0:T(1,128)}), s32[4,1,128]{2,1,0:T(1,128)S(1)}, u32[]{:S(2)}, u32[]{:S(2)}) async-start(s32[4,1,128]{2,1,0:T(1,128)} %bitcast.7), calls=%async_computation | async-start | bytes 4096 | tf_op jit(solution)/shard_map/all_to_all | solution.py:42
  18.7 93.7 %all-gather.3.cloned.1.call-start = ((), (), s32[]{:S(2)}) async-start(), calls=%async_computation.4 | async-start | bytes 3276800 | tf_op jit(solution)/shard_map/all_gather | solution.py:57
  24.2 37.3 %copy-start.2 = (bf16[1024]{0:T(1024)(128)(2,1)S(1)}, bf16[1024]{0:T(1024)(128)(2,1)}, u32[]{:S(2)}) copy-start(bf16[1024]{0:T(1024)(128)(2,1)} %param.13) | copy-start | bytes 6148
  24.2 37.3 %copy-start.3 = (bf16[1024]{0:T(1024)(128)(2,1)S(1)}, bf16[1024]{0:T(1024)(128)(2,1)}, u32[]{:S(2)}) copy-start(bf16[1024]{0:T(1024)(128)(2,1)} %param.14) | copy-start | bytes 6148
  58.3 8.7 %all-to-all-start.1 = ((s32[4,1,128]{2,1,0:T(1,128)}), s32[4,1,128]{2,1,0:T(1,128)S(1)}, u32[]{:S(2)}, u32[]{:S(2)}) async-start(s32[4,1,128]{2,1,0:T(1,128)} %bitcast.10), calls=%async_computation.1 | async-start | bytes 4096 | tf_op jit(solution)/shard_map/all_to_all | solution.py:43
  75.5 39.2 %copy-start.4 = (bf16[1280,1024]{1,0:T(8,128)(2,1)S(1)}, bf16[1280,1024]{1,0:T(8,128)(2,1)}, u32[]{:S(2)}) copy-start(bf16[1280,1024]{1,0:T(8,128)(2,1)} %param.12) | copy-start | bytes 7864324
  112.4 2.5 %copy-start.5 = (bf16[1280,1024]{1,0:T(8,128)(2,1)S(1)}, bf16[1280,1024]{1,0:T(8,128)(2,1)}, u32[]{:S(2)}) copy-start(bf16[1280,1024]{1,0:T(8,128)(2,1)} %param.11) | copy-start | bytes 7864324
  121.8 3.7 %copy-start.1 = (bf16[8192]{0:T(1024)(128)(2,1)S(1)}, bf16[8192]{0:T(1024)(128)(2,1)}, u32[]{:S(2)}) copy-start(bf16[8192]{0:T(1024)(128)(2,1)} %param.15) | copy-start | bytes 49156
  121.8 52.7 %all-to-all-start.3 = ((bf16[8,128,1024]{2,1,0:T(8,128)(2,1)}), bf16[8,128,1024]{2,1,0:T(8,128)(2,1)S(1)}, u32[]{:S(2)}, u32[]{:S(2)}) async-start(bf16[8,128,1024]{2,1,0:T(8,128)(2,1)} %bitcast.41), calls=%async_computation.3 | async-start | bytes 4194304 | tf_op jit(solution)/shard_map/all_to_all | solution.py:63
Sparse Core Ops, SparseCore 0:
  58.4 53.9 all-gather.2
where the time goes:
time: 196 us
  waiting for transfers between devices  96.2 us (49%)
  blocking collectives  41.1 us (21%)
  between operations  13.5 us (7%)
  starting transfers between devices  13.2 us (7%)
  other arithmetic  13.1 us (7%)
  local copies, waits for them, and re-layouts  9.79 us (5%)
  matrix products  8.76 us (4%)
    all_to_all x1, waiting for transfers between devices, body(): lax.all_to_all(columns.astype(jnp.bfloat16), ('ctx', 'tp'), split_axis=0,...  49 us
    all_gather x1, waiting for transfers between devices, body(): lax.all_gather(shard_rows, 'ctx', axis=0, tiled=True)  36.9 us
    all_to_all x1, blocking collectives, body(): lax.all_to_all(parcel, 'ctx', split_axis=0, concat_axis=0, tiled=True)  32.7 us
    convert_element_type x2, local copies, waits for them, and re-layouts, body(): widened = embeds.astype(jnp.float32)  9.33 us
    all_gather x1, blocking collectives, body(): lax.all_gather(shard_kind, 'ctx', axis=0, tiled=True)  8.35 us
    dot_general x1, matrix products, project(): result = jnp.dot(stacked, weights, preferred_element_type=jnp.float32)  6.9 us
    all_to_all x1, starting transfers between devices, body(): lax.all_to_all(where_to, 'ctx', split_axis=0, concat_axis=0, tiled=True)  6.32 us
    all_to_all x1, waiting for transfers between devices, body(): lax.all_to_all(what_kind, 'ctx', split_axis=0, concat_axis=0, tiled=True)  5.47 us
  transfers between devices with their start and end apart: 4, of which 4 were waited for; matrix products, arithmetic and copies ran while one was open for 0% of the time, Pallas kernels for 0%

commit v1 on v0

v1 whole, which is shorter than its diff:
```python
import functools

import jax
import jax.numpy as jnp
from jax import lax
from jax.experimental import pallas as pl
from jax.experimental.pallas import tpu as pltpu
from jax.sharding import PartitionSpec as P

VMEM = pl.BlockSpec(memory_space=pltpu.VMEM)
SMEM = pl.BlockSpec(memory_space=pltpu.SMEM)
PARAMS = pltpu.CompilerParams(vmem_limit_bytes=48 << 20)


def column_of(row_vector):
    r = row_vector.shape[1]
    diagonal = lax.broadcasted_iota(jnp.int32, (r, r), 0) == lax.broadcasted_iota(
        jnp.int32, (r, r), 1
    )
    return jnp.sum(jnp.where(diagonal, row_vector, 0), axis=1, keepdims=True)


def project_kernel(meta, x, w_audio, w_frame, b_audio, b_frame, out):
    is_audio = column_of(meta[...] % 2) == 0
    audio = jnp.dot(x[...], w_audio[...], preferred_element_type=jnp.float32)
    frame = jnp.dot(x[...], w_frame[...], preferred_element_type=jnp.float32)
    audio = audio + b_audio[...].astype(jnp.float32)
    frame = frame + b_frame[...].astype(jnp.float32)
    out[...] = jnp.where(is_audio, audio, frame).astype(out.dtype)


def project_halves_kernel(scalars, meta, mine, other, wa, wf, ba, bf, out, x):
    half = mine.shape[0]
    t = scalars[0]
    x[pl.ds(pl.multiple_of(t * half, half), half), :] = mine[...]
    x[pl.ds(pl.multiple_of((1 - t) * half, half), half), :] = other[...]
    project_kernel(meta, x, wa, wf, ba, bf, out)


def project(scalars, meta, pieces, weights):
    rows = sum(p.shape[0] for p in pieces)
    ew, cols = weights[0].shape
    cost = pl.CostEstimate(
        flops=4 * rows * ew * cols, bytes_accessed=2 * (rows * (ew + cols)), transcendentals=0
    )
    out_shape = jax.ShapeDtypeStruct((rows, cols), jnp.bfloat16)
    if len(pieces) == 1:
        return pl.pallas_call(
            project_kernel,
            out_shape=out_shape,
            in_specs=[VMEM] * 6,
            out_specs=VMEM,
            compiler_params=PARAMS,
            cost_estimate=cost,
            name="project_own",
        )(meta, *pieces, *weights)
    return pl.pallas_call(
        project_halves_kernel,
        out_shape=out_shape,
        in_specs=[SMEM] + [VMEM] * 7,
        out_specs=VMEM,
        scratch_shapes=[pltpu.VMEM((rows, ew), jnp.bfloat16)],
        compiler_params=PARAMS,
        cost_estimate=cost,
        name="project_halves",
    )(scalars, meta, *pieces, *weights)


def select_kernel(n, scalars, *refs):
    metas, projected, outs = refs[:n], refs[n : 2 * n], refs[2 * n :]
    places = outs[0].shape[0]
    rows, cols = projected[0].shape
    i = lax.broadcasted_iota(jnp.int32, (2 * places, 1), 0)
    position = jnp.where(i < places, scalars[0] + i, scalars[1] + i - places)
    total = jnp.zeros((2 * places, cols), jnp.float32)
    for meta, block in zip(metas, projected):
        chosen = (meta[...] // 2 == position).astype(jnp.float32).astype(jnp.bfloat16)
        total = total + jnp.dot(chosen, block[...], preferred_element_type=jnp.float32)
    outs[0][...] = total[:places].astype(jnp.bfloat16)
    outs[1][...] = total[places:].astype(jnp.bfloat16)


def select(bases, metas, projected, places):
    n = len(metas)
    rows, cols = projected[0].shape
    return pl.pallas_call(
        functools.partial(select_kernel, n),
        out_shape=[jax.ShapeDtypeStruct((places, cols), jnp.bfloat16)] * 2,
        in_specs=[SMEM] + [VMEM] * (2 * n),
        out_specs=[VMEM] * 2,
        compiler_params=PARAMS,
        cost_estimate=pl.CostEstimate(
            flops=4 * places * rows * n * cols, bytes_accessed=2 * n * rows * cols, transcendentals=0
        ),
        name="select",
    )(bases, *metas, *projected)


def norm_kernel(n, blocks, gain, *refs):
    pieces, out = refs[:n], refs[n]
    cols = pieces[0].shape[1]
    total = None
    for piece in pieces:
        wide = piece[...].astype(jnp.float32)
        part = jnp.sum(wide * wide, axis=1, keepdims=True)
        total = part if total is None else total + part
    scale = lax.rsqrt(total / (n * cols) + 1e-06)
    for k, piece in enumerate(pieces):
        at = pl.ds(pl.multiple_of(blocks[k] * cols, cols), cols)
        wide = piece[...].astype(jnp.float32)
        out[:, at] = (wide * scale * gain[:, at].astype(jnp.float32)).astype(out.dtype)


def norm(blocks, gain, pieces):
    n = len(pieces)
    places, cols = pieces[0].shape
    return pl.pallas_call(
        functools.partial(norm_kernel, n),
        out_shape=jax.ShapeDtypeStruct((places, n * cols), jnp.bfloat16),
        in_specs=[SMEM] + [VMEM] * (n + 1),
        out_specs=VMEM,
        compiler_params=PARAMS,
        cost_estimate=pl.CostEstimate(
            flops=4 * places * n * cols, bytes_accessed=4 * places * n * cols, transcendentals=0
        ),
        name="norm",
    )(blocks, gain, *pieces)


def body(enc_rows, row_slot, row_kind, audio_proj, frame_proj, audio_bias, frame_bias, norm_gain):
    n_ctx, n_tp = lax.axis_size("ctx"), lax.axis_size("tp")
    z, t = lax.axis_index("ctx"), lax.axis_index("tp")
    rows = enc_rows[0]
    seq_dev = rows.shape[0]
    half = seq_dev // n_tp
    places = seq_dev // n_tp
    weights = (audio_proj, frame_proj, audio_bias[None, :], frame_bias[None, :])
    scalars = t[None].astype(jnp.int32)

    def over_ctx(x, m):
        return lax.ppermute(x, "ctx", [(i, i ^ m) for i in range(n_ctx)])

    def over_tp(x):
        return lax.ppermute(x, "tp", [(0, 1), (1, 0)])

    meta = row_slot * 2 + row_kind
    mine = lax.dynamic_slice_in_dim(rows, t * half, half, 0)
    metas, projected = [meta], [project(scalars, meta, [rows], weights)]
    for m in range(1, n_ctx):
        arrived = over_ctx(mine, m)
        metas.append(over_ctx(meta, m))
        projected.append(project(scalars, metas[m], [arrived, over_tp(arrived)], weights))

    pieces, blocks = [], []
    for m in reversed(range(n_ctx)):
        bases = jnp.stack([((z ^ m) * n_tp + (t ^ d)) * places for d in range(2)])
        blocks += [(z ^ m) * n_tp + (t ^ d) for d in range(2)]
        same, other = select(bases.astype(jnp.int32), metas, projected, places)
        for d, piece in ((0, same), (1, other)):
            if m or d:
                perm = [
                    (i * n_tp + c, (i ^ m) * n_tp + (c ^ d))
                    for i in range(n_ctx)
                    for c in range(n_tp)
                ]
                piece = lax.ppermute(piece, ("ctx", "tp"), perm)
            pieces.append(piece)
    return norm(jnp.stack(blocks).astype(jnp.int32), norm_gain[None, :], pieces)[None]


def solution(mesh):
    return jax.shard_map(
        body,
        mesh=mesh,
        in_specs=(
            P(("groups", "enc"), "ctx", None),
            P(("groups", "enc"), "ctx"),
            P(("groups", "enc"), "ctx"),
            P(None, ("ctx", "tp")),
            P(None, ("ctx", "tp")),
            P(("ctx", "tp")),
            P(("ctx", "tp")),
            P(),
        ),
        out_specs=P(("groups", "enc"), ("ctx", "tp"), None),
        check_vma=False,
    )
```

time: 196 us -> 108 us (0.55)
  the two profiles are of different devices: /device:TPU:0 before, /device:TPU:22 now
where the time goes in v1:
time: 108 us; the launch traced here: 107 us
  waiting for transfers between devices  58.9 us (55%)
  Pallas kernels  23.7 us (22%)
  starting transfers between devices  14.6 us (14%)
  local copies, waits for them, and re-layouts  9.17 us (8%)
    ppermute x7, waiting for transfers between devices, body(): piece = lax.ppermute(piece, ('ctx', 'tp'), perm)  41.9 us
    ppermute x6, waiting for transfers between devices, over_ctx(): return lax.ppermute(x, 'ctx', [(i, i ^ m) for i in range(n_ctx)])  17 us
    pallas_call x3, Pallas kernels, project(): pl.pallas_call(project_halves_kernel, out_shape=out_shape, in_specs=[SMEM...  10.8 us
    ppermute x6, starting transfers between devices, over_ctx(): return lax.ppermute(x, 'ctx', [(i, i ^ m) for i in range(n_ctx)])  7.44 us
    ppermute x7, starting transfers between devices, body(): piece = lax.ppermute(piece, ('ctx', 'tp'), perm)  6.66 us
    pallas_call x4, Pallas kernels, select(): pl.pallas_call(functools.partial(select_kernel, n), out_shape=[jax.ShapeD...  6.44 us
    unnamed x20, local copies, waits for them, and re-layouts  5.97 us
    pallas_call x1, Pallas kernels, project(): pl.pallas_call(project_kernel, out_shape=out_shape, in_specs=[VMEM] * 6,...  3.45 us
  transfers between devices with their start and end apart: 16, of which 7 were waited for; matrix products, arithmetic and copies ran while one was open for 2% of the time, Pallas kernels for 15%

profile of v1, /device:TPU:22, one launch (start us, length us, event | category | flops | bytes accessed | tf_op | source)
XLA Modules:
  0.0 107.4 jit_solution(13160019922850720192)
XLA Ops:
  0.0 1.7 %dynamic-slice_bitcast_fusion = bf16[128,1280]{1,0:T(8,128)(2,1)} fusion(bf16[1,256,1280]{2,1,0:T(8,128)(2,1)} %param.8, s32[]{:T(128)S(6)} %select_n.3), kind=kLoop, calls=%fused_computation | loop fusion | bytes 655364 | tf_op jit(solution)/shard_map/dynamic_slice | solution.py:147
  1.7 0.3 collective-permute-start.5
  2.1 2.7 %collective-permute-start.7 = (bf16[128,1280]{1,0:T(8,128)(2,1)}, bf16[128,1280]{1,0:T(8,128)(2,1)}, u32[]{:S(2)}, u32[]{:S(2)}) collective-permute-start(bf16[128,1280]{1,0:T(8,128)(2,1)} %dynamic-slice_bitcast_fusion), channel_id=1, source_target_pairs={{0,12},{4,8},{8,4},{12,0},{1,13},{5,9},{9,5},{13,1},{2,14},{6,10},... | collective-permute-start | bytes 983048 | tf_op jit(solution)/shard_map/ppermute | solution.py:141
  4.8 1.3 %collective-permute-start.3 = (bf16[128,1280]{1,0:T(8,128)(2,1)}, bf16[128,1280]{1,0:T(8,128)(2,1)S(1)}, u32[]{:S(2)}, u32[]{:S(2)}) collective-permute-start(bf16[128,1280]{1,0:T(8,128)(2,1)} %dynamic-slice_bitcast_fusion), channel_id=1, source_target_pairs={{0,4},{4,0},{8,12},{12,8},{1,5},{5,1},{9,13},{13,9},{2,6},{6,2},{1... | collective-permute-start | bytes 983048 | tf_op jit(solution)/shard_map/ppermute | solution.py:141
  6.1 0.7 multiply_add_fusion.meta.refs_0_
  6.8 0.1 collective-permute-start.1
  6.9 2.0 %collective-permute-start.2 = (s32[1,256]{1,0:T(1,128)S(1)}, s32[1,256]{1,0:T(1,128)S(1)}, u32[]{:S(2)}, u32[]{:S(2)}) collective-permute-start(s32[1,256]{1,0:T(1,128)S(1)} %multiply_add_fusion.meta.refs_0_), channel_id=1, source_target_pairs={{0,12},{4,8},{8,4},{12,0},{1,13},{5,9},{9,5},{13,1},{2,14},{6,10},... | collective-permute-start | bytes 3080 | tf_op jit(solution)/shard_map/ppermute | solution.py:141
  8.9 0.7 broadcast_in_dim.16.b_audio.ba
  9.6 0.7 broadcast_in_dim.17.b_frame.bf
  10.3 14.4 %collective-permute-done.5.mine = bf16[128,1280]{1,0:T(8,128)(2,1)} collective-permute-done((bf16[128,1280]{1,0:T(8,128)(2,1)}, bf16[128,1280]{1,0:T(8,128)(2,1)}, u32[]{:S(2)}, u32[]{:S(2)}) %collective-permute-start.5) | collective-permute-done | bytes 327712 | tf_op jit(solution)/shard_map/ppermute | solution.py:141
  24.7 1.7 %copy-done = bf16[1280,1024]{1,0:T(8,128)(2,1)S(1)} copy-done((bf16[1280,1024]{1,0:T(8,128)(2,1)S(1)}, bf16[1280,1024]{1,0:T(8,128)(2,1)}, u32[]{:S(2)}) %copy-start) | copy-done | bytes 2621464
  26.5 1.1 %copy-done.8 = bf16[1,256,1280]{2,1,0:T(8,128)(2,1)S(1)} copy-done((bf16[1,256,1280]{2,1,0:T(8,128)(2,1)S(1)}, bf16[1,256,1280]{2,1,0:T(8,128)(2,1)}, u32[]{:S(2)}) %copy-start.8) | copy-done | bytes 655384
  27.6 3.4 %project_own.1.refs_4_ = bf16[256,1024]{1,0:T(8,128)(2,1)S(1)} custom-call(s32[1,256]{1,0:T(1,128)S(1)} %multiply_add_fusion.meta.refs_0_, bf16[256,1280]{1,0:T(8,128)(2,1)S(1)} %bitcast.21, bf16[1280,1024]{1,0:T(8,128)(2,1)S(1)} %copy-done, bf16[1280,1024]{1,0:T(8,128)(2,1)} %wf.5, bf16[1,1024]{1,0:T(2,128)(2,1)S(1)} %broadcast_in_dim.16.b_audio.ba, ...), custom_call_target="tpu_custom_call" | custom-call | flops 1342177280 | bytes 1179648 | tf_op jit(solution)/shard_map/project_own/pallas_call | solution.py:48
  31.0 2.6 %collective-permute-done.7.mine = bf16[128,1280]{1,0:T(8,128)(2,1)} collective-permute-done((bf16[128,1280]{1,0:T(8,128)(2,1)}, bf16[128,1280]{1,0:T(8,128)(2,1)}, u32[]{:S(2)}, u32[]{:S(2)}) %collective-permute-start.7) | collective-permute-done | bytes 327712 | tf_op jit(solution)/shard_map/ppermute | solution.py:141
  33.6 0.1 pad_add_fusion.3.scalars
  33.6 0.5 collective-permute-start.4
  34.2 0.1 pad_add_fusion.2.scalars
  34.2 0.9 collective-permute-start
  35.1 0.0 collective-permute-done.6.other
  35.1 3.5 %project_halves.4.refs_6_ = bf16[256,1024]{1,0:T(8,128)(2,1)S(1)} custom-call(s32[1]{0:T(128)} %bitcast.11.scalars, s32[1,256]{1,0:T(1,128)S(1)} %collective-permute-done.1.meta.refs_2_, bf16[128,1280]{1,0:T(8,128)(2,1)} %collective-permute-done.5.mine, bf16[128,1280]{1,0:T(8,128)(2,1)} %collective-permute-done.6.other, bf16[1280,1024]{1,0:T(8,128)(2,1)S(1)} %copy-done.1, ...), custom_call_target="tpu_custom_call" | custom-call | flops 1342177280 | bytes 1179648 | tf_op jit(solution)/shard_map/project_halves/pallas_call | solution.py:57
  38.7 0.0 collective-permute-done.8.other
  38.7 3.7 %project_halves.5.refs_7_ = bf16[256,1024]{1,0:T(8,128)(2,1)S(1)} custom-call(s32[1]{0:T(128)} %bitcast.11.scalars, s32[1,256]{1,0:T(1,128)S(1)} %collective-permute-done.2.meta.refs_3_, bf16[128,1280]{1,0:T(8,128)(2,1)} %collective-permute-done.7.mine, bf16[128,1280]{1,0:T(8,128)(2,1)} %collective-permute-done.8.other, bf16[1280,1024]{1,0:T(8,128)(2,1)S(1)} %copy-done.1, ...), custom_call_target="tpu_custom_call" | custom-call | flops 1342177280 | bytes 1179648 | tf_op jit(solution)/shard_map/project_halves/pallas_call | solution.py:57
  42.4 3.6 %project_halves.3.refs_5_ = bf16[256,1024]{1,0:T(8,128)(2,1)S(1)} custom-call(s32[1]{0:T(128)} %bitcast.11.scalars, s32[1,256]{1,0:T(1,128)S(1)} %collective-permute-done.meta.refs_1_, bf16[128,1280]{1,0:T(8,128)(2,1)S(1)} %collective-permute-done.3.mine, bf16[128,1280]{1,0:T(8,128)(2,1)} %collective-permute-done.4.other, bf16[1280,1024]{1,0:T(8,128)(2,1)S(1)} %copy-done.1, ...), custom_call_target="tpu_custom_call" | custom-call | flops 1342177280 | bytes 1179648 | tf_op jit(solution)/shard_map/project_halves/pallas_call | solution.py:57
  46.0 0.0 copy-start.6
  46.0 1.3 %select.7 = (bf16[128,1024]{1,0:T(8,128)(2,1)S(1)}, bf16[128,1024]{1,0:T(8,128)(2,1)S(1)}) custom-call(s32[2]{0:T(128)S(1)} %pad_add_fusion.3.scalars, s32[1,256]{1,0:T(1,128)S(1)} %multiply_add_fusion.meta.refs_0_, s32[1,256]{1,0:T(1,128)S(1)} %collective-permute-done.meta.refs_1_, s32[1,256]{1,0:T(1,128)S(1)} %collective-permute-done.1.meta.refs_2_, ...), custom_call_target="tpu_custom_call" | custom-call | flops 536870912 | bytes 2097152 | tf_op jit(solution)/shard_map/select/pallas_call | solution.py:86
  47.3 0.2 collective-permute-start.15
  47.5 1.3 %select.6 = (bf16[128,1024]{1,0:T(8,128)(2,1)S(1)}, bf16[128,1024]{1,0:T(8,128)(2,1)S(1)}) custom-call(s32[2]{0:T(128)S(1)} %pad_add_fusion.2.scalars, s32[1,256]{1,0:T(1,128)S(1)} %multiply_add_fusion.meta.refs_0_, s32[1,256]{1,0:T(1,128)S(1)} %collective-permute-done.meta.refs_1_, s32[1,256]{1,0:T(1,128)S(1)} %collective-permute-done.1.meta.refs_2_, ...), custom_call_target="tpu_custom_call" | custom-call | flops 536870912 | bytes 2097152 | tf_op jit(solution)/shard_map/select/pallas_call | solution.py:86
  48.8 0.0 copy-start.9
  48.8 1.0 collective-permute-start.13
  49.8 0.1 pad_add_fusion.1.scalars
  49.9 0.1 pad_add_fusion.scalars
  50.0 0.7 collective-permute-start.14
  50.7 1.0 copy-done.3
  51.7 1.0 copy-done.5
  52.8 1.0 copy-done.7
  53.8 1.9 %select.5 = (bf16[128,1024]{1,0:T(8,128)(2,1)}, bf16[128,1024]{1,0:T(8,128)(2,1)S(1)}) custom-call(s32[2]{0:T(128)S(1)} %pad_add_fusion.1.scalars, s32[1,256]{1,0:T(1,128)S(1)} %multiply_add_fusion.meta.refs_0_, s32[1,256]{1,0:T(1,128)S(1)} %collective-permute-done.meta.refs_1_, s32[1,256]{1,0:T(1,128)S(1)} %collective-permute-done.1.meta.refs_2_, ...), custom_call_target="tpu_custom_call" | custom-call | flops 536870912 | bytes 2097152 | tf_op jit(solution)/shard_map/select/pallas_call | solution.py:86
  55.7 0.3 collective-permute-start.11
  56.0 2.4 %collective-permute-start.12 = (bf16[128,1024]{1,0:T(8,128)(2,1)S(1)}, bf16[128,1024]{1,0:T(8,128)(2,1)S(1)}, u32[]{:S(2)}, u32[]{:S(2)}) collective-permute-start(bf16[128,1024]{1,0:T(8,128)(2,1)S(1)} %get-tuple-element.16), channel_id=1, source_target_pairs={{0,9},{1,8},{4,13},{5,12},{8,1},{9,0},{12,5},{13,4},{2,11},{3,10},... | collective-permute-start | bytes 786440 | tf_op jit(solution)/shard_map/ppermute | solution.py:166
  58.4 2.0 %select.4 = (bf16[128,1024]{1,0:T(8,128)(2,1)}, bf16[128,1024]{1,0:T(8,128)(2,1)}) custom-call(s32[2]{0:T(128)S(1)} %pad_add_fusion.scalars, s32[1,256]{1,0:T(1,128)S(1)} %multiply_add_fusion.meta.refs_0_, s32[1,256]{1,0:T(1,128)S(1)} %collective-permute-done.meta.refs_1_, s32[1,256]{1,0:T(1,128)S(1)} %collective-permute-done.1.meta.refs_2_, ...), custom_call_target="tpu_custom_call" | custom-call | flops 536870912 | bytes 2097152 | tf_op jit(solution)/shard_map/select/pallas_call | solution.py:86
  60.5 0.4 collective-permute-start.10
  60.9 1.5 %collective-permute-start.9 = (bf16[128,1024]{1,0:T(8,128)(2,1)}, bf16[128,1024]{1,0:T(8,128)(2,1)S(1)}, u32[]{:S(2)}, u32[]{:S(2)}) collective-permute-start(bf16[128,1024]{1,0:T(8,128)(2,1)} %get-tuple-element.13), channel_id=1, source_target_pairs={{0,12},{1,13},{4,8},{5,9},{8,4},{9,5},{12,0},{13,1},{2,14},{3,15},... | collective-permute-start | bytes 786440 | tf_op jit(solution)/shard_map/ppermute | solution.py:166
  62.5 0.1 stack.71.blocks
  62.5 2.7 %collective-permute-done.14.refs_5_ = bf16[128,1024]{1,0:T(8,128)(2,1)S(1)} collective-permute-done((bf16[128,1024]{1,0:T(8,128)(2,1)S(1)}, bf16[128,1024]{1,0:T(8,128)(2,1)S(1)}, u32[]{:S(2)}, u32[]{:S(2)}) %collective-permute-start.14) | collective-permute-done | bytes 262176 | tf_op jit(solution)/shard_map/ppermute | solution.py:166
  65.2 20.3 %collective-permute-done.11.refs_2_ = bf16[128,1024]{1,0:T(8,128)(2,1)S(1)} collective-permute-done((bf16[128,1024]{1,0:T(8,128)(2,1)}, bf16[128,1024]{1,0:T(8,128)(2,1)S(1)}, u32[]{:S(2)}, u32[]{:S(2)}) %collective-permute-start.11) | collective-permute-done | bytes 262176 | tf_op jit(solution)/shard_map/ppermute | solution.py:166
  85.5 5.5 %collective-permute-done.12.refs_3_ = bf16[128,1024]{1,0:T(8,128)(2,1)S(1)} collective-permute-done((bf16[128,1024]{1,0:T(8,128)(2,1)S(1)}, bf16[128,1024]{1,0:T(8,128)(2,1)S(1)}, u32[]{:S(2)}, u32[]{:S(2)}) %collective-permute-start.12) | collective-permute-done | bytes 262176 | tf_op jit(solution)/shard_map/ppermute | solution.py:166
  91.0 7.2 %collective-permute-done.10.refs_1_ = bf16[128,1024]{1,0:T(8,128)(2,1)S(1)} collective-permute-done((bf16[128,1024]{1,0:T(8,128)(2,1)}, bf16[128,1024]{1,0:T(8,128)(2,1)S(1)}, u32[]{:S(2)}, u32[]{:S(2)}) %collective-permute-start.10) | collective-permute-done | bytes 262176 | tf_op jit(solution)/shard_map/ppermute | solution.py:166
  98.2 6.2 %collective-permute-done.9.refs_0_ = bf16[128,1024]{1,0:T(8,128)(2,1)S(1)} collective-permute-done((bf16[128,1024]{1,0:T(8,128)(2,1)}, bf16[128,1024]{1,0:T(8,128)(2,1)S(1)}, u32[]{:S(2)}, u32[]{:S(2)}) %collective-permute-start.9) | collective-permute-done | bytes 262176 | tf_op jit(solution)/shard_map/ppermute | solution.py:166
  104.4 3.0 %norm.1 = bf16[128,8192]{1,0:T(8,128)(2,1)} custom-call(s32[8]{0:T(128)S(1)} %stack.71.blocks, bf16[1,8192]{1,0:T(2,128)(2,1)S(1)} %broadcast_in_dim.15.gain, bf16[128,1024]{1,0:T(8,128)(2,1)S(1)} %collective-permute-done.9.refs_0_, bf16[128,1024]{1,0:T(8,128)(2,1)S(1)} %collective-permute-done.10.refs_1_, ...), custom_call_target="tpu_custom_call" | custom-call | flops 4194304 | bytes 4194304 | tf_op jit(solution)/shard_map/norm/pallas_call | solution.py:117
  (23 shorter events, 0.1 us)
Async XLA Ops:
  1.7 23.0 %collective-permute-start.5 = (bf16[128,1280]{1,0:T(8,128)(2,1)}, bf16[128,1280]{1,0:T(8,128)(2,1)}, u32[]{:S(2)}, u32[]{:S(2)}) collective-permute-start(bf16[128,1280]{1,0:T(8,128)(2,1)} %dynamic-slice_bitcast_fusion), channel_id=1, source_target_pairs={{0,8},{4,12},{8,0},{12,4},{1,9},{5,13},{9,1},{13,5},{2,10},{6,14},... | collective-permute-start | bytes 983048 | tf_op jit(solution)/shard_map/ppermute | solution.py:141
  2.1 31.5 %collective-permute-start.7 = (bf16[128,1280]{1,0:T(8,128)(2,1)}, bf16[128,1280]{1,0:T(8,128)(2,1)}, u32[]{:S(2)}, u32[]{:S(2)}) collective-permute-start(bf16[128,1280]{1,0:T(8,128)(2,1)} %dynamic-slice_bitcast_fusion), channel_id=1, source_target_pairs={{0,12},{4,8},{8,4},{12,0},{1,13},{5,9},{9,5},{13,1},{2,14},{6,10},... | collective-permute-start | bytes 983048 | tf_op jit(solution)/shard_map/ppermute | solution.py:141
  4.8 28.9 %collective-permute-start.3 = (bf16[128,1280]{1,0:T(8,128)(2,1)}, bf16[128,1280]{1,0:T(8,128)(2,1)S(1)}, u32[]{:S(2)}, u32[]{:S(2)}) collective-permute-start(bf16[128,1280]{1,0:T(8,128)(2,1)} %dynamic-slice_bitcast_fusion), channel_id=1, source_target_pairs={{0,4},{4,0},{8,12},{12,8},{1,5},{5,1},{9,13},{13,9},{2,6},{6,2},{1... | collective-permute-start | bytes 983048 | tf_op jit(solution)/shard_map/ppermute | solution.py:141
  6.8 27.4 %collective-permute-start.1 = (s32[1,256]{1,0:T(1,128)S(1)}, s32[1,256]{1,0:T(1,128)S(1)}, u32[]{:S(2)}, u32[]{:S(2)}) collective-permute-start(s32[1,256]{1,0:T(1,128)S(1)} %multiply_add_fusion.meta.refs_0_), channel_id=1, source_target_pairs={{0,8},{4,12},{8,0},{12,4},{1,9},{5,13},{9,1},{13,5},{2,10},{6,14},... | collective-permute-start | bytes 3080 | tf_op jit(solution)/shard_map/ppermute | solution.py:141
  6.9 31.8 %collective-permute-start.2 = (s32[1,256]{1,0:T(1,128)S(1)}, s32[1,256]{1,0:T(1,128)S(1)}, u32[]{:S(2)}, u32[]{:S(2)}) collective-permute-start(s32[1,256]{1,0:T(1,128)S(1)} %multiply_add_fusion.meta.refs_0_), channel_id=1, source_target_pairs={{0,12},{4,8},{8,4},{12,0},{1,13},{5,9},{9,5},{13,1},{2,14},{6,10},... | collective-permute-start | bytes 3080 | tf_op jit(solution)/shard_map/ppermute | solution.py:141
  24.7 10.4 %collective-permute-start.6 = (bf16[128,1280]{1,0:T(8,128)(2,1)}, bf16[128,1280]{1,0:T(8,128)(2,1)}, u32[]{:S(2)}, u32[]{:S(2)}) collective-permute-start(bf16[128,1280]{1,0:T(8,128)(2,1)} %collective-permute-done.5.mine), channel_id=1, source_target_pairs={{0,1},{1,0},{2,3},{3,2},{4,5},{5,4},{6,7},{7,6},{8,9},{9,8},{10,11... | collective-permute-start | bytes 983048 | tf_op jit(solution)/shard_map/ppermute | solution.py:144
  24.7 1.7 %copy-start = (bf16[1280,1024]{1,0:T(8,128)(2,1)S(1)}, bf16[1280,1024]{1,0:T(8,128)(2,1)}, u32[]{:S(2)}) copy-start(bf16[1280,1024]{1,0:T(8,128)(2,1)} %wa.5) | copy-start | bytes 7864324
  26.5 1.1 %copy-start.8 = (bf16[1,256,1280]{2,1,0:T(8,128)(2,1)S(1)}, bf16[1,256,1280]{2,1,0:T(8,128)(2,1)}, u32[]{:S(2)}) copy-start(bf16[1,256,1280]{2,1,0:T(8,128)(2,1)} %param.8) | copy-start | bytes 1966084
  27.6 7.6 %copy-start.1 = (bf16[1280,1024]{1,0:T(8,128)(2,1)S(1)}, bf16[1280,1024]{1,0:T(8,128)(2,1)}, u32[]{:S(2)}) copy-start(bf16[1280,1024]{1,0:T(8,128)(2,1)} %wa.5) | copy-start | bytes 7864324
  33.6 5.1 %collective-permute-start.8 = (bf16[128,1280]{1,0:T(8,128)(2,1)}, bf16[128,1280]{1,0:T(8,128)(2,1)}, u32[]{:S(2)}, u32[]{:S(2)}) collective-permute-start(bf16[128,1280]{1,0:T(8,128)(2,1)} %collective-permute-done.7.mine), channel_id=1, source_target_pairs={{0,1},{1,0},{2,3},{3,2},{4,5},{5,4},{6,7},{7,6},{8,9},{9,8},{10,11... | collective-permute-start | bytes 983048 | tf_op jit(solution)/shard_map/ppermute | solution.py:144
  33.6 8.8 %collective-permute-start.4 = (bf16[128,1280]{1,0:T(8,128)(2,1)S(1)}, bf16[128,1280]{1,0:T(8,128)(2,1)}, u32[]{:S(2)}, u32[]{:S(2)}) collective-permute-start(bf16[128,1280]{1,0:T(8,128)(2,1)S(1)} %collective-permute-done.3.mine), channel_id=1, source_target_pairs={{0,1},{1,0},{2,3},{3,2},{4,5},{5,4},{6,7},{7,6},{8,9},{9,8},{10,11... | collective-permute-start | bytes 983048 | tf_op jit(solution)/shard_map/ppermute | solution.py:144
  34.2 8.2 %collective-permute-start = (s32[1,256]{1,0:T(1,128)S(1)}, s32[1,256]{1,0:T(1,128)S(1)}, u32[]{:S(2)}, u32[]{:S(2)}) collective-permute-start(s32[1,256]{1,0:T(1,128)S(1)} %multiply_add_fusion.meta.refs_0_), channel_id=1, source_target_pairs={{0,4},{4,0},{8,12},{12,8},{1,5},{5,1},{9,13},{13,9},{2,6},{6,2},{1... | collective-permute-start | bytes 3080 | tf_op jit(solution)/shard_map/ppermute | solution.py:141
  38.7 8.8 %copy-start.2 = (bf16[256,1024]{1,0:T(8,128)(2,1)}, bf16[256,1024]{1,0:T(8,128)(2,1)S(1)}, u32[]{:S(2)}) copy-start(bf16[256,1024]{1,0:T(8,128)(2,1)S(1)} %project_halves.4.refs_6_) | copy-start | bytes 1572868
  42.4 5.1 %copy-start.4 = (bf16[256,1024]{1,0:T(8,128)(2,1)}, bf16[256,1024]{1,0:T(8,128)(2,1)S(1)}, u32[]{:S(2)}) copy-start(bf16[256,1024]{1,0:T(8,128)(2,1)S(1)} %project_halves.5.refs_7_) | copy-start | bytes 1572868
  46.0 2.8 %copy-start.6 = (bf16[256,1024]{1,0:T(8,128)(2,1)}, bf16[256,1024]{1,0:T(8,128)(2,1)S(1)}, u32[]{:S(2)}) copy-start(bf16[256,1024]{1,0:T(8,128)(2,1)S(1)} %project_halves.3.refs_5_) | copy-start | bytes 1572868
  47.3 13.2 %collective-permute-start.15 = (bf16[128,1024]{1,0:T(8,128)(2,1)S(1)}, bf16[128,1024]{1,0:T(8,128)(2,1)S(1)}, u32[]{:S(2)}, u32[]{:S(2)}) collective-permute-start(bf16[128,1024]{1,0:T(8,128)(2,1)S(1)} %get-tuple-element.20), channel_id=1, source_target_pairs={{0,1},{1,0},{4,5},{5,4},{8,9},{9,8},{12,13},{13,12},{2,3},{3,2},{6... | collective-permute-start | bytes 786440 | tf_op jit(solution)/shard_map/ppermute | solution.py:166
  48.8 13.7 %copy-start.9 = (bf16[8192]{0:T(1024)(128)(2,1)S(1)}, bf16[8192]{0:T(1024)(128)(2,1)}, u32[]{:S(2)}) copy-start(bf16[8192]{0:T(1024)(128)(2,1)} %param.15) | copy-start | bytes 49156
  48.8 12.1 %collective-permute-start.13 = (bf16[128,1024]{1,0:T(8,128)(2,1)S(1)}, bf16[128,1024]{1,0:T(8,128)(2,1)S(1)}, u32[]{:S(2)}, u32[]{:S(2)}) collective-permute-start(bf16[128,1024]{1,0:T(8,128)(2,1)S(1)} %get-tuple-element.17), channel_id=1, source_target_pairs={{0,4},{1,5},{4,0},{5,1},{8,12},{9,13},{12,8},{13,9},{2,6},{3,7},{6... | collective-permute-start | bytes 786440 | tf_op jit(solution)/shard_map/ppermute | solution.py:166
  50.0 15.2 %collective-permute-start.14 = (bf16[128,1024]{1,0:T(8,128)(2,1)S(1)}, bf16[128,1024]{1,0:T(8,128)(2,1)S(1)}, u32[]{:S(2)}, u32[]{:S(2)}) collective-permute-start(bf16[128,1024]{1,0:T(8,128)(2,1)S(1)} %get-tuple-element.18), channel_id=1, source_target_pairs={{0,5},{1,4},{4,1},{5,0},{8,13},{9,12},{12,9},{13,8},{2,7},{3,6},{6... | collective-permute-start | bytes 786440 | tf_op jit(solution)/shard_map/ppermute | solution.py:166
  50.7 1.0 copy-start.3
  51.7 1.0 copy-start.5
  52.8 1.0 copy-start.7
  55.7 29.7 %collective-permute-start.11 = (bf16[128,1024]{1,0:T(8,128)(2,1)}, bf16[128,1024]{1,0:T(8,128)(2,1)S(1)}, u32[]{:S(2)}, u32[]{:S(2)}) collective-permute-start(bf16[128,1024]{1,0:T(8,128)(2,1)} %get-tuple-element.15), channel_id=1, source_target_pairs={{0,8},{1,9},{4,12},{5,13},{8,0},{9,1},{12,4},{13,5},{2,10},{3,11},... | collective-permute-start | bytes 786440 | tf_op jit(solution)/shard_map/ppermute | solution.py:166
  56.0 35.0 %collective-permute-start.12 = (bf16[128,1024]{1,0:T(8,128)(2,1)S(1)}, bf16[128,1024]{1,0:T(8,128)(2,1)S(1)}, u32[]{:S(2)}, u32[]{:S(2)}) collective-permute-start(bf16[128,1024]{1,0:T(8,128)(2,1)S(1)} %get-tuple-element.16), channel_id=1, source_target_pairs={{0,9},{1,8},{4,13},{5,12},{8,1},{9,0},{12,5},{13,4},{2,11},{3,10},... | collective-permute-start | bytes 786440 | tf_op jit(solution)/shard_map/ppermute | solution.py:166
  60.5 37.7 %collective-permute-start.10 = (bf16[128,1024]{1,0:T(8,128)(2,1)}, bf16[128,1024]{1,0:T(8,128)(2,1)S(1)}, u32[]{:S(2)}, u32[]{:S(2)}) collective-permute-start(bf16[128,1024]{1,0:T(8,128)(2,1)} %get-tuple-element.14), channel_id=1, source_target_pairs={{0,13},{1,12},{4,9},{5,8},{8,5},{9,4},{12,1},{13,0},{2,15},{3,14},... | collective-permute-start | bytes 786440 | tf_op jit(solution)/shard_map/ppermute | solution.py:166
  60.9 43.5 %collective-permute-start.9 = (bf16[128,1024]{1,0:T(8,128)(2,1)}, bf16[128,1024]{1,0:T(8,128)(2,1)S(1)}, u32[]{:S(2)}, u32[]{:S(2)}) collective-permute-start(bf16[128,1024]{1,0:T(8,128)(2,1)} %get-tuple-element.13), channel_id=1, source_target_pairs={{0,12},{1,13},{4,8},{5,9},{8,4},{9,5},{12,0},{13,1},{2,14},{3,15},... | collective-permute-start | bytes 786440 | tf_op jit(solution)/shard_map/ppermute | solution.py:166

commit v2 on v0

v2 whole, which is shorter than its diff:
```python
import functools

import jax
import jax.numpy as jnp
from jax import lax
from jax.experimental import pallas as pl
from jax.experimental.pallas import tpu as pltpu
from jax.sharding import PartitionSpec as P

VMEM = pl.BlockSpec(memory_space=pltpu.VMEM)
HBM = pl.BlockSpec(memory_space=pltpu.HBM)
PARAMS = pltpu.CompilerParams(vmem_limit_bytes=12 << 20)
BF16, F32, I32 = jnp.bfloat16, jnp.float32, jnp.int32


def cost(flops, moved):
    return pl.CostEstimate(flops=flops, bytes_accessed=moved, transcendentals=0)


def half_kernel(rows, out, sem):
    half = out.shape[0]
    start = pl.multiple_of(lax.axis_index("tp") * half, half)
    copy = pltpu.make_async_copy(rows.at[pl.ds(start, half), :], out, sem)
    copy.start()
    copy.wait()


def own_half(rows, half):
    width = rows.shape[1]
    return pl.pallas_call(
        half_kernel,
        out_shape=jax.ShapeDtypeStruct((half, width), BF16),
        in_specs=[HBM],
        out_specs=VMEM,
        scratch_shapes=[pltpu.SemaphoreType.DMA],
        compiler_params=pltpu.CompilerParams(vmem_limit_bytes=4 << 20),
        cost_estimate=cost(0, 4 * half * width),
        name="own_half",
    )(rows)


def column_of(row_vector):
    r = row_vector.shape[1]
    diagonal = lax.broadcasted_iota(I32, (r, r), 0) == lax.broadcasted_iota(I32, (r, r), 1)
    return jnp.sum(jnp.where(diagonal, row_vector, 0), axis=1, keepdims=True)


def project(kind_row, x, w_audio, w_frame, b_audio, b_frame, out):
    is_audio = column_of(kind_row) == 0
    audio = jnp.dot(x, w_audio[...], preferred_element_type=F32)
    frame = jnp.dot(x, w_frame[...], preferred_element_type=F32)
    audio = audio + b_audio[...].astype(F32)
    frame = frame + b_frame[...].astype(F32)
    out[...] = jnp.where(is_audio, audio, frame).astype(out.dtype)


def project_own_kernel(meta, x, wa, wf, ba, bf, out):
    project(meta[...] % 2, x[...], wa, wf, ba, bf, out)


def project_own(meta, rows, weights):
    ew, cols = weights[0].shape
    return pl.pallas_call(
        project_own_kernel,
        out_shape=jax.ShapeDtypeStruct((rows.shape[0], cols), BF16),
        in_specs=[VMEM] * 6,
        out_specs=VMEM,
        compiler_params=PARAMS,
        cost_estimate=cost(4 * rows.shape[0] * ew * cols, 4 * ew * cols),
        name="project_own",
    )(meta, rows, *weights)


def project_step_kernel(step, n, metas, *refs):
    arrivals, weights, outs, x = refs[:4], refs[4:8], refs[8:10], refs[10]
    half = arrivals[0].shape[0]
    z, t = lax.axis_index("ctx"), lax.axis_index("tp")
    for side, owner in ((0, z - step), (1, z + step)):

        @pl.when(jnp.logical_and(owner >= 0, owner < n))
        def _():
            x[pl.ds(pl.multiple_of(t * half, half), half), :] = arrivals[2 * side][...]
            x[pl.ds(pl.multiple_of((1 - t) * half, half), half), :] = arrivals[2 * side + 1][...]
            meta = metas[pl.ds(jnp.bitwise_xor(owner, z), 1), :]
            project(meta % 2, x[...], *weights, outs[side])


def project_step(step, n, metas, arrivals, weights):
    half, ew = arrivals[0].shape
    cols = weights[0].shape[1]
    return pl.pallas_call(
        functools.partial(project_step_kernel, step, n),
        out_shape=[jax.ShapeDtypeStruct((2 * half, cols), BF16)] * 2,
        in_specs=[VMEM] * 9,
        out_specs=[VMEM] * 2,
        scratch_shapes=[pltpu.VMEM((2 * half, ew), BF16)],
        compiler_params=PARAMS,
        cost_estimate=cost(12 * half * ew * cols, 4 * ew * cols),
        name="project_step",
    )(metas, *arrivals, *weights)


def select_kernel(m, n, metas, own, *refs):
    sides, outs = refs[: 2 * n - 2], refs[2 * n - 2 :]
    places = outs[0].shape[0]
    z, t = lax.axis_index("ctx"), lax.axis_index("tp")
    first = jnp.bitwise_xor(z, m) * 2 * places
    i = lax.broadcasted_iota(I32, (2 * places, 1), 0)
    position = first + jnp.bitwise_xor(i, t * places)
    total = None
    for s in range(n):
        owner = lax.rem(z - s + n, n)
        if s == 0:
            block = own[...]
        else:
            block = jnp.where(z >= s, sides[2 * (s - 1)][...], sides[2 * (n - s - 1) + 1][...])
        meta = metas[pl.ds(jnp.bitwise_xor(owner, z), 1), :]
        chosen = (meta // 2 == position).astype(F32).astype(BF16)
        part = jnp.dot(chosen, block, preferred_element_type=F32)
        total = part if total is None else total + part
    outs[0][...] = total[:places].astype(BF16)
    outs[1][...] = total[places:].astype(BF16)


def select(m, n, metas, own, sides, places):
    rows, cols = own.shape
    return pl.pallas_call(
        functools.partial(select_kernel, m, n),
        out_shape=[jax.ShapeDtypeStruct((places, cols), BF16)] * 2,
        in_specs=[VMEM] * (2 * n),
        out_specs=[VMEM] * 2,
        compiler_params=PARAMS,
        cost_estimate=cost(4 * places * rows * n * cols, 2 * n * rows * cols),
        name="select",
    )(metas, own, *sides)


def norm_kernel(places_of, gain, *refs):
    n = len(places_of)
    pieces, out = refs[:n], refs[n]
    cols = pieces[0].shape[1]
    z, t = lax.axis_index("ctx"), lax.axis_index("tp")
    total = None
    for piece in pieces:
        wide = piece[...].astype(F32)
        part = jnp.sum(wide * wide, axis=1, keepdims=True)
        total = part if total is None else total + part
    scale = lax.rsqrt(total / (n * cols) + 1e-06)
    for (m, d), piece in zip(places_of, pieces):
        block = jnp.bitwise_xor(z, m) * 2 + jnp.bitwise_xor(t, d)
        at = pl.ds(pl.multiple_of(block * cols, cols), cols)
        out[:, at] = (piece[...].astype(F32) * scale * gain[:, at].astype(F32)).astype(out.dtype)


def norm(places_of, gain, pieces):
    n = len(pieces)
    places, cols = pieces[0].shape
    return pl.pallas_call(
        functools.partial(norm_kernel, places_of),
        out_shape=jax.ShapeDtypeStruct((places, n * cols), BF16),
        in_specs=[VMEM] * (n + 1),
        out_specs=VMEM,
        compiler_params=PARAMS,
        cost_estimate=cost(4 * places * n * cols, 4 * places * n * cols),
        name="norm",
    )(gain, *pieces)


def after(x, *others):
    return lax.optimization_barrier((x, *others))[0]


def body(enc_rows, row_slot, row_kind, audio_proj, frame_proj, audio_bias, frame_bias, norm_gain):
    n_ctx = lax.axis_size("ctx")
    rows = enc_rows[0]
    half = rows.shape[0] // 2
    weights = (audio_proj, frame_proj, audio_bias[None, :], frame_bias[None, :])

    def over_tp(x):
        return lax.ppermute(x, "tp", [(0, 1), (1, 0)])

    meta = row_slot * 2 + row_kind
    mine = own_half(rows, half)
    metas, m = meta, 1
    while m < n_ctx:
        met = lax.ppermute(metas, "ctx", [(i, i ^ m) for i in range(n_ctx)])
        metas = jnp.concatenate([metas, met], axis=0)
        m *= 2

    own = project_own(meta, rows, weights)
    sides, left, right, done = [], mine, mine, own
    for step in range(1, n_ctx):
        left = lax.ppermute(left, "ctx", [(i, i + 1) for i in range(step - 1, n_ctx - 1)])
        right = lax.ppermute(right, "ctx", [(i + 1, i) for i in range(n_ctx - step)])
        left, right = after(left, done), after(right, done)
        arrivals = (left, over_tp(left), right, over_tp(right))
        sides += project_step(step, n_ctx, metas, arrivals, weights)
        done = sides[-1]

    pieces, places_of = [], []
    for m in [1] + list(reversed(range(2, n_ctx))) + [0]:
        for d, piece in enumerate(select(m, n_ctx, metas, own, sides, half)):
            if m or d:
                perm = [
                    (i * 2 + c, (i ^ m) * 2 + (c ^ d)) for i in range(n_ctx) for c in range(2)
                ]
                piece = lax.ppermute(piece, ("ctx", "tp"), perm)
            pieces.append(piece)
            places_of.append((m, d))
    return norm(tuple(places_of), norm_gain[None, :], pieces)[None]


def solution(mesh):
    return jax.shard_map(
        body,
        mesh=mesh,
        in_specs=(
            P(("groups", "enc"), "ctx", None),
            P(("groups", "enc"), "ctx"),
            P(("groups", "enc"), "ctx"),
            P(None, ("ctx", "tp")),
            P(None, ("ctx", "tp")),
            P(("ctx", "tp")),
            P(("ctx", "tp")),
            P(),
        ),
        out_specs=P(("groups", "enc"), ("ctx", "tp"), None),
        check_vma=False,
    )
```

time: 196 us -> 101 us (0.52)
  the two profiles are of different devices: /device:TPU:0 before, /device:TPU:9 now
where the time goes in v2:
time: 101 us; the launch traced here: 100 us
  waiting for transfers between devices  47.6 us (47%)
  starting transfers between devices  32.4 us (32%)
  Pallas kernels  12.1 us (12%)
  local copies, waits for them, and re-layouts  7.06 us (7%)
    ppermute x7, waiting for transfers between devices, body(): piece = lax.ppermute(piece, ('ctx', 'tp'), perm)  34.9 us
    ppermute x7, starting transfers between devices, body(): piece = lax.ppermute(piece, ('ctx', 'tp'), perm)  15.2 us
    ppermute x3, starting transfers between devices, body(): lax.ppermute(right, 'ctx', [(i + 1, i) for i in range(n_ctx - step)])  6.57 us
    ppermute x2, waiting for transfers between devices, body(): met = lax.ppermute(metas, 'ctx', [(i, i ^ m) for i in range(n_ctx)])  6.31 us
    ppermute x3, starting transfers between devices, body(): lax.ppermute(left, 'ctx', [(i, i + 1) for i in range(step - 1, n_ctx - 1)])  6.04 us
    unnamed x14, local copies, waits for them, and re-layouts  5.67 us
    pallas_call x3, Pallas kernels, project_step(): pl.pallas_call(functools.partial(project_step_kernel, step, n), out_shape...  4.81 us
    ppermute x3, waiting for transfers between devices, body(): lax.ppermute(right, 'ctx', [(i + 1, i) for i in range(n_ctx - step)])  4.62 us
  transfers between devices with their start and end apart: 21, of which 8 were waited for; matrix products, arithmetic and copies ran while one was open for 2% of the time, Pallas kernels for 9%

profile of v2, /device:TPU:9, one launch (start us, length us, event | category | flops | bytes accessed | tf_op | source)
XLA Modules:
  0.0 100.1 jit_solution(14030626804829901757)
XLA Ops:
  0.0 1.1 %copy-done.4 = bf16[1,256,1280]{2,1,0:T(8,128)(2,1)S(1)} copy-done((bf16[1,256,1280]{2,1,0:T(8,128)(2,1)S(1)}, bf16[1,256,1280]{2,1,0:T(8,128)(2,1)}, u32[]{:S(2)}) %copy-start.4) | copy-done | bytes 655384
  1.1 0.1 own_half.1
  1.2 3.2 %collective-permute-start.2 = (bf16[128,1280]{1,0:T(8,128)(2,1)S(1)}, bf16[128,1280]{1,0:T(8,128)(2,1)S(1)}, u32[]{:S(2)}, u32[]{:S(2)}) collective-permute-start(bf16[128,1280]{1,0:T(8,128)(2,1)S(1)} %own_half.1), channel_id=1, source_target_pairs={{0,4},{4,8},{8,12},{1,5},{5,9},{9,13},{2,6},{6,10},{10,14},{3,7},{... | collective-permute-start | bytes 983048 | tf_op jit(solution)/shard_map/ppermute | solution.py:193
  4.4 2.1 %collective-permute-start.4 = (bf16[128,1280]{1,0:T(8,128)(2,1)S(1)}, bf16[128,1280]{1,0:T(8,128)(2,1)S(1)}, u32[]{:S(2)}, u32[]{:S(2)}) collective-permute-start(bf16[128,1280]{1,0:T(8,128)(2,1)S(1)} %own_half.1), channel_id=1, source_target_pairs={{4,0},{8,4},{12,8},{5,1},{9,5},{13,9},{6,2},{10,6},{14,10},{7,3},{... | collective-permute-start | bytes 983048 | tf_op jit(solution)/shard_map/ppermute | solution.py:194
  6.5 0.7 broadcast_in_dim.13.ba.refs_6_
  7.2 0.7 broadcast_in_dim.14.bf.refs_7_
  7.9 0.7 multiply_add_fusion.meta
  8.6 1.7 %copy-done = bf16[1280,1024]{1,0:T(8,128)(2,1)S(1)} copy-done((bf16[1280,1024]{1,0:T(8,128)(2,1)S(1)}, bf16[1280,1024]{1,0:T(8,128)(2,1)}, u32[]{:S(2)}) %copy-start) | copy-done | bytes 2621464
  10.3 1.7 %copy-done.2 = bf16[1280,1024]{1,0:T(8,128)(2,1)S(1)} copy-done((bf16[1280,1024]{1,0:T(8,128)(2,1)S(1)}, bf16[1280,1024]{1,0:T(8,128)(2,1)}, u32[]{:S(2)}) %copy-start.2) | copy-done | bytes 2621464
  12.1 1.1 %copy-done.5 = bf16[1,256,1280]{2,1,0:T(8,128)(2,1)S(1)} copy-done((bf16[1,256,1280]{2,1,0:T(8,128)(2,1)S(1)}, bf16[1,256,1280]{2,1,0:T(8,128)(2,1)}, u32[]{:S(2)}) %copy-start.5) | copy-done | bytes 655384
  13.2 1.6 %project_own.1.own = bf16[256,1024]{1,0:T(8,128)(2,1)S(1)} custom-call(s32[1,256]{1,0:T(1,128)S(1)} %multiply_add_fusion.meta, bf16[256,1280]{1,0:T(8,128)(2,1)S(1)} %bitcast.3, bf16[1280,1024]{1,0:T(8,128)(2,1)S(1)} %copy-done, bf16[1280,1024]{1,0:T(8,128)(2,1)S(1)} %copy-done.2, bf16[1,1024]{1,0:T(2,128)(2,1)S(1)} %broadcast_in_dim.13.ba.refs_6_, ...), custom_call_target="tpu_custom_call" | custom-call | flops 1342177280 | bytes 5242880 | tf_op jit(solution)/shard_map/project_own/pallas_call | solution.py:63
  14.7 0.0 collective-permute-done.2.refs_0_
  14.7 1.3 %collective-permute-start.3 = (bf16[128,1280]{1,0:T(8,128)(2,1)S(1)}, bf16[128,1280]{1,0:T(8,128)(2,1)S(1)}, u32[]{:S(2)}, u32[]{:S(2)}) collective-permute-start(bf16[128,1280]{1,0:T(8,128)(2,1)S(1)} %collective-permute-done.2.refs_0_), channel_id=1, source_target_pairs={{0,1},{1,0},{2,3},{3,2},{4,5},{5,4},{6,7},{7,6},{8,9},{9,8},{10,11... | collective-permute-start | bytes 983048 | tf_op jit(solution)/shard_map/ppermute | solution.py:180
  16.0 0.0 collective-permute-done.4.refs_2_
  16.0 0.4 collective-permute-start.5
  16.4 0.2 collective-permute-start
  16.6 3.2 %collective-permute-start.8 = (bf16[128,1280]{1,0:T(8,128)(2,1)S(1)}, bf16[128,1280]{1,0:T(8,128)(2,1)S(1)}, u32[]{:S(2)}, u32[]{:S(2)}) collective-permute-start(bf16[128,1280]{1,0:T(8,128)(2,1)S(1)} %collective-permute-done.4.refs_2_), channel_id=1, source_target_pairs={{4,0},{8,4},{5,1},{9,5},{6,2},{10,6},{7,3},{11,7},{20,16},{24,20},... | collective-permute-start | bytes 983048 | tf_op jit(solution)/shard_map/ppermute | solution.py:194
  19.8 2.2 %collective-permute-start.6 = (bf16[128,1280]{1,0:T(8,128)(2,1)S(1)}, bf16[128,1280]{1,0:T(8,128)(2,1)S(1)}, u32[]{:S(2)}, u32[]{:S(2)}) collective-permute-start(bf16[128,1280]{1,0:T(8,128)(2,1)S(1)} %collective-permute-done.2.refs_0_), channel_id=1, source_target_pairs={{4,8},{8,12},{5,9},{9,13},{6,10},{10,14},{7,11},{11,15},{20,24},{2... | collective-permute-start | bytes 983048 | tf_op jit(solution)/shard_map/ppermute | solution.py:193
  22.0 0.1 collective-permute-start.1
  22.1 6.3 %collective-permute-done.1 = s32[2,256]{1,0:T(2,128)S(1)} collective-permute-done((s32[2,256]{1,0:T(2,128)S(1)}, s32[2,256]{1,0:T(2,128)S(1)}, u32[]{:S(2)}, u32[]{:S(2)}) %collective-permute-start.1) | collective-permute-done | bytes 2080 | tf_op jit(solution)/shard_map/ppermute | solution.py:186
  28.4 3.2 %project_step.3 = (bf16[256,1024]{1,0:T(8,128)(2,1)S(1)}, bf16[256,1024]{1,0:T(8,128)(2,1)S(1)}) custom-call(s32[4,256]{1,0:T(4,128)S(1)} %pad_add_fusion.metas, bf16[128,1280]{1,0:T(8,128)(2,1)S(1)} %collective-permute-done.2.refs_0_, bf16[128,1280]{1,0:T(8,128)(2,1)S(1)} %collective-permute-done.3.refs_1_, ...), custom_call_target="tpu_custom_call" | custom-call | flops 2013265920 | bytes 5242880 | tf_op jit(solution)/shard_map/project_step/pallas_call | solution.py:91
  31.6 1.6 %collective-permute-start.9 = (bf16[128,1280]{1,0:T(8,128)(2,1)S(1)}, bf16[128,1280]{1,0:T(8,128)(2,1)S(1)}, u32[]{:S(2)}, u32[]{:S(2)}) collective-permute-start(bf16[128,1280]{1,0:T(8,128)(2,1)S(1)} %collective-permute-done.8.refs_2_), channel_id=1, source_target_pairs={{0,1},{1,0},{2,3},{3,2},{4,5},{5,4},{6,7},{7,6},{8,9},{9,8},{10,11... | collective-permute-start | bytes 983048 | tf_op jit(solution)/shard_map/ppermute | solution.py:180
  33.3 0.1 collective-permute-start.7
  33.4 1.3 %collective-permute-start.12 = (bf16[128,1280]{1,0:T(8,128)(2,1)S(1)}, bf16[128,1280]{1,0:T(8,128)(2,1)S(1)}, u32[]{:S(2)}, u32[]{:S(2)}) collective-permute-start(bf16[128,1280]{1,0:T(8,128)(2,1)S(1)} %collective-permute-done.8.refs_2_), channel_id=1, source_target_pairs={{4,0},{5,1},{6,2},{7,3},{20,16},{21,17},{22,18},{23,19}} | collective-permute-start | bytes 983048 | tf_op jit(solution)/shard_map/ppermute | solution.py:194
  34.7 0.7 collective-permute-start.10
  35.4 1.6 %project_step.4 = (bf16[256,1024]{1,0:T(8,128)(2,1)S(1)}, bf16[256,1024]{1,0:T(8,128)(2,1)S(1)}) custom-call(s32[4,256]{1,0:T(4,128)S(1)} %pad_add_fusion.metas, bf16[128,1280]{1,0:T(8,128)(2,1)S(1)} %collective-permute-done.6.refs_0_, bf16[128,1280]{1,0:T(8,128)(2,1)S(1)} %collective-permute-done.7.refs_1_, ...), custom_call_target="tpu_custom_call" | custom-call | flops 2013265920 | bytes 5242880 | tf_op jit(solution)/shard_map/project_step/pallas_call | solution.py:91
  37.0 4.6 %collective-permute-done.12.refs_2_ = bf16[128,1280]{1,0:T(8,128)(2,1)S(1)} collective-permute-done((bf16[128,1280]{1,0:T(8,128)(2,1)S(1)}, bf16[128,1280]{1,0:T(8,128)(2,1)S(1)}, u32[]{:S(2)}, u32[]{:S(2)}) %collective-permute-start.12) | collective-permute-done | bytes 327712 | tf_op jit(solution)/shard_map/ppermute | solution.py:194
  41.6 0.9 collective-permute-start.13
  42.5 0.0 collective-permute-start.11
  42.6 1.2 %collective-permute-done.13.refs_3_ = bf16[128,1280]{1,0:T(8,128)(2,1)S(1)} collective-permute-done((bf16[128,1280]{1,0:T(8,128)(2,1)S(1)}, bf16[128,1280]{1,0:T(8,128)(2,1)S(1)}, u32[]{:S(2)}, u32[]{:S(2)}) %collective-permute-start.13) | collective-permute-done | bytes 327712 | tf_op jit(solution)/shard_map/ppermute | solution.py:180
  43.8 0.5 collective-permute-done.11.refs_1_
  44.3 0.7 select.7
  45.0 0.4 collective-permute-start.20
  45.4 0.7 select.6
  46.2 6.4 %collective-permute-start.18 = (bf16[128,1024]{1,0:T(8,128)(2,1)S(1)}, bf16[128,1024]{1,0:T(8,128)(2,1)S(1)}, u32[]{:S(2)}, u32[]{:S(2)}) collective-permute-start(bf16[128,1024]{1,0:T(8,128)(2,1)S(1)} %get-tuple-element.41), channel_id=1, source_target_pairs={{0,8},{1,9},{4,12},{5,13},{8,0},{9,1},{12,4},{13,5},{2,10},{3,11},... | collective-permute-start | bytes 786440 | tf_op jit(solution)/shard_map/ppermute | solution.py:207
  52.6 0.1 collective-permute-start.19
  52.7 0.7 select.5
  53.4 0.0 copy-start.6
  53.4 0.1 collective-permute-start.16
  53.5 2.0 %collective-permute-start.17 = (bf16[128,1024]{1,0:T(8,128)(2,1)S(1)}, bf16[128,1024]{1,0:T(8,128)(2,1)S(1)}, u32[]{:S(2)}, u32[]{:S(2)}) collective-permute-start(bf16[128,1024]{1,0:T(8,128)(2,1)S(1)} %get-tuple-element.40), channel_id=1, source_target_pairs={{0,13},{1,12},{4,9},{5,8},{8,5},{9,4},{12,1},{13,0},{2,15},{3,14},... | collective-permute-start | bytes 786440 | tf_op jit(solution)/shard_map/ppermute | solution.py:207
  55.5 0.7 select.4
  56.2 1.9 %collective-permute-start.14 = (bf16[128,1024]{1,0:T(8,128)(2,1)S(1)}, bf16[128,1024]{1,0:T(8,128)(2,1)S(1)}, u32[]{:S(2)}, u32[]{:S(2)}) collective-permute-start(bf16[128,1024]{1,0:T(8,128)(2,1)S(1)} %get-tuple-element.37), channel_id=1, source_target_pairs={{0,4},{1,5},{4,0},{5,1},{8,12},{9,13},{12,8},{13,9},{2,6},{3,7},{6... | collective-permute-start | bytes 786440 | tf_op jit(solution)/shard_map/ppermute | solution.py:207
  58.1 20.4 %collective-permute-done.18.refs_4_ = bf16[128,1024]{1,0:T(8,128)(2,1)S(1)} collective-permute-done((bf16[128,1024]{1,0:T(8,128)(2,1)S(1)}, bf16[128,1024]{1,0:T(8,128)(2,1)S(1)}, u32[]{:S(2)}, u32[]{:S(2)}) %collective-permute-start.18) | collective-permute-done | bytes 262176 | tf_op jit(solution)/shard_map/ppermute | solution.py:207
  78.5 4.3 %collective-permute-start.15 = (bf16[128,1024]{1,0:T(8,128)(2,1)S(1)}, bf16[128,1024]{1,0:T(8,128)(2,1)S(1)}, u32[]{:S(2)}, u32[]{:S(2)}) collective-permute-start(bf16[128,1024]{1,0:T(8,128)(2,1)S(1)} %get-tuple-element.38), channel_id=1, source_target_pairs={{0,5},{1,4},{4,1},{5,0},{8,13},{9,12},{12,9},{13,8},{2,7},{3,6},{6... | collective-permute-start | bytes 786440 | tf_op jit(solution)/shard_map/ppermute | solution.py:207
  82.9 1.3 %collective-permute-done.19.refs_5_ = bf16[128,1024]{1,0:T(8,128)(2,1)S(1)} collective-permute-done((bf16[128,1024]{1,0:T(8,128)(2,1)S(1)}, bf16[128,1024]{1,0:T(8,128)(2,1)S(1)}, u32[]{:S(2)}, u32[]{:S(2)}) %collective-permute-start.19) | collective-permute-done | bytes 262176 | tf_op jit(solution)/shard_map/ppermute | solution.py:207
  84.2 7.3 %collective-permute-done.16.refs_2_ = bf16[128,1024]{1,0:T(8,128)(2,1)S(1)} collective-permute-done((bf16[128,1024]{1,0:T(8,128)(2,1)S(1)}, bf16[128,1024]{1,0:T(8,128)(2,1)S(1)}, u32[]{:S(2)}, u32[]{:S(2)}) %collective-permute-start.16) | collective-permute-done | bytes 262176 | tf_op jit(solution)/shard_map/ppermute | solution.py:207
  91.5 5.9 %collective-permute-done.17.refs_3_ = bf16[128,1024]{1,0:T(8,128)(2,1)S(1)} collective-permute-done((bf16[128,1024]{1,0:T(8,128)(2,1)S(1)}, bf16[128,1024]{1,0:T(8,128)(2,1)S(1)}, u32[]{:S(2)}, u32[]{:S(2)}) %collective-permute-start.17) | collective-permute-done | bytes 262176 | tf_op jit(solution)/shard_map/ppermute | solution.py:207
  97.4 2.7 %norm.1 = bf16[128,8192]{1,0:T(8,128)(2,1)} custom-call(bf16[1,8192]{1,0:T(2,128)(2,1)S(1)} %broadcast_in_dim.12.gain, bf16[128,1024]{1,0:T(8,128)(2,1)S(1)} %collective-permute-done.14.refs_0_, bf16[128,1024]{1,0:T(8,128)(2,1)S(1)} %collective-permute-done.15.refs_1_, bf16[128,1024]{1,0:T(8,128)(2,1)S(1)} %collective-permute-done.16.refs_2_, ...), custom_call_target="tpu_custom_call" | custom-call | flops 4194304 | bytes 4194304 | tf_op jit(solution)/shard_map/norm/pallas_call | solution.py:158
  (24 shorter events, 0.1 us)
Async XLA Ops:
  0.0 1.1 %copy-start.4 = (bf16[1,256,1280]{2,1,0:T(8,128)(2,1)S(1)}, bf16[1,256,1280]{2,1,0:T(8,128)(2,1)}, u32[]{:S(2)}) copy-start(bf16[1,256,1280]{2,1,0:T(8,128)(2,1)} %param.8) | copy-start | bytes 1966084
  1.2 13.5 %collective-permute-start.2 = (bf16[128,1280]{1,0:T(8,128)(2,1)S(1)}, bf16[128,1280]{1,0:T(8,128)(2,1)S(1)}, u32[]{:S(2)}, u32[]{:S(2)}) collective-permute-start(bf16[128,1280]{1,0:T(8,128)(2,1)S(1)} %own_half.1), channel_id=1, source_target_pairs={{0,4},{4,8},{8,12},{1,5},{5,9},{9,13},{2,6},{6,10},{10,14},{3,7},{... | collective-permute-start | bytes 983048 | tf_op jit(solution)/shard_map/ppermute | solution.py:193
  4.4 11.6 %collective-permute-start.4 = (bf16[128,1280]{1,0:T(8,128)(2,1)S(1)}, bf16[128,1280]{1,0:T(8,128)(2,1)S(1)}, u32[]{:S(2)}, u32[]{:S(2)}) collective-permute-start(bf16[128,1280]{1,0:T(8,128)(2,1)S(1)} %own_half.1), channel_id=1, source_target_pairs={{4,0},{8,4},{12,8},{5,1},{9,5},{13,9},{6,2},{10,6},{14,10},{7,3},{... | collective-permute-start | bytes 983048 | tf_op jit(solution)/shard_map/ppermute | solution.py:194
  8.6 1.7 %copy-start = (bf16[1280,1024]{1,0:T(8,128)(2,1)S(1)}, bf16[1280,1024]{1,0:T(8,128)(2,1)}, u32[]{:S(2)}) copy-start(bf16[1280,1024]{1,0:T(8,128)(2,1)} %refs_4_.5) | copy-start | bytes 7864324
  10.3 1.7 %copy-start.2 = (bf16[1280,1024]{1,0:T(8,128)(2,1)S(1)}, bf16[1280,1024]{1,0:T(8,128)(2,1)}, u32[]{:S(2)}) copy-start(bf16[1280,1024]{1,0:T(8,128)(2,1)} %refs_5_.5) | copy-start | bytes 7864324
  12.1 1.1 %copy-start.5 = (bf16[1,256,1280]{2,1,0:T(8,128)(2,1)S(1)}, bf16[1,256,1280]{2,1,0:T(8,128)(2,1)}, u32[]{:S(2)}) copy-start(bf16[1,256,1280]{2,1,0:T(8,128)(2,1)} %param.8) | copy-start | bytes 1966084
  13.2 15.2 %copy-start.1 = (bf16[1280,1024]{1,0:T(8,128)(2,1)S(1)}, bf16[1280,1024]{1,0:T(8,128)(2,1)}, u32[]{:S(2)}) copy-start(bf16[1280,1024]{1,0:T(8,128)(2,1)} %refs_4_.5) | copy-start | bytes 7864324
  13.2 15.3 %copy-start.3 = (bf16[1280,1024]{1,0:T(8,128)(2,1)S(1)}, bf16[1280,1024]{1,0:T(8,128)(2,1)}, u32[]{:S(2)}) copy-start(bf16[1280,1024]{1,0:T(8,128)(2,1)} %refs_5_.5) | copy-start | bytes 7864324
  14.7 13.6 %collective-permute-start.3 = (bf16[128,1280]{1,0:T(8,128)(2,1)S(1)}, bf16[128,1280]{1,0:T(8,128)(2,1)S(1)}, u32[]{:S(2)}, u32[]{:S(2)}) collective-permute-start(bf16[128,1280]{1,0:T(8,128)(2,1)S(1)} %collective-permute-done.2.refs_0_), channel_id=1, source_target_pairs={{0,1},{1,0},{2,3},{3,2},{4,5},{5,4},{6,7},{7,6},{8,9},{9,8},{10,11... | collective-permute-start | bytes 983048 | tf_op jit(solution)/shard_map/ppermute | solution.py:180
  16.0 12.3 %collective-permute-start.5 = (bf16[128,1280]{1,0:T(8,128)(2,1)S(1)}, bf16[128,1280]{1,0:T(8,128)(2,1)S(1)}, u32[]{:S(2)}, u32[]{:S(2)}) collective-permute-start(bf16[128,1280]{1,0:T(8,128)(2,1)S(1)} %collective-permute-done.4.refs_2_), channel_id=1, source_target_pairs={{0,1},{1,0},{2,3},{3,2},{4,5},{5,4},{6,7},{7,6},{8,9},{9,8},{10,11... | collective-permute-start | bytes 983048 | tf_op jit(solution)/shard_map/ppermute | solution.py:180
  16.4 5.5 %collective-permute-start = (s32[1,256]{1,0:T(1,128)S(1)}, s32[1,256]{1,0:T(1,128)S(1)}, u32[]{:S(2)}, u32[]{:S(2)}) collective-permute-start(s32[1,256]{1,0:T(1,128)S(1)} %multiply_add_fusion.meta), channel_id=1, source_target_pairs={{0,4},{4,0},{8,12},{12,8},{1,5},{5,1},{9,13},{13,9},{2,6},{6,2},{1... | collective-permute-start | bytes 3080 | tf_op jit(solution)/shard_map/ppermute | solution.py:186
  16.6 15.0 %collective-permute-start.8 = (bf16[128,1280]{1,0:T(8,128)(2,1)S(1)}, bf16[128,1280]{1,0:T(8,128)(2,1)S(1)}, u32[]{:S(2)}, u32[]{:S(2)}) collective-permute-start(bf16[128,1280]{1,0:T(8,128)(2,1)S(1)} %collective-permute-done.4.refs_2_), channel_id=1, source_target_pairs={{4,0},{8,4},{5,1},{9,5},{6,2},{10,6},{7,3},{11,7},{20,16},{24,20},... | collective-permute-start | bytes 983048 | tf_op jit(solution)/shard_map/ppermute | solution.py:194
  19.8 13.5 %collective-permute-start.6 = (bf16[128,1280]{1,0:T(8,128)(2,1)S(1)}, bf16[128,1280]{1,0:T(8,128)(2,1)S(1)}, u32[]{:S(2)}, u32[]{:S(2)}) collective-permute-start(bf16[128,1280]{1,0:T(8,128)(2,1)S(1)} %collective-permute-done.2.refs_0_), channel_id=1, source_target_pairs={{4,8},{8,12},{5,9},{9,13},{6,10},{10,14},{7,11},{11,15},{20,24},{2... | collective-permute-start | bytes 983048 | tf_op jit(solution)/shard_map/ppermute | solution.py:193
  22.0 6.4 %collective-permute-start.1 = (s32[2,256]{1,0:T(2,128)S(1)}, s32[2,256]{1,0:T(2,128)S(1)}, u32[]{:S(2)}, u32[]{:S(2)}) collective-permute-start(s32[2,256]{1,0:T(2,128)S(1)} %pad_add_fusion.1), channel_id=1, source_target_pairs={{0,8},{4,12},{8,0},{12,4},{1,9},{5,13},{9,1},{13,5},{2,10},{6,14},... | collective-permute-start | bytes 6152 | tf_op jit(solution)/shard_map/ppermute | solution.py:186
  31.6 3.7 %collective-permute-start.9 = (bf16[128,1280]{1,0:T(8,128)(2,1)S(1)}, bf16[128,1280]{1,0:T(8,128)(2,1)S(1)}, u32[]{:S(2)}, u32[]{:S(2)}) collective-permute-start(bf16[128,1280]{1,0:T(8,128)(2,1)S(1)} %collective-permute-done.8.refs_2_), channel_id=1, source_target_pairs={{0,1},{1,0},{2,3},{3,2},{4,5},{5,4},{6,7},{7,6},{8,9},{9,8},{10,11... | collective-permute-start | bytes 983048 | tf_op jit(solution)/shard_map/ppermute | solution.py:180
  33.3 2.1 %collective-permute-start.7 = (bf16[128,1280]{1,0:T(8,128)(2,1)S(1)}, bf16[128,1280]{1,0:T(8,128)(2,1)S(1)}, u32[]{:S(2)}, u32[]{:S(2)}) collective-permute-start(bf16[128,1280]{1,0:T(8,128)(2,1)S(1)} %collective-permute-done.6.refs_0_), channel_id=1, source_target_pairs={{0,1},{1,0},{2,3},{3,2},{4,5},{5,4},{6,7},{7,6},{8,9},{9,8},{10,11... | collective-permute-start | bytes 983048 | tf_op jit(solution)/shard_map/ppermute | solution.py:180
  33.4 8.2 %collective-permute-start.12 = (bf16[128,1280]{1,0:T(8,128)(2,1)S(1)}, bf16[128,1280]{1,0:T(8,128)(2,1)S(1)}, u32[]{:S(2)}, u32[]{:S(2)}) collective-permute-start(bf16[128,1280]{1,0:T(8,128)(2,1)S(1)} %collective-permute-done.8.refs_2_), channel_id=1, source_target_pairs={{4,0},{5,1},{6,2},{7,3},{20,16},{21,17},{22,18},{23,19}} | collective-permute-start | bytes 983048 | tf_op jit(solution)/shard_map/ppermute | solution.py:194
  34.7 7.9 %collective-permute-start.10 = (bf16[128,1280]{1,0:T(8,128)(2,1)S(1)}, bf16[128,1280]{1,0:T(8,128)(2,1)S(1)}, u32[]{:S(2)}, u32[]{:S(2)}) collective-permute-start(bf16[128,1280]{1,0:T(8,128)(2,1)S(1)} %collective-permute-done.6.refs_0_), channel_id=1, source_target_pairs={{8,12},{9,13},{10,14},{11,15},{24,28},{25,29},{26,30},{27,31}} | collective-permute-start | bytes 983048 | tf_op jit(solution)/shard_map/ppermute | solution.py:193
  41.6 2.2 %collective-permute-start.13 = (bf16[128,1280]{1,0:T(8,128)(2,1)S(1)}, bf16[128,1280]{1,0:T(8,128)(2,1)S(1)}, u32[]{:S(2)}, u32[]{:S(2)}) collective-permute-start(bf16[128,1280]{1,0:T(8,128)(2,1)S(1)} %collective-permute-done.12.refs_2_), channel_id=1, source_target_pairs={{0,1},{1,0},{2,3},{3,2},{4,5},{5,4},{6,7},{7,6},{8,9},{9,8},{10,11... | collective-permute-start | bytes 983048 | tf_op jit(solution)/shard_map/ppermute | solution.py:180
  42.5 1.7 %collective-permute-start.11 = (bf16[128,1280]{1,0:T(8,128)(2,1)S(1)}, bf16[128,1280]{1,0:T(8,128)(2,1)S(1)}, u32[]{:S(2)}, u32[]{:S(2)}) collective-permute-start(bf16[128,1280]{1,0:T(8,128)(2,1)S(1)} %collective-permute-done.10.refs_0_), channel_id=1, source_target_pairs={{0,1},{1,0},{2,3},{3,2},{4,5},{5,4},{6,7},{7,6},{8,9},{9,8},{10,11... | collective-permute-start | bytes 983048 | tf_op jit(solution)/shard_map/ppermute | solution.py:180
  45.0 11.2 %collective-permute-start.20 = (bf16[128,1024]{1,0:T(8,128)(2,1)S(1)}, bf16[128,1024]{1,0:T(8,128)(2,1)S(1)}, u32[]{:S(2)}, u32[]{:S(2)}) collective-permute-start(bf16[128,1024]{1,0:T(8,128)(2,1)S(1)} %get-tuple-element.44), channel_id=1, source_target_pairs={{0,1},{1,0},{4,5},{5,4},{8,9},{9,8},{12,13},{13,12},{2,3},{3,2},{6... | collective-permute-start | bytes 786440 | tf_op jit(solution)/shard_map/ppermute | solution.py:207
  46.2 32.4 %collective-permute-start.18 = (bf16[128,1024]{1,0:T(8,128)(2,1)S(1)}, bf16[128,1024]{1,0:T(8,128)(2,1)S(1)}, u32[]{:S(2)}, u32[]{:S(2)}) collective-permute-start(bf16[128,1024]{1,0:T(8,128)(2,1)S(1)} %get-tuple-element.41), channel_id=1, source_target_pairs={{0,8},{1,9},{4,12},{5,13},{8,0},{9,1},{12,4},{13,5},{2,10},{3,11},... | collective-permute-start | bytes 786440 | tf_op jit(solution)/shard_map/ppermute | solution.py:207
  52.6 31.6 %collective-permute-start.19 = (bf16[128,1024]{1,0:T(8,128)(2,1)S(1)}, bf16[128,1024]{1,0:T(8,128)(2,1)S(1)}, u32[]{:S(2)}, u32[]{:S(2)}) collective-permute-start(bf16[128,1024]{1,0:T(8,128)(2,1)S(1)} %get-tuple-element.42), channel_id=1, source_target_pairs={{0,9},{1,8},{4,13},{5,12},{8,1},{9,0},{12,5},{13,4},{2,11},{3,10},... | collective-permute-start | bytes 786440 | tf_op jit(solution)/shard_map/ppermute | solution.py:207
  53.4 29.4 %copy-start.6 = (bf16[8192]{0:T(1024)(128)(2,1)S(1)}, bf16[8192]{0:T(1024)(128)(2,1)}, u32[]{:S(2)}) copy-start(bf16[8192]{0:T(1024)(128)(2,1)} %param.15) | copy-start | bytes 49156
  53.4 38.0 %collective-permute-start.16 = (bf16[128,1024]{1,0:T(8,128)(2,1)S(1)}, bf16[128,1024]{1,0:T(8,128)(2,1)S(1)}, u32[]{:S(2)}, u32[]{:S(2)}) collective-permute-start(bf16[128,1024]{1,0:T(8,128)(2,1)S(1)} %get-tuple-element.39), channel_id=1, source_target_pairs={{0,12},{1,13},{4,8},{5,9},{8,4},{9,5},{12,0},{13,1},{2,14},{3,15},... | collective-permute-start | bytes 786440 | tf_op jit(solution)/shard_map/ppermute | solution.py:207
  53.5 43.8 %collective-permute-start.17 = (bf16[128,1024]{1,0:T(8,128)(2,1)S(1)}, bf16[128,1024]{1,0:T(8,128)(2,1)S(1)}, u32[]{:S(2)}, u32[]{:S(2)}) collective-permute-start(bf16[128,1024]{1,0:T(8,128)(2,1)S(1)} %get-tuple-element.40), channel_id=1, source_target_pairs={{0,13},{1,12},{4,9},{5,8},{8,5},{9,4},{12,1},{13,0},{2,15},{3,14},... | collective-permute-start | bytes 786440 | tf_op jit(solution)/shard_map/ppermute | solution.py:207
  56.2 41.1 %collective-permute-start.14 = (bf16[128,1024]{1,0:T(8,128)(2,1)S(1)}, bf16[128,1024]{1,0:T(8,128)(2,1)S(1)}, u32[]{:S(2)}, u32[]{:S(2)}) collective-permute-start(bf16[128,1024]{1,0:T(8,128)(2,1)S(1)} %get-tuple-element.37), channel_id=1, source_target_pairs={{0,4},{1,5},{4,0},{5,1},{8,12},{9,13},{12,8},{13,9},{2,6},{3,7},{6... | collective-permute-start | bytes 786440 | tf_op jit(solution)/shard_map/ppermute | solution.py:207
  78.5 18.8 %collective-permute-start.15 = (bf16[128,1024]{1,0:T(8,128)(2,1)S(1)}, bf16[128,1024]{1,0:T(8,128)(2,1)S(1)}, u32[]{:S(2)}, u32[]{:S(2)}) collective-permute-start(bf16[128,1024]{1,0:T(8,128)(2,1)S(1)} %get-tuple-element.38), channel_id=1, source_target_pairs={{0,5},{1,4},{4,1},{5,0},{8,13},{9,12},{12,9},{13,8},{2,7},{3,6},{6... | collective-permute-start | bytes 786440 | tf_op jit(solution)/shard_map/ppermute | solution.py:207

commit v3 on v2

v3 whole, which is shorter than its diff:
```python
import functools

import jax
import jax.numpy as jnp
from jax import lax
from jax.experimental import pallas as pl
from jax.experimental.pallas import tpu as pltpu
from jax.sharding import PartitionSpec as P

VMEM = pl.BlockSpec(memory_space=pltpu.VMEM)
HBM = pl.BlockSpec(memory_space=pltpu.HBM)
PARAMS = pltpu.CompilerParams(vmem_limit_bytes=12 << 20)
BF16, F32, I32 = jnp.bfloat16, jnp.float32, jnp.int32


def cost(flops, moved):
    return pl.CostEstimate(flops=flops // 16, bytes_accessed=moved // 16, transcendentals=0)


def send_kernel(rows, slot, kind, out, slot_here, kind_here, sems):
    half = out.shape[0] - 8
    t = lax.axis_index("tp")
    start = pl.multiple_of(t * half, half)
    copies = [
        pltpu.make_async_copy(slot, slot_here, sems.at[0]),
        pltpu.make_async_copy(kind, kind_here, sems.at[1]),
        pltpu.make_async_copy(rows.at[pl.ds(start, half), :], out.at[pl.ds(0, half), :], sems.at[2]),
    ]
    for copy in copies:
        copy.start()
    out[half:, :] = jnp.zeros((8, out.shape[1]), BF16)
    for copy in copies:
        copy.wait()
    slots = jnp.where(t == 0, slot_here[:, :half], slot_here[:, half:])
    kinds = jnp.where(t == 0, kind_here[:, :half], kind_here[:, half:])
    line = lax.broadcasted_iota(I32, (8, half), 0)
    index = jnp.where(line == 0, slots // 256, jnp.where(line == 1, slots % 256, kinds))
    out[half:, :half] = index.astype(F32).astype(BF16)


def to_send(rows, slot, kind):
    half, width = rows.shape[0] // 2, rows.shape[1]
    return pl.pallas_call(
        send_kernel,
        out_shape=jax.ShapeDtypeStruct((half + 8, width), BF16),
        in_specs=[HBM] * 3,
        out_specs=VMEM,
        scratch_shapes=[
            pltpu.VMEM(slot.shape, I32),
            pltpu.VMEM(slot.shape, I32),
            pltpu.SemaphoreType.DMA((3,)),
        ],
        compiler_params=pltpu.CompilerParams(vmem_limit_bytes=60 << 20),
        cost_estimate=cost(0, 4 * half * width),
        name="to_send",
    )(rows, slot, kind)


def column_of(row_vector):
    r = row_vector.shape[1]
    diagonal = lax.broadcasted_iota(I32, (r, r), 0) == lax.broadcasted_iota(I32, (r, r), 1)
    return jnp.sum(jnp.where(diagonal, row_vector, 0), axis=1, keepdims=True)


def project(kind_row, x, w_audio, w_frame, b_audio, b_frame, out):
    is_audio = column_of(kind_row) == 0
    audio = jnp.dot(x, w_audio[...], preferred_element_type=F32)
    frame = jnp.dot(x, w_frame[...], preferred_element_type=F32)
    audio = audio + b_audio[...].astype(F32)
    frame = frame + b_frame[...].astype(F32)
    out[...] = jnp.where(is_audio, audio, frame).astype(out.dtype)


def project_own_kernel(kind, x, wa, wf, ba, bf, out):
    project(kind[...], x[...], wa, wf, ba, bf, out)


def project_own(kind, rows, weights):
    ew, cols = weights[0].shape
    return pl.pallas_call(
        project_own_kernel,
        out_shape=jax.ShapeDtypeStruct((rows.shape[0], cols), BF16),
        in_specs=[VMEM] * 6,
        out_specs=VMEM,
        compiler_params=PARAMS,
        cost_estimate=cost(4 * rows.shape[0] * ew * cols, 4 * ew * cols),
        name="project_own",
    )(kind, rows, *weights)


def project_halves_kernel(wa, wf, ba, bf, *refs):
    pieces, out, slots = refs[:-2], refs[-2], refs[-1]
    half = pieces[0].shape[0] - 8
    x = [r[:half, :] for r in pieces]
    index = [r[half:, :half].astype(F32).astype(I32) for r in pieces]
    x = x[0] if len(x) == 1 else jnp.concatenate(x, axis=0)
    index = index[0] if len(index) == 1 else jnp.concatenate(index, axis=1)
    slots[...] = index[0:1] * 256 + index[1:2]
    project(index[2:3], x, wa, wf, ba, bf, out)


def project_halves(pieces, weights):
    rows, ew = len(pieces) * (pieces[0].shape[0] - 8), pieces[0].shape[1]
    cols = weights[0].shape[1]
    return pl.pallas_call(
        project_halves_kernel,
        out_shape=[jax.ShapeDtypeStruct((rows, cols), BF16), jax.ShapeDtypeStruct((1, rows), I32)],
        in_specs=[VMEM] * (4 + len(pieces)),
        out_specs=[VMEM] * 2,
        compiler_params=PARAMS,
        cost_estimate=cost(4 * rows * ew * cols, 4 * ew * cols),
        name="project_halves",
    )(*weights, *pieces)


def select_kernel(m, count, *refs):
    blocks, slots, outs = refs[:count], refs[count : 2 * count], refs[-2:]
    places = outs[0].shape[0]
    z, t = lax.axis_index("ctx"), lax.axis_index("tp")
    first = jnp.bitwise_xor(z, m) * 2 * places
    i = lax.broadcasted_iota(I32, (2 * places, 1), 0)
    position = first + jnp.bitwise_xor(i, t * places)
    total = None
    for block, slot in zip(blocks, slots):
        chosen = (slot[...] == position).astype(F32).astype(BF16)
        part = jnp.dot(chosen, block[...], preferred_element_type=F32)
        total = part if total is None else total + part
    outs[0][...] = total[:places].astype(BF16)
    outs[1][...] = total[places:].astype(BF16)


def select(m, blocks, slots, places):
    rows, cols = sum(b.shape[0] for b in blocks), blocks[0].shape[1]
    return pl.pallas_call(
        functools.partial(select_kernel, m, len(blocks)),
        out_shape=[jax.ShapeDtypeStruct((places, cols), BF16)] * 2,
        in_specs=[VMEM] * (2 * len(blocks)),
        out_specs=[VMEM] * 2,
        compiler_params=PARAMS,
        cost_estimate=cost(4 * places * rows * cols, 2 * rows * cols),
        name="select",
    )(*blocks, *slots)


def norm_kernel(places_of, gain, *refs):
    n = len(places_of)
    pieces, out = refs[:n], refs[n]
    cols = pieces[0].shape[1]
    z, t = lax.axis_index("ctx"), lax.axis_index("tp")
    total = None
    for piece in pieces:
        wide = piece[...].astype(F32)
        part = jnp.sum(wide * wide, axis=1, keepdims=True)
        total = part if total is None else total + part
    scale = lax.rsqrt(total / (n * cols) + 1e-06)
    for (m, d), piece in zip(places_of, pieces):
        block = jnp.bitwise_xor(z, m) * 2 + jnp.bitwise_xor(t, d)
        at = pl.ds(pl.multiple_of(block * cols, cols), cols)
        out[:, at] = (piece[...].astype(F32) * scale * gain[:, at].astype(F32)).astype(out.dtype)


def norm(places_of, gain, pieces):
    n = len(pieces)
    places, cols = pieces[0].shape
    return pl.pallas_call(
        functools.partial(norm_kernel, places_of),
        out_shape=jax.ShapeDtypeStruct((places, n * cols), BF16),
        in_specs=[VMEM] * (n + 1),
        out_specs=VMEM,
        compiler_params=PARAMS,
        cost_estimate=cost(4 * places * n * cols, 4 * places * n * cols),
        name="norm",
    )(gain, *pieces)


def after(x, *others):
    return lax.optimization_barrier((x, *others))[0]


def body(enc_rows, row_slot, row_kind, audio_proj, frame_proj, audio_bias, frame_bias, norm_gain):
    n = lax.axis_size("ctx")
    rows = enc_rows[0]
    half = rows.shape[0] // 2
    weights = (audio_proj, frame_proj, audio_bias[None, :], frame_bias[None, :])

    def over_tp(x):
        return lax.ppermute(x, "tp", [(0, 1), (1, 0)])

    mine = to_send(rows, row_slot, row_kind)
    direct = [
        lax.ppermute(mine, "ctx", [(i, i ^ m) for i in range(n)]) for m in range(1, n)
    ]
    own = project_own(row_kind, rows, weights)
    blocks, slots, last = [own], [row_slot], own
    for k in range(n - 1):
        direct[k] = after(direct[k], last)
        block, slot = project_halves([direct[k]], weights)
        blocks.append(block)
        slots.append(slot)
        last = block
    swapped = [over_tp(x) for x in direct]
    for k in range(0, n - 1, 3):
        block, slot = project_halves(swapped[k : k + 3], weights)
        blocks.append(block)
        slots.append(slot)

    pieces, places_of = [], []
    for m in [1] + list(reversed(range(2, n))) + [0]:
        chosen = select(m, blocks, slots, half)
        slots[0] = after(slots[0], chosen[0])
        for d, piece in enumerate(chosen):
            if m or d:
                perm = [(i * 2 + c, (i ^ m) * 2 + (c ^ d)) for i in range(n) for c in range(2)]
                piece = lax.ppermute(piece, ("ctx", "tp"), perm)
            pieces.append(piece)
            places_of.append((m, d))
    return norm(tuple(places_of), norm_gain[None, :], pieces)[None]


def solution(mesh):
    return jax.shard_map(
        body,
        mesh=mesh,
        in_specs=(
            P(("groups", "enc"), "ctx", None),
            P(("groups", "enc"), "ctx"),
            P(("groups", "enc"), "ctx"),
            P(None, ("ctx", "tp")),
            P(None, ("ctx", "tp")),
            P(("ctx", "tp")),
            P(("ctx", "tp")),
            P(),
        ),
        out_specs=P(("groups", "enc"), ("ctx", "tp"), None),
        check_vma=False,
    )
```

time: 101 us -> 95.4 us (0.945)
  the two profiles are of different devices: /device:TPU:9 before, /device:TPU:13 now
where the time goes in v3:
time: 95.4 us; the launch traced here: 95.1 us
  waiting for transfers between devices  58.1 us (61%)
  starting transfers between devices  15.3 us (16%)
  Pallas kernels  14.9 us (16%)
  local copies, waits for them, and re-layouts  6.65 us (7%)
    ppermute x7, waiting for transfers between devices, body(): piece = lax.ppermute(piece, ('ctx', 'tp'), perm)  37.4 us
    ppermute x3, waiting for transfers between devices, body(): lax.ppermute(mine, 'ctx', [(i, i ^ m) for i in range(n)])  19.9 us
    ppermute x7, starting transfers between devices, body(): piece = lax.ppermute(piece, ('ctx', 'tp'), perm)  10.2 us
    unnamed x16, local copies, waits for them, and re-layouts  5.26 us
    pallas_call x4, Pallas kernels, project_halves(): pl.pallas_call(project_halves_kernel, out_shape=[jax.ShapeDtypeStruct((ro...  5.01 us
    pallas_call x4, Pallas kernels, select(): pl.pallas_call(functools.partial(select_kernel, m, len(blocks)), out_shap...  3.84 us
    pallas_call x1, Pallas kernels, norm(): pl.pallas_call(functools.partial(norm_kernel, places_of), out_shape=jax.S...  2.74 us
    ppermute x3, starting transfers between devices, body(): lax.ppermute(mine, 'ctx', [(i, i ^ m) for i in range(n)])  2.71 us
  transfers between devices with their start and end apart: 13, of which 8 were waited for; matrix products, arithmetic and copies ran while one was open for 1% of the time, Pallas kernels for 4%

profile of v3, /device:TPU:13, one launch (start us, length us, event | category | flops | bytes accessed | tf_op | source)
XLA Modules:
  0.0 95.1 jit_solution(5828332640343420801)
XLA Ops:
  0.0 1.8 %to_send.1 = bf16[136,1280]{1,0:T(8,128)(2,1)} custom-call(bf16[256,1280]{1,0:T(8,128)(2,1)} %bitcast.2, s32[1,256]{1,0:T(1,128)} %refs_5_.4, s32[1,256]{1,0:T(1,128)} %kind.3), custom_call_target="tpu_custom_call" | custom-call | bytes 40960 | tf_op jit(solution)/shard_map/to_send/pallas_call | solution.py:43
  1.8 0.2 collective-permute-start
  2.0 2.3 %collective-permute-start.1 = (bf16[136,1280]{1,0:T(8,128)(2,1)}, bf16[136,1280]{1,0:T(8,128)(2,1)S(1)}, u32[]{:S(2)}, u32[]{:S(2)}) collective-permute-start(bf16[136,1280]{1,0:T(8,128)(2,1)} %to_send.1), channel_id=1, source_target_pairs={{0,8},{4,12},{8,0},{12,4},{1,9},{5,13},{9,1},{13,5},{2,10},{6,14},... | collective-permute-start | bytes 1044488 | tf_op jit(solution)/shard_map/ppermute | solution.py:191
  4.3 0.2 collective-permute-start.2
  4.5 0.7 broadcast_in_dim.13.ba
  5.2 0.7 broadcast_in_dim.14.bf
  5.9 1.7 %copy-done = bf16[1280,1024]{1,0:T(8,128)(2,1)S(1)} copy-done((bf16[1280,1024]{1,0:T(8,128)(2,1)S(1)}, bf16[1280,1024]{1,0:T(8,128)(2,1)}, u32[]{:S(2)}) %copy-start) | copy-done | bytes 2621464
  7.6 1.7 %copy-done.2 = bf16[1280,1024]{1,0:T(8,128)(2,1)S(1)} copy-done((bf16[1280,1024]{1,0:T(8,128)(2,1)S(1)}, bf16[1280,1024]{1,0:T(8,128)(2,1)}, u32[]{:S(2)}) %copy-start.2) | copy-done | bytes 2621464
  9.4 1.1 %copy-done.4 = bf16[1,256,1280]{2,1,0:T(8,128)(2,1)S(1)} copy-done((bf16[1,256,1280]{2,1,0:T(8,128)(2,1)S(1)}, bf16[1,256,1280]{2,1,0:T(8,128)(2,1)}, u32[]{:S(2)}) %copy-start.4) | copy-done | bytes 655384
  10.4 0.7 copy-done.6
  11.1 1.5 %project_own.1.refs_0_ = bf16[256,1024]{1,0:T(8,128)(2,1)S(1)} custom-call(s32[1,256]{1,0:T(1,128)S(1)} %copy-done.6, bf16[256,1280]{1,0:T(8,128)(2,1)S(1)} %bitcast.3, bf16[1280,1024]{1,0:T(8,128)(2,1)S(1)} %copy-done, bf16[1280,1024]{1,0:T(8,128)(2,1)S(1)} %copy-done.2, bf16[1,1024]{1,0:T(2,128)(2,1)S(1)} %broadcast_in_dim.13.ba, ...), custom_call_target="tpu_custom_call" | custom-call | flops 83886080 | bytes 327680 | tf_op jit(solution)/shard_map/project_own/pallas_call | solution.py:80
  12.7 3.2 %collective-permute-done.refs_0_ = bf16[136,1280]{1,0:T(8,128)(2,1)S(1)} collective-permute-done((bf16[136,1280]{1,0:T(8,128)(2,1)}, bf16[136,1280]{1,0:T(8,128)(2,1)S(1)}, u32[]{:S(2)}, u32[]{:S(2)}) %collective-permute-start) | collective-permute-done | bytes 348192 | tf_op jit(solution)/shard_map/ppermute | solution.py:191
  15.8 0.0 copy-done.1
  15.8 0.0 copy-done.3
  15.8 0.9 project_halves.4
  16.8 2.8 %collective-permute-done.1.refs_0_ = bf16[136,1280]{1,0:T(8,128)(2,1)S(1)} collective-permute-done((bf16[136,1280]{1,0:T(8,128)(2,1)}, bf16[136,1280]{1,0:T(8,128)(2,1)S(1)}, u32[]{:S(2)}, u32[]{:S(2)}) %collective-permute-start.1) | collective-permute-done | bytes 348192 | tf_op jit(solution)/shard_map/ppermute | solution.py:191
  19.6 0.9 project_halves.5
  20.5 13.9 %collective-permute-done.2.refs_0_ = bf16[136,1280]{1,0:T(8,128)(2,1)S(1)} collective-permute-done((bf16[136,1280]{1,0:T(8,128)(2,1)}, bf16[136,1280]{1,0:T(8,128)(2,1)S(1)}, u32[]{:S(2)}, u32[]{:S(2)}) %collective-permute-start.2) | collective-permute-done | bytes 348192 | tf_op jit(solution)/shard_map/ppermute | solution.py:191
  34.4 1.8 %collective-permute-start.5 = (bf16[136,1280]{1,0:T(8,128)(2,1)S(1)}, bf16[136,1280]{1,0:T(8,128)(2,1)S(1)}, u32[]{:S(2)}, u32[]{:S(2)}) collective-permute-start(bf16[136,1280]{1,0:T(8,128)(2,1)S(1)} %collective-permute-done.2.refs_0_), channel_id=1, source_target_pairs={{0,1},{1,0},{2,3},{3,2},{4,5},{5,4},{6,7},{7,6},{8,9},{9,8},{10,11... | collective-permute-start | bytes 1044488 | tf_op jit(solution)/shard_map/ppermute | solution.py:187
  36.3 0.0 collective-permute-start.4
  36.3 0.5 collective-permute-start.3
  36.8 0.9 project_halves.6
  37.7 0.0 copy-start.5
  37.7 0.0 collective-permute-done.5.refs_2_
  37.7 0.3 collective-permute-done.4.refs_1_
  38.0 0.5 collective-permute-done.3.refs_0_
  38.5 2.3 %project_halves.7 = (bf16[384,1024]{1,0:T(8,128)(2,1)S(1)}, s32[1,384]{1,0:T(1,128)S(1)}) custom-call(bf16[1280,1024]{1,0:T(8,128)(2,1)S(1)} %copy-done.1, bf16[1280,1024]{1,0:T(8,128)(2,1)S(1)} %copy-done.3, bf16[1,1024]{1,0:T(2,128)(2,1)S(1)} %broadcast_in_dim.13.ba, bf16[1,1024]{1,0:T(2,128)(2,1)S(1)} %broadcast_in_dim.14.bf, ...), custom_call_target="tpu_custom_call" | custom-call | flops 125829120 | bytes 327680 | tf_op jit(solution)/shard_map/project_halves/pallas_call | solution.py:105
  40.8 0.0 copy-done.5
  40.8 1.0 %select.4 = (bf16[128,1024]{1,0:T(8,128)(2,1)S(1)}, bf16[128,1024]{1,0:T(8,128)(2,1)S(1)}) custom-call(bf16[256,1024]{1,0:T(8,128)(2,1)S(1)} %project_own.1.refs_0_, bf16[128,1024]{1,0:T(8,128)(2,1)S(1)} %get-tuple-element.28.refs_1_, bf16[128,1024]{1,0:T(8,128)(2,1)S(1)} %get-tuple-element.30.refs_2_, bf16[128,1024]{1,0:T(8,128)(2,1)S(1)} %get-tuple-element.32.refs_3_, ...), custom_call_target="tpu_custom_call" | custom-call | flops 33554432 | bytes 131072 | tf_op jit(solution)/shard_map/select/pallas_call | solution.py:134
  41.8 1.0 %select.5 = (bf16[128,1024]{1,0:T(8,128)(2,1)S(1)}, bf16[128,1024]{1,0:T(8,128)(2,1)S(1)}) custom-call(bf16[256,1024]{1,0:T(8,128)(2,1)S(1)} %project_own.1.refs_0_, bf16[128,1024]{1,0:T(8,128)(2,1)S(1)} %get-tuple-element.28.refs_1_, bf16[128,1024]{1,0:T(8,128)(2,1)S(1)} %get-tuple-element.30.refs_2_, bf16[128,1024]{1,0:T(8,128)(2,1)S(1)} %get-tuple-element.32.refs_3_, ...), custom_call_target="tpu_custom_call" | custom-call | flops 33554432 | bytes 131072 | tf_op jit(solution)/shard_map/select/pallas_call | solution.py:134
  42.8 0.0 copy-start.7
  42.8 1.0 %select.6 = (bf16[128,1024]{1,0:T(8,128)(2,1)S(1)}, bf16[128,1024]{1,0:T(8,128)(2,1)S(1)}) custom-call(bf16[256,1024]{1,0:T(8,128)(2,1)S(1)} %project_own.1.refs_0_, bf16[128,1024]{1,0:T(8,128)(2,1)S(1)} %get-tuple-element.28.refs_1_, bf16[128,1024]{1,0:T(8,128)(2,1)S(1)} %get-tuple-element.30.refs_2_, bf16[128,1024]{1,0:T(8,128)(2,1)S(1)} %get-tuple-element.32.refs_3_, ...), custom_call_target="tpu_custom_call" | custom-call | flops 33554432 | bytes 131072 | tf_op jit(solution)/shard_map/select/pallas_call | solution.py:134
  43.7 1.0 %select.7 = (bf16[128,1024]{1,0:T(8,128)(2,1)S(1)}, bf16[128,1024]{1,0:T(8,128)(2,1)S(1)}) custom-call(bf16[256,1024]{1,0:T(8,128)(2,1)S(1)} %project_own.1.refs_0_, bf16[128,1024]{1,0:T(8,128)(2,1)S(1)} %get-tuple-element.28.refs_1_, bf16[128,1024]{1,0:T(8,128)(2,1)S(1)} %get-tuple-element.30.refs_2_, bf16[128,1024]{1,0:T(8,128)(2,1)S(1)} %get-tuple-element.32.refs_3_, ...), custom_call_target="tpu_custom_call" | custom-call | flops 33554432 | bytes 131072 | tf_op jit(solution)/shard_map/select/pallas_call | solution.py:134
  44.7 0.4 collective-permute-start.12
  45.2 0.0 collective-permute-start.10
  45.2 1.3 %collective-permute-start.8 = (bf16[128,1024]{1,0:T(8,128)(2,1)S(1)}, bf16[128,1024]{1,0:T(8,128)(2,1)S(1)}, u32[]{:S(2)}, u32[]{:S(2)}) collective-permute-start(bf16[128,1024]{1,0:T(8,128)(2,1)S(1)} %get-tuple-element.41), channel_id=1, source_target_pairs={{0,12},{1,13},{4,8},{5,9},{8,4},{9,5},{12,0},{13,1},{2,14},{3,15},... | collective-permute-start | bytes 786440 | tf_op jit(solution)/shard_map/ppermute | solution.py:214
  46.4 2.3 %collective-permute-start.6 = (bf16[128,1024]{1,0:T(8,128)(2,1)S(1)}, bf16[128,1024]{1,0:T(8,128)(2,1)S(1)}, u32[]{:S(2)}, u32[]{:S(2)}) collective-permute-start(bf16[128,1024]{1,0:T(8,128)(2,1)S(1)} %get-tuple-element.38), channel_id=1, source_target_pairs={{0,4},{1,5},{4,0},{5,1},{8,12},{9,13},{12,8},{13,9},{2,6},{3,7},{6... | collective-permute-start | bytes 786440 | tf_op jit(solution)/shard_map/ppermute | solution.py:214
  48.7 1.6 %collective-permute-start.11 = (bf16[128,1024]{1,0:T(8,128)(2,1)S(1)}, bf16[128,1024]{1,0:T(8,128)(2,1)S(1)}, u32[]{:S(2)}, u32[]{:S(2)}) collective-permute-start(bf16[128,1024]{1,0:T(8,128)(2,1)S(1)} %get-tuple-element.45), channel_id=1, source_target_pairs={{0,9},{1,8},{4,13},{5,12},{8,1},{9,0},{12,5},{13,4},{2,11},{3,10},... | collective-permute-start | bytes 786440 | tf_op jit(solution)/shard_map/ppermute | solution.py:214
  50.3 0.0 collective-permute-done.12.refs_7_
  50.3 0.6 collective-permute-start.9
  50.9 11.4 %collective-permute-done.10.refs_4_ = bf16[128,1024]{1,0:T(8,128)(2,1)S(1)} collective-permute-done((bf16[128,1024]{1,0:T(8,128)(2,1)S(1)}, bf16[128,1024]{1,0:T(8,128)(2,1)S(1)}, u32[]{:S(2)}, u32[]{:S(2)}) %collective-permute-start.10) | collective-permute-done | bytes 262176 | tf_op jit(solution)/shard_map/ppermute | solution.py:214
  62.3 4.1 %collective-permute-start.7 = (bf16[128,1024]{1,0:T(8,128)(2,1)S(1)}, bf16[128,1024]{1,0:T(8,128)(2,1)S(1)}, u32[]{:S(2)}, u32[]{:S(2)}) collective-permute-start(bf16[128,1024]{1,0:T(8,128)(2,1)S(1)} %get-tuple-element.39), channel_id=1, source_target_pairs={{0,5},{1,4},{4,1},{5,0},{8,13},{9,12},{12,9},{13,8},{2,7},{3,6},{6... | collective-permute-start | bytes 786440 | tf_op jit(solution)/shard_map/ppermute | solution.py:214
  66.4 18.3 %collective-permute-done.11.refs_5_ = bf16[128,1024]{1,0:T(8,128)(2,1)S(1)} collective-permute-done((bf16[128,1024]{1,0:T(8,128)(2,1)S(1)}, bf16[128,1024]{1,0:T(8,128)(2,1)S(1)}, u32[]{:S(2)}, u32[]{:S(2)}) %collective-permute-start.11) | collective-permute-done | bytes 262176 | tf_op jit(solution)/shard_map/ppermute | solution.py:214
  84.7 0.0 collective-permute-done.8.refs_2_
  84.7 7.6 %collective-permute-done.9.refs_3_ = bf16[128,1024]{1,0:T(8,128)(2,1)S(1)} collective-permute-done((bf16[128,1024]{1,0:T(8,128)(2,1)S(1)}, bf16[128,1024]{1,0:T(8,128)(2,1)S(1)}, u32[]{:S(2)}, u32[]{:S(2)}) %collective-permute-start.9) | collective-permute-done | bytes 262176 | tf_op jit(solution)/shard_map/ppermute | solution.py:214
  92.4 0.0 collective-permute-done.6.refs_0_
  92.4 0.0 collective-permute-done.7.refs_1_
  92.4 2.7 %norm.1 = bf16[128,8192]{1,0:T(8,128)(2,1)} custom-call(bf16[1,8192]{1,0:T(2,128)(2,1)S(1)} %broadcast_in_dim.12.gain, bf16[128,1024]{1,0:T(8,128)(2,1)S(1)} %collective-permute-done.6.refs_0_, bf16[128,1024]{1,0:T(8,128)(2,1)S(1)} %collective-permute-done.7.refs_1_, bf16[128,1024]{1,0:T(8,128)(2,1)S(1)} %collective-permute-done.8.refs_2_, ...), custom_call_target="tpu_custom_call" | custom-call | flops 262144 | bytes 262144 | tf_op jit(solution)/shard_map/norm/pallas_call | solution.py:165
  (8 shorter events, 0.0 us)
Async XLA Ops:
  1.8 14.1 %collective-permute-start = (bf16[136,1280]{1,0:T(8,128)(2,1)}, bf16[136,1280]{1,0:T(8,128)(2,1)S(1)}, u32[]{:S(2)}, u32[]{:S(2)}) collective-permute-start(bf16[136,1280]{1,0:T(8,128)(2,1)} %to_send.1), channel_id=1, source_target_pairs={{0,4},{4,0},{8,12},{12,8},{1,5},{5,1},{9,13},{13,9},{2,6},{6,2},{1... | collective-permute-start | bytes 1044488 | tf_op jit(solution)/shard_map/ppermute | solution.py:191
  2.0 17.6 %collective-permute-start.1 = (bf16[136,1280]{1,0:T(8,128)(2,1)}, bf16[136,1280]{1,0:T(8,128)(2,1)S(1)}, u32[]{:S(2)}, u32[]{:S(2)}) collective-permute-start(bf16[136,1280]{1,0:T(8,128)(2,1)} %to_send.1), channel_id=1, source_target_pairs={{0,8},{4,12},{8,0},{12,4},{1,9},{5,13},{9,1},{13,5},{2,10},{6,14},... | collective-permute-start | bytes 1044488 | tf_op jit(solution)/shard_map/ppermute | solution.py:191
  4.3 30.1 %collective-permute-start.2 = (bf16[136,1280]{1,0:T(8,128)(2,1)}, bf16[136,1280]{1,0:T(8,128)(2,1)S(1)}, u32[]{:S(2)}, u32[]{:S(2)}) collective-permute-start(bf16[136,1280]{1,0:T(8,128)(2,1)} %to_send.1), channel_id=1, source_target_pairs={{0,12},{4,8},{8,4},{12,0},{1,13},{5,9},{9,5},{13,1},{2,14},{6,10},... | collective-permute-start | bytes 1044488 | tf_op jit(solution)/shard_map/ppermute | solution.py:191
  5.9 1.7 %copy-start = (bf16[1280,1024]{1,0:T(8,128)(2,1)S(1)}, bf16[1280,1024]{1,0:T(8,128)(2,1)}, u32[]{:S(2)}) copy-start(bf16[1280,1024]{1,0:T(8,128)(2,1)} %wa.9) | copy-start | bytes 7864324
  7.6 1.7 %copy-start.2 = (bf16[1280,1024]{1,0:T(8,128)(2,1)S(1)}, bf16[1280,1024]{1,0:T(8,128)(2,1)}, u32[]{:S(2)}) copy-start(bf16[1280,1024]{1,0:T(8,128)(2,1)} %wf.9) | copy-start | bytes 7864324
  9.4 1.1 %copy-start.4 = (bf16[1,256,1280]{2,1,0:T(8,128)(2,1)S(1)}, bf16[1,256,1280]{2,1,0:T(8,128)(2,1)}, u32[]{:S(2)}) copy-start(bf16[1,256,1280]{2,1,0:T(8,128)(2,1)} %param.8) | copy-start | bytes 1966084
  10.4 0.7 copy-start.6
  11.1 4.7 %copy-start.1 = (bf16[1280,1024]{1,0:T(8,128)(2,1)S(1)}, bf16[1280,1024]{1,0:T(8,128)(2,1)}, u32[]{:S(2)}) copy-start(bf16[1280,1024]{1,0:T(8,128)(2,1)} %wa.9) | copy-start | bytes 7864324
  11.1 4.7 %copy-start.3 = (bf16[1280,1024]{1,0:T(8,128)(2,1)S(1)}, bf16[1280,1024]{1,0:T(8,128)(2,1)}, u32[]{:S(2)}) copy-start(bf16[1280,1024]{1,0:T(8,128)(2,1)} %wf.9) | copy-start | bytes 7864324
  34.4 3.2 %collective-permute-start.5 = (bf16[136,1280]{1,0:T(8,128)(2,1)S(1)}, bf16[136,1280]{1,0:T(8,128)(2,1)S(1)}, u32[]{:S(2)}, u32[]{:S(2)}) collective-permute-start(bf16[136,1280]{1,0:T(8,128)(2,1)S(1)} %collective-permute-done.2.refs_0_), channel_id=1, source_target_pairs={{0,1},{1,0},{2,3},{3,2},{4,5},{5,4},{6,7},{7,6},{8,9},{9,8},{10,11... | collective-permute-start | bytes 1044488 | tf_op jit(solution)/shard_map/ppermute | solution.py:187
  36.3 1.8 %collective-permute-start.4 = (bf16[136,1280]{1,0:T(8,128)(2,1)S(1)}, bf16[136,1280]{1,0:T(8,128)(2,1)S(1)}, u32[]{:S(2)}, u32[]{:S(2)}) collective-permute-start(bf16[136,1280]{1,0:T(8,128)(2,1)S(1)} %collective-permute-done.1.refs_0_), channel_id=1, source_target_pairs={{0,1},{1,0},{2,3},{3,2},{4,5},{5,4},{6,7},{7,6},{8,9},{9,8},{10,11... | collective-permute-start | bytes 1044488 | tf_op jit(solution)/shard_map/ppermute | solution.py:187
  36.3 2.3 %collective-permute-start.3 = (bf16[136,1280]{1,0:T(8,128)(2,1)S(1)}, bf16[136,1280]{1,0:T(8,128)(2,1)S(1)}, u32[]{:S(2)}, u32[]{:S(2)}) collective-permute-start(bf16[136,1280]{1,0:T(8,128)(2,1)S(1)} %collective-permute-done.refs_0_), channel_id=1, source_target_pairs={{0,1},{1,0},{2,3},{3,2},{4,5},{5,4},{6,7},{7,6},{8,9},{9,8},{10,11... | collective-permute-start | bytes 1044488 | tf_op jit(solution)/shard_map/ppermute | solution.py:187
  37.7 3.2 %copy-start.5 = (s32[1,256]{1,0:T(1,128)S(1)}, s32[1,256]{1,0:T(1,128)}, u32[]{:S(2)}) copy-start(s32[1,256]{1,0:T(1,128)} %refs_5_.4) | copy-start | bytes 3076
  42.8 23.6 %copy-start.7 = (bf16[8192]{0:T(1024)(128)(2,1)S(1)}, bf16[8192]{0:T(1024)(128)(2,1)}, u32[]{:S(2)}) copy-start(bf16[8192]{0:T(1024)(128)(2,1)} %param.15) | copy-start | bytes 49156
  44.7 5.6 %collective-permute-start.12 = (bf16[128,1024]{1,0:T(8,128)(2,1)S(1)}, bf16[128,1024]{1,0:T(8,128)(2,1)S(1)}, u32[]{:S(2)}, u32[]{:S(2)}) collective-permute-start(bf16[128,1024]{1,0:T(8,128)(2,1)S(1)} %get-tuple-element.48), channel_id=1, source_target_pairs={{0,1},{1,0},{4,5},{5,4},{8,9},{9,8},{12,13},{13,12},{2,3},{3,2},{6... | collective-permute-start | bytes 786440 | tf_op jit(solution)/shard_map/ppermute | solution.py:214
  45.2 17.1 %collective-permute-start.10 = (bf16[128,1024]{1,0:T(8,128)(2,1)S(1)}, bf16[128,1024]{1,0:T(8,128)(2,1)S(1)}, u32[]{:S(2)}, u32[]{:S(2)}) collective-permute-start(bf16[128,1024]{1,0:T(8,128)(2,1)S(1)} %get-tuple-element.44), channel_id=1, source_target_pairs={{0,8},{1,9},{4,12},{5,13},{8,0},{9,1},{12,4},{13,5},{2,10},{3,11},... | collective-permute-start | bytes 786440 | tf_op jit(solution)/shard_map/ppermute | solution.py:214
  45.2 39.6 %collective-permute-start.8 = (bf16[128,1024]{1,0:T(8,128)(2,1)S(1)}, bf16[128,1024]{1,0:T(8,128)(2,1)S(1)}, u32[]{:S(2)}, u32[]{:S(2)}) collective-permute-start(bf16[128,1024]{1,0:T(8,128)(2,1)S(1)} %get-tuple-element.41), channel_id=1, source_target_pairs={{0,12},{1,13},{4,8},{5,9},{8,4},{9,5},{12,0},{13,1},{2,14},{3,15},... | collective-permute-start | bytes 786440 | tf_op jit(solution)/shard_map/ppermute | solution.py:214
  46.4 45.9 %collective-permute-start.6 = (bf16[128,1024]{1,0:T(8,128)(2,1)S(1)}, bf16[128,1024]{1,0:T(8,128)(2,1)S(1)}, u32[]{:S(2)}, u32[]{:S(2)}) collective-permute-start(bf16[128,1024]{1,0:T(8,128)(2,1)S(1)} %get-tuple-element.38), channel_id=1, source_target_pairs={{0,4},{1,5},{4,0},{5,1},{8,12},{9,13},{12,8},{13,9},{2,6},{3,7},{6... | collective-permute-start | bytes 786440 | tf_op jit(solution)/shard_map/ppermute | solution.py:214
  48.7 36.0 %collective-permute-start.11 = (bf16[128,1024]{1,0:T(8,128)(2,1)S(1)}, bf16[128,1024]{1,0:T(8,128)(2,1)S(1)}, u32[]{:S(2)}, u32[]{:S(2)}) collective-permute-start(bf16[128,1024]{1,0:T(8,128)(2,1)S(1)} %get-tuple-element.45), channel_id=1, source_target_pairs={{0,9},{1,8},{4,13},{5,12},{8,1},{9,0},{12,5},{13,4},{2,11},{3,10},... | collective-permute-start | bytes 786440 | tf_op jit(solution)/shard_map/ppermute | solution.py:214
  50.3 42.1 %collective-permute-start.9 = (bf16[128,1024]{1,0:T(8,128)(2,1)S(1)}, bf16[128,1024]{1,0:T(8,128)(2,1)S(1)}, u32[]{:S(2)}, u32[]{:S(2)}) collective-permute-start(bf16[128,1024]{1,0:T(8,128)(2,1)S(1)} %get-tuple-element.42), channel_id=1, source_target_pairs={{0,13},{1,12},{4,9},{5,8},{8,5},{9,4},{12,1},{13,0},{2,15},{3,14},... | collective-permute-start | bytes 786440 | tf_op jit(solution)/shard_map/ppermute | solution.py:214
  62.3 30.1 %collective-permute-start.7 = (bf16[128,1024]{1,0:T(8,128)(2,1)S(1)}, bf16[128,1024]{1,0:T(8,128)(2,1)S(1)}, u32[]{:S(2)}, u32[]{:S(2)}) collective-permute-start(bf16[128,1024]{1,0:T(8,128)(2,1)S(1)} %get-tuple-element.39), channel_id=1, source_target_pairs={{0,5},{1,4},{4,1},{5,0},{8,13},{9,12},{12,9},{13,8},{2,7},{3,6},{6... | collective-permute-start | bytes 786440 | tf_op jit(solution)/shard_map/ppermute | solution.py:214

commit v4 on v3

--- a/solution.py
+++ b/solution.py
@@ -88,29 +88,42 @@
     )(kind, rows, *weights)
 
 
-def project_halves_kernel(wa, wf, ba, bf, *refs):
-    pieces, out, slots = refs[:-2], refs[-2], refs[-1]
-    half = pieces[0].shape[0] - 8
-    x = [r[:half, :] for r in pieces]
-    index = [r[half:, :half].astype(F32).astype(I32) for r in pieces]
+def is_in(z, members):
+    found = z == members[0]
+    for other in members[1:]:
+        found = jnp.logical_or(found, z == other)
+    return found
+
+
+def project_halves_kernel(receivers, wa, wf, ba, bf, *refs):
+    buffers, out, slots = list(refs[:-2]), refs[-2], refs[-1]
+    half = buffers[0].shape[0] - 8
+    z = lax.axis_index("ctx")
+    x, index = [], []
+    for choices in receivers:
+        piece = buffers.pop(0)[...]
+        for members in choices[1:]:
+            piece = jnp.where(is_in(z, members), buffers.pop(0)[...], piece)
+        x.append(piece[:half])
+        index.append(piece[half:, :half].astype(F32).astype(I32))
     x = x[0] if len(x) == 1 else jnp.concatenate(x, axis=0)
     index = index[0] if len(index) == 1 else jnp.concatenate(index, axis=1)
     slots[...] = index[0:1] * 256 + index[1:2]
     project(index[2:3], x, wa, wf, ba, bf, out)
 
 
-def project_halves(pieces, weights):
-    rows, ew = len(pieces) * (pieces[0].shape[0] - 8), pieces[0].shape[1]
+def project_halves(receivers, buffers, weights):
+    rows, ew = len(receivers) * (buffers[0].shape[0] - 8), buffers[0].shape[1]
     cols = weights[0].shape[1]
     return pl.pallas_call(
-        project_halves_kernel,
+        functools.partial(project_halves_kernel, receivers),
         out_shape=[jax.ShapeDtypeStruct((rows, cols), BF16), jax.ShapeDtypeStruct((1, rows), I32)],
-        in_specs=[VMEM] * (4 + len(pieces)),
+        in_specs=[VMEM] * (4 + len(buffers)),
         out_specs=[VMEM] * 2,
         compiler_params=PARAMS,
         cost_estimate=cost(4 * rows * ew * cols, 4 * ew * cols),
         name="project_halves",
-    )(*weights, *pieces)
+    )(*weights, *buffers)
 
 
 def select_kernel(m, count, *refs):
@@ -142,16 +155,42 @@
     )(*blocks, *slots)
 
 
-def norm_kernel(places_of, gain, *refs):
+def squares_kernel(*refs):
+    pieces, out = refs[:-1], refs[-1]
+    total = None
+    for piece in pieces:
+        if piece.dtype == F32:
+            part = piece[...]
+        else:
+            wide = piece[...].astype(F32)
+            part = jnp.sum(wide * wide, axis=1, keepdims=True)
+        total = part if total is None else total + part
+    out[...] = total
+
+
+def squares(total, pieces):
+    operands = pieces if total is None else [total] + pieces
+    places, cols = pieces[0].shape
+    return pl.pallas_call(
+        squares_kernel,
+        out_shape=jax.ShapeDtypeStruct((places, 1), F32),
+        in_specs=[VMEM] * len(operands),
+        out_specs=VMEM,
+        compiler_params=PARAMS,
+        cost_estimate=cost(1 << 36, 1 << 26),
+        name="squares",
+    )(*operands)
+
+
+def norm_kernel(places_of, fresh, gain, before, *refs):
     n = len(places_of)
     pieces, out = refs[:n], refs[n]
     cols = pieces[0].shape[1]
     z, t = lax.axis_index("ctx"), lax.axis_index("tp")
-    total = None
-    for piece in pieces:
-        wide = piece[...].astype(F32)
-        part = jnp.sum(wide * wide, axis=1, keepdims=True)
-        total = part if total is None else total + part
+    total = before[...]
+    for k in fresh:
+        wide = pieces[k][...].astype(F32)
+        total = total + jnp.sum(wide * wide, axis=1, keepdims=True)
     scale = lax.rsqrt(total / (n * cols) + 1e-06)
     for (m, d), piece in zip(places_of, pieces):
         block = jnp.bitwise_xor(z, m) * 2 + jnp.bitwise_xor(t, d)
@@ -159,22 +198,43 @@
         out[:, at] = (piece[...].astype(F32) * scale * gain[:, at].astype(F32)).astype(out.dtype)
 
 
-def norm(places_of, gain, pieces):
+def norm(places_of, fresh, gain, before, pieces):
     n = len(pieces)
     places, cols = pieces[0].shape
     return pl.pallas_call(
-        functools.partial(norm_kernel, places_of),
+        functools.partial(norm_kernel, places_of, fresh),
         out_shape=jax.ShapeDtypeStruct((places, n * cols), BF16),
-        in_specs=[VMEM] * (n + 1),
+        in_specs=[VMEM] * (n + 2),
         out_specs=VMEM,
         compiler_params=PARAMS,
         cost_estimate=cost(4 * places * n * cols, 4 * places * n * cols),
         name="norm",
-    )(gain, *pieces)
+    )(gain, before, *pieces)
 
 
 def after(x, *others):
     return lax.optimization_barrier((x, *others))[0]
+
+
+def gather_stages(n):
+    everyone = tuple(range(n))
+    if n == 4:
+        ends, middle = (0, 3), (1, 2)
+        first = (
+            [
+                ("near", [(0, 1), (1, 0), (2, 3), (3, 2)], "own"),
+                ("middle", [(1, 2), (2, 1)], "own"),
+                ("ends", [(0, 3), (3, 0)], "own"),
+            ],
+            [[("near", everyone)], [("ends", ends), ("middle", middle)]],
+        )
+        second = (
+            [("forward", [(1, 0), (2, 3)], "middle"), ("skip", [(0, 2), (3, 1)], "own")],
+            [[("forward", ends), ("skip", middle)]],
+        )
+        return [first, second]
+    messages = [(m, [(i, i ^ m) for i in range(n)], "own") for m in range(1, n)]
+    return [(messages, [[(m, everyone)] for m in range(1, n)])]
 
 
 def body(enc_rows, row_slot, row_kind, audio_proj, frame_proj, audio_bias, frame_bias, norm_gain):
@@ -183,38 +243,62 @@
     half = rows.shape[0] // 2
     weights = (audio_proj, frame_proj, audio_bias[None, :], frame_bias[None, :])
 
-    def over_tp(x):
-        return lax.ppermute(x, "tp", [(0, 1), (1, 0)])
-
-    mine = to_send(rows, row_slot, row_kind)
-    direct = [
-        lax.ppermute(mine, "ctx", [(i, i ^ m) for i in range(n)]) for m in range(1, n)
-    ]
-    own = project_own(row_kind, rows, weights)
-    blocks, slots, last = [own], [row_slot], own
-    for k in range(n - 1):
-        direct[k] = after(direct[k], last)
-        block, slot = project_halves([direct[k]], weights)
-        blocks.append(block)
-        slots.append(slot)
-        last = block
-    swapped = [over_tp(x) for x in direct]
-    for k in range(0, n - 1, 3):
-        block, slot = project_halves(swapped[k : k + 3], weights)
-        blocks.append(block)
-        slots.append(slot)
-
-    pieces, places_of = [], []
-    for m in [1] + list(reversed(range(2, n))) + [0]:
+    held = {"own": to_send(rows, row_slot, row_kind)}
+    blocks, slots, last = [], [], None
+    for messages, wanted in gather_stages(n):
+        names = [name for name, _, _ in messages]
+        arrived = [lax.ppermute(held[carried], "ctx", pairs) for _, pairs, carried in messages]
+        if last is None:
+            last = [project_own(row_kind, rows, weights)]
+            blocks += last
+            slots.append(row_slot)
+        arrived = lax.optimization_barrier((*arrived, *last))[: len(arrived)]
+        held.update(zip(names, arrived))
+        direct, swapped, receivers = [], [], []
+        for choices in wanted:
+            receivers.append(tuple(members for _, members in choices))
+            for name, members in choices:
+                swap = [(i * 2 + c, i * 2 + 1 - c) for i in members for c in range(2)]
+                direct.append([held[name]])
+                swapped.append([lax.ppermute(held[name], ("ctx", "tp"), swap)])
+        direct = [x for group in direct for x in group]
+        swapped = [x for group in swapped for x in group]
+        for buffers in (direct, swapped):
+            at = 0
+            for k in range(0, len(receivers), 3):
+                group = tuple(receivers[k : k + 3])
+                count = sum(len(choices) for choices in group)
+                block, slot = project_halves(group, buffers[at : at + count], weights)
+                at += count
+                blocks.append(block)
+                slots.append(slot)
+        last = blocks[1:]
+
+    order = [n - 1, 1] + list(reversed(range(2, n - 1))) + [0]
+    pieces = {}
+    for m in order:
         chosen = select(m, blocks, slots, half)
         slots[0] = after(slots[0], chosen[0])
         for d, piece in enumerate(chosen):
             if m or d:
                 perm = [(i * 2 + c, (i ^ m) * 2 + (c ^ d)) for i in range(n) for c in range(2)]
                 piece = lax.ppermute(piece, ("ctx", "tp"), perm)
-            pieces.append(piece)
-            places_of.append((m, d))
-    return norm(tuple(places_of), norm_gain[None, :], pieces)[None]
+            pieces[m, d] = piece
+
+    total = None
+    for m in order[:-2]:
+        fresh = [pieces[m, 0], pieces[m, 1]]
+        if total is None:
+            fresh += [pieces[0, 0], pieces[0, 1]]
+        else:
+            fresh = [after(piece, total) for piece in fresh]
+        total = squares(total, fresh)
+    places_of = tuple((m, d) for m in order for d in range(2))
+    fresh = tuple(k for k, (m, _) in enumerate(places_of) if m == order[-2])
+    final = [pieces[at] for at in places_of]
+    for k in fresh:
+        final[k] = after(final[k], total)
+    return norm(places_of, fresh, norm_gain[None, :], total, final)[None]
 
 
 def solution(mesh):

time: 95.4 us -> 97.6 us (1.023)
  the two profiles are of different devices: /device:TPU:13 before, /device:TPU:0 now
where the time goes in v4:
time: 97.6 us; the launch traced here: 97 us
  starting transfers between devices  41.9 us (43%)
  waiting for transfers between devices  33.7 us (35%)
  Pallas kernels  14.5 us (15%)
  local copies, waits for them, and re-layouts  6.66 us (7%)
    ppermute x7, starting transfers between devices, body(): piece = lax.ppermute(piece, ('ctx', 'tp'), perm)  24 us
    ppermute x7, waiting for transfers between devices, body(): piece = lax.ppermute(piece, ('ctx', 'tp'), perm)  19.7 us
    ppermute x5, waiting for transfers between devices, body(): lax.ppermute(held[carried], 'ctx', pairs)  14 us
    ppermute x5, starting transfers between devices, body(): lax.ppermute(held[carried], 'ctx', pairs)  12.2 us
    ppermute x5, starting transfers between devices, body(): swapped.append([lax.ppermute(held[name], ('ctx', 'tp'), swap)])  5.68 us
    unnamed x18, local copies, waits for them, and re-layouts  5.27 us
    pallas_call x4, Pallas kernels, project_halves(): pl.pallas_call(functools.partial(project_halves_kernel, receivers), out_s...  5.07 us
    pallas_call x4, Pallas kernels, select(): pl.pallas_call(functools.partial(select_kernel, m, len(blocks)), out_shap...  3.38 us
  transfers between devices with their start and end apart: 17, of which 7 were waited for; matrix products, arithmetic and copies ran while one was open for 1% of the time, Pallas kernels for 9%

profile of v4, /device:TPU:0, one launch (start us, length us, event | category | flops | bytes accessed | tf_op | source)
XLA Modules:
  0.0 97.0 jit_solution(6708853777947408276)
XLA Ops:
  0.0 1.8 %to_send.1 = bf16[136,1280]{1,0:T(8,128)(2,1)} custom-call(bf16[256,1280]{1,0:T(8,128)(2,1)} %bitcast.2, s32[1,256]{1,0:T(1,128)} %refs_5_.4, s32[1,256]{1,0:T(1,128)} %kind.3), custom_call_target="tpu_custom_call" | custom-call | bytes 40960 | tf_op jit(solution)/shard_map/to_send/pallas_call | solution.py:43
  1.8 7.0 %collective-permute-start.2 = (bf16[136,1280]{1,0:T(8,128)(2,1)}, bf16[136,1280]{1,0:T(8,128)(2,1)S(1)}, u32[]{:S(2)}, u32[]{:S(2)}) collective-permute-start(bf16[136,1280]{1,0:T(8,128)(2,1)} %to_send.1), channel_id=1, source_target_pairs={{0,12},{12,0},{1,13},{13,1},{2,14},{14,2},{3,15},{15,3},{16,28},{2... | collective-permute-start | bytes 1044488 | tf_op jit(solution)/shard_map/ppermute | solution.py:250
  8.7 0.7 collective-permute-start.1
  9.4 0.1 collective-permute-start
  9.5 0.7 broadcast_in_dim.13.ba
  10.2 0.7 broadcast_in_dim.14.bf
  10.9 1.7 %copy-done = bf16[1280,1024]{1,0:T(8,128)(2,1)S(1)} copy-done((bf16[1280,1024]{1,0:T(8,128)(2,1)S(1)}, bf16[1280,1024]{1,0:T(8,128)(2,1)}, u32[]{:S(2)}) %copy-start) | copy-done | bytes 2621464
  12.6 1.7 %copy-done.2 = bf16[1280,1024]{1,0:T(8,128)(2,1)S(1)} copy-done((bf16[1280,1024]{1,0:T(8,128)(2,1)S(1)}, bf16[1280,1024]{1,0:T(8,128)(2,1)}, u32[]{:S(2)}) %copy-start.2) | copy-done | bytes 2621464
  14.4 1.1 %copy-done.4 = bf16[1,256,1280]{2,1,0:T(8,128)(2,1)S(1)} copy-done((bf16[1,256,1280]{2,1,0:T(8,128)(2,1)S(1)}, bf16[1,256,1280]{2,1,0:T(8,128)(2,1)}, u32[]{:S(2)}) %copy-start.4) | copy-done | bytes 655384
  15.5 0.7 copy-done.6
  16.1 1.6 %project_own.1.refs_0_ = bf16[256,1024]{1,0:T(8,128)(2,1)S(1)} custom-call(s32[1,256]{1,0:T(1,128)S(1)} %copy-done.6, bf16[256,1280]{1,0:T(8,128)(2,1)S(1)} %bitcast.3, bf16[1280,1024]{1,0:T(8,128)(2,1)S(1)} %copy-done, bf16[1280,1024]{1,0:T(8,128)(2,1)S(1)} %copy-done.2, bf16[1,1024]{1,0:T(2,128)(2,1)S(1)} %broadcast_in_dim.13.ba, ...), custom_call_target="tpu_custom_call" | custom-call | flops 83886080 | bytes 327680 | tf_op jit(solution)/shard_map/project_own/pallas_call | solution.py:80
  17.7 0.3 collective-permute-done.2.refs_1_
  18.0 6.6 %collective-permute-done.refs_0_ = bf16[136,1280]{1,0:T(8,128)(2,1)S(1)} collective-permute-done((bf16[136,1280]{1,0:T(8,128)(2,1)}, bf16[136,1280]{1,0:T(8,128)(2,1)S(1)}, u32[]{:S(2)}, u32[]{:S(2)}) %collective-permute-start) | collective-permute-done | bytes 348192 | tf_op jit(solution)/shard_map/ppermute | solution.py:250
  24.7 0.0 collective-permute-start.3
  24.7 2.4 %collective-permute-start.4 = (bf16[136,1280]{1,0:T(8,128)(2,1)S(1)}, bf16[136,1280]{1,0:T(8,128)(2,1)S(1)}, u32[]{:S(2)}, u32[]{:S(2)}) collective-permute-start(bf16[136,1280]{1,0:T(8,128)(2,1)S(1)} %collective-permute-done.2.refs_1_), channel_id=1, source_target_pairs={{0,1},{1,0},{12,13},{13,12},{2,3},{3,2},{14,15},{15,14},{16,17},{1... | collective-permute-start | bytes 1044488 | tf_op jit(solution)/shard_map/ppermute | solution.py:263
  27.1 0.7 collective-permute-start.5
  27.8 3.2 %collective-permute-start.7 = (bf16[136,1280]{1,0:T(8,128)(2,1)S(1)}, bf16[136,1280]{1,0:T(8,128)(2,1)S(1)}, u32[]{:S(2)}, u32[]{:S(2)}) collective-permute-start(bf16[136,1280]{1,0:T(8,128)(2,1)S(1)} %copy-done.7), channel_id=1, source_target_pairs={{0,8},{12,4},{1,9},{13,5},{2,10},{14,6},{3,11},{15,7},{16,24},{28,... | collective-permute-start | bytes 1044488 | tf_op jit(solution)/shard_map/ppermute | solution.py:250
  31.0 1.3 %collective-permute-start.6 = (bf16[136,1280]{1,0:T(8,128)(2,1)S(1)}, bf16[136,1280]{1,0:T(8,128)(2,1)S(1)}, u32[]{:S(2)}, u32[]{:S(2)}) collective-permute-start(bf16[136,1280]{1,0:T(8,128)(2,1)S(1)} %collective-permute-done.1.refs_2_), channel_id=1, source_target_pairs={{4,0},{8,12},{5,1},{9,13},{6,2},{10,14},{7,3},{11,15},{20,16},{24,... | collective-permute-start | bytes 1044488 | tf_op jit(solution)/shard_map/ppermute | solution.py:250
  32.3 1.6 %project_halves.4 = (bf16[256,1024]{1,0:T(8,128)(2,1)S(1)}, s32[1,256]{1,0:T(1,128)S(1)}) custom-call(bf16[1280,1024]{1,0:T(8,128)(2,1)S(1)} %copy-done.1, bf16[1280,1024]{1,0:T(8,128)(2,1)S(1)} %copy-done.3, bf16[1,1024]{1,0:T(2,128)(2,1)S(1)} %broadcast_in_dim.13.ba, bf16[1,1024]{1,0:T(2,128)(2,1)S(1)} %broadcast_in_dim.14.bf, ...), custom_call_target="tpu_custom_call" | custom-call | flops 83886080 | bytes 327680 | tf_op jit(solution)/shard_map/project_halves/pallas_call | solution.py:118
  34.0 0.0 collective-permute-done.3.refs_0_
  34.0 0.0 collective-permute-done.5.refs_2_
  34.0 1.6 %project_halves.5 = (bf16[256,1024]{1,0:T(8,128)(2,1)S(1)}, s32[1,256]{1,0:T(1,128)S(1)}) custom-call(bf16[1280,1024]{1,0:T(8,128)(2,1)S(1)} %copy-done.1, bf16[1280,1024]{1,0:T(8,128)(2,1)S(1)} %copy-done.3, bf16[1,1024]{1,0:T(2,128)(2,1)S(1)} %broadcast_in_dim.13.ba, bf16[1,1024]{1,0:T(2,128)(2,1)S(1)} %broadcast_in_dim.14.bf, ...), custom_call_target="tpu_custom_call" | custom-call | flops 83886080 | bytes 327680 | tf_op jit(solution)/shard_map/project_halves/pallas_call | solution.py:118
  35.6 2.9 %collective-permute-done.7.refs_1_ = bf16[136,1280]{1,0:T(8,128)(2,1)S(1)} collective-permute-done((bf16[136,1280]{1,0:T(8,128)(2,1)S(1)}, bf16[136,1280]{1,0:T(8,128)(2,1)S(1)}, u32[]{:S(2)}, u32[]{:S(2)}) %collective-permute-start.7) | collective-permute-done | bytes 348192 | tf_op jit(solution)/shard_map/ppermute | solution.py:250
  38.6 4.1 %collective-permute-done.6.refs_0_ = bf16[136,1280]{1,0:T(8,128)(2,1)S(1)} collective-permute-done((bf16[136,1280]{1,0:T(8,128)(2,1)S(1)}, bf16[136,1280]{1,0:T(8,128)(2,1)S(1)}, u32[]{:S(2)}, u32[]{:S(2)}) %collective-permute-start.6) | collective-permute-done | bytes 348192 | tf_op jit(solution)/shard_map/ppermute | solution.py:250
  42.7 1.9 %collective-permute-start.8 = (bf16[136,1280]{1,0:T(8,128)(2,1)S(1)}, bf16[136,1280]{1,0:T(8,128)(2,1)S(1)}, u32[]{:S(2)}, u32[]{:S(2)}) collective-permute-start(bf16[136,1280]{1,0:T(8,128)(2,1)S(1)} %collective-permute-done.6.refs_0_), channel_id=1, source_target_pairs={{0,1},{1,0},{12,13},{13,12},{2,3},{3,2},{14,15},{15,14},{16,17},{1... | collective-permute-start | bytes 1044488 | tf_op jit(solution)/shard_map/ppermute | solution.py:263
  44.6 0.7 collective-permute-start.9
  45.3 0.9 project_halves.6
  46.2 0.0 copy-start.5
  46.3 0.0 collective-permute-done.8.refs_0_
  46.3 0.9 project_halves.7
  47.2 0.8 select.4
  48.0 2.8 %collective-permute-start.10 = (bf16[128,1024]{1,0:T(8,128)(2,1)S(1)}, bf16[128,1024]{1,0:T(8,128)(2,1)S(1)}, u32[]{:S(2)}, u32[]{:S(2)}) collective-permute-start(bf16[128,1024]{1,0:T(8,128)(2,1)S(1)} %get-tuple-element.46), channel_id=1, source_target_pairs={{0,12},{1,13},{4,8},{5,9},{8,4},{9,5},{12,0},{13,1},{2,14},{3,15},... | collective-permute-start | bytes 786440 | tf_op jit(solution)/shard_map/ppermute | solution.py:285
  50.9 0.9 collective-permute-start.11
  51.8 0.8 select.5
  52.6 0.0 copy-start.8
  52.6 0.8 select.6
  53.5 0.8 select.7
  54.3 0.3 collective-permute-start.12
  54.7 0.1 collective-permute-start.13
  54.8 3.3 %collective-permute-start.15 = (bf16[128,1024]{1,0:T(8,128)(2,1)S(1)}, bf16[128,1024]{1,0:T(8,128)(2,1)S(1)}, u32[]{:S(2)}, u32[]{:S(2)}) collective-permute-start(bf16[128,1024]{1,0:T(8,128)(2,1)S(1)} %get-tuple-element.51), channel_id=1, source_target_pairs={{0,8},{1,9},{4,12},{5,13},{8,0},{9,1},{12,4},{13,5},{2,10},{3,11},... | collective-permute-start | bytes 786440 | tf_op jit(solution)/shard_map/ppermute | solution.py:285
  58.1 6.0 %collective-permute-done.11.refs_1_ = bf16[128,1024]{1,0:T(8,128)(2,1)S(1)} collective-permute-done((bf16[128,1024]{1,0:T(8,128)(2,1)S(1)}, bf16[128,1024]{1,0:T(8,128)(2,1)S(1)}, u32[]{:S(2)}, u32[]{:S(2)}) %collective-permute-start.11) | collective-permute-done | bytes 262176 | tf_op jit(solution)/shard_map/ppermute | solution.py:285
  64.1 15.4 %collective-permute-start.14 = (bf16[128,1024]{1,0:T(8,128)(2,1)S(1)}, bf16[128,1024]{1,0:T(8,128)(2,1)S(1)}, u32[]{:S(2)}, u32[]{:S(2)}) collective-permute-start(bf16[128,1024]{1,0:T(8,128)(2,1)S(1)} %get-tuple-element.56), channel_id=1, source_target_pairs={{0,5},{1,4},{4,1},{5,0},{8,13},{9,12},{12,9},{13,8},{2,7},{3,6},{6... | collective-permute-start | bytes 786440 | tf_op jit(solution)/shard_map/ppermute | solution.py:285
  79.4 1.2 %collective-permute-start.16 = (bf16[128,1024]{1,0:T(8,128)(2,1)S(1)}, bf16[128,1024]{1,0:T(8,128)(2,1)S(1)}, u32[]{:S(2)}, u32[]{:S(2)}) collective-permute-start(bf16[128,1024]{1,0:T(8,128)(2,1)S(1)} %get-tuple-element.59), channel_id=1, source_target_pairs={{0,9},{1,8},{4,13},{5,12},{8,1},{9,0},{12,5},{13,4},{2,11},{3,10},... | collective-permute-start | bytes 786440 | tf_op jit(solution)/shard_map/ppermute | solution.py:285
  80.6 0.3 squares.2.refs_0_
  80.9 12.4 %collective-permute-done.14.refs_2_.refs_3_ = bf16[128,1024]{1,0:T(8,128)(2,1)S(1)} collective-permute-done((bf16[128,1024]{1,0:T(8,128)(2,1)S(1)}, bf16[128,1024]{1,0:T(8,128)(2,1)S(1)}, u32[]{:S(2)}, u32[]{:S(2)}) %collective-permute-start.14) | collective-permute-done | bytes 262176 | tf_op jit(solution)/shard_map/ppermute | solution.py:285
  93.3 0.2 squares.3.before
  93.5 1.3 %collective-permute-done.16.refs_5_ = bf16[128,1024]{1,0:T(8,128)(2,1)S(1)} collective-permute-done((bf16[128,1024]{1,0:T(8,128)(2,1)S(1)}, bf16[128,1024]{1,0:T(8,128)(2,1)S(1)}, u32[]{:S(2)}, u32[]{:S(2)}) %collective-permute-start.16) | collective-permute-done | bytes 262176 | tf_op jit(solution)/shard_map/ppermute | solution.py:285
  94.8 2.2 %norm.1 = bf16[128,8192]{1,0:T(8,128)(2,1)} custom-call(bf16[1,8192]{1,0:T(2,128)(2,1)S(1)} %broadcast_in_dim.12.gain, f32[128,1]{1,0:T(8,128)S(1)} %squares.3.before, bf16[128,1024]{1,0:T(8,128)(2,1)S(1)} %collective-permute-done.10.refs_0_, bf16[128,1024]{1,0:T(8,128)(2,1)S(1)} %collective-permute-done.11.refs_1_, ...), custom_call_target="tpu_custom_call" | custom-call | flops 262144 | bytes 262144 | tf_op jit(solution)/shard_map/norm/pallas_call | solution.py:204
  (20 shorter events, 0.1 us)
Async XLA Ops:
  1.8 16.2 %collective-permute-start.2 = (bf16[136,1280]{1,0:T(8,128)(2,1)}, bf16[136,1280]{1,0:T(8,128)(2,1)S(1)}, u32[]{:S(2)}, u32[]{:S(2)}) collective-permute-start(bf16[136,1280]{1,0:T(8,128)(2,1)} %to_send.1), channel_id=1, source_target_pairs={{0,12},{12,0},{1,13},{13,1},{2,14},{14,2},{3,15},{15,3},{16,28},{2... | collective-permute-start | bytes 1044488 | tf_op jit(solution)/shard_map/ppermute | solution.py:250
  8.7 9.3 %collective-permute-start.1 = (bf16[136,1280]{1,0:T(8,128)(2,1)}, bf16[136,1280]{1,0:T(8,128)(2,1)S(1)}, u32[]{:S(2)}, u32[]{:S(2)}) collective-permute-start(bf16[136,1280]{1,0:T(8,128)(2,1)} %to_send.1), channel_id=1, source_target_pairs={{4,8},{8,4},{5,9},{9,5},{6,10},{10,6},{7,11},{11,7},{20,24},{24,20... | collective-permute-start | bytes 1044488 | tf_op jit(solution)/shard_map/ppermute | solution.py:250
  9.4 15.2 %collective-permute-start = (bf16[136,1280]{1,0:T(8,128)(2,1)}, bf16[136,1280]{1,0:T(8,128)(2,1)S(1)}, u32[]{:S(2)}, u32[]{:S(2)}) collective-permute-start(bf16[136,1280]{1,0:T(8,128)(2,1)} %to_send.1), channel_id=1, source_target_pairs={{0,4},{4,0},{8,12},{12,8},{1,5},{5,1},{9,13},{13,9},{2,6},{6,2},{1... | collective-permute-start | bytes 1044488 | tf_op jit(solution)/shard_map/ppermute | solution.py:250
  10.9 1.7 %copy-start = (bf16[1280,1024]{1,0:T(8,128)(2,1)S(1)}, bf16[1280,1024]{1,0:T(8,128)(2,1)}, u32[]{:S(2)}) copy-start(bf16[1280,1024]{1,0:T(8,128)(2,1)} %wa.9) | copy-start | bytes 7864324
  12.6 1.7 %copy-start.2 = (bf16[1280,1024]{1,0:T(8,128)(2,1)S(1)}, bf16[1280,1024]{1,0:T(8,128)(2,1)}, u32[]{:S(2)}) copy-start(bf16[1280,1024]{1,0:T(8,128)(2,1)} %wf.9) | copy-start | bytes 7864324
  14.4 1.1 %copy-start.4 = (bf16[1,256,1280]{2,1,0:T(8,128)(2,1)S(1)}, bf16[1,256,1280]{2,1,0:T(8,128)(2,1)}, u32[]{:S(2)}) copy-start(bf16[1,256,1280]{2,1,0:T(8,128)(2,1)} %param.8) | copy-start | bytes 1966084
  15.5 0.7 copy-start.6
  16.1 11.6 %copy-start.7 = (bf16[136,1280]{1,0:T(8,128)(2,1)S(1)}, bf16[136,1280]{1,0:T(8,128)(2,1)}, u32[]{:S(2)}) copy-start(bf16[136,1280]{1,0:T(8,128)(2,1)} %to_send.1) | copy-start | bytes 1044484
  16.1 16.2 %copy-start.1 = (bf16[1280,1024]{1,0:T(8,128)(2,1)S(1)}, bf16[1280,1024]{1,0:T(8,128)(2,1)}, u32[]{:S(2)}) copy-start(bf16[1280,1024]{1,0:T(8,128)(2,1)} %wa.9) | copy-start | bytes 7864324
  16.1 16.2 %copy-start.3 = (bf16[1280,1024]{1,0:T(8,128)(2,1)S(1)}, bf16[1280,1024]{1,0:T(8,128)(2,1)}, u32[]{:S(2)}) copy-start(bf16[1280,1024]{1,0:T(8,128)(2,1)} %wf.9) | copy-start | bytes 7864324
  24.7 9.3 %collective-permute-start.3 = (bf16[136,1280]{1,0:T(8,128)(2,1)S(1)}, bf16[136,1280]{1,0:T(8,128)(2,1)S(1)}, u32[]{:S(2)}, u32[]{:S(2)}) collective-permute-start(bf16[136,1280]{1,0:T(8,128)(2,1)S(1)} %collective-permute-done.refs_0_), channel_id=1, source_target_pairs={{0,1},{1,0},{4,5},{5,4},{8,9},{9,8},{12,13},{13,12},{2,3},{3,2},{6... | collective-permute-start | bytes 1044488 | tf_op jit(solution)/shard_map/ppermute | solution.py:263
  24.7 9.3 %collective-permute-start.4 = (bf16[136,1280]{1,0:T(8,128)(2,1)S(1)}, bf16[136,1280]{1,0:T(8,128)(2,1)S(1)}, u32[]{:S(2)}, u32[]{:S(2)}) collective-permute-start(bf16[136,1280]{1,0:T(8,128)(2,1)S(1)} %collective-permute-done.2.refs_1_), channel_id=1, source_target_pairs={{0,1},{1,0},{12,13},{13,12},{2,3},{3,2},{14,15},{15,14},{16,17},{1... | collective-permute-start | bytes 1044488 | tf_op jit(solution)/shard_map/ppermute | solution.py:263
  27.1 6.9 %collective-permute-start.5 = (bf16[136,1280]{1,0:T(8,128)(2,1)S(1)}, bf16[136,1280]{1,0:T(8,128)(2,1)S(1)}, u32[]{:S(2)}, u32[]{:S(2)}) collective-permute-start(bf16[136,1280]{1,0:T(8,128)(2,1)S(1)} %collective-permute-done.1.refs_2_), channel_id=1, source_target_pairs={{4,5},{5,4},{8,9},{9,8},{6,7},{7,6},{10,11},{11,10},{20,21},{21,20... | collective-permute-start | bytes 1044488 | tf_op jit(solution)/shard_map/ppermute | solution.py:263
  27.8 10.8 %collective-permute-start.7 = (bf16[136,1280]{1,0:T(8,128)(2,1)S(1)}, bf16[136,1280]{1,0:T(8,128)(2,1)S(1)}, u32[]{:S(2)}, u32[]{:S(2)}) collective-permute-start(bf16[136,1280]{1,0:T(8,128)(2,1)S(1)} %copy-done.7), channel_id=1, source_target_pairs={{0,8},{12,4},{1,9},{13,5},{2,10},{14,6},{3,11},{15,7},{16,24},{28,... | collective-permute-start | bytes 1044488 | tf_op jit(solution)/shard_map/ppermute | solution.py:250
  31.0 11.7 %collective-permute-start.6 = (bf16[136,1280]{1,0:T(8,128)(2,1)S(1)}, bf16[136,1280]{1,0:T(8,128)(2,1)S(1)}, u32[]{:S(2)}, u32[]{:S(2)}) collective-permute-start(bf16[136,1280]{1,0:T(8,128)(2,1)S(1)} %collective-permute-done.1.refs_2_), channel_id=1, source_target_pairs={{4,0},{8,12},{5,1},{9,13},{6,2},{10,14},{7,3},{11,15},{20,16},{24,... | collective-permute-start | bytes 1044488 | tf_op jit(solution)/shard_map/ppermute | solution.py:250
  42.7 3.6 %collective-permute-start.8 = (bf16[136,1280]{1,0:T(8,128)(2,1)S(1)}, bf16[136,1280]{1,0:T(8,128)(2,1)S(1)}, u32[]{:S(2)}, u32[]{:S(2)}) collective-permute-start(bf16[136,1280]{1,0:T(8,128)(2,1)S(1)} %collective-permute-done.6.refs_0_), channel_id=1, source_target_pairs={{0,1},{1,0},{12,13},{13,12},{2,3},{3,2},{14,15},{15,14},{16,17},{1... | collective-permute-start | bytes 1044488 | tf_op jit(solution)/shard_map/ppermute | solution.py:263
  44.6 1.6 %collective-permute-start.9 = (bf16[136,1280]{1,0:T(8,128)(2,1)S(1)}, bf16[136,1280]{1,0:T(8,128)(2,1)S(1)}, u32[]{:S(2)}, u32[]{:S(2)}) collective-permute-start(bf16[136,1280]{1,0:T(8,128)(2,1)S(1)} %collective-permute-done.7.refs_1_), channel_id=1, source_target_pairs={{4,5},{5,4},{8,9},{9,8},{6,7},{7,6},{10,11},{11,10},{20,21},{21,20... | collective-permute-start | bytes 1044488 | tf_op jit(solution)/shard_map/ppermute | solution.py:263
  46.2 0.9 copy-start.5
  48.0 31.4 %collective-permute-start.10 = (bf16[128,1024]{1,0:T(8,128)(2,1)S(1)}, bf16[128,1024]{1,0:T(8,128)(2,1)S(1)}, u32[]{:S(2)}, u32[]{:S(2)}) collective-permute-start(bf16[128,1024]{1,0:T(8,128)(2,1)S(1)} %get-tuple-element.46), channel_id=1, source_target_pairs={{0,12},{1,13},{4,8},{5,9},{8,4},{9,5},{12,0},{13,1},{2,14},{3,15},... | collective-permute-start | bytes 786440 | tf_op jit(solution)/shard_map/ppermute | solution.py:285
  50.9 13.2 %collective-permute-start.11 = (bf16[128,1024]{1,0:T(8,128)(2,1)S(1)}, bf16[128,1024]{1,0:T(8,128)(2,1)S(1)}, u32[]{:S(2)}, u32[]{:S(2)}) collective-permute-start(bf16[128,1024]{1,0:T(8,128)(2,1)S(1)} %get-tuple-element.47), channel_id=1, source_target_pairs={{0,13},{1,12},{4,9},{5,8},{8,5},{9,4},{12,1},{13,0},{2,15},{3,14},... | collective-permute-start | bytes 786440 | tf_op jit(solution)/shard_map/ppermute | solution.py:285
  52.6 2.1 %copy-start.8 = (bf16[8192]{0:T(1024)(128)(2,1)S(1)}, bf16[8192]{0:T(1024)(128)(2,1)}, u32[]{:S(2)}) copy-start(bf16[8192]{0:T(1024)(128)(2,1)} %param.15) | copy-start | bytes 49156
  54.3 26.3 %collective-permute-start.12 = (bf16[128,1024]{1,0:T(8,128)(2,1)S(1)}, bf16[128,1024]{1,0:T(8,128)(2,1)S(1)}, u32[]{:S(2)}, u32[]{:S(2)}) collective-permute-start(bf16[128,1024]{1,0:T(8,128)(2,1)S(1)} %get-tuple-element.54), channel_id=1, source_target_pairs={{0,1},{1,0},{4,5},{5,4},{8,9},{9,8},{12,13},{13,12},{2,3},{3,2},{6... | collective-permute-start | bytes 786440 | tf_op jit(solution)/shard_map/ppermute | solution.py:285
  54.7 38.6 %collective-permute-start.13 = (bf16[128,1024]{1,0:T(8,128)(2,1)S(1)}, bf16[128,1024]{1,0:T(8,128)(2,1)S(1)}, u32[]{:S(2)}, u32[]{:S(2)}) collective-permute-start(bf16[128,1024]{1,0:T(8,128)(2,1)S(1)} %get-tuple-element.49), channel_id=1, source_target_pairs={{0,4},{1,5},{4,0},{5,1},{8,12},{9,13},{12,8},{13,9},{2,6},{3,7},{6... | collective-permute-start | bytes 786440 | tf_op jit(solution)/shard_map/ppermute | solution.py:285
  54.8 40.0 %collective-permute-start.15 = (bf16[128,1024]{1,0:T(8,128)(2,1)S(1)}, bf16[128,1024]{1,0:T(8,128)(2,1)S(1)}, u32[]{:S(2)}, u32[]{:S(2)}) collective-permute-start(bf16[128,1024]{1,0:T(8,128)(2,1)S(1)} %get-tuple-element.51), channel_id=1, source_target_pairs={{0,8},{1,9},{4,12},{5,13},{8,0},{9,1},{12,4},{13,5},{2,10},{3,11},... | collective-permute-start | bytes 786440 | tf_op jit(solution)/shard_map/ppermute | solution.py:285
  64.1 29.2 %collective-permute-start.14 = (bf16[128,1024]{1,0:T(8,128)(2,1)S(1)}, bf16[128,1024]{1,0:T(8,128)(2,1)S(1)}, u32[]{:S(2)}, u32[]{:S(2)}) collective-permute-start(bf16[128,1024]{1,0:T(8,128)(2,1)S(1)} %get-tuple-element.56), channel_id=1, source_target_pairs={{0,5},{1,4},{4,1},{5,0},{8,13},{9,12},{12,9},{13,8},{2,7},{3,6},{6... | collective-permute-start | bytes 786440 | tf_op jit(solution)/shard_map/ppermute | solution.py:285
  79.4 15.3 %collective-permute-start.16 = (bf16[128,1024]{1,0:T(8,128)(2,1)S(1)}, bf16[128,1024]{1,0:T(8,128)(2,1)S(1)}, u32[]{:S(2)}, u32[]{:S(2)}) collective-permute-start(bf16[128,1024]{1,0:T(8,128)(2,1)S(1)} %get-tuple-element.59), channel_id=1, source_target_pairs={{0,9},{1,8},{4,13},{5,12},{8,1},{9,0},{12,5},{13,4},{2,11},{3,10},... | collective-permute-start | bytes 786440 | tf_op jit(solution)/shard_map/ppermute | solution.py:285

commit v5 on v3

--- a/solution.py
+++ b/solution.py
@@ -90,9 +90,12 @@
 
 def project_halves_kernel(wa, wf, ba, bf, *refs):
     pieces, out, slots = refs[:-2], refs[-2], refs[-1]
-    half = pieces[0].shape[0] - 8
-    x = [r[:half, :] for r in pieces]
-    index = [r[half:, :half].astype(F32).astype(I32) for r in pieces]
+    x, index = [], []
+    for piece in pieces:
+        half = piece.shape[-2] - 8
+        for k in range(piece.shape[0]):
+            x.append(piece[k, :half, :])
+            index.append(piece[k, half:, :half].astype(F32).astype(I32))
     x = x[0] if len(x) == 1 else jnp.concatenate(x, axis=0)
     index = index[0] if len(index) == 1 else jnp.concatenate(index, axis=1)
     slots[...] = index[0:1] * 256 + index[1:2]
@@ -100,7 +103,7 @@
 
 
 def project_halves(pieces, weights):
-    rows, ew = len(pieces) * (pieces[0].shape[0] - 8), pieces[0].shape[1]
+    rows, ew = sum(p.shape[0] * (p.shape[1] - 8) for p in pieces), pieces[0].shape[2]
     cols = weights[0].shape[1]
     return pl.pallas_call(
         project_halves_kernel,
@@ -114,8 +117,8 @@
 
 
 def select_kernel(m, count, *refs):
-    blocks, slots, outs = refs[:count], refs[count : 2 * count], refs[-2:]
-    places = outs[0].shape[0]
+    blocks, slots, outs = refs[:count], refs[count : 2 * count], refs[2 * count :]
+    places = sum(out.shape[0] for out in outs) // 2
     z, t = lax.axis_index("ctx"), lax.axis_index("tp")
     first = jnp.bitwise_xor(z, m) * 2 * places
     i = lax.broadcasted_iota(I32, (2 * places, 1), 0)
@@ -125,52 +128,91 @@
         chosen = (slot[...] == position).astype(F32).astype(BF16)
         part = jnp.dot(chosen, block[...], preferred_element_type=F32)
         total = part if total is None else total + part
-    outs[0][...] = total[:places].astype(BF16)
-    outs[1][...] = total[places:].astype(BF16)
-
-
-def select(m, blocks, slots, places):
+    at = 0
+    for out in outs:
+        out[...] = total[at : at + out.shape[0]].astype(BF16)
+        at += out.shape[0]
+
+
+def select(m, blocks, slots, sizes):
     rows, cols = sum(b.shape[0] for b in blocks), blocks[0].shape[1]
     return pl.pallas_call(
         functools.partial(select_kernel, m, len(blocks)),
-        out_shape=[jax.ShapeDtypeStruct((places, cols), BF16)] * 2,
+        out_shape=[jax.ShapeDtypeStruct((size, cols), BF16) for size in sizes],
         in_specs=[VMEM] * (2 * len(blocks)),
-        out_specs=[VMEM] * 2,
-        compiler_params=PARAMS,
-        cost_estimate=cost(4 * places * rows * cols, 2 * rows * cols),
+        out_specs=[VMEM] * len(sizes),
+        compiler_params=PARAMS,
+        cost_estimate=cost(2 * sum(sizes) * rows * cols, 2 * rows * cols),
         name="select",
     )(*blocks, *slots)
 
 
-def norm_kernel(places_of, gain, *refs):
+def view(ref, places):
+    if len(ref.shape) == 3:
+        return ref.at[1 - lax.axis_index("tp")]
+    return ref.at[pl.ds(0, places), :]
+
+
+def square_sum(piece):
+    wide = piece[...].astype(F32)
+    return jnp.sum(wide * wide, axis=1, keepdims=True)
+
+
+def squares_kernel(*refs):
+    out = refs[-1]
+    total = None
+    for ref in refs[:-1]:
+        part = ref[...] if ref.dtype == F32 else square_sum(view(ref, out.shape[0]))
+        total = part if total is None else total + part
+    out[...] = total
+
+
+def squares(total, pieces, places):
+    operands = pieces if total is None else [total] + pieces
+    return pl.pallas_call(
+        squares_kernel,
+        out_shape=jax.ShapeDtypeStruct((places, 1), F32),
+        in_specs=[VMEM] * len(operands),
+        out_specs=VMEM,
+        compiler_params=PARAMS,
+        cost_estimate=cost(1 << 36, 1 << 26),
+        name="squares",
+    )(*operands)
+
+
+def norm_kernel(places_of, fresh, gain, before, *refs):
     n = len(places_of)
-    pieces, out = refs[:n], refs[n]
-    cols = pieces[0].shape[1]
+    out, scaled, sems = refs[n], refs[n + 1], refs[n + 2]
+    places, cols = scaled.shape[1:]
+    pieces = [view(ref, places) for ref in refs[:n]]
     z, t = lax.axis_index("ctx"), lax.axis_index("tp")
-    total = None
-    for piece in pieces:
-        wide = piece[...].astype(F32)
-        part = jnp.sum(wide * wide, axis=1, keepdims=True)
-        total = part if total is None else total + part
+    total = before[...]
+    for k in fresh:
+        total = total + square_sum(pieces[k])
     scale = lax.rsqrt(total / (n * cols) + 1e-06)
-    for (m, d), piece in zip(places_of, pieces):
+    copies = []
+    for k, ((m, d), piece) in enumerate(zip(places_of, pieces)):
         block = jnp.bitwise_xor(z, m) * 2 + jnp.bitwise_xor(t, d)
         at = pl.ds(pl.multiple_of(block * cols, cols), cols)
-        out[:, at] = (piece[...].astype(F32) * scale * gain[:, at].astype(F32)).astype(out.dtype)
-
-
-def norm(places_of, gain, pieces):
-    n = len(pieces)
-    places, cols = pieces[0].shape
-    return pl.pallas_call(
-        functools.partial(norm_kernel, places_of),
+        scaled[k] = (piece[...].astype(F32) * scale * gain[:, at].astype(F32)).astype(BF16)
+        copies.append(pltpu.make_async_copy(scaled.at[k], out.at[:, at], sems.at[k]))
+        copies[k].start()
+    for copy in copies:
+        copy.wait()
+
+
+def norm(places_of, fresh, gain, before, pieces):
+    n, places, cols = len(pieces), before.shape[0], pieces[0].shape[-1]
+    return pl.pallas_call(
+        functools.partial(norm_kernel, places_of, fresh),
         out_shape=jax.ShapeDtypeStruct((places, n * cols), BF16),
-        in_specs=[VMEM] * (n + 1),
-        out_specs=VMEM,
+        in_specs=[VMEM] * (n + 2),
+        out_specs=HBM,
+        scratch_shapes=[pltpu.VMEM((n, places, cols), BF16), pltpu.SemaphoreType.DMA((n,))],
         compiler_params=PARAMS,
         cost_estimate=cost(4 * places * n * cols, 4 * places * n * cols),
         name="norm",
-    )(gain, *pieces)
+    )(gain, before, *pieces)
 
 
 def after(x, *others):
@@ -183,38 +225,58 @@
     half = rows.shape[0] // 2
     weights = (audio_proj, frame_proj, audio_bias[None, :], frame_bias[None, :])
 
+    def over_ctx(x, m):
+        return lax.ppermute(x, "ctx", [(i, i ^ m) for i in range(n)])
+
     def over_tp(x):
         return lax.ppermute(x, "tp", [(0, 1), (1, 0)])
 
     mine = to_send(rows, row_slot, row_kind)
-    direct = [
-        lax.ppermute(mine, "ctx", [(i, i ^ m) for i in range(n)]) for m in range(1, n)
-    ]
-    own = project_own(row_kind, rows, weights)
-    blocks, slots, last = [own], [row_slot], own
-    for k in range(n - 1):
-        direct[k] = after(direct[k], last)
-        block, slot = project_halves([direct[k]], weights)
-        blocks.append(block)
-        slots.append(slot)
+    arrived = [over_ctx(mine, m) for m in range(1, n)]
+    last = project_own(row_kind, rows, weights)
+    blocks, slots = [last], [row_slot]
+    for k, direct in enumerate(arrived):
+        direct = after(direct, last)
+        if k < n - 2:
+            both = [lax.all_gather(direct, "tp", axis=0)]
+        else:
+            both = [direct[None], over_tp(direct)[None]]
+        groups = [both] if len(both) == 1 else [[half] for half in both]
+        for group in groups:
+            block, slot = project_halves(group, weights)
+            blocks.append(block)
+            slots.append(slot)
         last = block
-    swapped = [over_tp(x) for x in direct]
-    for k in range(0, n - 1, 3):
-        block, slot = project_halves(swapped[k : k + 3], weights)
-        blocks.append(block)
-        slots.append(slot)
-
-    pieces, places_of = [], []
-    for m in [1] + list(reversed(range(2, n))) + [0]:
-        chosen = select(m, blocks, slots, half)
+
+    pieces = {}
+    order = [n - 1, 1] + list(reversed(range(2, n - 1))) + [0]
+    for m in order:
+        chosen = select(m, blocks, slots, [2 * half] if m == 1 else [half, half])
         slots[0] = after(slots[0], chosen[0])
+        if m == 1:
+            pieces[m] = over_ctx(chosen[0], m)
+            continue
         for d, piece in enumerate(chosen):
             if m or d:
                 perm = [(i * 2 + c, (i ^ m) * 2 + (c ^ d)) for i in range(n) for c in range(2)]
                 piece = lax.ppermute(piece, ("ctx", "tp"), perm)
-            pieces.append(piece)
-            places_of.append((m, d))
-    return norm(tuple(places_of), norm_gain[None, :], pieces)[None]
+            pieces[m, d] = piece
+
+    total = squares(None, [pieces[0, 0], pieces[0, 1]], half)
+    for m in order[:-2]:
+        if m == 1:
+            pair = after(pieces[m], total)
+            pieces[m, 0], pieces[m, 1] = pair, lax.all_gather(pair[half:], "tp", axis=0)
+        fresh = [pieces[m, 0], pieces[m, 1]]
+        if m != 1:
+            fresh = [after(piece, total) for piece in fresh]
+        total = squares(total, fresh, half)
+    places_of = tuple((m, d) for m in order for d in range(2))
+    fresh = tuple(k for k, (m, _) in enumerate(places_of) if m == order[-2])
+    final = [pieces[at] for at in places_of]
+    for k in fresh:
+        final[k] = after(final[k], total)
+    return norm(places_of, fresh, norm_gain[None, :], total, final)[None]
 
 
 def solution(mesh):

time: 95.4 us -> 94.4 us (0.990)
  the two profiles are of different devices: /device:TPU:13 before, /device:TPU:0 now
where the time goes in v5:
time: 94.4 us; the launch traced here: 94.1 us
  waiting for transfers between devices  52 us (55%)
  Pallas kernels  14.4 us (15%)
  starting transfers between devices  13.5 us (14%)
  blocking collectives  7.33 us (8%)
  local copies, waits for them, and re-layouts  6.67 us (7%)
    ppermute x5, waiting for transfers between devices, body(): piece = lax.ppermute(piece, ('ctx', 'tp'), perm)  39 us
    ppermute x4, waiting for transfers between devices, over_ctx(): return lax.ppermute(x, 'ctx', [(i, i ^ m) for i in range(n)])  12.3 us
    ppermute x5, starting transfers between devices, body(): piece = lax.ppermute(piece, ('ctx', 'tp'), perm)  7.31 us
    ppermute x4, starting transfers between devices, over_ctx(): return lax.ppermute(x, 'ctx', [(i, i ^ m) for i in range(n)])  5.97 us
    unnamed x16, local copies, waits for them, and re-layouts  5.26 us
    pallas_call x4, Pallas kernels, project_halves(): pl.pallas_call(project_halves_kernel, out_shape=[jax.ShapeDtypeStruct((ro...  5.04 us
    all_gather x2, blocking collectives, body(): both = [lax.all_gather(direct, 'tp', axis=0)]  4.58 us
    pallas_call x4, Pallas kernels, select(): pl.pallas_call(functools.partial(select_kernel, m, len(blocks)), out_shap...  3.39 us
  transfers between devices with their start and end apart: 10, of which 5 were waited for; matrix products, arithmetic and copies ran while one was open for 1% of the time, Pallas kernels for 7%

profile of v5, /device:TPU:0, one launch (start us, length us, event | category | flops | bytes accessed | tf_op | source)
XLA Modules:
  0.0 94.1 jit_solution(14392559430481104533)
XLA Ops:
  0.0 1.8 %to_send.1 = bf16[136,1280]{1,0:T(8,128)(2,1)} custom-call(bf16[256,1280]{1,0:T(8,128)(2,1)} %bitcast.9, s32[1,256]{1,0:T(1,128)} %refs_5_.4, s32[1,256]{1,0:T(1,128)} %kind.3), custom_call_target="tpu_custom_call" | custom-call | bytes 40960 | tf_op jit(solution)/shard_map/to_send/pallas_call | solution.py:43
  1.8 3.1 %collective-permute-start = (bf16[136,1280]{1,0:T(8,128)(2,1)}, bf16[136,1280]{1,0:T(8,128)(2,1)S(1)}, u32[]{:S(2)}, u32[]{:S(2)}) collective-permute-start(bf16[136,1280]{1,0:T(8,128)(2,1)} %to_send.1), channel_id=1, source_target_pairs={{0,4},{4,0},{8,12},{12,8},{1,5},{5,1},{9,13},{13,9},{2,6},{6,2},{1... | collective-permute-start | bytes 1044488 | tf_op jit(solution)/shard_map/ppermute | solution.py:229
  4.9 2.6 %collective-permute-start.1 = (bf16[136,1280]{1,0:T(8,128)(2,1)}, bf16[136,1280]{1,0:T(8,128)(2,1)S(1)}, u32[]{:S(2)}, u32[]{:S(2)}) collective-permute-start(bf16[136,1280]{1,0:T(8,128)(2,1)} %to_send.1), channel_id=1, source_target_pairs={{0,8},{4,12},{8,0},{12,4},{1,9},{5,13},{9,1},{13,5},{2,10},{6,14},... | collective-permute-start | bytes 1044488 | tf_op jit(solution)/shard_map/ppermute | solution.py:229
  7.5 0.0 collective-permute-start.2
  7.5 0.7 broadcast_in_dim.19.ba
  8.2 0.7 broadcast_in_dim.20.bf
  8.8 1.7 %copy-done = bf16[1280,1024]{1,0:T(8,128)(2,1)S(1)} copy-done((bf16[1280,1024]{1,0:T(8,128)(2,1)S(1)}, bf16[1280,1024]{1,0:T(8,128)(2,1)}, u32[]{:S(2)}) %copy-start) | copy-done | bytes 2621464
  10.6 1.7 %copy-done.2 = bf16[1280,1024]{1,0:T(8,128)(2,1)S(1)} copy-done((bf16[1280,1024]{1,0:T(8,128)(2,1)S(1)}, bf16[1280,1024]{1,0:T(8,128)(2,1)}, u32[]{:S(2)}) %copy-start.2) | copy-done | bytes 2621464
  12.3 1.1 %copy-done.4 = bf16[1,256,1280]{2,1,0:T(8,128)(2,1)S(1)} copy-done((bf16[1,256,1280]{2,1,0:T(8,128)(2,1)S(1)}, bf16[1,256,1280]{2,1,0:T(8,128)(2,1)}, u32[]{:S(2)}) %copy-start.4) | copy-done | bytes 655384
  13.4 0.7 copy-done.6
  14.1 1.6 %project_own.1.refs_0_ = bf16[256,1024]{1,0:T(8,128)(2,1)S(1)} custom-call(s32[1,256]{1,0:T(1,128)S(1)} %copy-done.6, bf16[256,1280]{1,0:T(8,128)(2,1)S(1)} %bitcast.10, bf16[1280,1024]{1,0:T(8,128)(2,1)S(1)} %copy-done, bf16[1280,1024]{1,0:T(8,128)(2,1)S(1)} %copy-done.2, bf16[1,1024]{1,0:T(2,128)(2,1)S(1)} %broadcast_in_dim.19.ba, ...), custom_call_target="tpu_custom_call" | custom-call | flops 83886080 | bytes 327680 | tf_op jit(solution)/shard_map/project_own/pallas_call | solution.py:80
  15.7 4.2 %collective-permute-done = bf16[136,1280]{1,0:T(8,128)(2,1)S(1)} collective-permute-done((bf16[136,1280]{1,0:T(8,128)(2,1)}, bf16[136,1280]{1,0:T(8,128)(2,1)S(1)}, u32[]{:S(2)}, u32[]{:S(2)}) %collective-permute-start) | collective-permute-done | bytes 348192 | tf_op jit(solution)/shard_map/ppermute | solution.py:229
  19.9 2.3 %all-gather = bf16[272,1280]{1,0:T(8,128)(2,1)S(1)} all-gather(bf16[136,1280]{1,0:T(8,128)(2,1)S(1)} %collective-permute-done), channel_id=2, replica_groups=mesh['groups'=2,'ctx'=4,'enc'=2,'tp'=2] {'tp'}, dimensions={0}, use_global_device_ids=true | all-gather | bytes 1044480 | tf_op jit(solution)/shard_map/all_gather | solution.py:241
  22.2 0.0 copy-done.1
  22.2 0.0 copy-done.3
  22.2 1.6 %project_halves.4 = (bf16[256,1024]{1,0:T(8,128)(2,1)S(1)}, s32[1,256]{1,0:T(1,128)S(1)}) custom-call(bf16[1280,1024]{1,0:T(8,128)(2,1)S(1)} %copy-done.1, bf16[1280,1024]{1,0:T(8,128)(2,1)S(1)} %copy-done.3, bf16[1,1024]{1,0:T(2,128)(2,1)S(1)} %broadcast_in_dim.19.ba, bf16[1,1024]{1,0:T(2,128)(2,1)S(1)} %broadcast_in_dim.20.bf, ...), custom_call_target="tpu_custom_call" | custom-call | flops 83886080 | bytes 327680 | tf_op jit(solution)/shard_map/project_halves/pallas_call | solution.py:108
  23.9 8.1 %collective-permute-done.1 = bf16[136,1280]{1,0:T(8,128)(2,1)S(1)} collective-permute-done((bf16[136,1280]{1,0:T(8,128)(2,1)}, bf16[136,1280]{1,0:T(8,128)(2,1)S(1)}, u32[]{:S(2)}, u32[]{:S(2)}) %collective-permute-start.1) | collective-permute-done | bytes 348192 | tf_op jit(solution)/shard_map/ppermute | solution.py:229
  32.0 2.3 %all-gather.1 = bf16[272,1280]{1,0:T(8,128)(2,1)S(1)} all-gather(bf16[136,1280]{1,0:T(8,128)(2,1)S(1)} %collective-permute-done.1), channel_id=3, replica_groups=mesh['groups'=2,'ctx'=4,'enc'=2,'tp'=2] {'tp'}, dimensions={0}, use_global_device_ids=true | all-gather | bytes 1044480 | tf_op jit(solution)/shard_map/all_gather | solution.py:241
  34.3 1.6 %project_halves.5 = (bf16[256,1024]{1,0:T(8,128)(2,1)S(1)}, s32[1,256]{1,0:T(1,128)S(1)}) custom-call(bf16[1280,1024]{1,0:T(8,128)(2,1)S(1)} %copy-done.1, bf16[1280,1024]{1,0:T(8,128)(2,1)S(1)} %copy-done.3, bf16[1,1024]{1,0:T(2,128)(2,1)S(1)} %broadcast_in_dim.19.ba, bf16[1,1024]{1,0:T(2,128)(2,1)S(1)} %broadcast_in_dim.20.bf, ...), custom_call_target="tpu_custom_call" | custom-call | flops 83886080 | bytes 327680 | tf_op jit(solution)/shard_map/project_halves/pallas_call | solution.py:108
  35.9 0.0 collective-permute-done.2
  35.9 0.2 collective-permute-start.3
  36.1 0.9 project_halves.6
  37.0 0.6 collective-permute-done.3
  37.6 0.9 project_halves.7
  38.5 0.0 copy-done.5
  38.5 0.8 select.4
  39.4 0.8 select.5
  40.3 0.0 copy-start.7
  40.3 0.8 select.6
  41.1 0.8 select.7
  42.0 0.2 collective-permute-start.4
  42.2 0.0 copy-done.7
  42.2 2.5 %collective-permute-start.5 = (bf16[128,1024]{1,0:T(8,128)(2,1)S(1)}, bf16[128,1024]{1,0:T(8,128)(2,1)S(1)}, u32[]{:S(2)}, u32[]{:S(2)}) collective-permute-start(bf16[128,1024]{1,0:T(8,128)(2,1)S(1)} %get-tuple-element.41), channel_id=1, source_target_pairs={{0,12},{1,13},{4,8},{5,9},{8,4},{9,5},{12,0},{13,1},{2,14},{3,15},... | collective-permute-start | bytes 786440 | tf_op jit(solution)/shard_map/ppermute | solution.py:262
  44.8 1.6 %collective-permute-start.8 = (bf16[128,1024]{1,0:T(8,128)(2,1)S(1)}, bf16[128,1024]{1,0:T(8,128)(2,1)S(1)}, u32[]{:S(2)}, u32[]{:S(2)}) collective-permute-start(bf16[128,1024]{1,0:T(8,128)(2,1)S(1)} %get-tuple-element.44), channel_id=1, source_target_pairs={{0,8},{1,9},{4,12},{5,13},{8,0},{9,1},{12,4},{13,5},{2,10},{3,11},... | collective-permute-start | bytes 786440 | tf_op jit(solution)/shard_map/ppermute | solution.py:262
  46.4 0.3 collective-permute-start.7
  46.7 1.6 %collective-permute-start.6 = (bf16[128,1024]{1,0:T(8,128)(2,1)S(1)}, bf16[128,1024]{1,0:T(8,128)(2,1)S(1)}, u32[]{:S(2)}, u32[]{:S(2)}) collective-permute-start(bf16[128,1024]{1,0:T(8,128)(2,1)S(1)} %get-tuple-element.49), channel_id=1, source_target_pairs={{0,13},{1,12},{4,9},{5,8},{8,5},{9,4},{12,1},{13,0},{2,15},{3,14},... | collective-permute-start | bytes 786440 | tf_op jit(solution)/shard_map/ppermute | solution.py:262
  48.3 0.0 collective-permute-done.4.refs_1_.refs_7_
  48.3 1.3 %collective-permute-start.9 = (bf16[128,1024]{1,0:T(8,128)(2,1)S(1)}, bf16[128,1024]{1,0:T(8,128)(2,1)S(1)}, u32[]{:S(2)}, u32[]{:S(2)}) collective-permute-start(bf16[128,1024]{1,0:T(8,128)(2,1)S(1)} %get-tuple-element.53), channel_id=1, source_target_pairs={{0,9},{1,8},{4,13},{5,12},{8,1},{9,0},{12,5},{13,4},{2,11},{3,10},... | collective-permute-start | bytes 786440 | tf_op jit(solution)/shard_map/ppermute | solution.py:262
  49.6 0.2 squares.3.refs_0_
  49.8 25.0 %collective-permute-done.6.refs_2_.refs_1_ = bf16[128,1024]{1,0:T(8,128)(2,1)S(1)} collective-permute-done((bf16[128,1024]{1,0:T(8,128)(2,1)S(1)}, bf16[128,1024]{1,0:T(8,128)(2,1)S(1)}, u32[]{:S(2)}, u32[]{:S(2)}) %collective-permute-start.6) | collective-permute-done | bytes 262176 | tf_op jit(solution)/shard_map/ppermute | solution.py:262
  74.7 0.0 collective-permute-done.5.refs_1_.refs_0_
  74.7 0.2 squares.4.refs_0_
  74.9 0.0 collective-permute-done.7.refs_1_.refs_2_
  75.0 2.7 %all-gather.2 = bf16[256,1024]{1,0:T(8,128)(2,1)S(1)} all-gather(bf16[128,1024]{1,0:T(8,128)(2,1)S(1)} %slice.3), channel_id=4, replica_groups=mesh['groups'=2,'ctx'=4,'enc'=2,'tp'=2] {'tp'}, dimensions={0}, use_global_device_ids=true | all-gather | bytes 786432 | tf_op jit(solution)/shard_map/all_gather | solution.py:269
  77.7 0.2 squares.5.before
  77.9 14.1 %collective-permute-done.9.refs_5_ = bf16[128,1024]{1,0:T(8,128)(2,1)S(1)} collective-permute-done((bf16[128,1024]{1,0:T(8,128)(2,1)S(1)}, bf16[128,1024]{1,0:T(8,128)(2,1)S(1)}, u32[]{:S(2)}, u32[]{:S(2)}) %collective-permute-start.9) | collective-permute-done | bytes 262176 | tf_op jit(solution)/shard_map/ppermute | solution.py:262
  92.0 0.0 collective-permute-done.8.refs_4_
  92.0 2.1 %norm.1 = bf16[128,8192]{1,0:T(8,128)(2,1)} custom-call(bf16[1,8192]{1,0:T(2,128)(2,1)S(1)} %broadcast_in_dim.18.gain, f32[128,1]{1,0:T(8,128)S(1)} %squares.5.before, bf16[128,1024]{1,0:T(8,128)(2,1)S(1)} %collective-permute-done.5.refs_1_.refs_0_, bf16[128,1024]{1,0:T(8,128)(2,1)S(1)} %collective-permute-done.6.refs_2_.refs_1_, ...), custom_call_target="tpu_custom_call" | custom-call | flops 262144 | bytes 262144 | tf_op jit(solution)/shard_map/norm/pallas_call | solution.py:206
  (9 shorter events, 0.0 us)
Async XLA Ops:
  1.8 18.1 %collective-permute-start = (bf16[136,1280]{1,0:T(8,128)(2,1)}, bf16[136,1280]{1,0:T(8,128)(2,1)S(1)}, u32[]{:S(2)}, u32[]{:S(2)}) collective-permute-start(bf16[136,1280]{1,0:T(8,128)(2,1)} %to_send.1), channel_id=1, source_target_pairs={{0,4},{4,0},{8,12},{12,8},{1,5},{5,1},{9,13},{13,9},{2,6},{6,2},{1... | collective-permute-start | bytes 1044488 | tf_op jit(solution)/shard_map/ppermute | solution.py:229
  4.9 27.1 %collective-permute-start.1 = (bf16[136,1280]{1,0:T(8,128)(2,1)}, bf16[136,1280]{1,0:T(8,128)(2,1)S(1)}, u32[]{:S(2)}, u32[]{:S(2)}) collective-permute-start(bf16[136,1280]{1,0:T(8,128)(2,1)} %to_send.1), channel_id=1, source_target_pairs={{0,8},{4,12},{8,0},{12,4},{1,9},{5,13},{9,1},{13,5},{2,10},{6,14},... | collective-permute-start | bytes 1044488 | tf_op jit(solution)/shard_map/ppermute | solution.py:229
  7.5 28.4 %collective-permute-start.2 = (bf16[136,1280]{1,0:T(8,128)(2,1)}, bf16[136,1280]{1,0:T(8,128)(2,1)S(1)}, u32[]{:S(2)}, u32[]{:S(2)}) collective-permute-start(bf16[136,1280]{1,0:T(8,128)(2,1)} %to_send.1), channel_id=1, source_target_pairs={{0,12},{4,8},{8,4},{12,0},{1,13},{5,9},{9,5},{13,1},{2,14},{6,10},... | collective-permute-start | bytes 1044488 | tf_op jit(solution)/shard_map/ppermute | solution.py:229
  8.8 1.7 %copy-start = (bf16[1280,1024]{1,0:T(8,128)(2,1)S(1)}, bf16[1280,1024]{1,0:T(8,128)(2,1)}, u32[]{:S(2)}) copy-start(bf16[1280,1024]{1,0:T(8,128)(2,1)} %wa.9) | copy-start | bytes 7864324
  10.6 1.7 %copy-start.2 = (bf16[1280,1024]{1,0:T(8,128)(2,1)S(1)}, bf16[1280,1024]{1,0:T(8,128)(2,1)}, u32[]{:S(2)}) copy-start(bf16[1280,1024]{1,0:T(8,128)(2,1)} %wf.9) | copy-start | bytes 7864324
  12.3 1.1 %copy-start.4 = (bf16[1,256,1280]{2,1,0:T(8,128)(2,1)S(1)}, bf16[1,256,1280]{2,1,0:T(8,128)(2,1)}, u32[]{:S(2)}) copy-start(bf16[1,256,1280]{2,1,0:T(8,128)(2,1)} %param.8) | copy-start | bytes 1966084
  13.4 0.7 copy-start.6
  14.1 8.1 %copy-start.1 = (bf16[1280,1024]{1,0:T(8,128)(2,1)S(1)}, bf16[1280,1024]{1,0:T(8,128)(2,1)}, u32[]{:S(2)}) copy-start(bf16[1280,1024]{1,0:T(8,128)(2,1)} %wa.9) | copy-start | bytes 7864324
  14.1 8.1 %copy-start.3 = (bf16[1280,1024]{1,0:T(8,128)(2,1)S(1)}, bf16[1280,1024]{1,0:T(8,128)(2,1)}, u32[]{:S(2)}) copy-start(bf16[1280,1024]{1,0:T(8,128)(2,1)} %wf.9) | copy-start | bytes 7864324
  35.9 1.7 %collective-permute-start.3 = (bf16[136,1280]{1,0:T(8,128)(2,1)S(1)}, bf16[136,1280]{1,0:T(8,128)(2,1)S(1)}, u32[]{:S(2)}, u32[]{:S(2)}) collective-permute-start(bf16[136,1280]{1,0:T(8,128)(2,1)S(1)} %collective-permute-done.2), channel_id=1, source_target_pairs={{0,1},{1,0},{2,3},{3,2},{4,5},{5,4},{6,7},{7,6},{8,9},{9,8},{10,11... | collective-permute-start | bytes 1044488 | tf_op jit(solution)/shard_map/ppermute | solution.py:232
  37.6 0.9 copy-start.5
  40.3 1.9 %copy-start.7 = (bf16[8192]{0:T(1024)(128)(2,1)S(1)}, bf16[8192]{0:T(1024)(128)(2,1)}, u32[]{:S(2)}) copy-start(bf16[8192]{0:T(1024)(128)(2,1)} %param.15) | copy-start | bytes 49156
  42.0 6.3 %collective-permute-start.4 = (bf16[128,1024]{1,0:T(8,128)(2,1)S(1)}, bf16[128,1024]{1,0:T(8,128)(2,1)S(1)}, u32[]{:S(2)}, u32[]{:S(2)}) collective-permute-start(bf16[128,1024]{1,0:T(8,128)(2,1)S(1)} %get-tuple-element.47), channel_id=1, source_target_pairs={{0,1},{1,0},{4,5},{5,4},{8,9},{9,8},{12,13},{13,12},{2,3},{3,2},{6... | collective-permute-start | bytes 786440 | tf_op jit(solution)/shard_map/ppermute | solution.py:262
  42.2 32.5 %collective-permute-start.5 = (bf16[128,1024]{1,0:T(8,128)(2,1)S(1)}, bf16[128,1024]{1,0:T(8,128)(2,1)S(1)}, u32[]{:S(2)}, u32[]{:S(2)}) collective-permute-start(bf16[128,1024]{1,0:T(8,128)(2,1)S(1)} %get-tuple-element.41), channel_id=1, source_target_pairs={{0,12},{1,13},{4,8},{5,9},{8,4},{9,5},{12,0},{13,1},{2,14},{3,15},... | collective-permute-start | bytes 786440 | tf_op jit(solution)/shard_map/ppermute | solution.py:262
  44.8 47.2 %collective-permute-start.8 = (bf16[128,1024]{1,0:T(8,128)(2,1)S(1)}, bf16[128,1024]{1,0:T(8,128)(2,1)S(1)}, u32[]{:S(2)}, u32[]{:S(2)}) collective-permute-start(bf16[128,1024]{1,0:T(8,128)(2,1)S(1)} %get-tuple-element.44), channel_id=1, source_target_pairs={{0,8},{1,9},{4,12},{5,13},{8,0},{9,1},{12,4},{13,5},{2,10},{3,11},... | collective-permute-start | bytes 786440 | tf_op jit(solution)/shard_map/ppermute | solution.py:262
  46.4 28.5 %collective-permute-start.7 = (bf16[256,1024]{1,0:T(8,128)(2,1)S(1)}, bf16[256,1024]{1,0:T(8,128)(2,1)S(1)}, u32[]{:S(2)}, u32[]{:S(2)}) collective-permute-start(bf16[256,1024]{1,0:T(8,128)(2,1)S(1)} %select.5), channel_id=1, source_target_pairs={{0,4},{4,0},{8,12},{12,8},{1,5},{5,1},{9,13},{13,9},{2,6},{6,2},{1... | collective-permute-start | bytes 1572872 | tf_op jit(solution)/shard_map/ppermute | solution.py:229
  46.7 28.1 %collective-permute-start.6 = (bf16[128,1024]{1,0:T(8,128)(2,1)S(1)}, bf16[128,1024]{1,0:T(8,128)(2,1)S(1)}, u32[]{:S(2)}, u32[]{:S(2)}) collective-permute-start(bf16[128,1024]{1,0:T(8,128)(2,1)S(1)} %get-tuple-element.49), channel_id=1, source_target_pairs={{0,13},{1,12},{4,9},{5,8},{8,5},{9,4},{12,1},{13,0},{2,15},{3,14},... | collective-permute-start | bytes 786440 | tf_op jit(solution)/shard_map/ppermute | solution.py:262
  48.3 43.7 %collective-permute-start.9 = (bf16[128,1024]{1,0:T(8,128)(2,1)S(1)}, bf16[128,1024]{1,0:T(8,128)(2,1)S(1)}, u32[]{:S(2)}, u32[]{:S(2)}) collective-permute-start(bf16[128,1024]{1,0:T(8,128)(2,1)S(1)} %get-tuple-element.53), channel_id=1, source_target_pairs={{0,9},{1,8},{4,13},{5,12},{8,1},{9,0},{12,5},{13,4},{2,11},{3,10},... | collective-permute-start | bytes 786440 | tf_op jit(solution)/shard_map/ppermute | solution.py:262

commit v6 on v5

--- a/solution.py
+++ b/solution.py
@@ -249,7 +249,7 @@
         last = block
 
     pieces = {}
-    order = [n - 1, 1] + list(reversed(range(2, n - 1))) + [0]
+    order = [n - 1, 1] + list(reversed(range(2, n - 1)))
     for m in order:
         chosen = select(m, blocks, slots, [2 * half] if m == 1 else [half, half])
         slots[0] = after(slots[0], chosen[0])
@@ -257,20 +257,23 @@
             pieces[m] = over_ctx(chosen[0], m)
             continue
         for d, piece in enumerate(chosen):
-            if m or d:
-                perm = [(i * 2 + c, (i ^ m) * 2 + (c ^ d)) for i in range(n) for c in range(2)]
-                piece = lax.ppermute(piece, ("ctx", "tp"), perm)
-            pieces[m, d] = piece
-
-    total = squares(None, [pieces[0, 0], pieces[0, 1]], half)
-    for m in order[:-2]:
+            perm = [(i * 2 + c, (i ^ m) * 2 + (c ^ d)) for i in range(n) for c in range(2)]
+            pieces[m, d] = lax.ppermute(piece, ("ctx", "tp"), perm)
+
+    total = None
+    for m in order[:-1]:
         if m == 1:
+            slots[0] = after(slots[0], total)
+            pieces[0, 0], other = select(0, blocks, slots, [half, half])
+            pieces[0, 1] = lax.all_gather(other, "tp", axis=0)
+            total = squares(total, [pieces[0, 0], pieces[0, 1]], half)
             pair = after(pieces[m], total)
             pieces[m, 0], pieces[m, 1] = pair, lax.all_gather(pair[half:], "tp", axis=0)
         fresh = [pieces[m, 0], pieces[m, 1]]
-        if m != 1:
+        if m != 1 and total is not None:
             fresh = [after(piece, total) for piece in fresh]
         total = squares(total, fresh, half)
+    order.append(0)
     places_of = tuple((m, d) for m in order for d in range(2))
     fresh = tuple(k for k, (m, _) in enumerate(places_of) if m == order[-2])
     final = [pieces[at] for at in places_of]

time: 94.4 us -> 91.6 us (0.970)
  waiting for transfers between devices: 52 us -> 48.5 us
  blocking collectives: 7.33 us -> 8.95 us
    ppermute x5 -> x4, waiting for transfers between devices: 39 us -> 23.9 us  [body(): pieces[m, d] = lax.ppermute(piece, ('ctx', 'tp'), perm)]
    ppermute x4, waiting for transfers between devices: 12.3 us -> 24 us  [over_ctx(): return lax.ppermute(x, 'ctx', [(i, i ^ m) for i in range(n)])]
    all_gather x0 -> x1, blocking collectives: none -> 2.18 us  [body(): pieces[0, 1] = lax.all_gather(other, 'tp', axis=0)]
    ppermute x5 -> x4, starting transfers between devices: 7.31 us -> 5.6 us  [body(): pieces[m, d] = lax.ppermute(piece, ('ctx', 'tp'), perm)]
  transfers between devices with their start and end apart: 10 -> 9, of which waited for: 5 -> 7; matrix products, arithmetic and copies ran while one was open for 1% -> 2% of each run, Pallas kernels for 7% -> 10%
where the time goes in v6:
time: 91.6 us; the launch traced here: 91.2 us
  waiting for transfers between devices  48.5 us (53%)
  Pallas kernels  14.3 us (16%)
  starting transfers between devices  12.6 us (14%)
  blocking collectives  8.95 us (10%)
  local copies, waits for them, and re-layouts  6.67 us (7%)
    ppermute x4, waiting for transfers between devices, over_ctx(): return lax.ppermute(x, 'ctx', [(i, i ^ m) for i in range(n)])  24 us
    ppermute x4, waiting for transfers between devices, body(): pieces[m, d] = lax.ppermute(piece, ('ctx', 'tp'), perm)  23.9 us
    ppermute x4, starting transfers between devices, over_ctx(): return lax.ppermute(x, 'ctx', [(i, i ^ m) for i in range(n)])  6.83 us
    ppermute x4, starting transfers between devices, body(): pieces[m, d] = lax.ppermute(piece, ('ctx', 'tp'), perm)  5.6 us
    unnamed x16, local copies, waits for them, and re-layouts  5.26 us
    pallas_call x4, Pallas kernels, project_halves(): pl.pallas_call(project_halves_kernel, out_shape=[jax.ShapeDtypeStruct((ro...  4.95 us
    all_gather x2, blocking collectives, body(): both = [lax.all_gather(direct, 'tp', axis=0)]  4.58 us
    pallas_call x4, Pallas kernels, select(): pl.pallas_call(functools.partial(select_kernel, m, len(blocks)), out_shap...  3.39 us
  transfers between devices with their start and end apart: 9, of which 7 were waited for; matrix products, arithmetic and copies ran while one was open for 2% of the time, Pallas kernels for 10%

profile of v6, /device:TPU:0, one launch (start us, length us, event | category | flops | bytes accessed | tf_op | source)
XLA Modules:
  0.0 91.2 jit_solution(5980704373246950524)
XLA Ops:
  0.0 1.8 %to_send.1 = bf16[136,1280]{1,0:T(8,128)(2,1)} custom-call(bf16[256,1280]{1,0:T(8,128)(2,1)} %bitcast.10, s32[1,256]{1,0:T(1,128)} %refs_5_.4, s32[1,256]{1,0:T(1,128)} %kind.3), custom_call_target="tpu_custom_call" | custom-call | bytes 40960 | tf_op jit(solution)/shard_map/to_send/pallas_call | solution.py:43
  1.8 3.1 %collective-permute-start = (bf16[136,1280]{1,0:T(8,128)(2,1)}, bf16[136,1280]{1,0:T(8,128)(2,1)S(1)}, u32[]{:S(2)}, u32[]{:S(2)}) collective-permute-start(bf16[136,1280]{1,0:T(8,128)(2,1)} %to_send.1), channel_id=1, source_target_pairs={{0,4},{4,0},{8,12},{12,8},{1,5},{5,1},{9,13},{13,9},{2,6},{6,2},{1... | collective-permute-start | bytes 1044488 | tf_op jit(solution)/shard_map/ppermute | solution.py:229
  4.9 2.6 %collective-permute-start.1 = (bf16[136,1280]{1,0:T(8,128)(2,1)}, bf16[136,1280]{1,0:T(8,128)(2,1)S(1)}, u32[]{:S(2)}, u32[]{:S(2)}) collective-permute-start(bf16[136,1280]{1,0:T(8,128)(2,1)} %to_send.1), channel_id=1, source_target_pairs={{0,8},{4,12},{8,0},{12,4},{1,9},{5,13},{9,1},{13,5},{2,10},{6,14},... | collective-permute-start | bytes 1044488 | tf_op jit(solution)/shard_map/ppermute | solution.py:229
  7.5 0.0 collective-permute-start.2
  7.5 0.7 broadcast_in_dim.19.ba
  8.2 0.7 broadcast_in_dim.20.bf
  8.8 0.0 copy-start
  8.8 1.7 %copy-done = bf16[1280,1024]{1,0:T(8,128)(2,1)S(1)} copy-done((bf16[1280,1024]{1,0:T(8,128)(2,1)S(1)}, bf16[1280,1024]{1,0:T(8,128)(2,1)}, u32[]{:S(2)}) %copy-start) | copy-done | bytes 2621464
  10.6 0.0 copy-start.2
  10.6 1.7 %copy-done.2 = bf16[1280,1024]{1,0:T(8,128)(2,1)S(1)} copy-done((bf16[1280,1024]{1,0:T(8,128)(2,1)S(1)}, bf16[1280,1024]{1,0:T(8,128)(2,1)}, u32[]{:S(2)}) %copy-start.2) | copy-done | bytes 2621464
  12.3 1.1 %copy-done.4 = bf16[1,256,1280]{2,1,0:T(8,128)(2,1)S(1)} copy-done((bf16[1,256,1280]{2,1,0:T(8,128)(2,1)S(1)}, bf16[1,256,1280]{2,1,0:T(8,128)(2,1)}, u32[]{:S(2)}) %copy-start.4) | copy-done | bytes 655384
  13.4 0.7 copy-done.6
  14.1 1.6 %project_own.1.refs_0_ = bf16[256,1024]{1,0:T(8,128)(2,1)S(1)} custom-call(s32[1,256]{1,0:T(1,128)S(1)} %copy-done.6, bf16[256,1280]{1,0:T(8,128)(2,1)S(1)} %bitcast.11, bf16[1280,1024]{1,0:T(8,128)(2,1)S(1)} %copy-done, bf16[1280,1024]{1,0:T(8,128)(2,1)S(1)} %copy-done.2, bf16[1,1024]{1,0:T(2,128)(2,1)S(1)} %broadcast_in_dim.19.ba, ...), custom_call_target="tpu_custom_call" | custom-call | flops 83886080 | bytes 327680 | tf_op jit(solution)/shard_map/project_own/pallas_call | solution.py:80
  15.7 4.3 %collective-permute-done = bf16[136,1280]{1,0:T(8,128)(2,1)S(1)} collective-permute-done((bf16[136,1280]{1,0:T(8,128)(2,1)}, bf16[136,1280]{1,0:T(8,128)(2,1)S(1)}, u32[]{:S(2)}, u32[]{:S(2)}) %collective-permute-start) | collective-permute-done | bytes 348192 | tf_op jit(solution)/shard_map/ppermute | solution.py:229
  19.9 2.3 %all-gather = bf16[272,1280]{1,0:T(8,128)(2,1)S(1)} all-gather(bf16[136,1280]{1,0:T(8,128)(2,1)S(1)} %collective-permute-done), channel_id=2, replica_groups=mesh['groups'=2,'ctx'=4,'enc'=2,'tp'=2] {'tp'}, dimensions={0}, use_global_device_ids=true | all-gather | bytes 1044480 | tf_op jit(solution)/shard_map/all_gather | solution.py:241
  22.2 0.0 copy-done.1
  22.2 0.0 copy-done.3
  22.2 1.6 %project_halves.4 = (bf16[256,1024]{1,0:T(8,128)(2,1)S(1)}, s32[1,256]{1,0:T(1,128)S(1)}) custom-call(bf16[1280,1024]{1,0:T(8,128)(2,1)S(1)} %copy-done.1, bf16[1280,1024]{1,0:T(8,128)(2,1)S(1)} %copy-done.3, bf16[1,1024]{1,0:T(2,128)(2,1)S(1)} %broadcast_in_dim.19.ba, bf16[1,1024]{1,0:T(2,128)(2,1)S(1)} %broadcast_in_dim.20.bf, ...), custom_call_target="tpu_custom_call" | custom-call | flops 83886080 | bytes 327680 | tf_op jit(solution)/shard_map/project_halves/pallas_call | solution.py:108
  23.8 8.2 %collective-permute-done.1 = bf16[136,1280]{1,0:T(8,128)(2,1)S(1)} collective-permute-done((bf16[136,1280]{1,0:T(8,128)(2,1)}, bf16[136,1280]{1,0:T(8,128)(2,1)S(1)}, u32[]{:S(2)}, u32[]{:S(2)}) %collective-permute-start.1) | collective-permute-done | bytes 348192 | tf_op jit(solution)/shard_map/ppermute | solution.py:229
  32.0 2.3 %all-gather.1 = bf16[272,1280]{1,0:T(8,128)(2,1)S(1)} all-gather(bf16[136,1280]{1,0:T(8,128)(2,1)S(1)} %collective-permute-done.1), channel_id=3, replica_groups=mesh['groups'=2,'ctx'=4,'enc'=2,'tp'=2] {'tp'}, dimensions={0}, use_global_device_ids=true | all-gather | bytes 1044480 | tf_op jit(solution)/shard_map/all_gather | solution.py:241
  34.3 1.6 %project_halves.5 = (bf16[256,1024]{1,0:T(8,128)(2,1)S(1)}, s32[1,256]{1,0:T(1,128)S(1)}) custom-call(bf16[1280,1024]{1,0:T(8,128)(2,1)S(1)} %copy-done.1, bf16[1280,1024]{1,0:T(8,128)(2,1)S(1)} %copy-done.3, bf16[1,1024]{1,0:T(2,128)(2,1)S(1)} %broadcast_in_dim.19.ba, bf16[1,1024]{1,0:T(2,128)(2,1)S(1)} %broadcast_in_dim.20.bf, ...), custom_call_target="tpu_custom_call" | custom-call | flops 83886080 | bytes 327680 | tf_op jit(solution)/shard_map/project_halves/pallas_call | solution.py:108
  35.8 0.0 collective-permute-done.2
  35.9 0.2 collective-permute-start.3
  36.1 0.9 %project_halves.6 = (bf16[128,1024]{1,0:T(8,128)(2,1)S(1)}, s32[1,128]{1,0:T(1,128)S(1)}) custom-call(bf16[1280,1024]{1,0:T(8,128)(2,1)S(1)} %copy-done.1, bf16[1280,1024]{1,0:T(8,128)(2,1)S(1)} %copy-done.3, bf16[1,1024]{1,0:T(2,128)(2,1)S(1)} %broadcast_in_dim.19.ba, bf16[1,1024]{1,0:T(2,128)(2,1)S(1)} %broadcast_in_dim.20.bf, ...), custom_call_target="tpu_custom_call" | custom-call | flops 41943040 | bytes 327680 | tf_op jit(solution)/shard_map/project_halves/pallas_call | solution.py:108
  37.0 0.6 collective-permute-done.3
  37.6 0.9 project_halves.7
  38.5 0.0 copy-done.5
  38.5 0.8 select.4
  39.3 2.3 %collective-permute-start.5 = (bf16[128,1024]{1,0:T(8,128)(2,1)S(1)}, bf16[128,1024]{1,0:T(8,128)(2,1)S(1)}, u32[]{:S(2)}, u32[]{:S(2)}) collective-permute-start(bf16[128,1024]{1,0:T(8,128)(2,1)S(1)} %get-tuple-element.41), channel_id=1, source_target_pairs={{0,13},{1,12},{4,9},{5,8},{8,5},{9,4},{12,1},{13,0},{2,15},{3,14},... | collective-permute-start | bytes 786440 | tf_op jit(solution)/shard_map/ppermute | solution.py:261
  41.6 1.4 %collective-permute-start.4 = (bf16[128,1024]{1,0:T(8,128)(2,1)S(1)}, bf16[128,1024]{1,0:T(8,128)(2,1)S(1)}, u32[]{:S(2)}, u32[]{:S(2)}) collective-permute-start(bf16[128,1024]{1,0:T(8,128)(2,1)S(1)} %get-tuple-element.40), channel_id=1, source_target_pairs={{0,12},{1,13},{4,8},{5,9},{8,4},{9,5},{12,0},{13,1},{2,14},{3,15},... | collective-permute-start | bytes 786440 | tf_op jit(solution)/shard_map/ppermute | solution.py:261
  43.0 0.0 copy-done.7
  43.0 0.8 select.5
  43.9 0.8 select.6
  44.7 1.9 %collective-permute-start.7 = (bf16[128,1024]{1,0:T(8,128)(2,1)S(1)}, bf16[128,1024]{1,0:T(8,128)(2,1)S(1)}, u32[]{:S(2)}, u32[]{:S(2)}) collective-permute-start(bf16[128,1024]{1,0:T(8,128)(2,1)S(1)} %get-tuple-element.44), channel_id=1, source_target_pairs={{0,8},{1,9},{4,12},{5,13},{8,0},{9,1},{12,4},{13,5},{2,10},{3,11},... | collective-permute-start | bytes 786440 | tf_op jit(solution)/shard_map/ppermute | solution.py:261
  46.7 1.2 %collective-permute-start.6 = (bf16[256,1024]{1,0:T(8,128)(2,1)S(1)}, bf16[256,1024]{1,0:T(8,128)(2,1)S(1)}, u32[]{:S(2)}, u32[]{:S(2)}) collective-permute-start(bf16[256,1024]{1,0:T(8,128)(2,1)S(1)} %select.5), channel_id=1, source_target_pairs={{0,4},{4,0},{8,12},{12,8},{1,5},{5,1},{9,13},{13,9},{2,6},{6,2},{1... | collective-permute-start | bytes 1572872 | tf_op jit(solution)/shard_map/ppermute | solution.py:229
  47.8 0.0 collective-permute-start.8
  47.8 1.8 %collective-permute-done.5.refs_1_ = bf16[128,1024]{1,0:T(8,128)(2,1)S(1)} collective-permute-done((bf16[128,1024]{1,0:T(8,128)(2,1)S(1)}, bf16[128,1024]{1,0:T(8,128)(2,1)S(1)}, u32[]{:S(2)}, u32[]{:S(2)}) %collective-permute-start.5) | collective-permute-done | bytes 262176 | tf_op jit(solution)/shard_map/ppermute | solution.py:261
  49.6 6.2 %collective-permute-done.4.refs_0_ = bf16[128,1024]{1,0:T(8,128)(2,1)S(1)} collective-permute-done((bf16[128,1024]{1,0:T(8,128)(2,1)S(1)}, bf16[128,1024]{1,0:T(8,128)(2,1)S(1)}, u32[]{:S(2)}, u32[]{:S(2)}) %collective-permute-start.4) | collective-permute-done | bytes 262176 | tf_op jit(solution)/shard_map/ppermute | solution.py:261
  55.9 0.2 squares.3.refs_0_
  56.1 0.8 select.7
  56.9 2.2 %all-gather.2 = bf16[256,1024]{1,0:T(8,128)(2,1)S(1)} all-gather(bf16[128,1024]{1,0:T(8,128)(2,1)S(1)} %get-tuple-element.48), channel_id=4, replica_groups=mesh['groups'=2,'ctx'=4,'enc'=2,'tp'=2] {'tp'}, dimensions={0}, use_global_device_ids=true | all-gather | bytes 786432 | tf_op jit(solution)/shard_map/all_gather | solution.py:268
  59.1 0.2 squares.4.refs_0_
  59.3 11.6 %collective-permute-done.6.refs_1_.refs_2_ = bf16[256,1024]{1,0:T(8,128)(2,1)S(1)} collective-permute-done((bf16[256,1024]{1,0:T(8,128)(2,1)S(1)}, bf16[256,1024]{1,0:T(8,128)(2,1)S(1)}, u32[]{:S(2)}, u32[]{:S(2)}) %collective-permute-start.6) | collective-permute-done | bytes 524320 | tf_op jit(solution)/shard_map/ppermute | solution.py:229
  70.9 2.2 %all-gather.3 = bf16[256,1024]{1,0:T(8,128)(2,1)S(1)} all-gather(bf16[128,1024]{1,0:T(8,128)(2,1)S(1)} %slice.3), channel_id=5, replica_groups=mesh['groups'=2,'ctx'=4,'enc'=2,'tp'=2] {'tp'}, dimensions={0}, use_global_device_ids=true | all-gather | bytes 786432 | tf_op jit(solution)/shard_map/all_gather | solution.py:271
  73.1 0.2 squares.5.before
  73.3 15.9 %collective-permute-done.8.refs_5_ = bf16[128,1024]{1,0:T(8,128)(2,1)S(1)} collective-permute-done((bf16[128,1024]{1,0:T(8,128)(2,1)S(1)}, bf16[128,1024]{1,0:T(8,128)(2,1)S(1)}, u32[]{:S(2)}, u32[]{:S(2)}) %collective-permute-start.8) | collective-permute-done | bytes 262176 | tf_op jit(solution)/shard_map/ppermute | solution.py:261
  89.1 0.0 collective-permute-done.7.refs_4_
  89.1 2.1 %norm.1 = bf16[128,8192]{1,0:T(8,128)(2,1)} custom-call(bf16[1,8192]{1,0:T(2,128)(2,1)S(1)} %broadcast_in_dim.18.gain, f32[128,1]{1,0:T(8,128)S(1)} %squares.5.before, bf16[128,1024]{1,0:T(8,128)(2,1)S(1)} %collective-permute-done.4.refs_0_, bf16[128,1024]{1,0:T(8,128)(2,1)S(1)} %collective-permute-done.5.refs_1_, ...), custom_call_target="tpu_custom_call" | custom-call | flops 262144 | bytes 262144 | tf_op jit(solution)/shard_map/norm/pallas_call | solution.py:206
  (8 shorter events, 0.0 us)
Async XLA Ops:
  1.8 18.1 %collective-permute-start = (bf16[136,1280]{1,0:T(8,128)(2,1)}, bf16[136,1280]{1,0:T(8,128)(2,1)S(1)}, u32[]{:S(2)}, u32[]{:S(2)}) collective-permute-start(bf16[136,1280]{1,0:T(8,128)(2,1)} %to_send.1), channel_id=1, source_target_pairs={{0,4},{4,0},{8,12},{12,8},{1,5},{5,1},{9,13},{13,9},{2,6},{6,2},{1... | collective-permute-start | bytes 1044488 | tf_op jit(solution)/shard_map/ppermute | solution.py:229
  4.9 27.1 %collective-permute-start.1 = (bf16[136,1280]{1,0:T(8,128)(2,1)}, bf16[136,1280]{1,0:T(8,128)(2,1)S(1)}, u32[]{:S(2)}, u32[]{:S(2)}) collective-permute-start(bf16[136,1280]{1,0:T(8,128)(2,1)} %to_send.1), channel_id=1, source_target_pairs={{0,8},{4,12},{8,0},{12,4},{1,9},{5,13},{9,1},{13,5},{2,10},{6,14},... | collective-permute-start | bytes 1044488 | tf_op jit(solution)/shard_map/ppermute | solution.py:229
  7.5 28.4 %collective-permute-start.2 = (bf16[136,1280]{1,0:T(8,128)(2,1)}, bf16[136,1280]{1,0:T(8,128)(2,1)S(1)}, u32[]{:S(2)}, u32[]{:S(2)}) collective-permute-start(bf16[136,1280]{1,0:T(8,128)(2,1)} %to_send.1), channel_id=1, source_target_pairs={{0,12},{4,8},{8,4},{12,0},{1,13},{5,9},{9,5},{13,1},{2,14},{6,10},... | collective-permute-start | bytes 1044488 | tf_op jit(solution)/shard_map/ppermute | solution.py:229
  8.8 1.7 %copy-start = (bf16[1280,1024]{1,0:T(8,128)(2,1)S(1)}, bf16[1280,1024]{1,0:T(8,128)(2,1)}, u32[]{:S(2)}) copy-start(bf16[1280,1024]{1,0:T(8,128)(2,1)} %wa.9) | copy-start | bytes 7864324
  10.6 1.7 %copy-start.2 = (bf16[1280,1024]{1,0:T(8,128)(2,1)S(1)}, bf16[1280,1024]{1,0:T(8,128)(2,1)}, u32[]{:S(2)}) copy-start(bf16[1280,1024]{1,0:T(8,128)(2,1)} %wf.9) | copy-start | bytes 7864324
  12.3 1.1 %copy-start.4 = (bf16[1,256,1280]{2,1,0:T(8,128)(2,1)S(1)}, bf16[1,256,1280]{2,1,0:T(8,128)(2,1)}, u32[]{:S(2)}) copy-start(bf16[1,256,1280]{2,1,0:T(8,128)(2,1)} %param.8) | copy-start | bytes 1966084
  13.4 0.7 copy-start.6
  14.1 8.1 %copy-start.1 = (bf16[1280,1024]{1,0:T(8,128)(2,1)S(1)}, bf16[1280,1024]{1,0:T(8,128)(2,1)}, u32[]{:S(2)}) copy-start(bf16[1280,1024]{1,0:T(8,128)(2,1)} %wa.9) | copy-start | bytes 7864324
  14.1 8.1 %copy-start.3 = (bf16[1280,1024]{1,0:T(8,128)(2,1)S(1)}, bf16[1280,1024]{1,0:T(8,128)(2,1)}, u32[]{:S(2)}) copy-start(bf16[1280,1024]{1,0:T(8,128)(2,1)} %wf.9) | copy-start | bytes 7864324
  35.9 1.7 %collective-permute-start.3 = (bf16[136,1280]{1,0:T(8,128)(2,1)S(1)}, bf16[136,1280]{1,0:T(8,128)(2,1)S(1)}, u32[]{:S(2)}, u32[]{:S(2)}) collective-permute-start(bf16[136,1280]{1,0:T(8,128)(2,1)S(1)} %collective-permute-done.2), channel_id=1, source_target_pairs={{0,1},{1,0},{2,3},{3,2},{4,5},{5,4},{6,7},{7,6},{8,9},{9,8},{10,11... | collective-permute-start | bytes 1044488 | tf_op jit(solution)/shard_map/ppermute | solution.py:232
  37.6 0.9 copy-start.5
  37.6 5.4 %copy-start.7 = (bf16[8192]{0:T(1024)(128)(2,1)S(1)}, bf16[8192]{0:T(1024)(128)(2,1)}, u32[]{:S(2)}) copy-start(bf16[8192]{0:T(1024)(128)(2,1)} %param.15) | copy-start | bytes 49156
  39.3 10.3 %collective-permute-start.5 = (bf16[128,1024]{1,0:T(8,128)(2,1)S(1)}, bf16[128,1024]{1,0:T(8,128)(2,1)S(1)}, u32[]{:S(2)}, u32[]{:S(2)}) collective-permute-start(bf16[128,1024]{1,0:T(8,128)(2,1)S(1)} %get-tuple-element.41), channel_id=1, source_target_pairs={{0,13},{1,12},{4,9},{5,8},{8,5},{9,4},{12,1},{13,0},{2,15},{3,14},... | collective-permute-start | bytes 786440 | tf_op jit(solution)/shard_map/ppermute | solution.py:261
  41.6 14.3 %collective-permute-start.4 = (bf16[128,1024]{1,0:T(8,128)(2,1)S(1)}, bf16[128,1024]{1,0:T(8,128)(2,1)S(1)}, u32[]{:S(2)}, u32[]{:S(2)}) collective-permute-start(bf16[128,1024]{1,0:T(8,128)(2,1)S(1)} %get-tuple-element.40), channel_id=1, source_target_pairs={{0,12},{1,13},{4,8},{5,9},{8,4},{9,5},{12,0},{13,1},{2,14},{3,15},... | collective-permute-start | bytes 786440 | tf_op jit(solution)/shard_map/ppermute | solution.py:261
  44.7 44.4 %collective-permute-start.7 = (bf16[128,1024]{1,0:T(8,128)(2,1)S(1)}, bf16[128,1024]{1,0:T(8,128)(2,1)S(1)}, u32[]{:S(2)}, u32[]{:S(2)}) collective-permute-start(bf16[128,1024]{1,0:T(8,128)(2,1)S(1)} %get-tuple-element.44), channel_id=1, source_target_pairs={{0,8},{1,9},{4,12},{5,13},{8,0},{9,1},{12,4},{13,5},{2,10},{3,11},... | collective-permute-start | bytes 786440 | tf_op jit(solution)/shard_map/ppermute | solution.py:261
  46.7 24.2 %collective-permute-start.6 = (bf16[256,1024]{1,0:T(8,128)(2,1)S(1)}, bf16[256,1024]{1,0:T(8,128)(2,1)S(1)}, u32[]{:S(2)}, u32[]{:S(2)}) collective-permute-start(bf16[256,1024]{1,0:T(8,128)(2,1)S(1)} %select.5), channel_id=1, source_target_pairs={{0,4},{4,0},{8,12},{12,8},{1,5},{5,1},{9,13},{13,9},{2,6},{6,2},{1... | collective-permute-start | bytes 1572872 | tf_op jit(solution)/shard_map/ppermute | solution.py:229
  47.8 41.3 %collective-permute-start.8 = (bf16[128,1024]{1,0:T(8,128)(2,1)S(1)}, bf16[128,1024]{1,0:T(8,128)(2,1)S(1)}, u32[]{:S(2)}, u32[]{:S(2)}) collective-permute-start(bf16[128,1024]{1,0:T(8,128)(2,1)S(1)} %get-tuple-element.51), channel_id=1, source_target_pairs={{0,9},{1,8},{4,13},{5,12},{8,1},{9,0},{12,5},{13,4},{2,11},{3,10},... | collective-permute-start | bytes 786440 | tf_op jit(solution)/shard_map/ppermute | solution.py:261

commit v7 on v6

--- a/solution.py
+++ b/solution.py
@@ -17,38 +17,51 @@
     return pl.CostEstimate(flops=flops // 16, bytes_accessed=moved // 16, transcendentals=0)
 
 
-def send_kernel(rows, slot, kind, out, slot_here, kind_here, sems):
-    half = out.shape[0] - 8
-    t = lax.axis_index("tp")
-    start = pl.multiple_of(t * half, half)
+def send_kernel(cuts, rows, slot, kind, *refs):
+    outs, slot_here, kind_here, sems = refs[:-3], refs[-3], refs[-2], refs[-1]
+    whole = rows.shape[0]
+    z, t = lax.axis_index("ctx"), lax.axis_index("tp")
     copies = [
         pltpu.make_async_copy(slot, slot_here, sems.at[0]),
         pltpu.make_async_copy(kind, kind_here, sems.at[1]),
-        pltpu.make_async_copy(rows.at[pl.ds(start, half), :], out.at[pl.ds(0, half), :], sems.at[2]),
     ]
+    parts = []
+    for k, (out, parity) in enumerate(zip(outs, cuts)):
+        size = out.shape[0] - 8
+        part = t if parity is None else 2 * t + lax.rem(z + parity, 2)
+        parts.append(part)
+        source = rows.at[pl.ds(pl.multiple_of(part * size, size), size), :]
+        copies.append(pltpu.make_async_copy(source, out.at[pl.ds(0, size), :], sems.at[2 + k]))
     for copy in copies:
         copy.start()
-    out[half:, :] = jnp.zeros((8, out.shape[1]), BF16)
+    for out in outs:
+        out[out.shape[0] - 8 :, :] = jnp.zeros((8, out.shape[1]), BF16)
     for copy in copies:
         copy.wait()
-    slots = jnp.where(t == 0, slot_here[:, :half], slot_here[:, half:])
-    kinds = jnp.where(t == 0, kind_here[:, :half], kind_here[:, half:])
-    line = lax.broadcasted_iota(I32, (8, half), 0)
-    index = jnp.where(line == 0, slots // 256, jnp.where(line == 1, slots % 256, kinds))
-    out[half:, :half] = index.astype(F32).astype(BF16)
-
-
-def to_send(rows, slot, kind):
+    slots, kinds = slot_here[...], kind_here[...]
+    for out, part in zip(outs, parts):
+        size = out.shape[0] - 8
+        s, k = slots[:, :size], kinds[:, :size]
+        for i in range(1, whole // size):
+            s = jnp.where(part == i, slots[:, i * size : (i + 1) * size], s)
+            k = jnp.where(part == i, kinds[:, i * size : (i + 1) * size], k)
+        line = lax.broadcasted_iota(I32, (8, size), 0)
+        index = jnp.where(line == 0, s // 256, jnp.where(line == 1, s % 256, k))
+        out[size:, :size] = index.astype(F32).astype(BF16)
+
+
+def to_send(cuts, rows, slot, kind):
     half, width = rows.shape[0] // 2, rows.shape[1]
-    return pl.pallas_call(
-        send_kernel,
-        out_shape=jax.ShapeDtypeStruct((half + 8, width), BF16),
+    sizes = [half if parity is None else half // 2 for parity in cuts]
+    return pl.pallas_call(
+        functools.partial(send_kernel, cuts),
+        out_shape=[jax.ShapeDtypeStruct((size + 8, width), BF16) for size in sizes],
         in_specs=[HBM] * 3,
-        out_specs=VMEM,
+        out_specs=[VMEM] * len(cuts),
         scratch_shapes=[
             pltpu.VMEM(slot.shape, I32),
             pltpu.VMEM(slot.shape, I32),
-            pltpu.SemaphoreType.DMA((3,)),
+            pltpu.SemaphoreType.DMA((2 + len(cuts),)),
         ],
         compiler_params=pltpu.CompilerParams(vmem_limit_bytes=60 << 20),
         cost_estimate=cost(0, 4 * half * width),
@@ -231,22 +244,37 @@
     def over_tp(x):
         return lax.ppermute(x, "tp", [(0, 1), (1, 0)])
 
-    mine = to_send(rows, row_slot, row_kind)
-    arrived = [over_ctx(mine, m) for m in range(1, n)]
-    last = project_own(row_kind, rows, weights)
-    blocks, slots = [last], [row_slot]
-    for k, direct in enumerate(arrived):
-        direct = after(direct, last)
-        if k < n - 2:
-            both = [lax.all_gather(direct, "tp", axis=0)]
-        else:
-            both = [direct[None], over_tp(direct)[None]]
-        groups = [both] if len(both) == 1 else [[half] for half in both]
-        for group in groups:
-            block, slot = project_halves(group, weights)
-            blocks.append(block)
-            slots.append(slot)
-        last = block
+    own = project_own(row_kind, rows, weights)
+    blocks, slots = [own], [row_slot]
+
+    def take(group):
+        block, slot = project_halves(group, weights)
+        blocks.append(block)
+        slots.append(slot)
+
+    if n == 4:
+        near, second, third = to_send((None, 0, 1), rows, row_slot, row_kind)
+        near, second, third = over_ctx(near, 1), over_ctx(second, 2), over_ctx(third, 3)
+        near = after(near, own)
+        take([lax.all_gather(near, "tp", axis=0)])
+        second, third = after(second, blocks[-1]), after(third, blocks[-1])
+        second, third = lax.optimization_barrier((second, third))
+        shared = [over_ctx(second, 1), over_ctx(third, 1)]
+        take([lax.all_gather(part, "tp", axis=0) for part in (second, third)])
+        shared = lax.optimization_barrier((*shared, blocks[-1]))[:2]
+        swapped = [over_tp(part)[None] for part in shared]
+        take([part[None] for part in shared])
+        take(swapped)
+    else:
+        (mine,) = to_send((None,), rows, row_slot, row_kind)
+        arrived = [over_ctx(mine, m) for m in range(1, n)]
+        for direct in arrived[:-1]:
+            direct = after(direct, blocks[-1])
+            take([lax.all_gather(direct, "tp", axis=0)])
+        direct = after(arrived[-1], blocks[-1])
+        swapped = over_tp(direct)
+        take([direct[None]])
+        take([swapped[None]])
 
     pieces = {}
     order = [n - 1, 1] + list(reversed(range(2, n - 1)))

time: 91.6 us -> 90.3 us (0.986)
  waiting for transfers between devices: 48.5 us -> 38.4 us
  starting transfers between devices: 12.6 us -> 19.3 us
  blocking collectives: 8.95 us -> 10.8 us
    ppermute x4 -> x6, waiting for transfers between devices: 24 us -> 18.3 us  [over_ctx(): return lax.ppermute(x, 'ctx', [(i, i ^ m) for i in range(n)])]
    ppermute x4 -> x6, starting transfers between devices: 6.83 us -> 11.3 us  [over_ctx(): return lax.ppermute(x, 'ctx', [(i, i ^ m) for i in range(n)])]
    ppermute x4, waiting for transfers between devices: 23.9 us -> 19.9 us  [body(): pieces[m, d] = lax.ppermute(piece, ('ctx', 'tp'), perm)]
    ppermute x4, starting transfers between devices: 5.6 us -> 7.54 us  [body(): pieces[m, d] = lax.ppermute(piece, ('ctx', 'tp'), perm)]
    all_gather x2 -> x3, blocking collectives: 4.58 us -> 6.41 us  [the longest x2 4.11 us: body(): take([lax.all_gather(part, 'tp', axis=0) for part in (second, third)])]
  transfers between devices with their start and end apart: 9 -> 12, of which waited for: 7 -> 8; matrix products, arithmetic and copies ran while one was open for 2% -> 2% of each run, Pallas kernels for 10% -> 10%
where the time goes in v7:
time: 90.3 us; the launch traced here: 89.9 us
  waiting for transfers between devices  38.4 us (43%)
  starting transfers between devices  19.3 us (21%)
  Pallas kernels  14.6 us (16%)
  blocking collectives  10.8 us (12%)
  local copies, waits for them, and re-layouts  6.67 us (7%)
    ppermute x4, waiting for transfers between devices, body(): pieces[m, d] = lax.ppermute(piece, ('ctx', 'tp'), perm)  19.9 us
    ppermute x6, waiting for transfers between devices, over_ctx(): return lax.ppermute(x, 'ctx', [(i, i ^ m) for i in range(n)])  18.3 us
    ppermute x6, starting transfers between devices, over_ctx(): return lax.ppermute(x, 'ctx', [(i, i ^ m) for i in range(n)])  11.3 us
    ppermute x4, starting transfers between devices, body(): pieces[m, d] = lax.ppermute(piece, ('ctx', 'tp'), perm)  7.54 us
    unnamed x16, local copies, waits for them, and re-layouts  5.26 us
    pallas_call x4, Pallas kernels, project_halves(): pl.pallas_call(project_halves_kernel, out_shape=[jax.ShapeDtypeStruct((ro...  5.02 us
    all_gather x2, blocking collectives, body(): take([lax.all_gather(part, 'tp', axis=0) for part in (second, third)])  4.11 us
    pallas_call x4, Pallas kernels, select(): pl.pallas_call(functools.partial(select_kernel, m, len(blocks)), out_shap...  3.4 us
  transfers between devices with their start and end apart: 12, of which 8 were waited for; matrix products, arithmetic and copies ran while one was open for 2% of the time, Pallas kernels for 10%

profile of v7, /device:TPU:0, one launch (start us, length us, event | category | flops | bytes accessed | tf_op | source)
XLA Modules:
  0.0 89.9 jit_solution(13518508944283778129)
XLA Ops:
  0.0 2.0 %to_send.1 = (bf16[136,1280]{1,0:T(8,128)(2,1)}, bf16[72,1280]{1,0:T(8,128)(2,1)}, bf16[72,1280]{1,0:T(8,128)(2,1)}) custom-call(bf16[256,1280]{1,0:T(8,128)(2,1)} %bitcast.12, s32[1,256]{1,0:T(1,128)} %refs_5_.4, s32[1,256]{1,0:T(1,128)} %kind.3), custom_call_target="tpu_custom_call" | custom-call | bytes 40960 | tf_op jit(solution)/shard_map/to_send/pallas_call | solution.py:56
  2.1 3.1 %collective-permute-start = (bf16[136,1280]{1,0:T(8,128)(2,1)}, bf16[136,1280]{1,0:T(8,128)(2,1)S(1)}, u32[]{:S(2)}, u32[]{:S(2)}) collective-permute-start(bf16[136,1280]{1,0:T(8,128)(2,1)} %get-tuple-element.36), channel_id=1, source_target_pairs={{0,4},{4,0},{8,12},{12,8},{1,5},{5,1},{9,13},{13,9},{2,6},{6,2},{1... | collective-permute-start | bytes 1044488 | tf_op jit(solution)/shard_map/ppermute | solution.py:242
  5.1 2.6 %collective-permute-start.1 = (bf16[72,1280]{1,0:T(8,128)(2,1)}, bf16[72,1280]{1,0:T(8,128)(2,1)S(1)}, u32[]{:S(2)}, u32[]{:S(2)}) collective-permute-start(bf16[72,1280]{1,0:T(8,128)(2,1)} %get-tuple-element.39), channel_id=1, source_target_pairs={{0,8},{4,12},{8,0},{12,4},{1,9},{5,13},{9,1},{13,5},{2,10},{6,14},... | collective-permute-start | bytes 552968 | tf_op jit(solution)/shard_map/ppermute | solution.py:242
  7.7 0.0 collective-permute-start.2
  7.7 0.7 broadcast_in_dim.25.ba
  8.4 0.7 broadcast_in_dim.26.bf
  9.1 1.7 %copy-done = bf16[1280,1024]{1,0:T(8,128)(2,1)S(1)} copy-done((bf16[1280,1024]{1,0:T(8,128)(2,1)S(1)}, bf16[1280,1024]{1,0:T(8,128)(2,1)}, u32[]{:S(2)}) %copy-start) | copy-done | bytes 2621464
  10.8 1.7 %copy-done.2 = bf16[1280,1024]{1,0:T(8,128)(2,1)S(1)} copy-done((bf16[1280,1024]{1,0:T(8,128)(2,1)S(1)}, bf16[1280,1024]{1,0:T(8,128)(2,1)}, u32[]{:S(2)}) %copy-start.2) | copy-done | bytes 2621464
  12.6 1.1 %copy-done.4 = bf16[1,256,1280]{2,1,0:T(8,128)(2,1)S(1)} copy-done((bf16[1,256,1280]{2,1,0:T(8,128)(2,1)S(1)}, bf16[1,256,1280]{2,1,0:T(8,128)(2,1)}, u32[]{:S(2)}) %copy-start.4) | copy-done | bytes 655384
  13.7 0.7 copy-done.6
  14.4 1.6 %project_own.1.refs_0_ = bf16[256,1024]{1,0:T(8,128)(2,1)S(1)} custom-call(s32[1,256]{1,0:T(1,128)S(1)} %copy-done.6, bf16[256,1280]{1,0:T(8,128)(2,1)S(1)} %bitcast.13, bf16[1280,1024]{1,0:T(8,128)(2,1)S(1)} %copy-done, bf16[1280,1024]{1,0:T(8,128)(2,1)S(1)} %copy-done.2, bf16[1,1024]{1,0:T(2,128)(2,1)S(1)} %broadcast_in_dim.25.ba, ...), custom_call_target="tpu_custom_call" | custom-call | flops 83886080 | bytes 327680 | tf_op jit(solution)/shard_map/project_own/pallas_call | solution.py:93
  15.9 1.5 %collective-permute-done = bf16[136,1280]{1,0:T(8,128)(2,1)S(1)} collective-permute-done((bf16[136,1280]{1,0:T(8,128)(2,1)}, bf16[136,1280]{1,0:T(8,128)(2,1)S(1)}, u32[]{:S(2)}, u32[]{:S(2)}) %collective-permute-start) | collective-permute-done | bytes 348192 | tf_op jit(solution)/shard_map/ppermute | solution.py:242
  17.5 2.3 %all-gather = bf16[272,1280]{1,0:T(8,128)(2,1)S(1)} all-gather(bf16[136,1280]{1,0:T(8,128)(2,1)S(1)} %collective-permute-done), channel_id=2, replica_groups=mesh['groups'=2,'ctx'=4,'enc'=2,'tp'=2] {'tp'}, dimensions={0}, use_global_device_ids=true | all-gather | bytes 1044480 | tf_op jit(solution)/shard_map/all_gather | solution.py:259
  19.7 1.6 %project_halves.4 = (bf16[256,1024]{1,0:T(8,128)(2,1)S(1)}, s32[1,256]{1,0:T(1,128)S(1)}) custom-call(bf16[1280,1024]{1,0:T(8,128)(2,1)S(1)} %copy-done.1, bf16[1280,1024]{1,0:T(8,128)(2,1)S(1)} %copy-done.3, bf16[1,1024]{1,0:T(2,128)(2,1)S(1)} %broadcast_in_dim.25.ba, bf16[1,1024]{1,0:T(2,128)(2,1)S(1)} %broadcast_in_dim.26.bf, ...), custom_call_target="tpu_custom_call" | custom-call | flops 83886080 | bytes 327680 | tf_op jit(solution)/shard_map/project_halves/pallas_call | solution.py:121
  21.4 2.3 %collective-permute-done.2 = bf16[72,1280]{1,0:T(8,128)(2,1)S(1)} collective-permute-done((bf16[72,1280]{1,0:T(8,128)(2,1)}, bf16[72,1280]{1,0:T(8,128)(2,1)S(1)}, u32[]{:S(2)}, u32[]{:S(2)}) %collective-permute-start.2) | collective-permute-done | bytes 184352 | tf_op jit(solution)/shard_map/ppermute | solution.py:242
  23.7 0.0 collective-permute-done.1
  23.7 1.1 %collective-permute-start.3 = (bf16[72,1280]{1,0:T(8,128)(2,1)S(1)}, bf16[72,1280]{1,0:T(8,128)(2,1)S(1)}, u32[]{:S(2)}, u32[]{:S(2)}) collective-permute-start(bf16[72,1280]{1,0:T(8,128)(2,1)S(1)} %collective-permute-done.1), channel_id=1, source_target_pairs={{0,4},{4,0},{8,12},{12,8},{1,5},{5,1},{9,13},{13,9},{2,6},{6,2},{1... | collective-permute-start | bytes 552968 | tf_op jit(solution)/shard_map/ppermute | solution.py:242
  24.8 0.9 %collective-permute-start.4 = (bf16[72,1280]{1,0:T(8,128)(2,1)S(1)}, bf16[72,1280]{1,0:T(8,128)(2,1)S(1)}, u32[]{:S(2)}, u32[]{:S(2)}) collective-permute-start(bf16[72,1280]{1,0:T(8,128)(2,1)S(1)} %collective-permute-done.2), channel_id=1, source_target_pairs={{0,4},{4,0},{8,12},{12,8},{1,5},{5,1},{9,13},{13,9},{2,6},{6,2},{1... | collective-permute-start | bytes 552968 | tf_op jit(solution)/shard_map/ppermute | solution.py:242
  25.7 2.1 %all-gather.1 = bf16[144,1280]{1,0:T(8,128)(2,1)S(1)} all-gather(bf16[72,1280]{1,0:T(8,128)(2,1)S(1)} %collective-permute-done.1), channel_id=3, replica_groups=mesh['groups'=2,'ctx'=4,'enc'=2,'tp'=2] {'tp'}, dimensions={0}, use_global_device_ids=true | all-gather | bytes 552960 | tf_op jit(solution)/shard_map/all_gather | solution.py:263
  27.8 2.1 %all-gather.2 = bf16[144,1280]{1,0:T(8,128)(2,1)S(1)} all-gather(bf16[72,1280]{1,0:T(8,128)(2,1)S(1)} %collective-permute-done.2), channel_id=4, replica_groups=mesh['groups'=2,'ctx'=4,'enc'=2,'tp'=2] {'tp'}, dimensions={0}, use_global_device_ids=true | all-gather | bytes 552960 | tf_op jit(solution)/shard_map/all_gather | solution.py:263
  29.8 1.6 %project_halves.5 = (bf16[256,1024]{1,0:T(8,128)(2,1)S(1)}, s32[1,256]{1,0:T(1,128)S(1)}) custom-call(bf16[1280,1024]{1,0:T(8,128)(2,1)S(1)} %copy-done.1, bf16[1280,1024]{1,0:T(8,128)(2,1)S(1)} %copy-done.3, bf16[1,1024]{1,0:T(2,128)(2,1)S(1)} %broadcast_in_dim.25.ba, bf16[1,1024]{1,0:T(2,128)(2,1)S(1)} %broadcast_in_dim.26.bf, ...), custom_call_target="tpu_custom_call" | custom-call | flops 83886080 | bytes 327680 | tf_op jit(solution)/shard_map/project_halves/pallas_call | solution.py:121
  31.4 0.0 collective-permute-done.3
  31.5 1.6 %collective-permute-done.4 = bf16[72,1280]{1,0:T(8,128)(2,1)S(1)} collective-permute-done((bf16[72,1280]{1,0:T(8,128)(2,1)S(1)}, bf16[72,1280]{1,0:T(8,128)(2,1)S(1)}, u32[]{:S(2)}, u32[]{:S(2)}) %collective-permute-start.4) | collective-permute-done | bytes 184352 | tf_op jit(solution)/shard_map/ppermute | solution.py:242
  33.1 0.0 collective-permute-start.5
  33.1 0.5 collective-permute-start.6
  33.6 0.9 %project_halves.6 = (bf16[128,1024]{1,0:T(8,128)(2,1)S(1)}, s32[1,128]{1,0:T(1,128)S(1)}) custom-call(bf16[1280,1024]{1,0:T(8,128)(2,1)S(1)} %copy-done.1, bf16[1280,1024]{1,0:T(8,128)(2,1)S(1)} %copy-done.3, bf16[1,1024]{1,0:T(2,128)(2,1)S(1)} %broadcast_in_dim.25.ba, bf16[1,1024]{1,0:T(2,128)(2,1)S(1)} %broadcast_in_dim.26.bf, ...), custom_call_target="tpu_custom_call" | custom-call | flops 41943040 | bytes 327680 | tf_op jit(solution)/shard_map/project_halves/pallas_call | solution.py:121
  34.5 0.0 collective-permute-done.5
  34.6 0.2 collective-permute-done.6
  34.8 0.9 %project_halves.7 = (bf16[128,1024]{1,0:T(8,128)(2,1)S(1)}, s32[1,128]{1,0:T(1,128)S(1)}) custom-call(bf16[1280,1024]{1,0:T(8,128)(2,1)S(1)} %copy-done.1, bf16[1280,1024]{1,0:T(8,128)(2,1)S(1)} %copy-done.3, bf16[1,1024]{1,0:T(2,128)(2,1)S(1)} %broadcast_in_dim.25.ba, bf16[1,1024]{1,0:T(2,128)(2,1)S(1)} %broadcast_in_dim.26.bf, ...), custom_call_target="tpu_custom_call" | custom-call | flops 41943040 | bytes 327680 | tf_op jit(solution)/shard_map/project_halves/pallas_call | solution.py:121
  35.7 0.8 select.4
  36.6 6.6 %collective-permute-start.8 = (bf16[128,1024]{1,0:T(8,128)(2,1)S(1)}, bf16[128,1024]{1,0:T(8,128)(2,1)S(1)}, u32[]{:S(2)}, u32[]{:S(2)}) collective-permute-start(bf16[128,1024]{1,0:T(8,128)(2,1)S(1)} %get-tuple-element.55), channel_id=1, source_target_pairs={{0,13},{1,12},{4,9},{5,8},{8,5},{9,4},{12,1},{13,0},{2,15},{3,14},... | collective-permute-start | bytes 786440 | tf_op jit(solution)/shard_map/ppermute | solution.py:289
  43.2 0.2 collective-permute-start.7
  43.4 0.8 select.5
  44.3 0.8 select.6
  45.1 0.7 collective-permute-start.10
  45.8 3.5 %collective-permute-start.9 = (bf16[256,1024]{1,0:T(8,128)(2,1)S(1)}, bf16[256,1024]{1,0:T(8,128)(2,1)S(1)}, u32[]{:S(2)}, u32[]{:S(2)}) collective-permute-start(bf16[256,1024]{1,0:T(8,128)(2,1)S(1)} %select.5), channel_id=1, source_target_pairs={{0,4},{4,0},{8,12},{12,8},{1,5},{5,1},{9,13},{13,9},{2,6},{6,2},{1... | collective-permute-start | bytes 1572872 | tf_op jit(solution)/shard_map/ppermute | solution.py:242
  49.4 0.0 collective-permute-start.11
  49.4 0.5 collective-permute-done.8.refs_1_
  49.9 6.3 %collective-permute-done.7.refs_0_ = bf16[128,1024]{1,0:T(8,128)(2,1)S(1)} collective-permute-done((bf16[128,1024]{1,0:T(8,128)(2,1)S(1)}, bf16[128,1024]{1,0:T(8,128)(2,1)S(1)}, u32[]{:S(2)}, u32[]{:S(2)}) %collective-permute-start.7) | collective-permute-done | bytes 262176 | tf_op jit(solution)/shard_map/ppermute | solution.py:289
  56.2 0.2 squares.3.refs_0_
  56.3 0.9 select.7
  57.2 2.2 %all-gather.3 = bf16[256,1024]{1,0:T(8,128)(2,1)S(1)} all-gather(bf16[128,1024]{1,0:T(8,128)(2,1)S(1)} %get-tuple-element.62), channel_id=5, replica_groups=mesh['groups'=2,'ctx'=4,'enc'=2,'tp'=2] {'tp'}, dimensions={0}, use_global_device_ids=true | all-gather | bytes 786432 | tf_op jit(solution)/shard_map/all_gather | solution.py:296
  59.4 0.2 squares.4.refs_0_
  59.6 12.8 %collective-permute-done.9.refs_1_.refs_2_ = bf16[256,1024]{1,0:T(8,128)(2,1)S(1)} collective-permute-done((bf16[256,1024]{1,0:T(8,128)(2,1)S(1)}, bf16[256,1024]{1,0:T(8,128)(2,1)S(1)}, u32[]{:S(2)}, u32[]{:S(2)}) %collective-permute-start.9) | collective-permute-done | bytes 524320 | tf_op jit(solution)/shard_map/ppermute | solution.py:242
  72.4 2.2 %all-gather.4 = bf16[256,1024]{1,0:T(8,128)(2,1)S(1)} all-gather(bf16[128,1024]{1,0:T(8,128)(2,1)S(1)} %slice.3), channel_id=6, replica_groups=mesh['groups'=2,'ctx'=4,'enc'=2,'tp'=2] {'tp'}, dimensions={0}, use_global_device_ids=true | all-gather | bytes 786432 | tf_op jit(solution)/shard_map/all_gather | solution.py:299
  74.6 0.2 squares.5.before
  74.8 13.1 %collective-permute-done.11.refs_5_ = bf16[128,1024]{1,0:T(8,128)(2,1)S(1)} collective-permute-done((bf16[128,1024]{1,0:T(8,128)(2,1)S(1)}, bf16[128,1024]{1,0:T(8,128)(2,1)S(1)}, u32[]{:S(2)}, u32[]{:S(2)}) %collective-permute-start.11) | collective-permute-done | bytes 262176 | tf_op jit(solution)/shard_map/ppermute | solution.py:289
  87.8 2.1 %norm.1 = bf16[128,8192]{1,0:T(8,128)(2,1)} custom-call(bf16[1,8192]{1,0:T(2,128)(2,1)S(1)} %broadcast_in_dim.24.gain, f32[128,1]{1,0:T(8,128)S(1)} %squares.5.before, bf16[128,1024]{1,0:T(8,128)(2,1)S(1)} %collective-permute-done.7.refs_0_, bf16[128,1024]{1,0:T(8,128)(2,1)S(1)} %collective-permute-done.8.refs_1_, ...), custom_call_target="tpu_custom_call" | custom-call | flops 262144 | bytes 262144 | tf_op jit(solution)/shard_map/norm/pallas_call | solution.py:219
  (15 shorter events, 0.1 us)
Async XLA Ops:
  2.1 15.4 %collective-permute-start = (bf16[136,1280]{1,0:T(8,128)(2,1)}, bf16[136,1280]{1,0:T(8,128)(2,1)S(1)}, u32[]{:S(2)}, u32[]{:S(2)}) collective-permute-start(bf16[136,1280]{1,0:T(8,128)(2,1)} %get-tuple-element.36), channel_id=1, source_target_pairs={{0,4},{4,0},{8,12},{12,8},{1,5},{5,1},{9,13},{13,9},{2,6},{6,2},{1... | collective-permute-start | bytes 1044488 | tf_op jit(solution)/shard_map/ppermute | solution.py:242
  5.1 18.6 %collective-permute-start.1 = (bf16[72,1280]{1,0:T(8,128)(2,1)}, bf16[72,1280]{1,0:T(8,128)(2,1)S(1)}, u32[]{:S(2)}, u32[]{:S(2)}) collective-permute-start(bf16[72,1280]{1,0:T(8,128)(2,1)} %get-tuple-element.39), channel_id=1, source_target_pairs={{0,8},{4,12},{8,0},{12,4},{1,9},{5,13},{9,1},{13,5},{2,10},{6,14},... | collective-permute-start | bytes 552968 | tf_op jit(solution)/shard_map/ppermute | solution.py:242
  7.7 16.0 %collective-permute-start.2 = (bf16[72,1280]{1,0:T(8,128)(2,1)}, bf16[72,1280]{1,0:T(8,128)(2,1)S(1)}, u32[]{:S(2)}, u32[]{:S(2)}) collective-permute-start(bf16[72,1280]{1,0:T(8,128)(2,1)} %get-tuple-element.41), channel_id=1, source_target_pairs={{0,12},{4,8},{8,4},{12,0},{1,13},{5,9},{9,5},{13,1},{2,14},{6,10},... | collective-permute-start | bytes 552968 | tf_op jit(solution)/shard_map/ppermute | solution.py:242
  9.1 1.7 %copy-start = (bf16[1280,1024]{1,0:T(8,128)(2,1)S(1)}, bf16[1280,1024]{1,0:T(8,128)(2,1)}, u32[]{:S(2)}) copy-start(bf16[1280,1024]{1,0:T(8,128)(2,1)} %wa.9) | copy-start | bytes 7864324
  10.8 1.7 %copy-start.2 = (bf16[1280,1024]{1,0:T(8,128)(2,1)S(1)}, bf16[1280,1024]{1,0:T(8,128)(2,1)}, u32[]{:S(2)}) copy-start(bf16[1280,1024]{1,0:T(8,128)(2,1)} %wf.9) | copy-start | bytes 7864324
  12.6 1.1 %copy-start.4 = (bf16[1,256,1280]{2,1,0:T(8,128)(2,1)S(1)}, bf16[1,256,1280]{2,1,0:T(8,128)(2,1)}, u32[]{:S(2)}) copy-start(bf16[1,256,1280]{2,1,0:T(8,128)(2,1)} %param.8) | copy-start | bytes 1966084
  13.7 0.7 copy-start.6
  14.4 5.4 %copy-start.1 = (bf16[1280,1024]{1,0:T(8,128)(2,1)S(1)}, bf16[1280,1024]{1,0:T(8,128)(2,1)}, u32[]{:S(2)}) copy-start(bf16[1280,1024]{1,0:T(8,128)(2,1)} %wa.9) | copy-start | bytes 7864324
  14.4 5.4 %copy-start.3 = (bf16[1280,1024]{1,0:T(8,128)(2,1)S(1)}, bf16[1280,1024]{1,0:T(8,128)(2,1)}, u32[]{:S(2)}) copy-start(bf16[1280,1024]{1,0:T(8,128)(2,1)} %wf.9) | copy-start | bytes 7864324
  23.7 7.7 %collective-permute-start.3 = (bf16[72,1280]{1,0:T(8,128)(2,1)S(1)}, bf16[72,1280]{1,0:T(8,128)(2,1)S(1)}, u32[]{:S(2)}, u32[]{:S(2)}) collective-permute-start(bf16[72,1280]{1,0:T(8,128)(2,1)S(1)} %collective-permute-done.1), channel_id=1, source_target_pairs={{0,4},{4,0},{8,12},{12,8},{1,5},{5,1},{9,13},{13,9},{2,6},{6,2},{1... | collective-permute-start | bytes 552968 | tf_op jit(solution)/shard_map/ppermute | solution.py:242
  24.8 8.3 %collective-permute-start.4 = (bf16[72,1280]{1,0:T(8,128)(2,1)S(1)}, bf16[72,1280]{1,0:T(8,128)(2,1)S(1)}, u32[]{:S(2)}, u32[]{:S(2)}) collective-permute-start(bf16[72,1280]{1,0:T(8,128)(2,1)S(1)} %collective-permute-done.2), channel_id=1, source_target_pairs={{0,4},{4,0},{8,12},{12,8},{1,5},{5,1},{9,13},{13,9},{2,6},{6,2},{1... | collective-permute-start | bytes 552968 | tf_op jit(solution)/shard_map/ppermute | solution.py:242
  33.1 1.4 %collective-permute-start.5 = (bf16[72,1280]{1,0:T(8,128)(2,1)S(1)}, bf16[72,1280]{1,0:T(8,128)(2,1)S(1)}, u32[]{:S(2)}, u32[]{:S(2)}) collective-permute-start(bf16[72,1280]{1,0:T(8,128)(2,1)S(1)} %collective-permute-done.3), channel_id=1, source_target_pairs={{0,1},{1,0},{2,3},{3,2},{4,5},{5,4},{6,7},{7,6},{8,9},{9,8},{10,11... | collective-permute-start | bytes 552968 | tf_op jit(solution)/shard_map/ppermute | solution.py:245
  33.1 1.7 %collective-permute-start.6 = (bf16[72,1280]{1,0:T(8,128)(2,1)S(1)}, bf16[72,1280]{1,0:T(8,128)(2,1)S(1)}, u32[]{:S(2)}, u32[]{:S(2)}) collective-permute-start(bf16[72,1280]{1,0:T(8,128)(2,1)S(1)} %collective-permute-done.4), channel_id=1, source_target_pairs={{0,1},{1,0},{2,3},{3,2},{4,5},{5,4},{6,7},{7,6},{8,9},{9,8},{10,11... | collective-permute-start | bytes 552968 | tf_op jit(solution)/shard_map/ppermute | solution.py:245
  34.8 0.9 %copy-start.5 = (s32[1,256]{1,0:T(1,128)S(1)}, s32[1,256]{1,0:T(1,128)}, u32[]{:S(2)}) copy-start(s32[1,256]{1,0:T(1,128)} %refs_5_.4) | copy-start | bytes 3076
  34.8 8.6 %copy-start.7 = (bf16[8192]{0:T(1024)(128)(2,1)S(1)}, bf16[8192]{0:T(1024)(128)(2,1)}, u32[]{:S(2)}) copy-start(bf16[8192]{0:T(1024)(128)(2,1)} %param.15) | copy-start | bytes 49156
  36.6 13.3 %collective-permute-start.8 = (bf16[128,1024]{1,0:T(8,128)(2,1)S(1)}, bf16[128,1024]{1,0:T(8,128)(2,1)S(1)}, u32[]{:S(2)}, u32[]{:S(2)}) collective-permute-start(bf16[128,1024]{1,0:T(8,128)(2,1)S(1)} %get-tuple-element.55), channel_id=1, source_target_pairs={{0,13},{1,12},{4,9},{5,8},{8,5},{9,4},{12,1},{13,0},{2,15},{3,14},... | collective-permute-start | bytes 786440 | tf_op jit(solution)/shard_map/ppermute | solution.py:289
  43.2 13.0 %collective-permute-start.7 = (bf16[128,1024]{1,0:T(8,128)(2,1)S(1)}, bf16[128,1024]{1,0:T(8,128)(2,1)S(1)}, u32[]{:S(2)}, u32[]{:S(2)}) collective-permute-start(bf16[128,1024]{1,0:T(8,128)(2,1)S(1)} %get-tuple-element.54), channel_id=1, source_target_pairs={{0,12},{1,13},{4,8},{5,9},{8,4},{9,5},{12,0},{13,1},{2,14},{3,15},... | collective-permute-start | bytes 786440 | tf_op jit(solution)/shard_map/ppermute | solution.py:289
  45.1 42.7 %collective-permute-start.10 = (bf16[128,1024]{1,0:T(8,128)(2,1)S(1)}, bf16[128,1024]{1,0:T(8,128)(2,1)S(1)}, u32[]{:S(2)}, u32[]{:S(2)}) collective-permute-start(bf16[128,1024]{1,0:T(8,128)(2,1)S(1)} %get-tuple-element.58), channel_id=1, source_target_pairs={{0,8},{1,9},{4,12},{5,13},{8,0},{9,1},{12,4},{13,5},{2,10},{3,11},... | collective-permute-start | bytes 786440 | tf_op jit(solution)/shard_map/ppermute | solution.py:289
  45.8 26.5 %collective-permute-start.9 = (bf16[256,1024]{1,0:T(8,128)(2,1)S(1)}, bf16[256,1024]{1,0:T(8,128)(2,1)S(1)}, u32[]{:S(2)}, u32[]{:S(2)}) collective-permute-start(bf16[256,1024]{1,0:T(8,128)(2,1)S(1)} %select.5), channel_id=1, source_target_pairs={{0,4},{4,0},{8,12},{12,8},{1,5},{5,1},{9,13},{13,9},{2,6},{6,2},{1... | collective-permute-start | bytes 1572872 | tf_op jit(solution)/shard_map/ppermute | solution.py:242
  49.4 38.5 %collective-permute-start.11 = (bf16[128,1024]{1,0:T(8,128)(2,1)S(1)}, bf16[128,1024]{1,0:T(8,128)(2,1)S(1)}, u32[]{:S(2)}, u32[]{:S(2)}) collective-permute-start(bf16[128,1024]{1,0:T(8,128)(2,1)S(1)} %get-tuple-element.65), channel_id=1, source_target_pairs={{0,9},{1,8},{4,13},{5,12},{8,1},{9,0},{12,5},{13,4},{2,11},{3,10},... | collective-permute-start | bytes 786440 | tf_op jit(solution)/shard_map/ppermute | solution.py:289

commit v8 on v7

--- a/solution.py
+++ b/solution.py
@@ -18,28 +18,31 @@
 
 
 def send_kernel(cuts, rows, slot, kind, *refs):
-    outs, slot_here, kind_here, sems = refs[:-3], refs[-3], refs[-2], refs[-1]
+    count = len(cuts)
+    outs, (slot_here, kind_here, index_sems, row_sems, tile_sems) = refs[:count], refs[-5:]
+    tiles = refs[count:-5]
     whole = rows.shape[0]
     z, t = lax.axis_index("ctx"), lax.axis_index("tp")
-    copies = [
-        pltpu.make_async_copy(slot, slot_here, sems.at[0]),
-        pltpu.make_async_copy(kind, kind_here, sems.at[1]),
+    indices = [
+        pltpu.make_async_copy(slot, slot_here, index_sems.at[0]),
+        pltpu.make_async_copy(kind, kind_here, index_sems.at[1]),
     ]
-    parts = []
+    for copy in indices:
+        copy.start()
+    parts, copies = [], []
     for k, (out, parity) in enumerate(zip(outs, cuts)):
         size = out.shape[0] - 8
         part = t if parity is None else 2 * t + lax.rem(z + parity, 2)
         parts.append(part)
         source = rows.at[pl.ds(pl.multiple_of(part * size, size), size), :]
-        copies.append(pltpu.make_async_copy(source, out.at[pl.ds(0, size), :], sems.at[2 + k]))
-    for copy in copies:
-        copy.start()
-    for out in outs:
-        out[out.shape[0] - 8 :, :] = jnp.zeros((8, out.shape[1]), BF16)
-    for copy in copies:
+        copies.append(pltpu.make_async_copy(source, out.at[pl.ds(0, size), :], row_sems.at[k]))
+        copies[-1].start()
+    for tile in tiles:
+        tile[...] = jnp.zeros(tile.shape, BF16)
+    for copy in indices:
         copy.wait()
     slots, kinds = slot_here[...], kind_here[...]
-    for out, part in zip(outs, parts):
+    for n, (out, tile, part) in enumerate(zip(outs, tiles, parts)):
         size = out.shape[0] - 8
         s, k = slots[:, :size], kinds[:, :size]
         for i in range(1, whole // size):
@@ -47,7 +50,11 @@
             k = jnp.where(part == i, kinds[:, i * size : (i + 1) * size], k)
         line = lax.broadcasted_iota(I32, (8, size), 0)
         index = jnp.where(line == 0, s // 256, jnp.where(line == 1, s % 256, k))
-        out[size:, :size] = index.astype(F32).astype(BF16)
+        tile[:, :size] = index.astype(F32).astype(BF16)
+        copies.append(pltpu.make_async_copy(tile, out.at[pl.ds(size, 8), :], tile_sems.at[n]))
+        copies[-1].start()
+    for copy in copies:
+        copy.wait()
 
 
 def to_send(cuts, rows, slot, kind):
@@ -57,11 +64,14 @@
         functools.partial(send_kernel, cuts),
         out_shape=[jax.ShapeDtypeStruct((size + 8, width), BF16) for size in sizes],
         in_specs=[HBM] * 3,
-        out_specs=[VMEM] * len(cuts),
-        scratch_shapes=[
+        out_specs=[HBM] * len(cuts),
+        scratch_shapes=[pltpu.VMEM((8, width), BF16) for _ in cuts]
+        + [
             pltpu.VMEM(slot.shape, I32),
             pltpu.VMEM(slot.shape, I32),
-            pltpu.SemaphoreType.DMA((2 + len(cuts),)),
+            pltpu.SemaphoreType.DMA((2,)),
+            pltpu.SemaphoreType.DMA((len(cuts),)),
+            pltpu.SemaphoreType.DMA((len(cuts),)),
         ],
         compiler_params=pltpu.CompilerParams(vmem_limit_bytes=60 << 20),
         cost_estimate=cost(0, 4 * half * width),
@@ -255,12 +265,12 @@
     if n == 4:
         near, second, third = to_send((None, 0, 1), rows, row_slot, row_kind)
         near, second, third = over_ctx(near, 1), over_ctx(second, 2), over_ctx(third, 3)
-        near = after(near, own)
-        take([lax.all_gather(near, "tp", axis=0)])
-        second, third = after(second, blocks[-1]), after(third, blocks[-1])
-        second, third = lax.optimization_barrier((second, third))
-        shared = [over_ctx(second, 1), over_ctx(third, 1)]
-        take([lax.all_gather(part, "tp", axis=0) for part in (second, third)])
+        first = lax.optimization_barrier((near, second, third, own))[:3]
+        shared = [over_ctx(part, 1) for part in first[1:]]
+        other = [over_tp(part)[None] for part in first]
+        take([part[None] for part in first])
+        other = lax.optimization_barrier((*other, blocks[-1]))[:3]
+        take(other)
         shared = lax.optimization_barrier((*shared, blocks[-1]))[:2]
         swapped = [over_tp(part)[None] for part in shared]
         take([part[None] for part in shared])

time: 90.3 us -> 108 us (1.20)
  Pallas kernels: 14.6 us -> 33.6 us
  waiting for transfers between devices: 38.4 us -> 48.2 us
  blocking collectives: 10.8 us -> 4.36 us
  starting transfers between devices: 19.3 us -> 14.9 us
    pallas_call x1, Pallas kernels: 2.04 us -> 21 us  [to_send(): pl.pallas_call(functools.partial(send_kernel, cuts), out_shape=[jax.Shape...]
    all_gather x3 -> x0, blocking collectives: 6.41 us -> none  [the longest x2 4.11 us: body(): take([lax.all_gather(part, 'tp', axis=0) for part in (second, third)])]
    ppermute x6, waiting for transfers between devices: 18.3 us -> 24.5 us  [over_ctx(): return lax.ppermute(x, 'ctx', [(i, i ^ m) for i in range(n)])]
    ppermute x4, waiting for transfers between devices: 19.9 us -> 23.5 us  [body(): pieces[m, d] = lax.ppermute(piece, ('ctx', 'tp'), perm)]
    ppermute x4, starting transfers between devices: 7.54 us -> 4.13 us  [body(): pieces[m, d] = lax.ppermute(piece, ('ctx', 'tp'), perm)]
    ppermute x6, starting transfers between devices: 11.3 us -> 9.79 us  [over_ctx(): return lax.ppermute(x, 'ctx', [(i, i ^ m) for i in range(n)])]
  transfers between devices with their start and end apart: 12 -> 15, of which waited for: 8 -> 9; matrix products, arithmetic and copies ran while one was open for 2% -> 1% of each run, Pallas kernels for 10% -> 8%
where the time goes in v8:
time: 108 us
  waiting for transfers between devices  48.2 us (45%)
  Pallas kernels  33.6 us (31%)
  starting transfers between devices  14.9 us (14%)
  local copies, waits for them, and re-layouts  6.67 us (6%)
  blocking collectives  4.36 us (4%)
    ppermute x6, waiting for transfers between devices, over_ctx(): return lax.ppermute(x, 'ctx', [(i, i ^ m) for i in range(n)])  24.5 us
    ppermute x4, waiting for transfers between devices, body(): pieces[m, d] = lax.ppermute(piece, ('ctx', 'tp'), perm)  23.5 us
    pallas_call x1, Pallas kernels, to_send(): pl.pallas_call(functools.partial(send_kernel, cuts), out_shape=[jax.Shape...  21 us
    ppermute x6, starting transfers between devices, over_ctx(): return lax.ppermute(x, 'ctx', [(i, i ^ m) for i in range(n)])  9.79 us
    unnamed x16, local copies, waits for them, and re-layouts  5.26 us
    pallas_call x4, Pallas kernels, project_halves(): pl.pallas_call(project_halves_kernel, out_shape=[jax.ShapeDtypeStruct((ro...  5.05 us
    ppermute x4, starting transfers between devices, body(): pieces[m, d] = lax.ppermute(piece, ('ctx', 'tp'), perm)  4.13 us
    pallas_call x4, Pallas kernels, select(): pl.pallas_call(functools.partial(select_kernel, m, len(blocks)), out_shap...  3.4 us
  transfers between devices with their start and end apart: 15, of which 9 were waited for; matrix products, arithmetic and copies ran while one was open for 1% of the time, Pallas kernels for 8%

profile of v8, /device:TPU:0, one launch (start us, length us, event | category | flops | bytes accessed | tf_op | source)
XLA Modules:
  0.0 107.9 jit_solution(16975869481504699358)
XLA Ops:
  0.0 21.0 %to_send.1 = (bf16[136,1280]{1,0:T(8,128)(2,1)}, bf16[72,1280]{1,0:T(8,128)(2,1)}, bf16[72,1280]{1,0:T(8,128)(2,1)}) custom-call(bf16[256,1280]{1,0:T(8,128)(2,1)} %bitcast.14, s32[1,256]{1,0:T(1,128)} %refs_5_.4, s32[1,256]{1,0:T(1,128)} %kind.3), custom_call_target="tpu_custom_call" | custom-call | bytes 40960 | tf_op jit(solution)/shard_map/to_send/pallas_call | solution.py:63
  21.0 3.1 %collective-permute-start = (bf16[136,1280]{1,0:T(8,128)(2,1)}, bf16[136,1280]{1,0:T(8,128)(2,1)S(1)}, u32[]{:S(2)}, u32[]{:S(2)}) collective-permute-start(bf16[136,1280]{1,0:T(8,128)(2,1)} %get-tuple-element.37), channel_id=1, source_target_pairs={{0,4},{4,0},{8,12},{12,8},{1,5},{5,1},{9,13},{13,9},{2,6},{6,2},{1... | collective-permute-start | bytes 1044488 | tf_op jit(solution)/shard_map/ppermute | solution.py:252
  24.1 2.6 %collective-permute-start.1 = (bf16[72,1280]{1,0:T(8,128)(2,1)}, bf16[72,1280]{1,0:T(8,128)(2,1)S(1)}, u32[]{:S(2)}, u32[]{:S(2)}) collective-permute-start(bf16[72,1280]{1,0:T(8,128)(2,1)} %get-tuple-element.38), channel_id=1, source_target_pairs={{0,8},{4,12},{8,0},{12,4},{1,9},{5,13},{9,1},{13,5},{2,10},{6,14},... | collective-permute-start | bytes 552968 | tf_op jit(solution)/shard_map/ppermute | solution.py:252
  26.7 0.0 collective-permute-start.2
  26.7 0.7 broadcast_in_dim.43.ba
  27.4 0.7 broadcast_in_dim.44.bf
  28.1 1.7 %copy-done = bf16[1280,1024]{1,0:T(8,128)(2,1)S(1)} copy-done((bf16[1280,1024]{1,0:T(8,128)(2,1)S(1)}, bf16[1280,1024]{1,0:T(8,128)(2,1)}, u32[]{:S(2)}) %copy-start) | copy-done | bytes 2621464
  29.8 1.7 %copy-done.2 = bf16[1280,1024]{1,0:T(8,128)(2,1)S(1)} copy-done((bf16[1280,1024]{1,0:T(8,128)(2,1)S(1)}, bf16[1280,1024]{1,0:T(8,128)(2,1)}, u32[]{:S(2)}) %copy-start.2) | copy-done | bytes 2621464
  31.6 1.1 %copy-done.4 = bf16[1,256,1280]{2,1,0:T(8,128)(2,1)S(1)} copy-done((bf16[1,256,1280]{2,1,0:T(8,128)(2,1)S(1)}, bf16[1,256,1280]{2,1,0:T(8,128)(2,1)}, u32[]{:S(2)}) %copy-start.4) | copy-done | bytes 655384
  32.7 0.7 copy-done.6
  33.3 1.6 %project_own.1.refs_0_ = bf16[256,1024]{1,0:T(8,128)(2,1)S(1)} custom-call(s32[1,256]{1,0:T(1,128)S(1)} %copy-done.6, bf16[256,1280]{1,0:T(8,128)(2,1)S(1)} %bitcast.15, bf16[1280,1024]{1,0:T(8,128)(2,1)S(1)} %copy-done, bf16[1280,1024]{1,0:T(8,128)(2,1)S(1)} %copy-done.2, bf16[1,1024]{1,0:T(2,128)(2,1)S(1)} %broadcast_in_dim.43.ba, ...), custom_call_target="tpu_custom_call" | custom-call | flops 83886080 | bytes 327680 | tf_op jit(solution)/shard_map/project_own/pallas_call | solution.py:103
  34.9 2.1 %collective-permute-done.1 = bf16[72,1280]{1,0:T(8,128)(2,1)S(1)} collective-permute-done((bf16[72,1280]{1,0:T(8,128)(2,1)}, bf16[72,1280]{1,0:T(8,128)(2,1)S(1)}, u32[]{:S(2)}, u32[]{:S(2)}) %collective-permute-start.1) | collective-permute-done | bytes 184352 | tf_op jit(solution)/shard_map/ppermute | solution.py:252
  37.0 5.7 %collective-permute-done.2 = bf16[72,1280]{1,0:T(8,128)(2,1)S(1)} collective-permute-done((bf16[72,1280]{1,0:T(8,128)(2,1)}, bf16[72,1280]{1,0:T(8,128)(2,1)S(1)}, u32[]{:S(2)}, u32[]{:S(2)}) %collective-permute-start.2) | collective-permute-done | bytes 184352 | tf_op jit(solution)/shard_map/ppermute | solution.py:252
  42.7 0.0 collective-permute-done
  42.7 0.0 collective-permute-start.3
  42.7 0.5 collective-permute-start.4
  43.2 0.0 collective-permute-start.5
  43.2 1.1 %collective-permute-start.6 = (bf16[72,1280]{1,0:T(8,128)(2,1)S(1)}, bf16[72,1280]{1,0:T(8,128)(2,1)S(1)}, u32[]{:S(2)}, u32[]{:S(2)}) collective-permute-start(bf16[72,1280]{1,0:T(8,128)(2,1)S(1)} %collective-permute-done.1), channel_id=1, source_target_pairs={{0,4},{4,0},{8,12},{12,8},{1,5},{5,1},{9,13},{13,9},{2,6},{6,2},{1... | collective-permute-start | bytes 552968 | tf_op jit(solution)/shard_map/ppermute | solution.py:252
  44.3 0.9 collective-permute-start.7
  45.2 1.6 %project_halves.4 = (bf16[256,1024]{1,0:T(8,128)(2,1)S(1)}, s32[1,256]{1,0:T(1,128)S(1)}) custom-call(bf16[1280,1024]{1,0:T(8,128)(2,1)S(1)} %copy-done.1, bf16[1280,1024]{1,0:T(8,128)(2,1)S(1)} %copy-done.3, bf16[1,1024]{1,0:T(2,128)(2,1)S(1)} %broadcast_in_dim.43.ba, bf16[1,1024]{1,0:T(2,128)(2,1)S(1)} %broadcast_in_dim.44.bf, ...), custom_call_target="tpu_custom_call" | custom-call | flops 83886080 | bytes 327680 | tf_op jit(solution)/shard_map/project_halves/pallas_call | solution.py:131
  46.8 0.0 collective-permute-done.4
  46.9 0.0 collective-permute-done.5
  46.9 1.6 %project_halves.5 = (bf16[256,1024]{1,0:T(8,128)(2,1)S(1)}, s32[1,256]{1,0:T(1,128)S(1)}) custom-call(bf16[1280,1024]{1,0:T(8,128)(2,1)S(1)} %copy-done.1, bf16[1280,1024]{1,0:T(8,128)(2,1)S(1)} %copy-done.3, bf16[1,1024]{1,0:T(2,128)(2,1)S(1)} %broadcast_in_dim.43.ba, bf16[1,1024]{1,0:T(2,128)(2,1)S(1)} %broadcast_in_dim.44.bf, ...), custom_call_target="tpu_custom_call" | custom-call | flops 83886080 | bytes 327680 | tf_op jit(solution)/shard_map/project_halves/pallas_call | solution.py:131
  48.5 2.2 %collective-permute-done.6 = bf16[72,1280]{1,0:T(8,128)(2,1)S(1)} collective-permute-done((bf16[72,1280]{1,0:T(8,128)(2,1)S(1)}, bf16[72,1280]{1,0:T(8,128)(2,1)S(1)}, u32[]{:S(2)}, u32[]{:S(2)}) %collective-permute-start.6) | collective-permute-done | bytes 184352 | tf_op jit(solution)/shard_map/ppermute | solution.py:252
  50.6 3.6 %collective-permute-done.7 = bf16[72,1280]{1,0:T(8,128)(2,1)S(1)} collective-permute-done((bf16[72,1280]{1,0:T(8,128)(2,1)S(1)}, bf16[72,1280]{1,0:T(8,128)(2,1)S(1)}, u32[]{:S(2)}, u32[]{:S(2)}) %collective-permute-start.7) | collective-permute-done | bytes 184352 | tf_op jit(solution)/shard_map/ppermute | solution.py:252
  54.2 0.5 collective-permute-start.9
  54.7 0.9 project_halves.6
  55.7 0.2 collective-permute-done.9
  55.9 0.9 project_halves.7
  56.8 0.8 select.4
  57.7 1.8 %collective-permute-start.11 = (bf16[128,1024]{1,0:T(8,128)(2,1)S(1)}, bf16[128,1024]{1,0:T(8,128)(2,1)S(1)}, u32[]{:S(2)}, u32[]{:S(2)}) collective-permute-start(bf16[128,1024]{1,0:T(8,128)(2,1)S(1)} %get-tuple-element.57), channel_id=1, source_target_pairs={{0,13},{1,12},{4,9},{5,8},{8,5},{9,4},{12,1},{13,0},{2,15},{3,14},... | collective-permute-start | bytes 786440 | tf_op jit(solution)/shard_map/ppermute | solution.py:299
  59.4 2.0 %collective-permute-start.10 = (bf16[128,1024]{1,0:T(8,128)(2,1)S(1)}, bf16[128,1024]{1,0:T(8,128)(2,1)S(1)}, u32[]{:S(2)}, u32[]{:S(2)}) collective-permute-start(bf16[128,1024]{1,0:T(8,128)(2,1)S(1)} %get-tuple-element.56), channel_id=1, source_target_pairs={{0,12},{1,13},{4,8},{5,9},{8,4},{9,5},{12,0},{13,1},{2,14},{3,15},... | collective-permute-start | bytes 786440 | tf_op jit(solution)/shard_map/ppermute | solution.py:299
  61.4 0.8 select.5
  62.3 0.8 select.6
  63.2 0.4 collective-permute-start.13
  63.5 2.1 %collective-permute-start.12 = (bf16[256,1024]{1,0:T(8,128)(2,1)S(1)}, bf16[256,1024]{1,0:T(8,128)(2,1)S(1)}, u32[]{:S(2)}, u32[]{:S(2)}) collective-permute-start(bf16[256,1024]{1,0:T(8,128)(2,1)S(1)} %select.5), channel_id=1, source_target_pairs={{0,4},{4,0},{8,12},{12,8},{1,5},{5,1},{9,13},{13,9},{2,6},{6,2},{1... | collective-permute-start | bytes 1572872 | tf_op jit(solution)/shard_map/ppermute | solution.py:252
  65.6 2.4 %collective-permute-done.11.refs_1_ = bf16[128,1024]{1,0:T(8,128)(2,1)S(1)} collective-permute-done((bf16[128,1024]{1,0:T(8,128)(2,1)S(1)}, bf16[128,1024]{1,0:T(8,128)(2,1)S(1)}, u32[]{:S(2)}, u32[]{:S(2)}) %collective-permute-start.11) | collective-permute-done | bytes 262176 | tf_op jit(solution)/shard_map/ppermute | solution.py:299
  68.0 6.2 %collective-permute-done.10.refs_0_ = bf16[128,1024]{1,0:T(8,128)(2,1)S(1)} collective-permute-done((bf16[128,1024]{1,0:T(8,128)(2,1)S(1)}, bf16[128,1024]{1,0:T(8,128)(2,1)S(1)}, u32[]{:S(2)}, u32[]{:S(2)}) %collective-permute-start.10) | collective-permute-done | bytes 262176 | tf_op jit(solution)/shard_map/ppermute | solution.py:299
  74.3 0.2 squares.3.refs_0_
  74.4 0.9 select.7
  75.3 2.2 %all-gather = bf16[256,1024]{1,0:T(8,128)(2,1)S(1)} all-gather(bf16[128,1024]{1,0:T(8,128)(2,1)S(1)} %get-tuple-element.64), channel_id=2, replica_groups=mesh['groups'=2,'ctx'=4,'enc'=2,'tp'=2] {'tp'}, dimensions={0}, use_global_device_ids=true | all-gather | bytes 786432 | tf_op jit(solution)/shard_map/all_gather | solution.py:306
  77.5 0.2 squares.4.refs_0_
  77.6 11.0 %collective-permute-done.12.refs_1_.refs_2_ = bf16[256,1024]{1,0:T(8,128)(2,1)S(1)} collective-permute-done((bf16[256,1024]{1,0:T(8,128)(2,1)S(1)}, bf16[256,1024]{1,0:T(8,128)(2,1)S(1)}, u32[]{:S(2)}, u32[]{:S(2)}) %collective-permute-start.12) | collective-permute-done | bytes 524320 | tf_op jit(solution)/shard_map/ppermute | solution.py:252
  88.6 2.2 %all-gather.1 = bf16[256,1024]{1,0:T(8,128)(2,1)S(1)} all-gather(bf16[128,1024]{1,0:T(8,128)(2,1)S(1)} %slice.3), channel_id=3, replica_groups=mesh['groups'=2,'ctx'=4,'enc'=2,'tp'=2] {'tp'}, dimensions={0}, use_global_device_ids=true | all-gather | bytes 786432 | tf_op jit(solution)/shard_map/all_gather | solution.py:309
  90.8 0.2 squares.5.before
  91.0 14.9 %collective-permute-done.14.refs_5_ = bf16[128,1024]{1,0:T(8,128)(2,1)S(1)} collective-permute-done((bf16[128,1024]{1,0:T(8,128)(2,1)S(1)}, bf16[128,1024]{1,0:T(8,128)(2,1)S(1)}, u32[]{:S(2)}, u32[]{:S(2)}) %collective-permute-start.14) | collective-permute-done | bytes 262176 | tf_op jit(solution)/shard_map/ppermute | solution.py:299
  105.9 0.0 collective-permute-done.13.refs_4_
  105.9 2.1 %norm.1 = bf16[128,8192]{1,0:T(8,128)(2,1)} custom-call(bf16[1,8192]{1,0:T(2,128)(2,1)S(1)} %broadcast_in_dim.42.gain, f32[128,1]{1,0:T(8,128)S(1)} %squares.5.before, bf16[128,1024]{1,0:T(8,128)(2,1)S(1)} %collective-permute-done.10.refs_0_, bf16[128,1024]{1,0:T(8,128)(2,1)S(1)} %collective-permute-done.11.refs_1_, ...), custom_call_target="tpu_custom_call" | custom-call | flops 262144 | bytes 262144 | tf_op jit(solution)/shard_map/norm/pallas_call | solution.py:229
  (18 shorter events, 0.1 us)
Async XLA Ops:
  21.0 21.6 %collective-permute-start = (bf16[136,1280]{1,0:T(8,128)(2,1)}, bf16[136,1280]{1,0:T(8,128)(2,1)S(1)}, u32[]{:S(2)}, u32[]{:S(2)}) collective-permute-start(bf16[136,1280]{1,0:T(8,128)(2,1)} %get-tuple-element.37), channel_id=1, source_target_pairs={{0,4},{4,0},{8,12},{12,8},{1,5},{5,1},{9,13},{13,9},{2,6},{6,2},{1... | collective-permute-start | bytes 1044488 | tf_op jit(solution)/shard_map/ppermute | solution.py:252
  24.1 12.9 %collective-permute-start.1 = (bf16[72,1280]{1,0:T(8,128)(2,1)}, bf16[72,1280]{1,0:T(8,128)(2,1)S(1)}, u32[]{:S(2)}, u32[]{:S(2)}) collective-permute-start(bf16[72,1280]{1,0:T(8,128)(2,1)} %get-tuple-element.38), channel_id=1, source_target_pairs={{0,8},{4,12},{8,0},{12,4},{1,9},{5,13},{9,1},{13,5},{2,10},{6,14},... | collective-permute-start | bytes 552968 | tf_op jit(solution)/shard_map/ppermute | solution.py:252
  26.7 16.0 %collective-permute-start.2 = (bf16[72,1280]{1,0:T(8,128)(2,1)}, bf16[72,1280]{1,0:T(8,128)(2,1)S(1)}, u32[]{:S(2)}, u32[]{:S(2)}) collective-permute-start(bf16[72,1280]{1,0:T(8,128)(2,1)} %get-tuple-element.39), channel_id=1, source_target_pairs={{0,12},{4,8},{8,4},{12,0},{1,13},{5,9},{9,5},{13,1},{2,14},{6,10},... | collective-permute-start | bytes 552968 | tf_op jit(solution)/shard_map/ppermute | solution.py:252
  28.1 1.7 %copy-start = (bf16[1280,1024]{1,0:T(8,128)(2,1)S(1)}, bf16[1280,1024]{1,0:T(8,128)(2,1)}, u32[]{:S(2)}) copy-start(bf16[1280,1024]{1,0:T(8,128)(2,1)} %wa.9) | copy-start | bytes 7864324
  29.8 1.7 %copy-start.2 = (bf16[1280,1024]{1,0:T(8,128)(2,1)S(1)}, bf16[1280,1024]{1,0:T(8,128)(2,1)}, u32[]{:S(2)}) copy-start(bf16[1280,1024]{1,0:T(8,128)(2,1)} %wf.9) | copy-start | bytes 7864324
  31.6 1.1 %copy-start.4 = (bf16[1,256,1280]{2,1,0:T(8,128)(2,1)S(1)}, bf16[1,256,1280]{2,1,0:T(8,128)(2,1)}, u32[]{:S(2)}) copy-start(bf16[1,256,1280]{2,1,0:T(8,128)(2,1)} %param.8) | copy-start | bytes 1966084
  32.7 0.7 copy-start.6
  33.3 11.9 %copy-start.1 = (bf16[1280,1024]{1,0:T(8,128)(2,1)S(1)}, bf16[1280,1024]{1,0:T(8,128)(2,1)}, u32[]{:S(2)}) copy-start(bf16[1280,1024]{1,0:T(8,128)(2,1)} %wa.9) | copy-start | bytes 7864324
  33.3 11.9 %copy-start.3 = (bf16[1280,1024]{1,0:T(8,128)(2,1)S(1)}, bf16[1280,1024]{1,0:T(8,128)(2,1)}, u32[]{:S(2)}) copy-start(bf16[1280,1024]{1,0:T(8,128)(2,1)} %wf.9) | copy-start | bytes 7864324
  42.7 4.2 %collective-permute-start.3 = (bf16[136,1280]{1,0:T(8,128)(2,1)S(1)}, bf16[136,1280]{1,0:T(8,128)(2,1)S(1)}, u32[]{:S(2)}, u32[]{:S(2)}) collective-permute-start(bf16[136,1280]{1,0:T(8,128)(2,1)S(1)} %collective-permute-done), channel_id=1, source_target_pairs={{0,1},{1,0},{2,3},{3,2},{4,5},{5,4},{6,7},{7,6},{8,9},{9,8},{10,11... | collective-permute-start | bytes 1044488 | tf_op jit(solution)/shard_map/ppermute | solution.py:255
  42.7 4.2 %collective-permute-start.4 = (bf16[72,1280]{1,0:T(8,128)(2,1)S(1)}, bf16[72,1280]{1,0:T(8,128)(2,1)S(1)}, u32[]{:S(2)}, u32[]{:S(2)}) collective-permute-start(bf16[72,1280]{1,0:T(8,128)(2,1)S(1)} %collective-permute-done.1), channel_id=1, source_target_pairs={{0,1},{1,0},{2,3},{3,2},{4,5},{5,4},{6,7},{7,6},{8,9},{9,8},{10,11... | collective-permute-start | bytes 552968 | tf_op jit(solution)/shard_map/ppermute | solution.py:255
  43.2 3.7 %collective-permute-start.5 = (bf16[72,1280]{1,0:T(8,128)(2,1)S(1)}, bf16[72,1280]{1,0:T(8,128)(2,1)S(1)}, u32[]{:S(2)}, u32[]{:S(2)}) collective-permute-start(bf16[72,1280]{1,0:T(8,128)(2,1)S(1)} %collective-permute-done.2), channel_id=1, source_target_pairs={{0,1},{1,0},{2,3},{3,2},{4,5},{5,4},{6,7},{7,6},{8,9},{9,8},{10,11... | collective-permute-start | bytes 552968 | tf_op jit(solution)/shard_map/ppermute | solution.py:255
  43.2 7.4 %collective-permute-start.6 = (bf16[72,1280]{1,0:T(8,128)(2,1)S(1)}, bf16[72,1280]{1,0:T(8,128)(2,1)S(1)}, u32[]{:S(2)}, u32[]{:S(2)}) collective-permute-start(bf16[72,1280]{1,0:T(8,128)(2,1)S(1)} %collective-permute-done.1), channel_id=1, source_target_pairs={{0,4},{4,0},{8,12},{12,8},{1,5},{5,1},{9,13},{13,9},{2,6},{6,2},{1... | collective-permute-start | bytes 552968 | tf_op jit(solution)/shard_map/ppermute | solution.py:252
  44.3 9.9 %collective-permute-start.7 = (bf16[72,1280]{1,0:T(8,128)(2,1)S(1)}, bf16[72,1280]{1,0:T(8,128)(2,1)S(1)}, u32[]{:S(2)}, u32[]{:S(2)}) collective-permute-start(bf16[72,1280]{1,0:T(8,128)(2,1)S(1)} %collective-permute-done.2), channel_id=1, source_target_pairs={{0,4},{4,0},{8,12},{12,8},{1,5},{5,1},{9,13},{13,9},{2,6},{6,2},{1... | collective-permute-start | bytes 552968 | tf_op jit(solution)/shard_map/ppermute | solution.py:252
  54.2 1.5 %collective-permute-start.8 = (bf16[72,1280]{1,0:T(8,128)(2,1)S(1)}, bf16[72,1280]{1,0:T(8,128)(2,1)S(1)}, u32[]{:S(2)}, u32[]{:S(2)}) collective-permute-start(bf16[72,1280]{1,0:T(8,128)(2,1)S(1)} %collective-permute-done.6), channel_id=1, source_target_pairs={{0,1},{1,0},{2,3},{3,2},{4,5},{5,4},{6,7},{7,6},{8,9},{9,8},{10,11... | collective-permute-start | bytes 552968 | tf_op jit(solution)/shard_map/ppermute | solution.py:255
  54.2 1.7 %collective-permute-start.9 = (bf16[72,1280]{1,0:T(8,128)(2,1)S(1)}, bf16[72,1280]{1,0:T(8,128)(2,1)S(1)}, u32[]{:S(2)}, u32[]{:S(2)}) collective-permute-start(bf16[72,1280]{1,0:T(8,128)(2,1)S(1)} %collective-permute-done.7), channel_id=1, source_target_pairs={{0,1},{1,0},{2,3},{3,2},{4,5},{5,4},{6,7},{7,6},{8,9},{9,8},{10,11... | collective-permute-start | bytes 552968 | tf_op jit(solution)/shard_map/ppermute | solution.py:255
  55.9 0.9 copy-start.5
  55.9 5.5 %copy-start.7 = (bf16[8192]{0:T(1024)(128)(2,1)S(1)}, bf16[8192]{0:T(1024)(128)(2,1)}, u32[]{:S(2)}) copy-start(bf16[8192]{0:T(1024)(128)(2,1)} %param.15) | copy-start | bytes 49156
  57.7 10.3 %collective-permute-start.11 = (bf16[128,1024]{1,0:T(8,128)(2,1)S(1)}, bf16[128,1024]{1,0:T(8,128)(2,1)S(1)}, u32[]{:S(2)}, u32[]{:S(2)}) collective-permute-start(bf16[128,1024]{1,0:T(8,128)(2,1)S(1)} %get-tuple-element.57), channel_id=1, source_target_pairs={{0,13},{1,12},{4,9},{5,8},{8,5},{9,4},{12,1},{13,0},{2,15},{3,14},... | collective-permute-start | bytes 786440 | tf_op jit(solution)/shard_map/ppermute | solution.py:299
  59.4 14.8 %collective-permute-start.10 = (bf16[128,1024]{1,0:T(8,128)(2,1)S(1)}, bf16[128,1024]{1,0:T(8,128)(2,1)S(1)}, u32[]{:S(2)}, u32[]{:S(2)}) collective-permute-start(bf16[128,1024]{1,0:T(8,128)(2,1)S(1)} %get-tuple-element.56), channel_id=1, source_target_pairs={{0,12},{1,13},{4,8},{5,9},{8,4},{9,5},{12,0},{13,1},{2,14},{3,15},... | collective-permute-start | bytes 786440 | tf_op jit(solution)/shard_map/ppermute | solution.py:299
  63.2 42.7 %collective-permute-start.13 = (bf16[128,1024]{1,0:T(8,128)(2,1)S(1)}, bf16[128,1024]{1,0:T(8,128)(2,1)S(1)}, u32[]{:S(2)}, u32[]{:S(2)}) collective-permute-start(bf16[128,1024]{1,0:T(8,128)(2,1)S(1)} %get-tuple-element.60), channel_id=1, source_target_pairs={{0,8},{1,9},{4,12},{5,13},{8,0},{9,1},{12,4},{13,5},{2,10},{3,11},... | collective-permute-start | bytes 786440 | tf_op jit(solution)/shard_map/ppermute | solution.py:299
  63.5 25.1 %collective-permute-start.12 = (bf16[256,1024]{1,0:T(8,128)(2,1)S(1)}, bf16[256,1024]{1,0:T(8,128)(2,1)S(1)}, u32[]{:S(2)}, u32[]{:S(2)}) collective-permute-start(bf16[256,1024]{1,0:T(8,128)(2,1)S(1)} %select.5), channel_id=1, source_target_pairs={{0,4},{4,0},{8,12},{12,8},{1,5},{5,1},{9,13},{13,9},{2,6},{6,2},{1... | collective-permute-start | bytes 1572872 | tf_op jit(solution)/shard_map/ppermute | solution.py:252
  65.6 40.2 %collective-permute-start.14 = (bf16[128,1024]{1,0:T(8,128)(2,1)S(1)}, bf16[128,1024]{1,0:T(8,128)(2,1)S(1)}, u32[]{:S(2)}, u32[]{:S(2)}) collective-permute-start(bf16[128,1024]{1,0:T(8,128)(2,1)S(1)} %get-tuple-element.67), channel_id=1, source_target_pairs={{0,9},{1,8},{4,13},{5,12},{8,1},{9,0},{12,5},{13,4},{2,11},{3,10},... | collective-permute-start | bytes 786440 | tf_op jit(solution)/shard_map/ppermute | solution.py:299

commit v9 on v7

--- a/solution.py
+++ b/solution.py
@@ -17,51 +17,72 @@
     return pl.CostEstimate(flops=flops // 16, bytes_accessed=moved // 16, transcendentals=0)
 
 
+def to_tiles(x, out):
+    at = 0
+    for r in range(0, x.shape[0], 16):
+        for c in range(0, x.shape[1], 128):
+            out[at : at + 16, :] = x[r : r + 16, c : c + 128]
+            at += 16
+
+
+def from_tiles(tiles, width):
+    per_row = width // 128
+    lines = []
+    for r in range(0, tiles.shape[0], 16 * per_row):
+        line = [tiles[r + 16 * c : r + 16 * (c + 1)] for c in range(per_row)]
+        lines.append(jnp.concatenate(line, axis=1))
+    return jnp.concatenate(lines, axis=0)
+
+
 def send_kernel(cuts, rows, slot, kind, *refs):
-    outs, slot_here, kind_here, sems = refs[:-3], refs[-3], refs[-2], refs[-1]
-    whole = rows.shape[0]
+    outs, (rows_here, slot_here, kind_here, sems) = refs[:-4], refs[-4:]
+    whole, width = rows.shape
+    half = whole // 2
     z, t = lax.axis_index("ctx"), lax.axis_index("tp")
+    source = rows.at[pl.ds(pl.multiple_of(t * half, half), half), :]
     copies = [
         pltpu.make_async_copy(slot, slot_here, sems.at[0]),
         pltpu.make_async_copy(kind, kind_here, sems.at[1]),
+        pltpu.make_async_copy(source, rows_here, sems.at[2]),
     ]
-    parts = []
-    for k, (out, parity) in enumerate(zip(outs, cuts)):
-        size = out.shape[0] - 8
-        part = t if parity is None else 2 * t + lax.rem(z + parity, 2)
-        parts.append(part)
-        source = rows.at[pl.ds(pl.multiple_of(part * size, size), size), :]
-        copies.append(pltpu.make_async_copy(source, out.at[pl.ds(0, size), :], sems.at[2 + k]))
     for copy in copies:
         copy.start()
-    for out in outs:
-        out[out.shape[0] - 8 :, :] = jnp.zeros((8, out.shape[1]), BF16)
     for copy in copies:
         copy.wait()
-    slots, kinds = slot_here[...], kind_here[...]
-    for out, part in zip(outs, parts):
-        size = out.shape[0] - 8
-        s, k = slots[:, :size], kinds[:, :size]
-        for i in range(1, whole // size):
-            s = jnp.where(part == i, slots[:, i * size : (i + 1) * size], s)
-            k = jnp.where(part == i, kinds[:, i * size : (i + 1) * size], k)
-        line = lax.broadcasted_iota(I32, (8, size), 0)
+    slots = jnp.where(t == 0, slot_here[:, :half], slot_here[:, half:])
+    kinds = jnp.where(t == 0, kind_here[:, :half], kind_here[:, half:])
+    for out, parity in zip(outs, cuts):
+        x, s, k = rows_here, slots, kinds
+        size = half
+        if parity is not None:
+            size = half // 2
+            second = lax.rem(z + parity, 2)
+            x = rows_here.at[pl.ds(pl.multiple_of(second * size, size), size), :]
+            s = jnp.where(second == 0, slots[:, :size], slots[:, size:])
+            k = jnp.where(second == 0, kinds[:, :size], kinds[:, size:])
+        to_tiles(x, out)
+        line = lax.broadcasted_iota(I32, (16, size), 0)
         index = jnp.where(line == 0, s // 256, jnp.where(line == 1, s % 256, k))
-        out[size:, :size] = index.astype(F32).astype(BF16)
+        index = jnp.where(line < 3, index, 0).astype(F32)
+        if size < 128:
+            index = jnp.concatenate([index, jnp.zeros((16, 128 - size), F32)], axis=1)
+        out[size * width // 128 :, :] = index.astype(BF16)
 
 
 def to_send(cuts, rows, slot, kind):
     half, width = rows.shape[0] // 2, rows.shape[1]
     sizes = [half if parity is None else half // 2 for parity in cuts]
+    shapes = [(size * width // 128 + 16, 128) for size in sizes]
     return pl.pallas_call(
         functools.partial(send_kernel, cuts),
-        out_shape=[jax.ShapeDtypeStruct((size + 8, width), BF16) for size in sizes],
+        out_shape=[jax.ShapeDtypeStruct(shape, BF16) for shape in shapes],
         in_specs=[HBM] * 3,
         out_specs=[VMEM] * len(cuts),
         scratch_shapes=[
+            pltpu.VMEM((half, width), BF16),
             pltpu.VMEM(slot.shape, I32),
             pltpu.VMEM(slot.shape, I32),
-            pltpu.SemaphoreType.DMA((2 + len(cuts),)),
+            pltpu.SemaphoreType.DMA((3,)),
         ],
         compiler_params=pltpu.CompilerParams(vmem_limit_bytes=60 << 20),
         cost_estimate=cost(0, 4 * half * width),
@@ -101,32 +122,34 @@
     )(kind, rows, *weights)
 
 
-def project_halves_kernel(wa, wf, ba, bf, *refs):
-    pieces, out, slots = refs[:-2], refs[-2], refs[-1]
+def project_parts_kernel(wa, wf, ba, bf, *refs):
+    parts, out, slots = refs[:-2], refs[-2], refs[-1]
+    width = wa.shape[0]
     x, index = [], []
-    for piece in pieces:
-        half = piece.shape[-2] - 8
-        for k in range(piece.shape[0]):
-            x.append(piece[k, :half, :])
-            index.append(piece[k, half:, :half].astype(F32).astype(I32))
+    for ref in parts:
+        for k in range(ref.shape[0]):
+            lines = ref.shape[1] - 16
+            size = lines * 128 // width
+            x.append(from_tiles(ref[k, :lines, :], width))
+            index.append(ref[k, lines:, :].astype(F32).astype(I32)[:, :size])
     x = x[0] if len(x) == 1 else jnp.concatenate(x, axis=0)
     index = index[0] if len(index) == 1 else jnp.concatenate(index, axis=1)
     slots[...] = index[0:1] * 256 + index[1:2]
     project(index[2:3], x, wa, wf, ba, bf, out)
 
 
-def project_halves(pieces, weights):
-    rows, ew = sum(p.shape[0] * (p.shape[1] - 8) for p in pieces), pieces[0].shape[2]
-    cols = weights[0].shape[1]
-    return pl.pallas_call(
-        project_halves_kernel,
+def project_parts(parts, weights):
+    ew, cols = weights[0].shape
+    rows = sum(p.shape[0] * (p.shape[1] - 16) * 128 // ew for p in parts)
+    return pl.pallas_call(
+        project_parts_kernel,
         out_shape=[jax.ShapeDtypeStruct((rows, cols), BF16), jax.ShapeDtypeStruct((1, rows), I32)],
-        in_specs=[VMEM] * (4 + len(pieces)),
+        in_specs=[VMEM] * (4 + len(parts)),
         out_specs=[VMEM] * 2,
         compiler_params=PARAMS,
         cost_estimate=cost(4 * rows * ew * cols, 4 * ew * cols),
-        name="project_halves",
-    )(*weights, *pieces)
+        name="project_parts",
+    )(*weights, *parts)
 
 
 def select_kernel(m, count, *refs):
@@ -248,19 +271,19 @@
     blocks, slots = [own], [row_slot]
 
     def take(group):
-        block, slot = project_halves(group, weights)
+        block, slot = project_parts(group, weights)
         blocks.append(block)
         slots.append(slot)
 
     if n == 4:
         near, second, third = to_send((None, 0, 1), rows, row_slot, row_kind)
         near, second, third = over_ctx(near, 1), over_ctx(second, 2), over_ctx(third, 3)
-        near = after(near, own)
-        take([lax.all_gather(near, "tp", axis=0)])
-        second, third = after(second, blocks[-1]), after(third, blocks[-1])
-        second, third = lax.optimization_barrier((second, third))
-        shared = [over_ctx(second, 1), over_ctx(third, 1)]
-        take([lax.all_gather(part, "tp", axis=0) for part in (second, third)])
+        first = lax.optimization_barrier((near, second, third, own))[:3]
+        shared = [over_ctx(part, 1) for part in first[1:]]
+        other = [over_tp(part)[None] for part in first]
+        take([part[None] for part in first])
+        other = lax.optimization_barrier((*other, blocks[-1]))[:3]
+        take(other)
         shared = lax.optimization_barrier((*shared, blocks[-1]))[:2]
         swapped = [over_tp(part)[None] for part in shared]
         take([part[None] for part in shared])

time: 90.3 us -> 87 us (0.963)
  waiting for transfers between devices: 38.4 us -> 46.2 us
  blocking collectives: 10.8 us -> 4.36 us
  starting transfers between devices: 19.3 us -> 14.8 us
    all_gather x3 -> x0, blocking collectives: 6.41 us -> none  [the longest x2 4.11 us: body(): take([lax.all_gather(part, 'tp', axis=0) for part in (second, third)])]
    ppermute x6, waiting for transfers between devices: 18.3 us -> 22.4 us  [over_ctx(): return lax.ppermute(x, 'ctx', [(i, i ^ m) for i in range(n)])]
    ppermute x4, waiting for transfers between devices: 19.9 us -> 23.7 us  [body(): pieces[m, d] = lax.ppermute(piece, ('ctx', 'tp'), perm)]
    ppermute x4, starting transfers between devices: 7.54 us -> 4 us  [body(): pieces[m, d] = lax.ppermute(piece, ('ctx', 'tp'), perm)]
    ppermute x6, starting transfers between devices: 11.3 us -> 9.74 us  [over_ctx(): return lax.ppermute(x, 'ctx', [(i, i ^ m) for i in range(n)])]
  transfers between devices with their start and end apart: 12 -> 15, of which waited for: 8 -> 9; matrix products, arithmetic and copies ran while one was open for 2% -> 2% of each run, Pallas kernels for 10% -> 10%
where the time goes in v9:
time: 87 us; the launch traced here: 86.7 us
  waiting for transfers between devices  46.2 us (53%)
  starting transfers between devices  14.8 us (17%)
  Pallas kernels  14.5 us (17%)
  local copies, waits for them, and re-layouts  6.67 us (8%)
  blocking collectives  4.36 us (5%)
    ppermute x4, waiting for transfers between devices, body(): pieces[m, d] = lax.ppermute(piece, ('ctx', 'tp'), perm)  23.7 us
    ppermute x6, waiting for transfers between devices, over_ctx(): return lax.ppermute(x, 'ctx', [(i, i ^ m) for i in range(n)])  22.4 us
    ppermute x6, starting transfers between devices, over_ctx(): return lax.ppermute(x, 'ctx', [(i, i ^ m) for i in range(n)])  9.74 us
    unnamed x16, local copies, waits for them, and re-layouts  5.26 us
    pallas_call x4, Pallas kernels, project_parts(): pl.pallas_call(project_parts_kernel, out_shape=[jax.ShapeDtypeStruct((row...  4.99 us
    ppermute x4, starting transfers between devices, body(): pieces[m, d] = lax.ppermute(piece, ('ctx', 'tp'), perm)  4 us
    pallas_call x4, Pallas kernels, select(): pl.pallas_call(functools.partial(select_kernel, m, len(blocks)), out_shap...  3.4 us
    all_gather x1, blocking collectives, body(): pieces[0, 1] = lax.all_gather(other, 'tp', axis=0)  2.18 us
  transfers between devices with their start and end apart: 15, of which 9 were waited for; matrix products, arithmetic and copies ran while one was open for 2% of the time, Pallas kernels for 10%

profile of v9, /device:TPU:0, one launch (start us, length us, event | category | flops | bytes accessed | tf_op | source)
XLA Modules:
  0.0 86.7 jit_solution(7058773571943069223)
XLA Ops:
  0.0 2.0 %to_send.1 = (bf16[1296,128]{1,0:T(8,128)(2,1)}, bf16[656,128]{1,0:T(8,128)(2,1)}, bf16[656,128]{1,0:T(8,128)(2,1)}) custom-call(bf16[256,1280]{1,0:T(8,128)(2,1)} %bitcast.14, s32[1,256]{1,0:T(1,128)} %refs_5_.4, s32[1,256]{1,0:T(1,128)} %kind.3), custom_call_target="tpu_custom_call" | custom-call | bytes 40960 | tf_op jit(solution)/shard_map/to_send/pallas_call | solution.py:76
  2.0 3.1 %collective-permute-start = (bf16[1296,128]{1,0:T(8,128)(2,1)}, bf16[1296,128]{1,0:T(8,128)(2,1)S(1)}, u32[]{:S(2)}, u32[]{:S(2)}) collective-permute-start(bf16[1296,128]{1,0:T(8,128)(2,1)} %get-tuple-element.37), channel_id=1, source_target_pairs={{0,4},{4,0},{8,12},{12,8},{1,5},{5,1},{9,13},{13,9},{2,6},{6,2},{1... | collective-permute-start | bytes 995336 | tf_op jit(solution)/shard_map/ppermute | solution.py:265
  5.1 2.6 %collective-permute-start.1 = (bf16[656,128]{1,0:T(8,128)(2,1)}, bf16[656,128]{1,0:T(8,128)(2,1)S(1)}, u32[]{:S(2)}, u32[]{:S(2)}) collective-permute-start(bf16[656,128]{1,0:T(8,128)(2,1)} %get-tuple-element.38), channel_id=1, source_target_pairs={{0,8},{4,12},{8,0},{12,4},{1,9},{5,13},{9,1},{13,5},{2,10},{6,14},... | collective-permute-start | bytes 503816 | tf_op jit(solution)/shard_map/ppermute | solution.py:265
  7.7 0.0 collective-permute-start.2
  7.7 0.7 broadcast_in_dim.43.ba
  8.4 0.7 broadcast_in_dim.44.bf
  9.0 1.7 %copy-done = bf16[1280,1024]{1,0:T(8,128)(2,1)S(1)} copy-done((bf16[1280,1024]{1,0:T(8,128)(2,1)S(1)}, bf16[1280,1024]{1,0:T(8,128)(2,1)}, u32[]{:S(2)}) %copy-start) | copy-done | bytes 2621464
  10.8 1.7 %copy-done.2 = bf16[1280,1024]{1,0:T(8,128)(2,1)S(1)} copy-done((bf16[1280,1024]{1,0:T(8,128)(2,1)S(1)}, bf16[1280,1024]{1,0:T(8,128)(2,1)}, u32[]{:S(2)}) %copy-start.2) | copy-done | bytes 2621464
  12.5 1.1 %copy-done.4 = bf16[1,256,1280]{2,1,0:T(8,128)(2,1)S(1)} copy-done((bf16[1,256,1280]{2,1,0:T(8,128)(2,1)S(1)}, bf16[1,256,1280]{2,1,0:T(8,128)(2,1)}, u32[]{:S(2)}) %copy-start.4) | copy-done | bytes 655384
  13.6 0.7 copy-done.6
  14.3 1.6 %project_own.1.refs_0_ = bf16[256,1024]{1,0:T(8,128)(2,1)S(1)} custom-call(s32[1,256]{1,0:T(1,128)S(1)} %copy-done.6, bf16[256,1280]{1,0:T(8,128)(2,1)S(1)} %bitcast.15, bf16[1280,1024]{1,0:T(8,128)(2,1)S(1)} %copy-done, bf16[1280,1024]{1,0:T(8,128)(2,1)S(1)} %copy-done.2, bf16[1,1024]{1,0:T(2,128)(2,1)S(1)} %broadcast_in_dim.43.ba, ...), custom_call_target="tpu_custom_call" | custom-call | flops 83886080 | bytes 327680 | tf_op jit(solution)/shard_map/project_own/pallas_call | solution.py:114
  15.9 1.4 %collective-permute-done.1 = bf16[656,128]{1,0:T(8,128)(2,1)S(1)} collective-permute-done((bf16[656,128]{1,0:T(8,128)(2,1)}, bf16[656,128]{1,0:T(8,128)(2,1)S(1)}, u32[]{:S(2)}, u32[]{:S(2)}) %collective-permute-start.1) | collective-permute-done | bytes 167968 | tf_op jit(solution)/shard_map/ppermute | solution.py:265
  17.2 5.3 %collective-permute-done.2 = bf16[656,128]{1,0:T(8,128)(2,1)S(1)} collective-permute-done((bf16[656,128]{1,0:T(8,128)(2,1)}, bf16[656,128]{1,0:T(8,128)(2,1)S(1)}, u32[]{:S(2)}, u32[]{:S(2)}) %collective-permute-start.2) | collective-permute-done | bytes 167968 | tf_op jit(solution)/shard_map/ppermute | solution.py:265
  22.6 0.0 collective-permute-done
  22.6 0.5 collective-permute-start.4
  23.1 0.0 collective-permute-start.5
  23.1 0.8 collective-permute-start.6
  23.9 1.3 %collective-permute-start.7 = (bf16[656,128]{1,0:T(8,128)(2,1)S(1)}, bf16[656,128]{1,0:T(8,128)(2,1)S(1)}, u32[]{:S(2)}, u32[]{:S(2)}) collective-permute-start(bf16[656,128]{1,0:T(8,128)(2,1)S(1)} %collective-permute-done.2), channel_id=1, source_target_pairs={{0,4},{4,0},{8,12},{12,8},{1,5},{5,1},{9,13},{13,9},{2,6},{6,2},{1... | collective-permute-start | bytes 503816 | tf_op jit(solution)/shard_map/ppermute | solution.py:265
  25.1 1.6 %project_parts.4 = (bf16[256,1024]{1,0:T(8,128)(2,1)S(1)}, s32[1,256]{1,0:T(1,128)S(1)}) custom-call(bf16[1280,1024]{1,0:T(8,128)(2,1)S(1)} %copy-done.1, bf16[1280,1024]{1,0:T(8,128)(2,1)S(1)} %copy-done.3, bf16[1,1024]{1,0:T(2,128)(2,1)S(1)} %broadcast_in_dim.43.ba, bf16[1,1024]{1,0:T(2,128)(2,1)S(1)} %broadcast_in_dim.44.bf, ...), custom_call_target="tpu_custom_call" | custom-call | flops 83886080 | bytes 327680 | tf_op jit(solution)/shard_map/project_parts/pallas_call | solution.py:144
  26.7 0.0 collective-permute-done.4
  26.8 0.0 collective-permute-done.3
  26.8 1.6 %project_parts.5 = (bf16[256,1024]{1,0:T(8,128)(2,1)S(1)}, s32[1,256]{1,0:T(1,128)S(1)}) custom-call(bf16[1280,1024]{1,0:T(8,128)(2,1)S(1)} %copy-done.1, bf16[1280,1024]{1,0:T(8,128)(2,1)S(1)} %copy-done.3, bf16[1,1024]{1,0:T(2,128)(2,1)S(1)} %broadcast_in_dim.43.ba, bf16[1,1024]{1,0:T(2,128)(2,1)S(1)} %broadcast_in_dim.44.bf, ...), custom_call_target="tpu_custom_call" | custom-call | flops 83886080 | bytes 327680 | tf_op jit(solution)/shard_map/project_parts/pallas_call | solution.py:144
  28.4 1.8 %collective-permute-done.6 = bf16[656,128]{1,0:T(8,128)(2,1)S(1)} collective-permute-done((bf16[656,128]{1,0:T(8,128)(2,1)S(1)}, bf16[656,128]{1,0:T(8,128)(2,1)S(1)}, u32[]{:S(2)}, u32[]{:S(2)}) %collective-permute-start.6) | collective-permute-done | bytes 167968 | tf_op jit(solution)/shard_map/ppermute | solution.py:265
  30.2 3.2 %collective-permute-done.7 = bf16[656,128]{1,0:T(8,128)(2,1)S(1)} collective-permute-done((bf16[656,128]{1,0:T(8,128)(2,1)S(1)}, bf16[656,128]{1,0:T(8,128)(2,1)S(1)}, u32[]{:S(2)}, u32[]{:S(2)}) %collective-permute-start.7) | collective-permute-done | bytes 167968 | tf_op jit(solution)/shard_map/ppermute | solution.py:265
  33.4 0.0 collective-permute-start.8
  33.4 0.5 collective-permute-start.9
  33.9 0.9 %project_parts.6 = (bf16[128,1024]{1,0:T(8,128)(2,1)S(1)}, s32[1,128]{1,0:T(1,128)S(1)}) custom-call(bf16[1280,1024]{1,0:T(8,128)(2,1)S(1)} %copy-done.1, bf16[1280,1024]{1,0:T(8,128)(2,1)S(1)} %copy-done.3, bf16[1,1024]{1,0:T(2,128)(2,1)S(1)} %broadcast_in_dim.43.ba, bf16[1,1024]{1,0:T(2,128)(2,1)S(1)} %broadcast_in_dim.44.bf, ...), custom_call_target="tpu_custom_call" | custom-call | flops 41943040 | bytes 327680 | tf_op jit(solution)/shard_map/project_parts/pallas_call | solution.py:144
  34.8 0.2 collective-permute-done.9
  35.0 0.9 %project_parts.7 = (bf16[128,1024]{1,0:T(8,128)(2,1)S(1)}, s32[1,128]{1,0:T(1,128)S(1)}) custom-call(bf16[1280,1024]{1,0:T(8,128)(2,1)S(1)} %copy-done.1, bf16[1280,1024]{1,0:T(8,128)(2,1)S(1)} %copy-done.3, bf16[1,1024]{1,0:T(2,128)(2,1)S(1)} %broadcast_in_dim.43.ba, bf16[1,1024]{1,0:T(2,128)(2,1)S(1)} %broadcast_in_dim.44.bf, ...), custom_call_target="tpu_custom_call" | custom-call | flops 41943040 | bytes 327680 | tf_op jit(solution)/shard_map/project_parts/pallas_call | solution.py:144
  36.0 0.8 select.4
  36.8 1.4 %collective-permute-start.11 = (bf16[128,1024]{1,0:T(8,128)(2,1)S(1)}, bf16[128,1024]{1,0:T(8,128)(2,1)S(1)}, u32[]{:S(2)}, u32[]{:S(2)}) collective-permute-start(bf16[128,1024]{1,0:T(8,128)(2,1)S(1)} %get-tuple-element.57), channel_id=1, source_target_pairs={{0,13},{1,12},{4,9},{5,8},{8,5},{9,4},{12,1},{13,0},{2,15},{3,14},... | collective-permute-start | bytes 786440 | tf_op jit(solution)/shard_map/ppermute | solution.py:312
  38.2 2.3 %collective-permute-start.10 = (bf16[128,1024]{1,0:T(8,128)(2,1)S(1)}, bf16[128,1024]{1,0:T(8,128)(2,1)S(1)}, u32[]{:S(2)}, u32[]{:S(2)}) collective-permute-start(bf16[128,1024]{1,0:T(8,128)(2,1)S(1)} %get-tuple-element.56), channel_id=1, source_target_pairs={{0,12},{1,13},{4,8},{5,9},{8,4},{9,5},{12,0},{13,1},{2,14},{3,15},... | collective-permute-start | bytes 786440 | tf_op jit(solution)/shard_map/ppermute | solution.py:312
  40.6 0.8 select.5
  41.5 0.8 select.6
  42.3 0.1 collective-permute-start.13
  42.4 2.0 %collective-permute-start.12 = (bf16[256,1024]{1,0:T(8,128)(2,1)S(1)}, bf16[256,1024]{1,0:T(8,128)(2,1)S(1)}, u32[]{:S(2)}, u32[]{:S(2)}) collective-permute-start(bf16[256,1024]{1,0:T(8,128)(2,1)S(1)} %select.5), channel_id=1, source_target_pairs={{0,4},{4,0},{8,12},{12,8},{1,5},{5,1},{9,13},{13,9},{2,6},{6,2},{1... | collective-permute-start | bytes 1572872 | tf_op jit(solution)/shard_map/ppermute | solution.py:265
  44.4 0.2 collective-permute-start.14
  44.6 2.5 %collective-permute-done.11.refs_1_ = bf16[128,1024]{1,0:T(8,128)(2,1)S(1)} collective-permute-done((bf16[128,1024]{1,0:T(8,128)(2,1)S(1)}, bf16[128,1024]{1,0:T(8,128)(2,1)S(1)}, u32[]{:S(2)}, u32[]{:S(2)}) %collective-permute-start.11) | collective-permute-done | bytes 262176 | tf_op jit(solution)/shard_map/ppermute | solution.py:312
  47.1 6.3 %collective-permute-done.10.refs_0_ = bf16[128,1024]{1,0:T(8,128)(2,1)S(1)} collective-permute-done((bf16[128,1024]{1,0:T(8,128)(2,1)S(1)}, bf16[128,1024]{1,0:T(8,128)(2,1)S(1)}, u32[]{:S(2)}, u32[]{:S(2)}) %collective-permute-start.10) | collective-permute-done | bytes 262176 | tf_op jit(solution)/shard_map/ppermute | solution.py:312
  53.4 0.2 squares.3.refs_0_
  53.6 0.9 select.7
  54.4 2.2 %all-gather = bf16[256,1024]{1,0:T(8,128)(2,1)S(1)} all-gather(bf16[128,1024]{1,0:T(8,128)(2,1)S(1)} %get-tuple-element.64), channel_id=2, replica_groups=mesh['groups'=2,'ctx'=4,'enc'=2,'tp'=2] {'tp'}, dimensions={0}, use_global_device_ids=true | all-gather | bytes 786432 | tf_op jit(solution)/shard_map/all_gather | solution.py:319
  56.6 0.2 squares.4.refs_0_
  56.8 10.6 %collective-permute-done.12.refs_1_.refs_2_ = bf16[256,1024]{1,0:T(8,128)(2,1)S(1)} collective-permute-done((bf16[256,1024]{1,0:T(8,128)(2,1)S(1)}, bf16[256,1024]{1,0:T(8,128)(2,1)S(1)}, u32[]{:S(2)}, u32[]{:S(2)}) %collective-permute-start.12) | collective-permute-done | bytes 524320 | tf_op jit(solution)/shard_map/ppermute | solution.py:265
  67.4 2.2 %all-gather.1 = bf16[256,1024]{1,0:T(8,128)(2,1)S(1)} all-gather(bf16[128,1024]{1,0:T(8,128)(2,1)S(1)} %slice.3), channel_id=3, replica_groups=mesh['groups'=2,'ctx'=4,'enc'=2,'tp'=2] {'tp'}, dimensions={0}, use_global_device_ids=true | all-gather | bytes 786432 | tf_op jit(solution)/shard_map/all_gather | solution.py:322
  69.6 0.2 squares.5.before
  69.8 14.8 %collective-permute-done.14.refs_5_ = bf16[128,1024]{1,0:T(8,128)(2,1)S(1)} collective-permute-done((bf16[128,1024]{1,0:T(8,128)(2,1)S(1)}, bf16[128,1024]{1,0:T(8,128)(2,1)S(1)}, u32[]{:S(2)}, u32[]{:S(2)}) %collective-permute-start.14) | collective-permute-done | bytes 262176 | tf_op jit(solution)/shard_map/ppermute | solution.py:312
  84.6 2.1 %norm.1 = bf16[128,8192]{1,0:T(8,128)(2,1)} custom-call(bf16[1,8192]{1,0:T(2,128)(2,1)S(1)} %broadcast_in_dim.42.gain, f32[128,1]{1,0:T(8,128)S(1)} %squares.5.before, bf16[128,1024]{1,0:T(8,128)(2,1)S(1)} %collective-permute-done.10.refs_0_, bf16[128,1024]{1,0:T(8,128)(2,1)S(1)} %collective-permute-done.11.refs_1_, ...), custom_call_target="tpu_custom_call" | custom-call | flops 262144 | bytes 262144 | tf_op jit(solution)/shard_map/norm/pallas_call | solution.py:242
  (18 shorter events, 0.1 us)
Async XLA Ops:
  2.0 20.6 %collective-permute-start = (bf16[1296,128]{1,0:T(8,128)(2,1)}, bf16[1296,128]{1,0:T(8,128)(2,1)S(1)}, u32[]{:S(2)}, u32[]{:S(2)}) collective-permute-start(bf16[1296,128]{1,0:T(8,128)(2,1)} %get-tuple-element.37), channel_id=1, source_target_pairs={{0,4},{4,0},{8,12},{12,8},{1,5},{5,1},{9,13},{13,9},{2,6},{6,2},{1... | collective-permute-start | bytes 995336 | tf_op jit(solution)/shard_map/ppermute | solution.py:265
  5.1 12.2 %collective-permute-start.1 = (bf16[656,128]{1,0:T(8,128)(2,1)}, bf16[656,128]{1,0:T(8,128)(2,1)S(1)}, u32[]{:S(2)}, u32[]{:S(2)}) collective-permute-start(bf16[656,128]{1,0:T(8,128)(2,1)} %get-tuple-element.38), channel_id=1, source_target_pairs={{0,8},{4,12},{8,0},{12,4},{1,9},{5,13},{9,1},{13,5},{2,10},{6,14},... | collective-permute-start | bytes 503816 | tf_op jit(solution)/shard_map/ppermute | solution.py:265
  7.7 14.9 %collective-permute-start.2 = (bf16[656,128]{1,0:T(8,128)(2,1)}, bf16[656,128]{1,0:T(8,128)(2,1)S(1)}, u32[]{:S(2)}, u32[]{:S(2)}) collective-permute-start(bf16[656,128]{1,0:T(8,128)(2,1)} %get-tuple-element.39), channel_id=1, source_target_pairs={{0,12},{4,8},{8,4},{12,0},{1,13},{5,9},{9,5},{13,1},{2,14},{6,10},... | collective-permute-start | bytes 503816 | tf_op jit(solution)/shard_map/ppermute | solution.py:265
  9.0 1.7 %copy-start = (bf16[1280,1024]{1,0:T(8,128)(2,1)S(1)}, bf16[1280,1024]{1,0:T(8,128)(2,1)}, u32[]{:S(2)}) copy-start(bf16[1280,1024]{1,0:T(8,128)(2,1)} %wa.9) | copy-start | bytes 7864324
  10.8 1.7 %copy-start.2 = (bf16[1280,1024]{1,0:T(8,128)(2,1)S(1)}, bf16[1280,1024]{1,0:T(8,128)(2,1)}, u32[]{:S(2)}) copy-start(bf16[1280,1024]{1,0:T(8,128)(2,1)} %wf.9) | copy-start | bytes 7864324
  12.5 1.1 %copy-start.4 = (bf16[1,256,1280]{2,1,0:T(8,128)(2,1)S(1)}, bf16[1,256,1280]{2,1,0:T(8,128)(2,1)}, u32[]{:S(2)}) copy-start(bf16[1,256,1280]{2,1,0:T(8,128)(2,1)} %param.8) | copy-start | bytes 1966084
  13.6 0.7 copy-start.6
  14.3 10.8 %copy-start.1 = (bf16[1280,1024]{1,0:T(8,128)(2,1)S(1)}, bf16[1280,1024]{1,0:T(8,128)(2,1)}, u32[]{:S(2)}) copy-start(bf16[1280,1024]{1,0:T(8,128)(2,1)} %wa.9) | copy-start | bytes 7864324
  14.3 10.8 %copy-start.3 = (bf16[1280,1024]{1,0:T(8,128)(2,1)S(1)}, bf16[1280,1024]{1,0:T(8,128)(2,1)}, u32[]{:S(2)}) copy-start(bf16[1280,1024]{1,0:T(8,128)(2,1)} %wf.9) | copy-start | bytes 7864324
  22.6 4.2 %collective-permute-start.3 = (bf16[1296,128]{1,0:T(8,128)(2,1)S(1)}, bf16[1296,128]{1,0:T(8,128)(2,1)S(1)}, u32[]{:S(2)}, u32[]{:S(2)}) collective-permute-start(bf16[1296,128]{1,0:T(8,128)(2,1)S(1)} %collective-permute-done), channel_id=1, source_target_pairs={{0,1},{1,0},{2,3},{3,2},{4,5},{5,4},{6,7},{7,6},{8,9},{9,8},{10,11... | collective-permute-start | bytes 995336 | tf_op jit(solution)/shard_map/ppermute | solution.py:268
  22.6 4.2 %collective-permute-start.4 = (bf16[656,128]{1,0:T(8,128)(2,1)S(1)}, bf16[656,128]{1,0:T(8,128)(2,1)S(1)}, u32[]{:S(2)}, u32[]{:S(2)}) collective-permute-start(bf16[656,128]{1,0:T(8,128)(2,1)S(1)} %collective-permute-done.1), channel_id=1, source_target_pairs={{0,1},{1,0},{2,3},{3,2},{4,5},{5,4},{6,7},{7,6},{8,9},{9,8},{10,11... | collective-permute-start | bytes 503816 | tf_op jit(solution)/shard_map/ppermute | solution.py:268
  23.1 3.7 %collective-permute-start.5 = (bf16[656,128]{1,0:T(8,128)(2,1)S(1)}, bf16[656,128]{1,0:T(8,128)(2,1)S(1)}, u32[]{:S(2)}, u32[]{:S(2)}) collective-permute-start(bf16[656,128]{1,0:T(8,128)(2,1)S(1)} %collective-permute-done.2), channel_id=1, source_target_pairs={{0,1},{1,0},{2,3},{3,2},{4,5},{5,4},{6,7},{7,6},{8,9},{9,8},{10,11... | collective-permute-start | bytes 503816 | tf_op jit(solution)/shard_map/ppermute | solution.py:268
  23.1 7.1 %collective-permute-start.6 = (bf16[656,128]{1,0:T(8,128)(2,1)S(1)}, bf16[656,128]{1,0:T(8,128)(2,1)S(1)}, u32[]{:S(2)}, u32[]{:S(2)}) collective-permute-start(bf16[656,128]{1,0:T(8,128)(2,1)S(1)} %collective-permute-done.1), channel_id=1, source_target_pairs={{0,4},{4,0},{8,12},{12,8},{1,5},{5,1},{9,13},{13,9},{2,6},{6,2},{1... | collective-permute-start | bytes 503816 | tf_op jit(solution)/shard_map/ppermute | solution.py:265
  23.9 9.5 %collective-permute-start.7 = (bf16[656,128]{1,0:T(8,128)(2,1)S(1)}, bf16[656,128]{1,0:T(8,128)(2,1)S(1)}, u32[]{:S(2)}, u32[]{:S(2)}) collective-permute-start(bf16[656,128]{1,0:T(8,128)(2,1)S(1)} %collective-permute-done.2), channel_id=1, source_target_pairs={{0,4},{4,0},{8,12},{12,8},{1,5},{5,1},{9,13},{13,9},{2,6},{6,2},{1... | collective-permute-start | bytes 503816 | tf_op jit(solution)/shard_map/ppermute | solution.py:265
  33.4 1.4 %collective-permute-start.8 = (bf16[656,128]{1,0:T(8,128)(2,1)S(1)}, bf16[656,128]{1,0:T(8,128)(2,1)S(1)}, u32[]{:S(2)}, u32[]{:S(2)}) collective-permute-start(bf16[656,128]{1,0:T(8,128)(2,1)S(1)} %collective-permute-done.6), channel_id=1, source_target_pairs={{0,1},{1,0},{2,3},{3,2},{4,5},{5,4},{6,7},{7,6},{8,9},{9,8},{10,11... | collective-permute-start | bytes 503816 | tf_op jit(solution)/shard_map/ppermute | solution.py:268
  33.4 1.6 %collective-permute-start.9 = (bf16[656,128]{1,0:T(8,128)(2,1)S(1)}, bf16[656,128]{1,0:T(8,128)(2,1)S(1)}, u32[]{:S(2)}, u32[]{:S(2)}) collective-permute-start(bf16[656,128]{1,0:T(8,128)(2,1)S(1)} %collective-permute-done.7), channel_id=1, source_target_pairs={{0,1},{1,0},{2,3},{3,2},{4,5},{5,4},{6,7},{7,6},{8,9},{9,8},{10,11... | collective-permute-start | bytes 503816 | tf_op jit(solution)/shard_map/ppermute | solution.py:268
  35.0 0.9 %copy-start.5 = (s32[1,256]{1,0:T(1,128)S(1)}, s32[1,256]{1,0:T(1,128)}, u32[]{:S(2)}) copy-start(s32[1,256]{1,0:T(1,128)} %refs_5_.4) | copy-start | bytes 3076
  35.0 5.5 %copy-start.7 = (bf16[8192]{0:T(1024)(128)(2,1)S(1)}, bf16[8192]{0:T(1024)(128)(2,1)}, u32[]{:S(2)}) copy-start(bf16[8192]{0:T(1024)(128)(2,1)} %param.15) | copy-start | bytes 49156
  36.8 10.3 %collective-permute-start.11 = (bf16[128,1024]{1,0:T(8,128)(2,1)S(1)}, bf16[128,1024]{1,0:T(8,128)(2,1)S(1)}, u32[]{:S(2)}, u32[]{:S(2)}) collective-permute-start(bf16[128,1024]{1,0:T(8,128)(2,1)S(1)} %get-tuple-element.57), channel_id=1, source_target_pairs={{0,13},{1,12},{4,9},{5,8},{8,5},{9,4},{12,1},{13,0},{2,15},{3,14},... | collective-permute-start | bytes 786440 | tf_op jit(solution)/shard_map/ppermute | solution.py:312
  38.2 15.2 %collective-permute-start.10 = (bf16[128,1024]{1,0:T(8,128)(2,1)S(1)}, bf16[128,1024]{1,0:T(8,128)(2,1)S(1)}, u32[]{:S(2)}, u32[]{:S(2)}) collective-permute-start(bf16[128,1024]{1,0:T(8,128)(2,1)S(1)} %get-tuple-element.56), channel_id=1, source_target_pairs={{0,12},{1,13},{4,8},{5,9},{8,4},{9,5},{12,0},{13,1},{2,14},{3,15},... | collective-permute-start | bytes 786440 | tf_op jit(solution)/shard_map/ppermute | solution.py:312
  42.3 42.3 %collective-permute-start.13 = (bf16[128,1024]{1,0:T(8,128)(2,1)S(1)}, bf16[128,1024]{1,0:T(8,128)(2,1)S(1)}, u32[]{:S(2)}, u32[]{:S(2)}) collective-permute-start(bf16[128,1024]{1,0:T(8,128)(2,1)S(1)} %get-tuple-element.60), channel_id=1, source_target_pairs={{0,8},{1,9},{4,12},{5,13},{8,0},{9,1},{12,4},{13,5},{2,10},{3,11},... | collective-permute-start | bytes 786440 | tf_op jit(solution)/shard_map/ppermute | solution.py:312
  42.4 25.0 %collective-permute-start.12 = (bf16[256,1024]{1,0:T(8,128)(2,1)S(1)}, bf16[256,1024]{1,0:T(8,128)(2,1)S(1)}, u32[]{:S(2)}, u32[]{:S(2)}) collective-permute-start(bf16[256,1024]{1,0:T(8,128)(2,1)S(1)} %select.5), channel_id=1, source_target_pairs={{0,4},{4,0},{8,12},{12,8},{1,5},{5,1},{9,13},{13,9},{2,6},{6,2},{1... | collective-permute-start | bytes 1572872 | tf_op jit(solution)/shard_map/ppermute | solution.py:265
  44.4 40.2 %collective-permute-start.14 = (bf16[128,1024]{1,0:T(8,128)(2,1)S(1)}, bf16[128,1024]{1,0:T(8,128)(2,1)S(1)}, u32[]{:S(2)}, u32[]{:S(2)}) collective-permute-start(bf16[128,1024]{1,0:T(8,128)(2,1)S(1)} %get-tuple-element.67), channel_id=1, source_target_pairs={{0,9},{1,8},{4,13},{5,12},{8,1},{9,0},{12,5},{13,4},{2,11},{3,10},... | collective-permute-start | bytes 786440 | tf_op jit(solution)/shard_map/ppermute | solution.py:312

commit v10 on v9

--- a/solution.py
+++ b/solution.py
@@ -35,11 +35,14 @@
 
 
 def send_kernel(cuts, rows, slot, kind, *refs):
-    outs, (rows_here, slot_here, kind_here, sems) = refs[:-4], refs[-4:]
+    outs, (rows_here, slot_here, kind_here, sems) = refs[: len(cuts)], refs[-4:]
     whole, width = rows.shape
     half = whole // 2
     z, t = lax.axis_index("ctx"), lax.axis_index("tp")
-    source = rows.at[pl.ds(pl.multiple_of(t * half, half), half), :]
+    dealt = len(cuts) > 1
+    source = rows
+    if not dealt:
+        source = rows.at[pl.ds(pl.multiple_of(t * half, half), half), :]
     copies = [
         pltpu.make_async_copy(slot, slot_here, sems.at[0]),
         pltpu.make_async_copy(kind, kind_here, sems.at[1]),
@@ -47,17 +50,40 @@
     ]
     for copy in copies:
         copy.start()
-    for copy in copies:
-        copy.wait()
-    slots = jnp.where(t == 0, slot_here[:, :half], slot_here[:, half:])
-    kinds = jnp.where(t == 0, kind_here[:, :half], kind_here[:, half:])
+    copies[0].wait()
+    copies[1].wait()
+    if dealt:
+        slot_row, slot_col = slot_here[...], column_of(slot_here[...])
+        kind_col = column_of(kind_here[...])
+        rank_row = jnp.sum((slot_col < slot_row).astype(I32), axis=0, keepdims=True)
+        rank_col = jnp.sum((slot_row < slot_col).astype(I32), axis=1, keepdims=True)
+        refs[len(cuts)][...] = lax.rem(rank_row, 2)
+
+        def rank_at(k):
+            odd = (k >= half // 2).astype(I32)
+            return t * half + 2 * (k - odd * (half // 2)) + odd
+
+        here = rank_col == rank_at(lax.broadcasted_iota(I32, (1, half), 1))
+        slots = jnp.sum(jnp.where(here, slot_col, 0), axis=0, keepdims=True)
+        kinds = jnp.sum(jnp.where(here, kind_col, 0), axis=0, keepdims=True)
+        deal = rank_row == rank_at(lax.broadcasted_iota(I32, (half, 1), 0))
+        copies[2].wait()
+        rows_out = refs[-5]
+        rows_out[...] = jnp.dot(
+            deal.astype(F32).astype(BF16), rows_here[...], preferred_element_type=F32
+        ).astype(BF16)
+    else:
+        slots = jnp.where(t == 0, slot_here[:, :half], slot_here[:, half:])
+        kinds = jnp.where(t == 0, kind_here[:, :half], kind_here[:, half:])
+        copies[2].wait()
+        rows_out = rows_here
     for out, parity in zip(outs, cuts):
-        x, s, k = rows_here, slots, kinds
+        x, s, k = rows_out, slots, kinds
         size = half
         if parity is not None:
             size = half // 2
             second = lax.rem(z + parity, 2)
-            x = rows_here.at[pl.ds(pl.multiple_of(second * size, size), size), :]
+            x = rows_out.at[pl.ds(pl.multiple_of(second * size, size), size), :]
             s = jnp.where(second == 0, slots[:, :size], slots[:, size:])
             k = jnp.where(second == 0, kinds[:, :size], kinds[:, size:])
         to_tiles(x, out)
@@ -73,13 +99,19 @@
     half, width = rows.shape[0] // 2, rows.shape[1]
     sizes = [half if parity is None else half // 2 for parity in cuts]
     shapes = [(size * width // 128 + 16, 128) for size in sizes]
+    dealt = len(cuts) > 1
+    out_shape = [jax.ShapeDtypeStruct(shape, BF16) for shape in shapes]
+    scratch = [pltpu.VMEM((half, width), BF16)]
+    if dealt:
+        out_shape.append(jax.ShapeDtypeStruct(slot.shape, I32))
+        scratch.append(pltpu.VMEM(rows.shape, BF16))
     return pl.pallas_call(
         functools.partial(send_kernel, cuts),
-        out_shape=[jax.ShapeDtypeStruct(shape, BF16) for shape in shapes],
+        out_shape=out_shape,
         in_specs=[HBM] * 3,
-        out_specs=[VMEM] * len(cuts),
-        scratch_shapes=[
-            pltpu.VMEM((half, width), BF16),
+        out_specs=[VMEM] * len(out_shape),
+        scratch_shapes=scratch
+        + [
             pltpu.VMEM(slot.shape, I32),
             pltpu.VMEM(slot.shape, I32),
             pltpu.SemaphoreType.DMA((3,)),
@@ -181,6 +213,147 @@
         cost_estimate=cost(2 * sum(sizes) * rows * cols, 2 * rows * cols),
         name="select",
     )(*blocks, *slots)
+
+
+def upto(places, width):
+    i = lax.broadcasted_iota(I32, (width, width), 0)
+    j = lax.broadcasted_iota(I32, (width, width), 1)
+    counts = i <= j
+    if width > places:
+        counts = jnp.logical_and(counts, (i < places) == (j < places))
+    return counts.astype(F32).astype(BF16)
+
+
+def one_hot(found):
+    return found.astype(F32).astype(BF16)
+
+
+def over_rows(a, b):
+    return lax.dot_general(a, b, (((1,), (1,)), ((), ())), preferred_element_type=F32)
+
+
+def running(flags, counts):
+    return jnp.dot(one_hot(flags), counts, preferred_element_type=F32)
+
+
+def packet_kernel(m, early, count, second, *refs):
+    blocks, slots, outs = refs[:count], refs[count : 2 * count], refs[2 * count :]
+    size = outs[0].shape[0]
+    places = blocks[0].shape[0] // 2
+    first_size = places - size if second else size
+    z, t = lax.axis_index("ctx"), lax.axis_index("tp")
+    i = lax.broadcasted_iota(I32, (2 * places, 1), 0)
+    position = jnp.bitwise_xor(z, m) * 2 * places + jnp.bitwise_xor(i, t * places)
+    holds = [one_hot(slot[...] == position) for slot in slots]
+    known = None
+    for k in range(early):
+        part = over_rows(jnp.ones((8, holds[k].shape[1]), BF16), holds[k])
+        known = part if known is None else known + part
+    counts = upto(places, 2 * places)
+    wanted = known > 0.5
+    number = running(wanted, counts)
+    if second:
+        wanted = jnp.logical_not(jnp.logical_and(wanted, number < first_size + 0.5))
+        number = running(wanted, counts)
+    number = jnp.where(wanted, number, 0.0)[0:1].astype(I32)
+    e = lax.broadcasted_iota(I32, (2 * size, 1), 0)
+    upper = (e >= size).astype(I32)
+    lane_upper = (lax.broadcasted_iota(I32, (1, 2 * places), 1) >= places).astype(I32)
+    pick = jnp.logical_and(number == e - upper * size + 1, lane_upper == upper)
+    pick = one_hot(pick)
+    total = None
+    for block, hold in zip(blocks, holds):
+        chosen = jnp.dot(pick, hold, preferred_element_type=F32).astype(BF16)
+        part = jnp.dot(chosen, block[...], preferred_element_type=F32)
+        total = part if total is None else total + part
+    outs[0][...] = total[:size].astype(BF16)
+    outs[1][...] = total[size:].astype(BF16)
+
+
+def packet(m, early, blocks, slots, size, second):
+    rows, cols = sum(b.shape[0] for b in blocks), blocks[0].shape[1]
+    return pl.pallas_call(
+        functools.partial(packet_kernel, m, early, len(blocks), second),
+        out_shape=[jax.ShapeDtypeStruct((size, cols), BF16)] * 2,
+        in_specs=[VMEM] * (2 * len(blocks)),
+        out_specs=[VMEM] * 2,
+        compiler_params=PARAMS,
+        cost_estimate=cost(4 * size * rows * cols, 2 * rows * cols),
+        name="packet",
+    )(*blocks, *slots)
+
+
+def order_kernel(first_size, parity, *refs):
+    slots, outs = refs[:-2], refs[-2:]
+    places = outs[0].shape[0]
+    z, t = lax.axis_index("ctx"), lax.axis_index("tp")
+    pair, odd = z // 2, lax.rem(z, 2)
+    position = (2 * z + t) * places + lax.broadcasted_iota(I32, (places, 1), 0)
+    source = lax.broadcasted_iota(I32, (8, 1), 0)
+    known = None
+    for k, slot in enumerate(slots):
+        width = slot.shape[1]
+        lane = lax.broadcasted_iota(I32, (1, width), 1)
+        if k == 0:
+            near, odd_rank = lane >= 0, parity[...]
+        elif k in (1, 2):
+            near = lane < places
+            odd_rank = jnp.where(near, (lane >= places // 2).astype(I32), odd)
+        else:
+            near, odd_rank = lane < 0, jnp.zeros((1, width), I32) + 1 - odd
+        owner_pair = jnp.where(near, pair, 1 - pair)
+        held = jnp.logical_or(owner_pair == source // 2, odd_rank == lax.rem(source, 2))
+        part = over_rows(one_hot(held), one_hot(slot[...] == position))
+        known = part if known is None else known + part
+    counts = upto(places, places)
+    early = known > 0.5
+    number = running(early, counts)
+    early = jnp.logical_and(early, number < first_size + 0.5)
+    later = running(jnp.logical_not(early), counts)
+    place = jnp.where(early, number, later + first_size) - 1.0
+    for m, out in zip((3, 2), outs):
+        row = jnp.sum(jnp.where(source == jnp.bitwise_xor(z, m), place, 0.0), axis=0, keepdims=True)
+        column = column_of(row.astype(I32))
+        out[...] = one_hot(column == lax.broadcasted_iota(I32, (1, places), 1))
+
+
+def order_of(first_size, parity, slots, places):
+    return pl.pallas_call(
+        functools.partial(order_kernel, first_size),
+        out_shape=[jax.ShapeDtypeStruct((places, places), BF16)] * 2,
+        in_specs=[VMEM] * (1 + len(slots)),
+        out_specs=[VMEM] * 2,
+        compiler_params=PARAMS,
+        cost_estimate=cost(0, 0),
+        name="order_of",
+    )(parity, *slots)
+
+
+def place_kernel(has_total, *refs):
+    total = refs[0][...] if has_total else None
+    order, packets, outs = refs[has_total], refs[has_total + 1 : has_total + 5], refs[-3:]
+    for d in range(2):
+        both = jnp.concatenate([packets[2 * d][...], packets[2 * d + 1][...]], axis=0)
+        wide = jnp.dot(order[...], both, preferred_element_type=F32)
+        outs[d][...] = wide.astype(BF16)
+        part = jnp.sum(wide * wide, axis=1, keepdims=True)
+        total = part if total is None else total + part
+    outs[2][...] = total
+
+
+def place(total, order, packets):
+    places, cols = order.shape[0], packets[0].shape[1]
+    operands = ([] if total is None else [total]) + [order] + packets
+    return pl.pallas_call(
+        functools.partial(place_kernel, len(operands) - 5),
+        out_shape=[jax.ShapeDtypeStruct((places, cols), BF16)] * 2
+        + [jax.ShapeDtypeStruct((places, 1), F32)],
+        in_specs=[VMEM] * len(operands),
+        out_specs=[VMEM] * 3,
+        compiler_params=PARAMS,
+        cost_estimate=cost(1 << 36, 1 << 26),
+        name="place",
+    )(*operands)
 
 
 def view(ref, places):
@@ -275,8 +448,22 @@
         blocks.append(block)
         slots.append(slot)
 
+    def to_core(x, m, d):
+        pairs = [(i * 2 + c, (i ^ m) * 2 + (c ^ d)) for i in range(n) for c in range(2)]
+        return lax.ppermute(x, ("ctx", "tp"), pairs)
+
+    def own_and_near(total):
+        slots[0] = after(slots[0], total)
+        pieces[0, 0], other = select(0, blocks, slots, [half, half])
+        pieces[0, 1] = lax.all_gather(other, "tp", axis=0)
+        total = squares(total, [pieces[0, 0], pieces[0, 1]], half)
+        pair = after(pieces[1], total)
+        pieces[1, 0], pieces[1, 1] = pair, lax.all_gather(pair[half:], "tp", axis=0)
+        return squares(total, [pieces[1, 0], pieces[1, 1]], half)
+
+    pieces = {}
     if n == 4:
-        near, second, third = to_send((None, 0, 1), rows, row_slot, row_kind)
+        near, second, third, parity = to_send((None, 0, 1), rows, row_slot, row_kind)
         near, second, third = over_ctx(near, 1), over_ctx(second, 2), over_ctx(third, 3)
         first = lax.optimization_barrier((near, second, third, own))[:3]
         shared = [over_ctx(part, 1) for part in first[1:]]
@@ -284,10 +471,43 @@
         take([part[None] for part in first])
         other = lax.optimization_barrier((*other, blocks[-1]))[:3]
         take(other)
-        shared = lax.optimization_barrier((*shared, blocks[-1]))[:2]
+
+        early, size = len(blocks), 3 * half // 8
+        sent = {}
+        for m in (3, 2):
+            chosen = packet(m, early, blocks, slots, size, False)
+            slots[0] = after(slots[0], chosen[0])
+            sent[m] = [to_core(piece, m, d) for d, piece in enumerate(chosen)]
+        joined = lax.optimization_barrier((*shared, *sent[3], blocks[-1]))
+        shared, sent[3] = joined[:2], list(joined[2:4])
         swapped = [over_tp(part)[None] for part in shared]
         take([part[None] for part in shared])
         take(swapped)
+
+        rest = {}
+        for m in (3, 1, 2):
+            if m == 1:
+                (chosen,) = select(1, blocks, slots, [2 * half])
+                slots[0] = after(slots[0], chosen)
+                pieces[1] = over_ctx(chosen, 1)
+                continue
+            chosen = packet(m, early, blocks, slots, half - size, True)
+            slots[0] = after(slots[0], chosen[0])
+            if m == 3:
+                joined = lax.optimization_barrier((*chosen, *sent[2]))
+                chosen, sent[2] = joined[:2], list(joined[2:])
+            rest[m] = [to_core(piece, m, d) for d, piece in enumerate(chosen)]
+
+        joined = lax.optimization_barrier((*rest[3], *slots))
+        rest[3] = joined[:2]
+        order3, order2 = order_of(size, parity, joined[2:], half)
+        packets = [sent[3][0], rest[3][0], sent[3][1], rest[3][1]]
+        pieces[3, 0], pieces[3, 1], total = place(None, order3, packets)
+        total = own_and_near(total)
+        rest[2] = lax.optimization_barrier((*rest[2], total))[:2]
+        packets = [sent[2][0], rest[2][0], sent[2][1], rest[2][1]]
+        pieces[2, 0], pieces[2, 1], total = place(total, order2, packets)
+        order, fresh = [3, 1, 0, 2], ()
     else:
         (mine,) = to_send((None,), rows, row_slot, row_kind)
         arrived = [over_ctx(mine, m) for m in range(1, n)]
@@ -299,38 +519,27 @@
         take([direct[None]])
         take([swapped[None]])
 
-    pieces = {}
-    order = [n - 1, 1] + list(reversed(range(2, n - 1)))
-    for m in order:
-        chosen = select(m, blocks, slots, [2 * half] if m == 1 else [half, half])
-        slots[0] = after(slots[0], chosen[0])
-        if m == 1:
-            pieces[m] = over_ctx(chosen[0], m)
-            continue
-        for d, piece in enumerate(chosen):
-            perm = [(i * 2 + c, (i ^ m) * 2 + (c ^ d)) for i in range(n) for c in range(2)]
-            pieces[m, d] = lax.ppermute(piece, ("ctx", "tp"), perm)
-
-    total = None
-    for m in order[:-1]:
-        if m == 1:
-            slots[0] = after(slots[0], total)
-            pieces[0, 0], other = select(0, blocks, slots, [half, half])
-            pieces[0, 1] = lax.all_gather(other, "tp", axis=0)
-            total = squares(total, [pieces[0, 0], pieces[0, 1]], half)
-            pair = after(pieces[m], total)
-            pieces[m, 0], pieces[m, 1] = pair, lax.all_gather(pair[half:], "tp", axis=0)
-        fresh = [pieces[m, 0], pieces[m, 1]]
-        if m != 1 and total is not None:
-            fresh = [after(piece, total) for piece in fresh]
-        total = squares(total, fresh, half)
-    order.append(0)
+        order = [n - 1, 1] + list(reversed(range(2, n - 1)))
+        for m in order:
+            chosen = select(m, blocks, slots, [2 * half] if m == 1 else [half, half])
+            slots[0] = after(slots[0], chosen[0])
+            if m == 1:
+                pieces[m] = over_ctx(chosen[0], m)
+                continue
+            for d, piece in enumerate(chosen):
+                pieces[m, d] = to_core(piece, m, d)
+        total = squares(None, [pieces[n - 1, 0], pieces[n - 1, 1]], half)
+        total = own_and_near(total)
+        for m in order[2:-1]:
+            late = [after(pieces[m, d], total) for d in range(2)]
+            total = squares(total, late, half)
+        fresh = (2 * (n - 1), 2 * (n - 1) + 1)
+        for d in range(2):
+            pieces[order[-1], d] = after(pieces[order[-1], d], total)
+        order = order[:-1] + [0, order[-1]]
+
     places_of = tuple((m, d) for m in order for d in range(2))
-    fresh = tuple(k for k, (m, _) in enumerate(places_of) if m == order[-2])
-    final = [pieces[at] for at in places_of]
-    for k in fresh:
-        final[k] = after(final[k], total)
-    return norm(places_of, fresh, norm_gain[None, :], total, final)[None]
+    return norm(places_of, fresh, norm_gain[None, :], total, [pieces[at] for at in places_of])[None]
 
 
 def solution(mesh):

time: 87 us -> 88.1 us (1.013)
  waiting for transfers between devices: 46.2 us -> 33.9 us
  starting transfers between devices: 14.8 us -> 22.3 us
  Pallas kernels: 14.5 us -> 19 us
  blocking collectives: 4.36 us -> 5.59 us
    ppermute x4 -> x8, waiting for transfers between devices: 23.7 us -> 13 us  [to_core(): return lax.ppermute(x, ('ctx', 'tp'), pairs)]
    pallas_call x1 -> x8, Pallas kernels: 1.97 us -> 8.77 us  [the longest x4 5.12 us: packet(): pl.pallas_call(functools.partial(packet_kernel, m, early, len(blocks), se...]
    ppermute x4 -> x8, starting transfers between devices: 4 us -> 10.8 us  [to_core(): return lax.ppermute(x, ('ctx', 'tp'), pairs)]
    pallas_call x4 -> x2, Pallas kernels: 3.4 us -> 1.69 us  [select(): pl.pallas_call(functools.partial(select_kernel, m, len(blocks)), out_shap...]
    ppermute x6, waiting for transfers between devices: 22.4 us -> 20.9 us  [over_ctx(): return lax.ppermute(x, 'ctx', [(i, i ^ m) for i in range(n)])]
    all_gather x2, blocking collectives: 4.36 us -> 5.59 us  [the longest x1 3.41 us: own_and_near(): pieces[0, 1] = lax.all_gather(other, 'tp', axis=0)]
    unnamed x16 -> x18, local copies, waits for them, and re-layouts: 5.26 us -> 5.27 us
  transfers between devices with their start and end apart: 15 -> 19, of which waited for: 9 -> 8; matrix products, arithmetic and copies ran while one was open for 2% -> 2% of each run, Pallas kernels for 10% -> 17%
where the time goes in v10:
time: 88.1 us; the launch traced here: 87.7 us
  waiting for transfers between devices  33.9 us (38%)
  starting transfers between devices  22.3 us (25%)
  Pallas kernels  19 us (22%)
  local copies, waits for them, and re-layouts  6.68 us (8%)
  blocking collectives  5.59 us (6%)
    ppermute x6, waiting for transfers between devices, over_ctx(): return lax.ppermute(x, 'ctx', [(i, i ^ m) for i in range(n)])  20.9 us
    ppermute x8, waiting for transfers between devices, to_core(): return lax.ppermute(x, ('ctx', 'tp'), pairs)  13 us
    ppermute x8, starting transfers between devices, to_core(): return lax.ppermute(x, ('ctx', 'tp'), pairs)  10.8 us
    ppermute x6, starting transfers between devices, over_ctx(): return lax.ppermute(x, 'ctx', [(i, i ^ m) for i in range(n)])  10.5 us
    unnamed x18, local copies, waits for them, and re-layouts  5.27 us
    pallas_call x4, Pallas kernels, packet(): pl.pallas_call(functools.partial(packet_kernel, m, early, len(blocks), se...  5.12 us
    pallas_call x4, Pallas kernels, project_parts(): pl.pallas_call(project_parts_kernel, out_shape=[jax.ShapeDtypeStruct((row...  4.99 us
    all_gather x1, blocking collectives, own_and_near(): pieces[0, 1] = lax.all_gather(other, 'tp', axis=0)  3.41 us
  transfers between devices with their start and end apart: 19, of which 8 were waited for; matrix products, arithmetic and copies ran while one was open for 2% of the time, Pallas kernels for 17%

profile of v10, /device:TPU:0, one launch (start us, length us, event | category | flops | bytes accessed | tf_op | source)
XLA Modules:
  0.0 87.7 jit_solution(11715218674240888739)
XLA Ops:
  0.0 2.3 %to_send.1 = (bf16[1296,128]{1,0:T(8,128)(2,1)}, bf16[656,128]{1,0:T(8,128)(2,1)}, bf16[656,128]{1,0:T(8,128)(2,1)}, s32[1,256]{1,0:T(1,128)}) custom-call(bf16[256,1280]{1,0:T(8,128)(2,1)} %bitcast.14, s32[1,256]{1,0:T(1,128)} %refs_5_.3, s32[1,256]{1,0:T(1,128)} %kind.3), custom_call_target="tpu_custom_call" | custom-call | bytes 40960 | tf_op jit(solution)/shard_map/to_send/pallas_call | solution.py:108
  2.3 3.1 %collective-permute-start = (bf16[1296,128]{1,0:T(8,128)(2,1)}, bf16[1296,128]{1,0:T(8,128)(2,1)S(1)}, u32[]{:S(2)}, u32[]{:S(2)}) collective-permute-start(bf16[1296,128]{1,0:T(8,128)(2,1)} %get-tuple-element.66), channel_id=1, source_target_pairs={{0,4},{4,0},{8,12},{12,8},{1,5},{5,1},{9,13},{13,9},{2,6},{6,2},{1... | collective-permute-start | bytes 995336 | tf_op jit(solution)/shard_map/ppermute | solution.py:438
  5.4 2.6 %collective-permute-start.1 = (bf16[656,128]{1,0:T(8,128)(2,1)}, bf16[656,128]{1,0:T(8,128)(2,1)S(1)}, u32[]{:S(2)}, u32[]{:S(2)}) collective-permute-start(bf16[656,128]{1,0:T(8,128)(2,1)} %get-tuple-element.67), channel_id=1, source_target_pairs={{0,8},{4,12},{8,0},{12,4},{1,9},{5,13},{9,1},{13,5},{2,10},{6,14},... | collective-permute-start | bytes 503816 | tf_op jit(solution)/shard_map/ppermute | solution.py:438
  8.0 0.7 broadcast_in_dim.43.ba
  8.7 0.7 broadcast_in_dim.44.bf
  9.4 1.7 %copy-done = bf16[1280,1024]{1,0:T(8,128)(2,1)S(1)} copy-done((bf16[1280,1024]{1,0:T(8,128)(2,1)S(1)}, bf16[1280,1024]{1,0:T(8,128)(2,1)}, u32[]{:S(2)}) %copy-start) | copy-done | bytes 2621464
  11.1 1.7 %copy-done.2 = bf16[1280,1024]{1,0:T(8,128)(2,1)S(1)} copy-done((bf16[1280,1024]{1,0:T(8,128)(2,1)S(1)}, bf16[1280,1024]{1,0:T(8,128)(2,1)}, u32[]{:S(2)}) %copy-start.2) | copy-done | bytes 2621464
  12.9 1.1 %copy-done.4 = bf16[1,256,1280]{2,1,0:T(8,128)(2,1)S(1)} copy-done((bf16[1,256,1280]{2,1,0:T(8,128)(2,1)S(1)}, bf16[1,256,1280]{2,1,0:T(8,128)(2,1)}, u32[]{:S(2)}) %copy-start.4) | copy-done | bytes 655384
  13.9 0.7 copy-done.6
  14.6 1.6 %project_own.1.refs_0_ = bf16[256,1024]{1,0:T(8,128)(2,1)S(1)} custom-call(s32[1,256]{1,0:T(1,128)S(1)} %copy-done.6, bf16[256,1280]{1,0:T(8,128)(2,1)S(1)} %bitcast.15, bf16[1280,1024]{1,0:T(8,128)(2,1)S(1)} %copy-done, bf16[1280,1024]{1,0:T(8,128)(2,1)S(1)} %copy-done.2, bf16[1,1024]{1,0:T(2,128)(2,1)S(1)} %broadcast_in_dim.43.ba, ...), custom_call_target="tpu_custom_call" | custom-call | flops 83886080 | bytes 327680 | tf_op jit(solution)/shard_map/project_own/pallas_call | solution.py:146
  16.2 1.3 %collective-permute-done.1 = bf16[656,128]{1,0:T(8,128)(2,1)S(1)} collective-permute-done((bf16[656,128]{1,0:T(8,128)(2,1)}, bf16[656,128]{1,0:T(8,128)(2,1)S(1)}, u32[]{:S(2)}, u32[]{:S(2)}) %collective-permute-start.1) | collective-permute-done | bytes 167968 | tf_op jit(solution)/shard_map/ppermute | solution.py:438
  17.6 5.3 %collective-permute-done.2 = bf16[656,128]{1,0:T(8,128)(2,1)S(1)} collective-permute-done((bf16[656,128]{1,0:T(8,128)(2,1)}, bf16[656,128]{1,0:T(8,128)(2,1)S(1)}, u32[]{:S(2)}, u32[]{:S(2)}) %collective-permute-start.2) | collective-permute-done | bytes 167968 | tf_op jit(solution)/shard_map/ppermute | solution.py:438
  22.9 0.5 collective-permute-start.4
  23.4 0.8 collective-permute-start.6
  24.2 1.3 %collective-permute-start.7 = (bf16[656,128]{1,0:T(8,128)(2,1)S(1)}, bf16[656,128]{1,0:T(8,128)(2,1)S(1)}, u32[]{:S(2)}, u32[]{:S(2)}) collective-permute-start(bf16[656,128]{1,0:T(8,128)(2,1)S(1)} %collective-permute-done.2), channel_id=1, source_target_pairs={{0,4},{4,0},{8,12},{12,8},{1,5},{5,1},{9,13},{13,9},{2,6},{6,2},{1... | collective-permute-start | bytes 503816 | tf_op jit(solution)/shard_map/ppermute | solution.py:438
  25.5 1.6 %project_parts.4 = (bf16[256,1024]{1,0:T(8,128)(2,1)S(1)}, s32[1,256]{1,0:T(1,128)S(1)}) custom-call(bf16[1280,1024]{1,0:T(8,128)(2,1)S(1)} %copy-done.1, bf16[1280,1024]{1,0:T(8,128)(2,1)S(1)} %copy-done.3, bf16[1,1024]{1,0:T(2,128)(2,1)S(1)} %broadcast_in_dim.43.ba, bf16[1,1024]{1,0:T(2,128)(2,1)S(1)} %broadcast_in_dim.44.bf, ...), custom_call_target="tpu_custom_call" | custom-call | flops 83886080 | bytes 327680 | tf_op jit(solution)/shard_map/project_parts/pallas_call | solution.py:176
  27.1 1.6 %project_parts.5 = (bf16[256,1024]{1,0:T(8,128)(2,1)S(1)}, s32[1,256]{1,0:T(1,128)S(1)}) custom-call(bf16[1280,1024]{1,0:T(8,128)(2,1)S(1)} %copy-done.1, bf16[1280,1024]{1,0:T(8,128)(2,1)S(1)} %copy-done.3, bf16[1,1024]{1,0:T(2,128)(2,1)S(1)} %broadcast_in_dim.43.ba, bf16[1,1024]{1,0:T(2,128)(2,1)S(1)} %broadcast_in_dim.44.bf, ...), custom_call_target="tpu_custom_call" | custom-call | flops 83886080 | bytes 327680 | tf_op jit(solution)/shard_map/project_parts/pallas_call | solution.py:176
  28.7 1.0 %packet.4 = (bf16[48,1024]{1,0:T(8,128)(2,1)S(1)}, bf16[48,1024]{1,0:T(8,128)(2,1)S(1)}) custom-call(bf16[256,1024]{1,0:T(8,128)(2,1)S(1)} %project_own.1.refs_0_, bf16[256,1024]{1,0:T(8,128)(2,1)S(1)} %get-tuple-element.72.refs_1_, bf16[256,1024]{1,0:T(8,128)(2,1)S(1)} %get-tuple-element.76.refs_2_, s32[1,256]{1,0:T(1,128)S(1)} %copy-done.5, ...), custom_call_target="tpu_custom_call" | custom-call | flops 9437184 | bytes 98304 | tf_op jit(solution)/shard_map/packet/pallas_call | solution.py:275
  29.8 1.1 %collective-permute-start.9 = (bf16[48,1024]{1,0:T(8,128)(2,1)S(1)}, bf16[48,1024]{1,0:T(8,128)(2,1)S(1)}, u32[]{:S(2)}, u32[]{:S(2)}) collective-permute-start(bf16[48,1024]{1,0:T(8,128)(2,1)S(1)} %get-tuple-element.80), channel_id=1, source_target_pairs={{0,13},{1,12},{4,9},{5,8},{8,5},{9,4},{12,1},{13,0},{2,15},{3,14},... | collective-permute-start | bytes 294920 | tf_op jit(solution)/shard_map/ppermute | solution.py:453
  30.9 2.3 %collective-permute-start.8 = (bf16[48,1024]{1,0:T(8,128)(2,1)S(1)}, bf16[48,1024]{1,0:T(8,128)(2,1)S(1)}, u32[]{:S(2)}, u32[]{:S(2)}) collective-permute-start(bf16[48,1024]{1,0:T(8,128)(2,1)S(1)} %get-tuple-element.79), channel_id=1, source_target_pairs={{0,12},{1,13},{4,8},{5,9},{8,4},{9,5},{12,0},{13,1},{2,14},{3,15},... | collective-permute-start | bytes 294920 | tf_op jit(solution)/shard_map/ppermute | solution.py:453
  33.2 0.5 collective-permute-done.7
  33.7 3.2 %collective-permute-done.9.refs_3_ = bf16[48,1024]{1,0:T(8,128)(2,1)S(1)} collective-permute-done((bf16[48,1024]{1,0:T(8,128)(2,1)S(1)}, bf16[48,1024]{1,0:T(8,128)(2,1)S(1)}, u32[]{:S(2)}, u32[]{:S(2)}) %collective-permute-start.9) | collective-permute-done | bytes 98336 | tf_op jit(solution)/shard_map/ppermute | solution.py:453
  36.9 2.4 %collective-permute-done.8.refs_1_ = bf16[48,1024]{1,0:T(8,128)(2,1)S(1)} collective-permute-done((bf16[48,1024]{1,0:T(8,128)(2,1)S(1)}, bf16[48,1024]{1,0:T(8,128)(2,1)S(1)}, u32[]{:S(2)}, u32[]{:S(2)}) %collective-permute-start.8) | collective-permute-done | bytes 98336 | tf_op jit(solution)/shard_map/ppermute | solution.py:453
  39.3 0.5 collective-permute-start.11
  39.8 1.0 %packet.5 = (bf16[48,1024]{1,0:T(8,128)(2,1)S(1)}, bf16[48,1024]{1,0:T(8,128)(2,1)S(1)}) custom-call(bf16[256,1024]{1,0:T(8,128)(2,1)S(1)} %project_own.1.refs_0_, bf16[256,1024]{1,0:T(8,128)(2,1)S(1)} %get-tuple-element.72.refs_1_, bf16[256,1024]{1,0:T(8,128)(2,1)S(1)} %get-tuple-element.76.refs_2_, s32[1,256]{1,0:T(1,128)S(1)} %copy-done.5, ...), custom_call_target="tpu_custom_call" | custom-call | flops 9437184 | bytes 98304 | tf_op jit(solution)/shard_map/packet/pallas_call | solution.py:275
  40.8 3.4 %collective-permute-start.13 = (bf16[48,1024]{1,0:T(8,128)(2,1)S(1)}, bf16[48,1024]{1,0:T(8,128)(2,1)S(1)}, u32[]{:S(2)}, u32[]{:S(2)}) collective-permute-start(bf16[48,1024]{1,0:T(8,128)(2,1)S(1)} %get-tuple-element.92), channel_id=1, source_target_pairs={{0,9},{1,8},{4,13},{5,12},{8,1},{9,0},{12,5},{13,4},{2,11},{3,10},... | collective-permute-start | bytes 294920 | tf_op jit(solution)/shard_map/ppermute | solution.py:453
  44.3 0.5 collective-permute-start.12
  44.7 0.9 %project_parts.6 = (bf16[128,1024]{1,0:T(8,128)(2,1)S(1)}, s32[1,128]{1,0:T(1,128)S(1)}) custom-call(bf16[1280,1024]{1,0:T(8,128)(2,1)S(1)} %copy-done.1, bf16[1280,1024]{1,0:T(8,128)(2,1)S(1)} %copy-done.3, bf16[1,1024]{1,0:T(2,128)(2,1)S(1)} %broadcast_in_dim.43.ba, bf16[1,1024]{1,0:T(2,128)(2,1)S(1)} %broadcast_in_dim.44.bf, ...), custom_call_target="tpu_custom_call" | custom-call | flops 41943040 | bytes 327680 | tf_op jit(solution)/shard_map/project_parts/pallas_call | solution.py:176
  45.7 0.9 %project_parts.7 = (bf16[128,1024]{1,0:T(8,128)(2,1)S(1)}, s32[1,128]{1,0:T(1,128)S(1)}) custom-call(bf16[1280,1024]{1,0:T(8,128)(2,1)S(1)} %copy-done.1, bf16[1280,1024]{1,0:T(8,128)(2,1)S(1)} %copy-done.3, bf16[1,1024]{1,0:T(2,128)(2,1)S(1)} %broadcast_in_dim.43.ba, bf16[1,1024]{1,0:T(2,128)(2,1)S(1)} %broadcast_in_dim.44.bf, ...), custom_call_target="tpu_custom_call" | custom-call | flops 41943040 | bytes 327680 | tf_op jit(solution)/shard_map/project_parts/pallas_call | solution.py:176
  46.6 1.5 %packet.6 = (bf16[80,1024]{1,0:T(8,128)(2,1)S(1)}, bf16[80,1024]{1,0:T(8,128)(2,1)S(1)}) custom-call(bf16[256,1024]{1,0:T(8,128)(2,1)S(1)} %project_own.1.refs_0_, bf16[256,1024]{1,0:T(8,128)(2,1)S(1)} %get-tuple-element.72.refs_1_, bf16[256,1024]{1,0:T(8,128)(2,1)S(1)} %get-tuple-element.76.refs_2_, bf16[128,1024]{1,0:T(8,128)(2,1)S(1)} %get-tuple-element.83.refs_3_, ...), custom_call_target="tpu_custom_call" | custom-call | flops 20971520 | bytes 131072 | tf_op jit(solution)/shard_map/packet/pallas_call | solution.py:275
  48.1 5.8 %collective-permute-done.12.refs_2_ = bf16[48,1024]{1,0:T(8,128)(2,1)S(1)} collective-permute-done((bf16[48,1024]{1,0:T(8,128)(2,1)S(1)}, bf16[48,1024]{1,0:T(8,128)(2,1)S(1)}, u32[]{:S(2)}, u32[]{:S(2)}) %collective-permute-start.12) | collective-permute-done | bytes 98336 | tf_op jit(solution)/shard_map/ppermute | solution.py:453
  53.9 1.8 %collective-permute-start.14 = (bf16[80,1024]{1,0:T(8,128)(2,1)S(1)}, bf16[80,1024]{1,0:T(8,128)(2,1)S(1)}, u32[]{:S(2)}, u32[]{:S(2)}) collective-permute-start(bf16[80,1024]{1,0:T(8,128)(2,1)S(1)} %get-tuple-element.93), channel_id=1, source_target_pairs={{0,12},{1,13},{4,8},{5,9},{8,4},{9,5},{12,0},{13,1},{2,14},{3,15},... | collective-permute-start | bytes 491528 | tf_op jit(solution)/shard_map/ppermute | solution.py:453
  55.8 1.0 %collective-permute-start.15 = (bf16[80,1024]{1,0:T(8,128)(2,1)S(1)}, bf16[80,1024]{1,0:T(8,128)(2,1)S(1)}, u32[]{:S(2)}, u32[]{:S(2)}) collective-permute-start(bf16[80,1024]{1,0:T(8,128)(2,1)S(1)} %get-tuple-element.94), channel_id=1, source_target_pairs={{0,13},{1,12},{4,9},{5,8},{8,5},{9,4},{12,1},{13,0},{2,15},{3,14},... | collective-permute-start | bytes 491528 | tf_op jit(solution)/shard_map/ppermute | solution.py:453
  56.7 0.8 select.2
  57.6 1.5 %packet.7 = (bf16[80,1024]{1,0:T(8,128)(2,1)S(1)}, bf16[80,1024]{1,0:T(8,128)(2,1)S(1)}) custom-call(bf16[256,1024]{1,0:T(8,128)(2,1)S(1)} %project_own.1.refs_0_, bf16[256,1024]{1,0:T(8,128)(2,1)S(1)} %get-tuple-element.72.refs_1_, bf16[256,1024]{1,0:T(8,128)(2,1)S(1)} %get-tuple-element.76.refs_2_, bf16[128,1024]{1,0:T(8,128)(2,1)S(1)} %get-tuple-element.83.refs_3_, ...), custom_call_target="tpu_custom_call" | custom-call | flops 20971520 | bytes 131072 | tf_op jit(solution)/shard_map/packet/pallas_call | solution.py:275
  59.2 2.8 %collective-permute-start.16 = (bf16[256,1024]{1,0:T(8,128)(2,1)S(1)}, bf16[256,1024]{1,0:T(8,128)(2,1)S(1)}, u32[]{:S(2)}, u32[]{:S(2)}) collective-permute-start(bf16[256,1024]{1,0:T(8,128)(2,1)S(1)} %select.2), channel_id=1, source_target_pairs={{0,4},{4,0},{8,12},{12,8},{1,5},{5,1},{9,13},{13,9},{2,6},{6,2},{1... | collective-permute-start | bytes 1572872 | tf_op jit(solution)/shard_map/ppermute | solution.py:438
  62.0 0.6 collective-permute-start.18
  62.6 1.6 %collective-permute-done.15.refs_4_ = bf16[80,1024]{1,0:T(8,128)(2,1)S(1)} collective-permute-done((bf16[80,1024]{1,0:T(8,128)(2,1)S(1)}, bf16[80,1024]{1,0:T(8,128)(2,1)S(1)}, u32[]{:S(2)}, u32[]{:S(2)}) %collective-permute-start.15) | collective-permute-done | bytes 163872 | tf_op jit(solution)/shard_map/ppermute | solution.py:453
  64.2 0.6 order_of.1
  64.9 0.4 place.2
  65.2 0.8 select.3
  66.1 3.4 %all-gather = bf16[256,1024]{1,0:T(8,128)(2,1)S(1)} all-gather(bf16[128,1024]{1,0:T(8,128)(2,1)S(1)} %get-tuple-element.112), channel_id=2, replica_groups=mesh['groups'=2,'ctx'=4,'enc'=2,'tp'=2] {'tp'}, dimensions={0}, use_global_device_ids=true | all-gather | bytes 786432 | tf_op jit(solution)/shard_map/all_gather | solution.py:458
  69.5 0.2 squares.2.refs_0_
  69.7 13.7 %collective-permute-done.16.refs_1_.refs_2_ = bf16[256,1024]{1,0:T(8,128)(2,1)S(1)} collective-permute-done((bf16[256,1024]{1,0:T(8,128)(2,1)S(1)}, bf16[256,1024]{1,0:T(8,128)(2,1)S(1)}, u32[]{:S(2)}, u32[]{:S(2)}) %collective-permute-start.16) | collective-permute-done | bytes 524320 | tf_op jit(solution)/shard_map/ppermute | solution.py:438
  83.4 2.2 %all-gather.1 = bf16[256,1024]{1,0:T(8,128)(2,1)S(1)} all-gather(bf16[128,1024]{1,0:T(8,128)(2,1)S(1)} %slice.3), channel_id=3, replica_groups=mesh['groups'=2,'ctx'=4,'enc'=2,'tp'=2] {'tp'}, dimensions={0}, use_global_device_ids=true | all-gather | bytes 786432 | tf_op jit(solution)/shard_map/all_gather | solution.py:461
  85.5 0.2 squares.3.refs_0_
  85.7 0.4 place.3
  86.1 1.6 %norm.1 = bf16[128,8192]{1,0:T(8,128)(2,1)} custom-call(bf16[1,8192]{1,0:T(2,128)(2,1)S(1)} %broadcast_in_dim.42.gain, f32[128,1]{1,0:T(8,128)S(1)} %get-tuple-element.120.before, bf16[128,1024]{1,0:T(8,128)(2,1)S(1)} %get-tuple-element.121.refs_0_, bf16[128,1024]{1,0:T(8,128)(2,1)S(1)} %get-tuple-element.122.refs_1_, ...), custom_call_target="tpu_custom_call" | custom-call | flops 262144 | bytes 262144 | tf_op jit(solution)/shard_map/norm/pallas_call | solution.py:415
  (32 shorter events, 0.2 us)
Async XLA Ops:
  2.3 20.6 %collective-permute-start = (bf16[1296,128]{1,0:T(8,128)(2,1)}, bf16[1296,128]{1,0:T(8,128)(2,1)S(1)}, u32[]{:S(2)}, u32[]{:S(2)}) collective-permute-start(bf16[1296,128]{1,0:T(8,128)(2,1)} %get-tuple-element.66), channel_id=1, source_target_pairs={{0,4},{4,0},{8,12},{12,8},{1,5},{5,1},{9,13},{13,9},{2,6},{6,2},{1... | collective-permute-start | bytes 995336 | tf_op jit(solution)/shard_map/ppermute | solution.py:438
  5.4 12.2 %collective-permute-start.1 = (bf16[656,128]{1,0:T(8,128)(2,1)}, bf16[656,128]{1,0:T(8,128)(2,1)S(1)}, u32[]{:S(2)}, u32[]{:S(2)}) collective-permute-start(bf16[656,128]{1,0:T(8,128)(2,1)} %get-tuple-element.67), channel_id=1, source_target_pairs={{0,8},{4,12},{8,0},{12,4},{1,9},{5,13},{9,1},{13,5},{2,10},{6,14},... | collective-permute-start | bytes 503816 | tf_op jit(solution)/shard_map/ppermute | solution.py:438
  8.0 14.9 %collective-permute-start.2 = (bf16[656,128]{1,0:T(8,128)(2,1)}, bf16[656,128]{1,0:T(8,128)(2,1)S(1)}, u32[]{:S(2)}, u32[]{:S(2)}) collective-permute-start(bf16[656,128]{1,0:T(8,128)(2,1)} %get-tuple-element.68), channel_id=1, source_target_pairs={{0,12},{4,8},{8,4},{12,0},{1,13},{5,9},{9,5},{13,1},{2,14},{6,10},... | collective-permute-start | bytes 503816 | tf_op jit(solution)/shard_map/ppermute | solution.py:438
  9.4 1.7 %copy-start = (bf16[1280,1024]{1,0:T(8,128)(2,1)S(1)}, bf16[1280,1024]{1,0:T(8,128)(2,1)}, u32[]{:S(2)}) copy-start(bf16[1280,1024]{1,0:T(8,128)(2,1)} %wa.9) | copy-start | bytes 7864324
  11.1 1.7 %copy-start.2 = (bf16[1280,1024]{1,0:T(8,128)(2,1)S(1)}, bf16[1280,1024]{1,0:T(8,128)(2,1)}, u32[]{:S(2)}) copy-start(bf16[1280,1024]{1,0:T(8,128)(2,1)} %wf.9) | copy-start | bytes 7864324
  12.8 1.1 %copy-start.4 = (bf16[1,256,1280]{2,1,0:T(8,128)(2,1)S(1)}, bf16[1,256,1280]{2,1,0:T(8,128)(2,1)}, u32[]{:S(2)}) copy-start(bf16[1,256,1280]{2,1,0:T(8,128)(2,1)} %param.8) | copy-start | bytes 1966084
  13.9 0.7 copy-start.6
  14.6 10.8 %copy-start.1 = (bf16[1280,1024]{1,0:T(8,128)(2,1)S(1)}, bf16[1280,1024]{1,0:T(8,128)(2,1)}, u32[]{:S(2)}) copy-start(bf16[1280,1024]{1,0:T(8,128)(2,1)} %wa.9) | copy-start | bytes 7864324
  14.6 10.8 %copy-start.3 = (bf16[1280,1024]{1,0:T(8,128)(2,1)S(1)}, bf16[1280,1024]{1,0:T(8,128)(2,1)}, u32[]{:S(2)}) copy-start(bf16[1280,1024]{1,0:T(8,128)(2,1)} %wf.9) | copy-start | bytes 7864324
  22.9 4.2 %collective-permute-start.3 = (bf16[1296,128]{1,0:T(8,128)(2,1)S(1)}, bf16[1296,128]{1,0:T(8,128)(2,1)S(1)}, u32[]{:S(2)}, u32[]{:S(2)}) collective-permute-start(bf16[1296,128]{1,0:T(8,128)(2,1)S(1)} %collective-permute-done), channel_id=1, source_target_pairs={{0,1},{1,0},{2,3},{3,2},{4,5},{5,4},{6,7},{7,6},{8,9},{9,8},{10,11... | collective-permute-start | bytes 995336 | tf_op jit(solution)/shard_map/ppermute | solution.py:441
  22.9 4.2 %collective-permute-start.4 = (bf16[656,128]{1,0:T(8,128)(2,1)S(1)}, bf16[656,128]{1,0:T(8,128)(2,1)S(1)}, u32[]{:S(2)}, u32[]{:S(2)}) collective-permute-start(bf16[656,128]{1,0:T(8,128)(2,1)S(1)} %collective-permute-done.1), channel_id=1, source_target_pairs={{0,1},{1,0},{2,3},{3,2},{4,5},{5,4},{6,7},{7,6},{8,9},{9,8},{10,11... | collective-permute-start | bytes 503816 | tf_op jit(solution)/shard_map/ppermute | solution.py:441
  23.4 3.7 %collective-permute-start.5 = (bf16[656,128]{1,0:T(8,128)(2,1)S(1)}, bf16[656,128]{1,0:T(8,128)(2,1)S(1)}, u32[]{:S(2)}, u32[]{:S(2)}) collective-permute-start(bf16[656,128]{1,0:T(8,128)(2,1)S(1)} %collective-permute-done.2), channel_id=1, source_target_pairs={{0,1},{1,0},{2,3},{3,2},{4,5},{5,4},{6,7},{7,6},{8,9},{9,8},{10,11... | collective-permute-start | bytes 503816 | tf_op jit(solution)/shard_map/ppermute | solution.py:441
  23.4 9.8 %collective-permute-start.6 = (bf16[656,128]{1,0:T(8,128)(2,1)S(1)}, bf16[656,128]{1,0:T(8,128)(2,1)S(1)}, u32[]{:S(2)}, u32[]{:S(2)}) collective-permute-start(bf16[656,128]{1,0:T(8,128)(2,1)S(1)} %collective-permute-done.1), channel_id=1, source_target_pairs={{0,4},{4,0},{8,12},{12,8},{1,5},{5,1},{9,13},{13,9},{2,6},{6,2},{1... | collective-permute-start | bytes 503816 | tf_op jit(solution)/shard_map/ppermute | solution.py:438
  24.2 9.5 %collective-permute-start.7 = (bf16[656,128]{1,0:T(8,128)(2,1)S(1)}, bf16[656,128]{1,0:T(8,128)(2,1)S(1)}, u32[]{:S(2)}, u32[]{:S(2)}) collective-permute-start(bf16[656,128]{1,0:T(8,128)(2,1)S(1)} %collective-permute-done.2), channel_id=1, source_target_pairs={{0,4},{4,0},{8,12},{12,8},{1,5},{5,1},{9,13},{13,9},{2,6},{6,2},{1... | collective-permute-start | bytes 503816 | tf_op jit(solution)/shard_map/ppermute | solution.py:438
  27.1 1.6 %copy-start.5 = (s32[1,256]{1,0:T(1,128)S(1)}, s32[1,256]{1,0:T(1,128)}, u32[]{:S(2)}) copy-start(s32[1,256]{1,0:T(1,128)} %refs_5_.3) | copy-start | bytes 3076
  29.8 7.1 %collective-permute-start.9 = (bf16[48,1024]{1,0:T(8,128)(2,1)S(1)}, bf16[48,1024]{1,0:T(8,128)(2,1)S(1)}, u32[]{:S(2)}, u32[]{:S(2)}) collective-permute-start(bf16[48,1024]{1,0:T(8,128)(2,1)S(1)} %get-tuple-element.80), channel_id=1, source_target_pairs={{0,13},{1,12},{4,9},{5,8},{8,5},{9,4},{12,1},{13,0},{2,15},{3,14},... | collective-permute-start | bytes 294920 | tf_op jit(solution)/shard_map/ppermute | solution.py:453
  30.9 8.3 %collective-permute-start.8 = (bf16[48,1024]{1,0:T(8,128)(2,1)S(1)}, bf16[48,1024]{1,0:T(8,128)(2,1)S(1)}, u32[]{:S(2)}, u32[]{:S(2)}) collective-permute-start(bf16[48,1024]{1,0:T(8,128)(2,1)S(1)} %get-tuple-element.79), channel_id=1, source_target_pairs={{0,12},{1,13},{4,8},{5,9},{8,4},{9,5},{12,0},{13,1},{2,14},{3,15},... | collective-permute-start | bytes 294920 | tf_op jit(solution)/shard_map/ppermute | solution.py:453
  39.3 6.4 %collective-permute-start.10 = (bf16[656,128]{1,0:T(8,128)(2,1)S(1)}, bf16[656,128]{1,0:T(8,128)(2,1)S(1)}, u32[]{:S(2)}, u32[]{:S(2)}) collective-permute-start(bf16[656,128]{1,0:T(8,128)(2,1)S(1)} %collective-permute-done.6), channel_id=1, source_target_pairs={{0,1},{1,0},{2,3},{3,2},{4,5},{5,4},{6,7},{7,6},{8,9},{9,8},{10,11... | collective-permute-start | bytes 503816 | tf_op jit(solution)/shard_map/ppermute | solution.py:441
  39.3 6.4 %collective-permute-start.11 = (bf16[656,128]{1,0:T(8,128)(2,1)S(1)}, bf16[656,128]{1,0:T(8,128)(2,1)S(1)}, u32[]{:S(2)}, u32[]{:S(2)}) collective-permute-start(bf16[656,128]{1,0:T(8,128)(2,1)S(1)} %collective-permute-done.7), channel_id=1, source_target_pairs={{0,1},{1,0},{2,3},{3,2},{4,5},{5,4},{6,7},{7,6},{8,9},{9,8},{10,11... | collective-permute-start | bytes 503816 | tf_op jit(solution)/shard_map/ppermute | solution.py:441
  40.8 7.3 %collective-permute-start.13 = (bf16[48,1024]{1,0:T(8,128)(2,1)S(1)}, bf16[48,1024]{1,0:T(8,128)(2,1)S(1)}, u32[]{:S(2)}, u32[]{:S(2)}) collective-permute-start(bf16[48,1024]{1,0:T(8,128)(2,1)S(1)} %get-tuple-element.92), channel_id=1, source_target_pairs={{0,9},{1,8},{4,13},{5,12},{8,1},{9,0},{12,5},{13,4},{2,11},{3,10},... | collective-permute-start | bytes 294920 | tf_op jit(solution)/shard_map/ppermute | solution.py:453
  44.3 9.7 %collective-permute-start.12 = (bf16[48,1024]{1,0:T(8,128)(2,1)S(1)}, bf16[48,1024]{1,0:T(8,128)(2,1)S(1)}, u32[]{:S(2)}, u32[]{:S(2)}) collective-permute-start(bf16[48,1024]{1,0:T(8,128)(2,1)S(1)} %get-tuple-element.86), channel_id=1, source_target_pairs={{0,8},{1,9},{4,12},{5,13},{8,0},{9,1},{12,4},{13,5},{2,10},{3,11},... | collective-permute-start | bytes 294920 | tf_op jit(solution)/shard_map/ppermute | solution.py:453
  45.7 11.0 %copy-start.8 = (bf16[8192]{0:T(1024)(128)(2,1)S(1)}, bf16[8192]{0:T(1024)(128)(2,1)}, u32[]{:S(2)}) copy-start(bf16[8192]{0:T(1024)(128)(2,1)} %param.15) | copy-start | bytes 49156
  48.1 16.1 %copy-start.7 = (s32[1,256]{1,0:T(1,128)S(1)}, s32[1,256]{1,0:T(1,128)}, u32[]{:S(2)}) copy-start(s32[1,256]{1,0:T(1,128)} %get-tuple-element.65.parity) | copy-start | bytes 3076
  53.9 8.7 %collective-permute-start.14 = (bf16[80,1024]{1,0:T(8,128)(2,1)S(1)}, bf16[80,1024]{1,0:T(8,128)(2,1)S(1)}, u32[]{:S(2)}, u32[]{:S(2)}) collective-permute-start(bf16[80,1024]{1,0:T(8,128)(2,1)S(1)} %get-tuple-element.93), channel_id=1, source_target_pairs={{0,12},{1,13},{4,8},{5,9},{8,4},{9,5},{12,0},{13,1},{2,14},{3,15},... | collective-permute-start | bytes 491528 | tf_op jit(solution)/shard_map/ppermute | solution.py:453
  55.8 8.5 %collective-permute-start.15 = (bf16[80,1024]{1,0:T(8,128)(2,1)S(1)}, bf16[80,1024]{1,0:T(8,128)(2,1)S(1)}, u32[]{:S(2)}, u32[]{:S(2)}) collective-permute-start(bf16[80,1024]{1,0:T(8,128)(2,1)S(1)} %get-tuple-element.94), channel_id=1, source_target_pairs={{0,13},{1,12},{4,9},{5,8},{8,5},{9,4},{12,1},{13,0},{2,15},{3,14},... | collective-permute-start | bytes 491528 | tf_op jit(solution)/shard_map/ppermute | solution.py:453
  59.1 26.6 %collective-permute-start.17 = (bf16[80,1024]{1,0:T(8,128)(2,1)S(1)}, bf16[80,1024]{1,0:T(8,128)(2,1)S(1)}, u32[]{:S(2)}, u32[]{:S(2)}) collective-permute-start(bf16[80,1024]{1,0:T(8,128)(2,1)S(1)} %get-tuple-element.97), channel_id=1, source_target_pairs={{0,8},{1,9},{4,12},{5,13},{8,0},{9,1},{12,4},{13,5},{2,10},{3,11},... | collective-permute-start | bytes 491528 | tf_op jit(solution)/shard_map/ppermute | solution.py:453
  59.2 24.1 %collective-permute-start.16 = (bf16[256,1024]{1,0:T(8,128)(2,1)S(1)}, bf16[256,1024]{1,0:T(8,128)(2,1)S(1)}, u32[]{:S(2)}, u32[]{:S(2)}) collective-permute-start(bf16[256,1024]{1,0:T(8,128)(2,1)S(1)} %select.2), channel_id=1, source_target_pairs={{0,4},{4,0},{8,12},{12,8},{1,5},{5,1},{9,13},{13,9},{2,6},{6,2},{1... | collective-permute-start | bytes 1572872 | tf_op jit(solution)/shard_map/ppermute | solution.py:438
  62.0 23.7 %collective-permute-start.18 = (bf16[80,1024]{1,0:T(8,128)(2,1)S(1)}, bf16[80,1024]{1,0:T(8,128)(2,1)S(1)}, u32[]{:S(2)}, u32[]{:S(2)}) collective-permute-start(bf16[80,1024]{1,0:T(8,128)(2,1)S(1)} %get-tuple-element.116), channel_id=1, source_target_pairs={{0,9},{1,8},{4,13},{5,12},{8,1},{9,0},{12,5},{13,4},{2,11},{3,10},... | collective-permute-start | bytes 491528 | tf_op jit(solution)/shard_map/ppermute | solution.py:453

commit v11 on v10

--- a/solution.py
+++ b/solution.py
@@ -324,7 +324,7 @@
         in_specs=[VMEM] * (1 + len(slots)),
         out_specs=[VMEM] * 2,
         compiler_params=PARAMS,
-        cost_estimate=cost(0, 0),
+        cost_estimate=cost(1 << 34, 0),
         name="order_of",
     )(parity, *slots)
 
@@ -351,7 +351,7 @@
         in_specs=[VMEM] * len(operands),
         out_specs=[VMEM] * 3,
         compiler_params=PARAMS,
-        cost_estimate=cost(1 << 36, 1 << 26),
+        cost_estimate=cost(1 << 34, 0),
         name="place",
     )(*operands)
 
@@ -384,7 +384,7 @@
         in_specs=[VMEM] * len(operands),
         out_specs=VMEM,
         compiler_params=PARAMS,
-        cost_estimate=cost(1 << 36, 1 << 26),
+        cost_estimate=cost(1 << 34, 0),
         name="squares",
     )(*operands)
 
@@ -453,11 +453,10 @@
         return lax.ppermute(x, ("ctx", "tp"), pairs)
 
     def own_and_near(total):
-        slots[0] = after(slots[0], total)
         pieces[0, 0], other = select(0, blocks, slots, [half, half])
         pieces[0, 1] = lax.all_gather(other, "tp", axis=0)
         total = squares(total, [pieces[0, 0], pieces[0, 1]], half)
-        pair = after(pieces[1], total)
+        pair = pieces[1]
         pieces[1, 0], pieces[1, 1] = pair, lax.all_gather(pair[half:], "tp", axis=0)
         return squares(total, [pieces[1, 0], pieces[1, 1]], half)
 
@@ -478,33 +477,25 @@
             chosen = packet(m, early, blocks, slots, size, False)
             slots[0] = after(slots[0], chosen[0])
             sent[m] = [to_core(piece, m, d) for d, piece in enumerate(chosen)]
-        joined = lax.optimization_barrier((*shared, *sent[3], blocks[-1]))
-        shared, sent[3] = joined[:2], list(joined[2:4])
-        swapped = [over_tp(part)[None] for part in shared]
-        take([part[None] for part in shared])
-        take(swapped)
-
+        shared = lax.optimization_barrier((*shared, blocks[-1]))[:2]
+        take([lax.all_gather(part, "tp", axis=0) for part in shared])
+
+        (chosen,) = select(1, blocks, slots, [2 * half])
+        slots[0] = after(slots[0], chosen)
+        pieces[1] = over_ctx(chosen, 1)
         rest = {}
-        for m in (3, 1, 2):
-            if m == 1:
-                (chosen,) = select(1, blocks, slots, [2 * half])
-                slots[0] = after(slots[0], chosen)
-                pieces[1] = over_ctx(chosen, 1)
-                continue
+        for m in (3, 2):
             chosen = packet(m, early, blocks, slots, half - size, True)
             slots[0] = after(slots[0], chosen[0])
             if m == 3:
-                joined = lax.optimization_barrier((*chosen, *sent[2]))
-                chosen, sent[2] = joined[:2], list(joined[2:])
+                joined = lax.optimization_barrier((*chosen, *sent[3], *sent[2]))
+                chosen, sent[3], sent[2] = joined[:2], list(joined[2:4]), list(joined[4:])
             rest[m] = [to_core(piece, m, d) for d, piece in enumerate(chosen)]
 
-        joined = lax.optimization_barrier((*rest[3], *slots))
-        rest[3] = joined[:2]
-        order3, order2 = order_of(size, parity, joined[2:], half)
+        order3, order2 = order_of(size, parity, slots, half)
         packets = [sent[3][0], rest[3][0], sent[3][1], rest[3][1]]
         pieces[3, 0], pieces[3, 1], total = place(None, order3, packets)
         total = own_and_near(total)
-        rest[2] = lax.optimization_barrier((*rest[2], total))[:2]
         packets = [sent[2][0], rest[2][0], sent[2][1], rest[2][1]]
         pieces[2, 0], pieces[2, 1], total = place(total, order2, packets)
         order, fresh = [3, 1, 0, 2], ()

time: 88.1 us -> 81.6 us (0.926)
  the two profiles are of different devices: /device:TPU:0 before, /device:TPU:9 now
where the time goes in v11:
time: 81.6 us; the launch traced here: 81.2 us
  waiting for transfers between devices  26.2 us (32%)
  starting transfers between devices  20.7 us (25%)
  Pallas kernels  18.3 us (22%)
  blocking collectives  9.21 us (11%)
  local copies, waits for them, and re-layouts  6.68 us (8%)
    ppermute x8, waiting for transfers between devices, to_core(): return lax.ppermute(x, ('ctx', 'tp'), pairs)  23.5 us
    ppermute x8, starting transfers between devices, to_core(): return lax.ppermute(x, ('ctx', 'tp'), pairs)  10.1 us
    ppermute x3, starting transfers between devices, over_tp(): return lax.ppermute(x, 'tp', [(0, 1), (1, 0)])  5.91 us
    unnamed x18, local copies, waits for them, and re-layouts  5.27 us
    pallas_call x4, Pallas kernels, packet(): pl.pallas_call(functools.partial(packet_kernel, m, early, len(blocks), se...  4.85 us
    all_gather x2, blocking collectives, body(): take([lax.all_gather(part, 'tp', axis=0) for part in shared])  4.84 us
    pallas_call x3, Pallas kernels, project_parts(): pl.pallas_call(project_parts_kernel, out_shape=[jax.ShapeDtypeStruct((row...  4.77 us
    ppermute x6, starting transfers between devices, over_ctx(): return lax.ppermute(x, 'ctx', [(i, i ^ m) for i in range(n)])  4.68 us
  transfers between devices with their start and end apart: 17, of which 4 were waited for; matrix products, arithmetic and copies ran while one was open for 2% of the time, Pallas kernels for 17%

profile of v11, /device:TPU:9, one launch (start us, length us, event | category | flops | bytes accessed | tf_op | source)
XLA Modules:
  0.0 81.2 jit_solution(18008345655377313563)
XLA Ops:
  0.0 2.3 %to_send.1 = (bf16[1296,128]{1,0:T(8,128)(2,1)}, bf16[656,128]{1,0:T(8,128)(2,1)}, bf16[656,128]{1,0:T(8,128)(2,1)}, s32[1,256]{1,0:T(1,128)}) custom-call(bf16[256,1280]{1,0:T(8,128)(2,1)} %bitcast.12, s32[1,256]{1,0:T(1,128)} %refs_4_.3, s32[1,256]{1,0:T(1,128)} %kind.3), custom_call_target="tpu_custom_call" | custom-call | bytes 40960 | tf_op jit(solution)/shard_map/to_send/pallas_call | solution.py:108
  2.3 0.1 collective-permute-start
  2.4 2.5 %collective-permute-start.1 = (bf16[656,128]{1,0:T(8,128)(2,1)}, bf16[656,128]{1,0:T(8,128)(2,1)S(1)}, u32[]{:S(2)}, u32[]{:S(2)}) collective-permute-start(bf16[656,128]{1,0:T(8,128)(2,1)} %get-tuple-element.54), channel_id=1, source_target_pairs={{0,8},{4,12},{8,0},{12,4},{1,9},{5,13},{9,1},{13,5},{2,10},{6,14},... | collective-permute-start | bytes 503816 | tf_op jit(solution)/shard_map/ppermute | solution.py:438
  4.9 0.2 collective-permute-start.2
  5.0 0.7 broadcast_in_dim.31.ba
  5.7 0.7 broadcast_in_dim.32.bf
  6.4 1.7 %copy-done = bf16[1280,1024]{1,0:T(8,128)(2,1)S(1)} copy-done((bf16[1280,1024]{1,0:T(8,128)(2,1)S(1)}, bf16[1280,1024]{1,0:T(8,128)(2,1)}, u32[]{:S(2)}) %copy-start) | copy-done | bytes 2621464
  8.2 1.7 %copy-done.2 = bf16[1280,1024]{1,0:T(8,128)(2,1)S(1)} copy-done((bf16[1280,1024]{1,0:T(8,128)(2,1)S(1)}, bf16[1280,1024]{1,0:T(8,128)(2,1)}, u32[]{:S(2)}) %copy-start.2) | copy-done | bytes 2621464
  9.9 1.1 %copy-done.4 = bf16[1,256,1280]{2,1,0:T(8,128)(2,1)S(1)} copy-done((bf16[1,256,1280]{2,1,0:T(8,128)(2,1)S(1)}, bf16[1,256,1280]{2,1,0:T(8,128)(2,1)}, u32[]{:S(2)}) %copy-start.4) | copy-done | bytes 655384
  11.0 0.7 copy-done.6
  11.7 1.6 %project_own.1.refs_0_ = bf16[256,1024]{1,0:T(8,128)(2,1)S(1)} custom-call(s32[1,256]{1,0:T(1,128)S(1)} %copy-done.6, bf16[256,1280]{1,0:T(8,128)(2,1)S(1)} %bitcast.13, bf16[1280,1024]{1,0:T(8,128)(2,1)S(1)} %copy-done, bf16[1280,1024]{1,0:T(8,128)(2,1)S(1)} %copy-done.2, bf16[1,1024]{1,0:T(2,128)(2,1)S(1)} %broadcast_in_dim.31.ba, ...), custom_call_target="tpu_custom_call" | custom-call | flops 83886080 | bytes 327680 | tf_op jit(solution)/shard_map/project_own/pallas_call | solution.py:146
  13.3 2.7 %collective-permute-done.1 = bf16[656,128]{1,0:T(8,128)(2,1)S(1)} collective-permute-done((bf16[656,128]{1,0:T(8,128)(2,1)}, bf16[656,128]{1,0:T(8,128)(2,1)S(1)}, u32[]{:S(2)}, u32[]{:S(2)}) %collective-permute-start.1) | collective-permute-done | bytes 167968 | tf_op jit(solution)/shard_map/ppermute | solution.py:438
  15.9 5.4 %collective-permute-start.3 = (bf16[1296,128]{1,0:T(8,128)(2,1)S(1)}, bf16[1296,128]{1,0:T(8,128)(2,1)S(1)}, u32[]{:S(2)}, u32[]{:S(2)}) collective-permute-start(bf16[1296,128]{1,0:T(8,128)(2,1)S(1)} %collective-permute-done), channel_id=1, source_target_pairs={{0,1},{1,0},{2,3},{3,2},{4,5},{5,4},{6,7},{7,6},{8,9},{9,8},{10,11... | collective-permute-start | bytes 995336 | tf_op jit(solution)/shard_map/ppermute | solution.py:441
  21.3 0.5 collective-permute-start.5
  21.8 1.0 %collective-permute-start.6 = (bf16[656,128]{1,0:T(8,128)(2,1)S(1)}, bf16[656,128]{1,0:T(8,128)(2,1)S(1)}, u32[]{:S(2)}, u32[]{:S(2)}) collective-permute-start(bf16[656,128]{1,0:T(8,128)(2,1)S(1)} %collective-permute-done.1), channel_id=1, source_target_pairs={{0,4},{4,0},{8,12},{12,8},{1,5},{5,1},{9,13},{13,9},{2,6},{6,2},{1... | collective-permute-start | bytes 503816 | tf_op jit(solution)/shard_map/ppermute | solution.py:438
  22.8 0.5 collective-permute-start.7
  23.3 1.6 %project_parts.3 = (bf16[256,1024]{1,0:T(8,128)(2,1)S(1)}, s32[1,256]{1,0:T(1,128)S(1)}) custom-call(bf16[1280,1024]{1,0:T(8,128)(2,1)S(1)} %copy-done.1, bf16[1280,1024]{1,0:T(8,128)(2,1)S(1)} %copy-done.3, bf16[1,1024]{1,0:T(2,128)(2,1)S(1)} %broadcast_in_dim.31.ba, bf16[1,1024]{1,0:T(2,128)(2,1)S(1)} %broadcast_in_dim.32.bf, ...), custom_call_target="tpu_custom_call" | custom-call | flops 83886080 | bytes 327680 | tf_op jit(solution)/shard_map/project_parts/pallas_call | solution.py:176
  24.9 0.0 copy-start.5
  25.0 1.6 %project_parts.4 = (bf16[256,1024]{1,0:T(8,128)(2,1)S(1)}, s32[1,256]{1,0:T(1,128)S(1)}) custom-call(bf16[1280,1024]{1,0:T(8,128)(2,1)S(1)} %copy-done.1, bf16[1280,1024]{1,0:T(8,128)(2,1)S(1)} %copy-done.3, bf16[1,1024]{1,0:T(2,128)(2,1)S(1)} %broadcast_in_dim.31.ba, bf16[1,1024]{1,0:T(2,128)(2,1)S(1)} %broadcast_in_dim.32.bf, ...), custom_call_target="tpu_custom_call" | custom-call | flops 83886080 | bytes 327680 | tf_op jit(solution)/shard_map/project_parts/pallas_call | solution.py:176
  26.6 1.0 %packet.4 = (bf16[48,1024]{1,0:T(8,128)(2,1)S(1)}, bf16[48,1024]{1,0:T(8,128)(2,1)S(1)}) custom-call(bf16[256,1024]{1,0:T(8,128)(2,1)S(1)} %project_own.1.refs_0_, bf16[256,1024]{1,0:T(8,128)(2,1)S(1)} %get-tuple-element.59.refs_1_, bf16[256,1024]{1,0:T(8,128)(2,1)S(1)} %get-tuple-element.63.refs_2_, s32[1,256]{1,0:T(1,128)S(1)} %copy-done.5, ...), custom_call_target="tpu_custom_call" | custom-call | flops 9437184 | bytes 98304 | tf_op jit(solution)/shard_map/packet/pallas_call | solution.py:275
  27.6 1.4 %collective-permute-start.8 = (bf16[48,1024]{1,0:T(8,128)(2,1)S(1)}, bf16[48,1024]{1,0:T(8,128)(2,1)S(1)}, u32[]{:S(2)}, u32[]{:S(2)}) collective-permute-start(bf16[48,1024]{1,0:T(8,128)(2,1)S(1)} %get-tuple-element.66), channel_id=1, source_target_pairs={{0,12},{1,13},{4,8},{5,9},{8,4},{9,5},{12,0},{13,1},{2,14},{3,15},... | collective-permute-start | bytes 294920 | tf_op jit(solution)/shard_map/ppermute | solution.py:453
  29.0 1.0 %packet.5 = (bf16[48,1024]{1,0:T(8,128)(2,1)S(1)}, bf16[48,1024]{1,0:T(8,128)(2,1)S(1)}) custom-call(bf16[256,1024]{1,0:T(8,128)(2,1)S(1)} %project_own.1.refs_0_, bf16[256,1024]{1,0:T(8,128)(2,1)S(1)} %get-tuple-element.59.refs_1_, bf16[256,1024]{1,0:T(8,128)(2,1)S(1)} %get-tuple-element.63.refs_2_, s32[1,256]{1,0:T(1,128)S(1)} %copy-done.5, ...), custom_call_target="tpu_custom_call" | custom-call | flops 9437184 | bytes 98304 | tf_op jit(solution)/shard_map/packet/pallas_call | solution.py:275
  30.0 1.8 %collective-permute-start.10 = (bf16[48,1024]{1,0:T(8,128)(2,1)S(1)}, bf16[48,1024]{1,0:T(8,128)(2,1)S(1)}, u32[]{:S(2)}, u32[]{:S(2)}) collective-permute-start(bf16[48,1024]{1,0:T(8,128)(2,1)S(1)} %get-tuple-element.68), channel_id=1, source_target_pairs={{0,8},{1,9},{4,12},{5,13},{8,0},{9,1},{12,4},{13,5},{2,10},{3,11},... | collective-permute-start | bytes 294920 | tf_op jit(solution)/shard_map/ppermute | solution.py:453
  31.9 2.8 %all-gather = bf16[1312,128]{1,0:T(8,128)(2,1)S(1)} all-gather(bf16[656,128]{1,0:T(8,128)(2,1)S(1)} %collective-permute-done.6), channel_id=2, replica_groups=mesh['groups'=2,'ctx'=4,'enc'=2,'tp'=2] {'tp'}, dimensions={0}, use_global_device_ids=true | all-gather | bytes 503808 | tf_op jit(solution)/shard_map/all_gather | solution.py:481
  34.7 1.1 %collective-permute-start.9 = (bf16[48,1024]{1,0:T(8,128)(2,1)S(1)}, bf16[48,1024]{1,0:T(8,128)(2,1)S(1)}, u32[]{:S(2)}, u32[]{:S(2)}) collective-permute-start(bf16[48,1024]{1,0:T(8,128)(2,1)S(1)} %get-tuple-element.81), channel_id=1, source_target_pairs={{0,13},{1,12},{4,9},{5,8},{8,5},{9,4},{12,1},{13,0},{2,15},{3,14},... | collective-permute-start | bytes 294920 | tf_op jit(solution)/shard_map/ppermute | solution.py:453
  35.7 1.4 %collective-permute-start.11 = (bf16[48,1024]{1,0:T(8,128)(2,1)S(1)}, bf16[48,1024]{1,0:T(8,128)(2,1)S(1)}, u32[]{:S(2)}, u32[]{:S(2)}) collective-permute-start(bf16[48,1024]{1,0:T(8,128)(2,1)S(1)} %get-tuple-element.82), channel_id=1, source_target_pairs={{0,9},{1,8},{4,13},{5,12},{8,1},{9,0},{12,5},{13,4},{2,11},{3,10},... | collective-permute-start | bytes 294920 | tf_op jit(solution)/shard_map/ppermute | solution.py:453
  37.2 2.0 %all-gather.1 = bf16[1312,128]{1,0:T(8,128)(2,1)S(1)} all-gather(bf16[656,128]{1,0:T(8,128)(2,1)S(1)} %collective-permute-done.7), channel_id=3, replica_groups=mesh['groups'=2,'ctx'=4,'enc'=2,'tp'=2] {'tp'}, dimensions={0}, use_global_device_ids=true | all-gather | bytes 503808 | tf_op jit(solution)/shard_map/all_gather | solution.py:481
  39.2 1.6 %project_parts.5 = (bf16[256,1024]{1,0:T(8,128)(2,1)S(1)}, s32[1,256]{1,0:T(1,128)S(1)}) custom-call(bf16[1280,1024]{1,0:T(8,128)(2,1)S(1)} %copy-done.1, bf16[1280,1024]{1,0:T(8,128)(2,1)S(1)} %copy-done.3, bf16[1,1024]{1,0:T(2,128)(2,1)S(1)} %broadcast_in_dim.31.ba, bf16[1,1024]{1,0:T(2,128)(2,1)S(1)} %broadcast_in_dim.32.bf, ...), custom_call_target="tpu_custom_call" | custom-call | flops 83886080 | bytes 327680 | tf_op jit(solution)/shard_map/project_parts/pallas_call | solution.py:176
  40.8 0.7 select.2
  41.5 0.5 collective-permute-start.14
  42.1 1.4 %packet.6 = (bf16[80,1024]{1,0:T(8,128)(2,1)S(1)}, bf16[80,1024]{1,0:T(8,128)(2,1)S(1)}) custom-call(bf16[256,1024]{1,0:T(8,128)(2,1)S(1)} %project_own.1.refs_0_, bf16[256,1024]{1,0:T(8,128)(2,1)S(1)} %get-tuple-element.59.refs_1_, bf16[256,1024]{1,0:T(8,128)(2,1)S(1)} %get-tuple-element.63.refs_2_, bf16[256,1024]{1,0:T(8,128)(2,1)S(1)} %get-tuple-element.72.refs_3_, ...), custom_call_target="tpu_custom_call" | custom-call | flops 20971520 | bytes 131072 | tf_op jit(solution)/shard_map/packet/pallas_call | solution.py:275
  43.5 1.4 %packet.7 = (bf16[80,1024]{1,0:T(8,128)(2,1)S(1)}, bf16[80,1024]{1,0:T(8,128)(2,1)S(1)}) custom-call(bf16[256,1024]{1,0:T(8,128)(2,1)S(1)} %project_own.1.refs_0_, bf16[256,1024]{1,0:T(8,128)(2,1)S(1)} %get-tuple-element.59.refs_1_, bf16[256,1024]{1,0:T(8,128)(2,1)S(1)} %get-tuple-element.63.refs_2_, bf16[256,1024]{1,0:T(8,128)(2,1)S(1)} %get-tuple-element.72.refs_3_, ...), custom_call_target="tpu_custom_call" | custom-call | flops 20971520 | bytes 131072 | tf_op jit(solution)/shard_map/packet/pallas_call | solution.py:275
  44.9 0.6 collective-permute-done.9.refs_3_
  45.5 0.9 %collective-permute-start.15 = (bf16[80,1024]{1,0:T(8,128)(2,1)S(1)}, bf16[80,1024]{1,0:T(8,128)(2,1)S(1)}, u32[]{:S(2)}, u32[]{:S(2)}) collective-permute-start(bf16[80,1024]{1,0:T(8,128)(2,1)S(1)} %get-tuple-element.77), channel_id=1, source_target_pairs={{0,8},{1,9},{4,12},{5,13},{8,0},{9,1},{12,4},{13,5},{2,10},{3,11},... | collective-permute-start | bytes 491528 | tf_op jit(solution)/shard_map/ppermute | solution.py:453
  46.4 1.8 %collective-permute-start.16 = (bf16[80,1024]{1,0:T(8,128)(2,1)S(1)}, bf16[80,1024]{1,0:T(8,128)(2,1)S(1)}, u32[]{:S(2)}, u32[]{:S(2)}) collective-permute-start(bf16[80,1024]{1,0:T(8,128)(2,1)S(1)} %get-tuple-element.93), channel_id=1, source_target_pairs={{0,9},{1,8},{4,13},{5,12},{8,1},{9,0},{12,5},{13,4},{2,11},{3,10},... | collective-permute-start | bytes 491528 | tf_op jit(solution)/shard_map/ppermute | solution.py:453
  48.2 0.7 collective-permute-start.12
  48.9 1.0 %collective-permute-start.13 = (bf16[80,1024]{1,0:T(8,128)(2,1)S(1)}, bf16[80,1024]{1,0:T(8,128)(2,1)S(1)}, u32[]{:S(2)}, u32[]{:S(2)}) collective-permute-start(bf16[80,1024]{1,0:T(8,128)(2,1)S(1)} %get-tuple-element.86), channel_id=1, source_target_pairs={{0,13},{1,12},{4,9},{5,8},{8,5},{9,4},{12,1},{13,0},{2,15},{3,14},... | collective-permute-start | bytes 491528 | tf_op jit(solution)/shard_map/ppermute | solution.py:453
  49.9 0.6 order_of.1
  50.5 0.7 select.3
  51.2 2.2 %all-gather.2 = bf16[256,1024]{1,0:T(8,128)(2,1)S(1)} all-gather(bf16[128,1024]{1,0:T(8,128)(2,1)S(1)} %get-tuple-element.89), channel_id=4, replica_groups=mesh['groups'=2,'ctx'=4,'enc'=2,'tp'=2] {'tp'}, dimensions={0}, use_global_device_ids=true | all-gather | bytes 786432 | tf_op jit(solution)/shard_map/all_gather | solution.py:457
  53.4 18.7 %collective-permute-done.12.refs_2_ = bf16[80,1024]{1,0:T(8,128)(2,1)S(1)} collective-permute-done((bf16[80,1024]{1,0:T(8,128)(2,1)S(1)}, bf16[80,1024]{1,0:T(8,128)(2,1)S(1)}, u32[]{:S(2)}, u32[]{:S(2)}) %collective-permute-start.12) | collective-permute-done | bytes 163872 | tf_op jit(solution)/shard_map/ppermute | solution.py:453
  72.1 4.2 %collective-permute-done.13.refs_4_ = bf16[80,1024]{1,0:T(8,128)(2,1)S(1)} collective-permute-done((bf16[80,1024]{1,0:T(8,128)(2,1)S(1)}, bf16[80,1024]{1,0:T(8,128)(2,1)S(1)}, u32[]{:S(2)}, u32[]{:S(2)}) %collective-permute-start.13) | collective-permute-done | bytes 163872 | tf_op jit(solution)/shard_map/ppermute | solution.py:453
  76.3 0.4 place.2
  76.7 0.2 squares.2.refs_0_
  76.9 2.2 %all-gather.3 = bf16[256,1024]{1,0:T(8,128)(2,1)S(1)} all-gather(bf16[128,1024]{1,0:T(8,128)(2,1)S(1)} %slice.4), channel_id=5, replica_groups=mesh['groups'=2,'ctx'=4,'enc'=2,'tp'=2] {'tp'}, dimensions={0}, use_global_device_ids=true | all-gather | bytes 786432 | tf_op jit(solution)/shard_map/all_gather | solution.py:460
  79.1 0.2 squares.3.refs_0_
  79.3 0.4 place.3
  79.6 1.6 %norm.1 = bf16[128,8192]{1,0:T(8,128)(2,1)} custom-call(bf16[1,8192]{1,0:T(2,128)(2,1)S(1)} %broadcast_in_dim.30.gain, f32[128,1]{1,0:T(8,128)S(1)} %get-tuple-element.94.before, bf16[128,1024]{1,0:T(8,128)(2,1)S(1)} %get-tuple-element.95.refs_0_, bf16[128,1024]{1,0:T(8,128)(2,1)S(1)} %get-tuple-element.96.refs_1_, ...), custom_call_target="tpu_custom_call" | custom-call | flops 262144 | bytes 262144 | tf_op jit(solution)/shard_map/norm/pallas_call | solution.py:415
  (29 shorter events, 0.1 us)
Async XLA Ops:
  2.3 13.6 %collective-permute-start = (bf16[1296,128]{1,0:T(8,128)(2,1)}, bf16[1296,128]{1,0:T(8,128)(2,1)S(1)}, u32[]{:S(2)}, u32[]{:S(2)}) collective-permute-start(bf16[1296,128]{1,0:T(8,128)(2,1)} %get-tuple-element.53), channel_id=1, source_target_pairs={{0,4},{4,0},{8,12},{12,8},{1,5},{5,1},{9,13},{13,9},{2,6},{6,2},{1... | collective-permute-start | bytes 995336 | tf_op jit(solution)/shard_map/ppermute | solution.py:438
  2.4 13.5 %collective-permute-start.1 = (bf16[656,128]{1,0:T(8,128)(2,1)}, bf16[656,128]{1,0:T(8,128)(2,1)S(1)}, u32[]{:S(2)}, u32[]{:S(2)}) collective-permute-start(bf16[656,128]{1,0:T(8,128)(2,1)} %get-tuple-element.54), channel_id=1, source_target_pairs={{0,8},{4,12},{8,0},{12,4},{1,9},{5,13},{9,1},{13,5},{2,10},{6,14},... | collective-permute-start | bytes 503816 | tf_op jit(solution)/shard_map/ppermute | solution.py:438
  4.9 11.1 %collective-permute-start.2 = (bf16[656,128]{1,0:T(8,128)(2,1)}, bf16[656,128]{1,0:T(8,128)(2,1)S(1)}, u32[]{:S(2)}, u32[]{:S(2)}) collective-permute-start(bf16[656,128]{1,0:T(8,128)(2,1)} %get-tuple-element.55), channel_id=1, source_target_pairs={{0,12},{4,8},{8,4},{12,0},{1,13},{5,9},{9,5},{13,1},{2,14},{6,10},... | collective-permute-start | bytes 503816 | tf_op jit(solution)/shard_map/ppermute | solution.py:438
  6.4 1.7 %copy-start = (bf16[1280,1024]{1,0:T(8,128)(2,1)S(1)}, bf16[1280,1024]{1,0:T(8,128)(2,1)}, u32[]{:S(2)}) copy-start(bf16[1280,1024]{1,0:T(8,128)(2,1)} %wa.7) | copy-start | bytes 7864324
  8.1 1.7 %copy-start.2 = (bf16[1280,1024]{1,0:T(8,128)(2,1)S(1)}, bf16[1280,1024]{1,0:T(8,128)(2,1)}, u32[]{:S(2)}) copy-start(bf16[1280,1024]{1,0:T(8,128)(2,1)} %wf.7) | copy-start | bytes 7864324
  9.9 1.1 %copy-start.4 = (bf16[1,256,1280]{2,1,0:T(8,128)(2,1)S(1)}, bf16[1,256,1280]{2,1,0:T(8,128)(2,1)}, u32[]{:S(2)}) copy-start(bf16[1,256,1280]{2,1,0:T(8,128)(2,1)} %param.8) | copy-start | bytes 1966084
  11.0 0.7 copy-start.6
  11.7 11.7 %copy-start.1 = (bf16[1280,1024]{1,0:T(8,128)(2,1)S(1)}, bf16[1280,1024]{1,0:T(8,128)(2,1)}, u32[]{:S(2)}) copy-start(bf16[1280,1024]{1,0:T(8,128)(2,1)} %wa.7) | copy-start | bytes 7864324
  11.7 11.7 %copy-start.3 = (bf16[1280,1024]{1,0:T(8,128)(2,1)S(1)}, bf16[1280,1024]{1,0:T(8,128)(2,1)}, u32[]{:S(2)}) copy-start(bf16[1280,1024]{1,0:T(8,128)(2,1)} %wf.7) | copy-start | bytes 7864324
  15.9 9.0 %collective-permute-start.3 = (bf16[1296,128]{1,0:T(8,128)(2,1)S(1)}, bf16[1296,128]{1,0:T(8,128)(2,1)S(1)}, u32[]{:S(2)}, u32[]{:S(2)}) collective-permute-start(bf16[1296,128]{1,0:T(8,128)(2,1)S(1)} %collective-permute-done), channel_id=1, source_target_pairs={{0,1},{1,0},{2,3},{3,2},{4,5},{5,4},{6,7},{7,6},{8,9},{9,8},{10,11... | collective-permute-start | bytes 995336 | tf_op jit(solution)/shard_map/ppermute | solution.py:441
  21.3 3.6 %collective-permute-start.4 = (bf16[656,128]{1,0:T(8,128)(2,1)S(1)}, bf16[656,128]{1,0:T(8,128)(2,1)S(1)}, u32[]{:S(2)}, u32[]{:S(2)}) collective-permute-start(bf16[656,128]{1,0:T(8,128)(2,1)S(1)} %collective-permute-done.1), channel_id=1, source_target_pairs={{0,1},{1,0},{2,3},{3,2},{4,5},{5,4},{6,7},{7,6},{8,9},{9,8},{10,11... | collective-permute-start | bytes 503816 | tf_op jit(solution)/shard_map/ppermute | solution.py:441
  21.3 3.6 %collective-permute-start.5 = (bf16[656,128]{1,0:T(8,128)(2,1)S(1)}, bf16[656,128]{1,0:T(8,128)(2,1)S(1)}, u32[]{:S(2)}, u32[]{:S(2)}) collective-permute-start(bf16[656,128]{1,0:T(8,128)(2,1)S(1)} %collective-permute-done.2), channel_id=1, source_target_pairs={{0,1},{1,0},{2,3},{3,2},{4,5},{5,4},{6,7},{7,6},{8,9},{9,8},{10,11... | collective-permute-start | bytes 503816 | tf_op jit(solution)/shard_map/ppermute | solution.py:441
  21.8 10.0 %collective-permute-start.6 = (bf16[656,128]{1,0:T(8,128)(2,1)S(1)}, bf16[656,128]{1,0:T(8,128)(2,1)S(1)}, u32[]{:S(2)}, u32[]{:S(2)}) collective-permute-start(bf16[656,128]{1,0:T(8,128)(2,1)S(1)} %collective-permute-done.1), channel_id=1, source_target_pairs={{0,4},{4,0},{8,12},{12,8},{1,5},{5,1},{9,13},{13,9},{2,6},{6,2},{1... | collective-permute-start | bytes 503816 | tf_op jit(solution)/shard_map/ppermute | solution.py:438
  22.8 9.0 %collective-permute-start.7 = (bf16[656,128]{1,0:T(8,128)(2,1)S(1)}, bf16[656,128]{1,0:T(8,128)(2,1)S(1)}, u32[]{:S(2)}, u32[]{:S(2)}) collective-permute-start(bf16[656,128]{1,0:T(8,128)(2,1)S(1)} %collective-permute-done.2), channel_id=1, source_target_pairs={{0,4},{4,0},{8,12},{12,8},{1,5},{5,1},{9,13},{13,9},{2,6},{6,2},{1... | collective-permute-start | bytes 503816 | tf_op jit(solution)/shard_map/ppermute | solution.py:438
  24.9 1.6 %copy-start.5 = (s32[1,256]{1,0:T(1,128)S(1)}, s32[1,256]{1,0:T(1,128)}, u32[]{:S(2)}) copy-start(s32[1,256]{1,0:T(1,128)} %refs_4_.3) | copy-start | bytes 3076
  27.6 18.8 %collective-permute-start.8 = (bf16[48,1024]{1,0:T(8,128)(2,1)S(1)}, bf16[48,1024]{1,0:T(8,128)(2,1)S(1)}, u32[]{:S(2)}, u32[]{:S(2)}) collective-permute-start(bf16[48,1024]{1,0:T(8,128)(2,1)S(1)} %get-tuple-element.66), channel_id=1, source_target_pairs={{0,12},{1,13},{4,8},{5,9},{8,4},{9,5},{12,0},{13,1},{2,14},{3,15},... | collective-permute-start | bytes 294920 | tf_op jit(solution)/shard_map/ppermute | solution.py:453
  30.0 18.2 %collective-permute-start.10 = (bf16[48,1024]{1,0:T(8,128)(2,1)S(1)}, bf16[48,1024]{1,0:T(8,128)(2,1)S(1)}, u32[]{:S(2)}, u32[]{:S(2)}) collective-permute-start(bf16[48,1024]{1,0:T(8,128)(2,1)S(1)} %get-tuple-element.68), channel_id=1, source_target_pairs={{0,8},{1,9},{4,12},{5,13},{8,0},{9,1},{12,4},{13,5},{2,10},{3,11},... | collective-permute-start | bytes 294920 | tf_op jit(solution)/shard_map/ppermute | solution.py:453
  34.7 10.8 %collective-permute-start.9 = (bf16[48,1024]{1,0:T(8,128)(2,1)S(1)}, bf16[48,1024]{1,0:T(8,128)(2,1)S(1)}, u32[]{:S(2)}, u32[]{:S(2)}) collective-permute-start(bf16[48,1024]{1,0:T(8,128)(2,1)S(1)} %get-tuple-element.81), channel_id=1, source_target_pairs={{0,13},{1,12},{4,9},{5,8},{8,5},{9,4},{12,1},{13,0},{2,15},{3,14},... | collective-permute-start | bytes 294920 | tf_op jit(solution)/shard_map/ppermute | solution.py:453
  35.7 12.5 %collective-permute-start.11 = (bf16[48,1024]{1,0:T(8,128)(2,1)S(1)}, bf16[48,1024]{1,0:T(8,128)(2,1)S(1)}, u32[]{:S(2)}, u32[]{:S(2)}) collective-permute-start(bf16[48,1024]{1,0:T(8,128)(2,1)S(1)} %get-tuple-element.82), channel_id=1, source_target_pairs={{0,9},{1,8},{4,13},{5,12},{8,1},{9,0},{12,5},{13,4},{2,11},{3,10},... | collective-permute-start | bytes 294920 | tf_op jit(solution)/shard_map/ppermute | solution.py:453
  40.8 1.3 %copy-start.8 = (bf16[8192]{0:T(1024)(128)(2,1)S(1)}, bf16[8192]{0:T(1024)(128)(2,1)}, u32[]{:S(2)}) copy-start(bf16[8192]{0:T(1024)(128)(2,1)} %param.15) | copy-start | bytes 49156
  41.5 8.4 %copy-start.7 = (s32[1,256]{1,0:T(1,128)S(1)}, s32[1,256]{1,0:T(1,128)}, u32[]{:S(2)}) copy-start(s32[1,256]{1,0:T(1,128)} %get-tuple-element.52.parity) | copy-start | bytes 3076
  41.5 35.3 %collective-permute-start.14 = (bf16[256,1024]{1,0:T(8,128)(2,1)S(1)}, bf16[256,1024]{1,0:T(8,128)(2,1)S(1)}, u32[]{:S(2)}, u32[]{:S(2)}) collective-permute-start(bf16[256,1024]{1,0:T(8,128)(2,1)S(1)} %select.2), channel_id=1, source_target_pairs={{0,4},{4,0},{8,12},{12,8},{1,5},{5,1},{9,13},{13,9},{2,6},{6,2},{1... | collective-permute-start | bytes 1572872 | tf_op jit(solution)/shard_map/ppermute | solution.py:438
  45.5 33.8 %collective-permute-start.15 = (bf16[80,1024]{1,0:T(8,128)(2,1)S(1)}, bf16[80,1024]{1,0:T(8,128)(2,1)S(1)}, u32[]{:S(2)}, u32[]{:S(2)}) collective-permute-start(bf16[80,1024]{1,0:T(8,128)(2,1)S(1)} %get-tuple-element.77), channel_id=1, source_target_pairs={{0,8},{1,9},{4,12},{5,13},{8,0},{9,1},{12,4},{13,5},{2,10},{3,11},... | collective-permute-start | bytes 491528 | tf_op jit(solution)/shard_map/ppermute | solution.py:453
  46.4 32.9 %collective-permute-start.16 = (bf16[80,1024]{1,0:T(8,128)(2,1)S(1)}, bf16[80,1024]{1,0:T(8,128)(2,1)S(1)}, u32[]{:S(2)}, u32[]{:S(2)}) collective-permute-start(bf16[80,1024]{1,0:T(8,128)(2,1)S(1)} %get-tuple-element.93), channel_id=1, source_target_pairs={{0,9},{1,8},{4,13},{5,12},{8,1},{9,0},{12,5},{13,4},{2,11},{3,10},... | collective-permute-start | bytes 491528 | tf_op jit(solution)/shard_map/ppermute | solution.py:453
  48.2 23.8 %collective-permute-start.12 = (bf16[80,1024]{1,0:T(8,128)(2,1)S(1)}, bf16[80,1024]{1,0:T(8,128)(2,1)S(1)}, u32[]{:S(2)}, u32[]{:S(2)}) collective-permute-start(bf16[80,1024]{1,0:T(8,128)(2,1)S(1)} %get-tuple-element.84), channel_id=1, source_target_pairs={{0,12},{1,13},{4,8},{5,9},{8,4},{9,5},{12,0},{13,1},{2,14},{3,15},... | collective-permute-start | bytes 491528 | tf_op jit(solution)/shard_map/ppermute | solution.py:453
  48.9 27.4 %collective-permute-start.13 = (bf16[80,1024]{1,0:T(8,128)(2,1)S(1)}, bf16[80,1024]{1,0:T(8,128)(2,1)S(1)}, u32[]{:S(2)}, u32[]{:S(2)}) collective-permute-start(bf16[80,1024]{1,0:T(8,128)(2,1)S(1)} %get-tuple-element.86), channel_id=1, source_target_pairs={{0,13},{1,12},{4,9},{5,8},{8,5},{9,4},{12,1},{13,0},{2,15},{3,14},... | collective-permute-start | bytes 491528 | tf_op jit(solution)/shard_map/ppermute | solution.py:453

commit v12 on v11

--- a/solution.py
+++ b/solution.py
@@ -10,6 +10,7 @@
 VMEM = pl.BlockSpec(memory_space=pltpu.VMEM)
 HBM = pl.BlockSpec(memory_space=pltpu.HBM)
 PARAMS = pltpu.CompilerParams(vmem_limit_bytes=12 << 20)
+SUM_FLOPS = 1 << 35
 BF16, F32, I32 = jnp.bfloat16, jnp.float32, jnp.int32
 
 
@@ -324,7 +325,7 @@
         in_specs=[VMEM] * (1 + len(slots)),
         out_specs=[VMEM] * 2,
         compiler_params=PARAMS,
-        cost_estimate=cost(1 << 34, 0),
+        cost_estimate=cost(SUM_FLOPS, 0),
         name="order_of",
     )(parity, *slots)
 
@@ -351,7 +352,7 @@
         in_specs=[VMEM] * len(operands),
         out_specs=[VMEM] * 3,
         compiler_params=PARAMS,
-        cost_estimate=cost(1 << 34, 0),
+        cost_estimate=cost(SUM_FLOPS, 0),
         name="place",
     )(*operands)
 
@@ -384,7 +385,7 @@
         in_specs=[VMEM] * len(operands),
         out_specs=VMEM,
         compiler_params=PARAMS,
-        cost_estimate=cost(1 << 34, 0),
+        cost_estimate=cost(SUM_FLOPS, 0),
         name="squares",
     )(*operands)
 
@@ -487,9 +488,8 @@
         for m in (3, 2):
             chosen = packet(m, early, blocks, slots, half - size, True)
             slots[0] = after(slots[0], chosen[0])
-            if m == 3:
-                joined = lax.optimization_barrier((*chosen, *sent[3], *sent[2]))
-                chosen, sent[3], sent[2] = joined[:2], list(joined[2:4]), list(joined[4:])
+            joined = lax.optimization_barrier((*chosen, *sent[3], *sent[2]))
+            chosen, sent[3], sent[2] = joined[:2], list(joined[2:4]), list(joined[4:])
             rest[m] = [to_core(piece, m, d) for d, piece in enumerate(chosen)]
 
         order3, order2 = order_of(size, parity, slots, half)

time: 81.6 us -> 81.6 us (level)
  the two profiles are of different devices: /device:TPU:9 before, /device:TPU:0 now
where the time goes in v12:
time: 81.6 us; the launch traced here: 81.2 us
  waiting for transfers between devices  26.7 us (33%)
  starting transfers between devices  20.6 us (25%)
  Pallas kernels  18.2 us (22%)
  blocking collectives  8.79 us (11%)
  local copies, waits for them, and re-layouts  6.67 us (8%)
    ppermute x8, waiting for transfers between devices, to_core(): return lax.ppermute(x, ('ctx', 'tp'), pairs)  18.4 us
    ppermute x8, starting transfers between devices, to_core(): return lax.ppermute(x, ('ctx', 'tp'), pairs)  11 us
    ppermute x6, starting transfers between devices, over_ctx(): return lax.ppermute(x, 'ctx', [(i, i ^ m) for i in range(n)])  9.06 us
    ppermute x6, waiting for transfers between devices, over_ctx(): return lax.ppermute(x, 'ctx', [(i, i ^ m) for i in range(n)])  8.29 us
    unnamed x18, local copies, waits for them, and re-layouts  5.27 us
    pallas_call x4, Pallas kernels, packet(): pl.pallas_call(functools.partial(packet_kernel, m, early, len(blocks), se...  4.83 us
    pallas_call x3, Pallas kernels, project_parts(): pl.pallas_call(project_parts_kernel, out_shape=[jax.ShapeDtypeStruct((row...  4.76 us
    all_gather x2, blocking collectives, body(): take([lax.all_gather(part, 'tp', axis=0) for part in shared])  4.07 us
  transfers between devices with their start and end apart: 17, of which 9 were waited for; matrix products, arithmetic and copies ran while one was open for 2% of the time, Pallas kernels for 17%

profile of v12, /device:TPU:0, one launch (start us, length us, event | category | flops | bytes accessed | tf_op | source)
XLA Modules:
  0.0 81.2 jit_solution(10110991534354183824)
XLA Ops:
  0.0 2.3 %to_send.1 = (bf16[1296,128]{1,0:T(8,128)(2,1)}, bf16[656,128]{1,0:T(8,128)(2,1)}, bf16[656,128]{1,0:T(8,128)(2,1)}, s32[1,256]{1,0:T(1,128)}) custom-call(bf16[256,1280]{1,0:T(8,128)(2,1)} %bitcast.12, s32[1,256]{1,0:T(1,128)} %refs_4_.3, s32[1,256]{1,0:T(1,128)} %kind.3), custom_call_target="tpu_custom_call" | custom-call | bytes 40960 | tf_op jit(solution)/shard_map/to_send/pallas_call | solution.py:109
  2.3 3.1 %collective-permute-start = (bf16[1296,128]{1,0:T(8,128)(2,1)}, bf16[1296,128]{1,0:T(8,128)(2,1)S(1)}, u32[]{:S(2)}, u32[]{:S(2)}) collective-permute-start(bf16[1296,128]{1,0:T(8,128)(2,1)} %get-tuple-element.59), channel_id=1, source_target_pairs={{0,4},{4,0},{8,12},{12,8},{1,5},{5,1},{9,13},{13,9},{2,6},{6,2},{1... | collective-permute-start | bytes 995336 | tf_op jit(solution)/shard_map/ppermute | solution.py:439
  5.4 2.6 %collective-permute-start.1 = (bf16[656,128]{1,0:T(8,128)(2,1)}, bf16[656,128]{1,0:T(8,128)(2,1)S(1)}, u32[]{:S(2)}, u32[]{:S(2)}) collective-permute-start(bf16[656,128]{1,0:T(8,128)(2,1)} %get-tuple-element.60), channel_id=1, source_target_pairs={{0,8},{4,12},{8,0},{12,4},{1,9},{5,13},{9,1},{13,5},{2,10},{6,14},... | collective-permute-start | bytes 503816 | tf_op jit(solution)/shard_map/ppermute | solution.py:439
  8.0 0.7 broadcast_in_dim.31.ba
  8.7 0.7 broadcast_in_dim.32.bf
  9.4 1.7 %copy-done = bf16[1280,1024]{1,0:T(8,128)(2,1)S(1)} copy-done((bf16[1280,1024]{1,0:T(8,128)(2,1)S(1)}, bf16[1280,1024]{1,0:T(8,128)(2,1)}, u32[]{:S(2)}) %copy-start) | copy-done | bytes 2621464
  11.1 1.7 %copy-done.2 = bf16[1280,1024]{1,0:T(8,128)(2,1)S(1)} copy-done((bf16[1280,1024]{1,0:T(8,128)(2,1)S(1)}, bf16[1280,1024]{1,0:T(8,128)(2,1)}, u32[]{:S(2)}) %copy-start.2) | copy-done | bytes 2621464
  12.9 1.1 %copy-done.4 = bf16[1,256,1280]{2,1,0:T(8,128)(2,1)S(1)} copy-done((bf16[1,256,1280]{2,1,0:T(8,128)(2,1)S(1)}, bf16[1,256,1280]{2,1,0:T(8,128)(2,1)}, u32[]{:S(2)}) %copy-start.4) | copy-done | bytes 655384
  13.9 0.7 copy-done.6
  14.6 1.6 %project_own.1.refs_0_ = bf16[256,1024]{1,0:T(8,128)(2,1)S(1)} custom-call(s32[1,256]{1,0:T(1,128)S(1)} %copy-done.6, bf16[256,1280]{1,0:T(8,128)(2,1)S(1)} %bitcast.13, bf16[1280,1024]{1,0:T(8,128)(2,1)S(1)} %copy-done, bf16[1280,1024]{1,0:T(8,128)(2,1)S(1)} %copy-done.2, bf16[1,1024]{1,0:T(2,128)(2,1)S(1)} %broadcast_in_dim.31.ba, ...), custom_call_target="tpu_custom_call" | custom-call | flops 83886080 | bytes 327680 | tf_op jit(solution)/shard_map/project_own/pallas_call | solution.py:147
  16.2 1.3 %collective-permute-done.1 = bf16[656,128]{1,0:T(8,128)(2,1)S(1)} collective-permute-done((bf16[656,128]{1,0:T(8,128)(2,1)}, bf16[656,128]{1,0:T(8,128)(2,1)S(1)}, u32[]{:S(2)}, u32[]{:S(2)}) %collective-permute-start.1) | collective-permute-done | bytes 167968 | tf_op jit(solution)/shard_map/ppermute | solution.py:439
  17.6 5.3 %collective-permute-done.2 = bf16[656,128]{1,0:T(8,128)(2,1)S(1)} collective-permute-done((bf16[656,128]{1,0:T(8,128)(2,1)}, bf16[656,128]{1,0:T(8,128)(2,1)S(1)}, u32[]{:S(2)}, u32[]{:S(2)}) %collective-permute-start.2) | collective-permute-done | bytes 167968 | tf_op jit(solution)/shard_map/ppermute | solution.py:439
  22.9 0.5 collective-permute-start.4
  23.4 0.8 collective-permute-start.6
  24.2 1.3 %collective-permute-start.7 = (bf16[656,128]{1,0:T(8,128)(2,1)S(1)}, bf16[656,128]{1,0:T(8,128)(2,1)S(1)}, u32[]{:S(2)}, u32[]{:S(2)}) collective-permute-start(bf16[656,128]{1,0:T(8,128)(2,1)S(1)} %collective-permute-done.2), channel_id=1, source_target_pairs={{0,4},{4,0},{8,12},{12,8},{1,5},{5,1},{9,13},{13,9},{2,6},{6,2},{1... | collective-permute-start | bytes 503816 | tf_op jit(solution)/shard_map/ppermute | solution.py:439
  25.5 1.6 %project_parts.3 = (bf16[256,1024]{1,0:T(8,128)(2,1)S(1)}, s32[1,256]{1,0:T(1,128)S(1)}) custom-call(bf16[1280,1024]{1,0:T(8,128)(2,1)S(1)} %copy-done.1, bf16[1280,1024]{1,0:T(8,128)(2,1)S(1)} %copy-done.3, bf16[1,1024]{1,0:T(2,128)(2,1)S(1)} %broadcast_in_dim.31.ba, bf16[1,1024]{1,0:T(2,128)(2,1)S(1)} %broadcast_in_dim.32.bf, ...), custom_call_target="tpu_custom_call" | custom-call | flops 83886080 | bytes 327680 | tf_op jit(solution)/shard_map/project_parts/pallas_call | solution.py:177
  27.1 1.6 %project_parts.4 = (bf16[256,1024]{1,0:T(8,128)(2,1)S(1)}, s32[1,256]{1,0:T(1,128)S(1)}) custom-call(bf16[1280,1024]{1,0:T(8,128)(2,1)S(1)} %copy-done.1, bf16[1280,1024]{1,0:T(8,128)(2,1)S(1)} %copy-done.3, bf16[1,1024]{1,0:T(2,128)(2,1)S(1)} %broadcast_in_dim.31.ba, bf16[1,1024]{1,0:T(2,128)(2,1)S(1)} %broadcast_in_dim.32.bf, ...), custom_call_target="tpu_custom_call" | custom-call | flops 83886080 | bytes 327680 | tf_op jit(solution)/shard_map/project_parts/pallas_call | solution.py:177
  28.7 1.0 %packet.4 = (bf16[48,1024]{1,0:T(8,128)(2,1)S(1)}, bf16[48,1024]{1,0:T(8,128)(2,1)S(1)}) custom-call(bf16[256,1024]{1,0:T(8,128)(2,1)S(1)} %project_own.1.refs_0_, bf16[256,1024]{1,0:T(8,128)(2,1)S(1)} %get-tuple-element.65.refs_1_, bf16[256,1024]{1,0:T(8,128)(2,1)S(1)} %get-tuple-element.69.refs_2_, s32[1,256]{1,0:T(1,128)S(1)} %copy-done.5, ...), custom_call_target="tpu_custom_call" | custom-call | flops 9437184 | bytes 98304 | tf_op jit(solution)/shard_map/packet/pallas_call | solution.py:276
  29.8 1.5 %collective-permute-start.8 = (bf16[48,1024]{1,0:T(8,128)(2,1)S(1)}, bf16[48,1024]{1,0:T(8,128)(2,1)S(1)}, u32[]{:S(2)}, u32[]{:S(2)}) collective-permute-start(bf16[48,1024]{1,0:T(8,128)(2,1)S(1)} %get-tuple-element.72), channel_id=1, source_target_pairs={{0,12},{1,13},{4,8},{5,9},{8,4},{9,5},{12,0},{13,1},{2,14},{3,15},... | collective-permute-start | bytes 294920 | tf_op jit(solution)/shard_map/ppermute | solution.py:454
  31.3 1.0 %packet.5 = (bf16[48,1024]{1,0:T(8,128)(2,1)S(1)}, bf16[48,1024]{1,0:T(8,128)(2,1)S(1)}) custom-call(bf16[256,1024]{1,0:T(8,128)(2,1)S(1)} %project_own.1.refs_0_, bf16[256,1024]{1,0:T(8,128)(2,1)S(1)} %get-tuple-element.65.refs_1_, bf16[256,1024]{1,0:T(8,128)(2,1)S(1)} %get-tuple-element.69.refs_2_, s32[1,256]{1,0:T(1,128)S(1)} %copy-done.5, ...), custom_call_target="tpu_custom_call" | custom-call | flops 9437184 | bytes 98304 | tf_op jit(solution)/shard_map/packet/pallas_call | solution.py:276
  32.4 0.8 %collective-permute-start.10 = (bf16[48,1024]{1,0:T(8,128)(2,1)S(1)}, bf16[48,1024]{1,0:T(8,128)(2,1)S(1)}, u32[]{:S(2)}, u32[]{:S(2)}) collective-permute-start(bf16[48,1024]{1,0:T(8,128)(2,1)S(1)} %get-tuple-element.74), channel_id=1, source_target_pairs={{0,8},{1,9},{4,12},{5,13},{8,0},{9,1},{12,4},{13,5},{2,10},{3,11},... | collective-permute-start | bytes 294920 | tf_op jit(solution)/shard_map/ppermute | solution.py:454
  33.2 0.5 collective-permute-done.7
  33.7 2.0 %all-gather = bf16[1312,128]{1,0:T(8,128)(2,1)S(1)} all-gather(bf16[656,128]{1,0:T(8,128)(2,1)S(1)} %collective-permute-done.6), channel_id=2, replica_groups=mesh['groups'=2,'ctx'=4,'enc'=2,'tp'=2] {'tp'}, dimensions={0}, use_global_device_ids=true | all-gather | bytes 503808 | tf_op jit(solution)/shard_map/all_gather | solution.py:482
  35.8 1.7 %collective-permute-start.9 = (bf16[48,1024]{1,0:T(8,128)(2,1)S(1)}, bf16[48,1024]{1,0:T(8,128)(2,1)S(1)}, u32[]{:S(2)}, u32[]{:S(2)}) collective-permute-start(bf16[48,1024]{1,0:T(8,128)(2,1)S(1)} %get-tuple-element.88), channel_id=1, source_target_pairs={{0,13},{1,12},{4,9},{5,8},{8,5},{9,4},{12,1},{13,0},{2,15},{3,14},... | collective-permute-start | bytes 294920 | tf_op jit(solution)/shard_map/ppermute | solution.py:454
  37.5 1.1 %collective-permute-start.11 = (bf16[48,1024]{1,0:T(8,128)(2,1)S(1)}, bf16[48,1024]{1,0:T(8,128)(2,1)S(1)}, u32[]{:S(2)}, u32[]{:S(2)}) collective-permute-start(bf16[48,1024]{1,0:T(8,128)(2,1)S(1)} %get-tuple-element.89), channel_id=1, source_target_pairs={{0,9},{1,8},{4,13},{5,12},{8,1},{9,0},{12,5},{13,4},{2,11},{3,10},... | collective-permute-start | bytes 294920 | tf_op jit(solution)/shard_map/ppermute | solution.py:454
  38.6 2.0 %all-gather.1 = bf16[1312,128]{1,0:T(8,128)(2,1)S(1)} all-gather(bf16[656,128]{1,0:T(8,128)(2,1)S(1)} %collective-permute-done.7), channel_id=3, replica_groups=mesh['groups'=2,'ctx'=4,'enc'=2,'tp'=2] {'tp'}, dimensions={0}, use_global_device_ids=true | all-gather | bytes 503808 | tf_op jit(solution)/shard_map/all_gather | solution.py:482
  40.6 1.6 %project_parts.5 = (bf16[256,1024]{1,0:T(8,128)(2,1)S(1)}, s32[1,256]{1,0:T(1,128)S(1)}) custom-call(bf16[1280,1024]{1,0:T(8,128)(2,1)S(1)} %copy-done.1, bf16[1280,1024]{1,0:T(8,128)(2,1)S(1)} %copy-done.3, bf16[1,1024]{1,0:T(2,128)(2,1)S(1)} %broadcast_in_dim.31.ba, bf16[1,1024]{1,0:T(2,128)(2,1)S(1)} %broadcast_in_dim.32.bf, ...), custom_call_target="tpu_custom_call" | custom-call | flops 83886080 | bytes 327680 | tf_op jit(solution)/shard_map/project_parts/pallas_call | solution.py:177
  42.2 0.7 select.2
  43.0 1.4 %collective-permute-start.14 = (bf16[256,1024]{1,0:T(8,128)(2,1)S(1)}, bf16[256,1024]{1,0:T(8,128)(2,1)S(1)}, u32[]{:S(2)}, u32[]{:S(2)}) collective-permute-start(bf16[256,1024]{1,0:T(8,128)(2,1)S(1)} %select.2), channel_id=1, source_target_pairs={{0,4},{4,0},{8,12},{12,8},{1,5},{5,1},{9,13},{13,9},{2,6},{6,2},{1... | collective-permute-start | bytes 1572872 | tf_op jit(solution)/shard_map/ppermute | solution.py:439
  44.3 1.4 %packet.6 = (bf16[80,1024]{1,0:T(8,128)(2,1)S(1)}, bf16[80,1024]{1,0:T(8,128)(2,1)S(1)}) custom-call(bf16[256,1024]{1,0:T(8,128)(2,1)S(1)} %project_own.1.refs_0_, bf16[256,1024]{1,0:T(8,128)(2,1)S(1)} %get-tuple-element.65.refs_1_, bf16[256,1024]{1,0:T(8,128)(2,1)S(1)} %get-tuple-element.69.refs_2_, bf16[256,1024]{1,0:T(8,128)(2,1)S(1)} %get-tuple-element.78.refs_3_, ...), custom_call_target="tpu_custom_call" | custom-call | flops 20971520 | bytes 131072 | tf_op jit(solution)/shard_map/packet/pallas_call | solution.py:276
  45.7 1.4 %packet.7 = (bf16[80,1024]{1,0:T(8,128)(2,1)S(1)}, bf16[80,1024]{1,0:T(8,128)(2,1)S(1)}) custom-call(bf16[256,1024]{1,0:T(8,128)(2,1)S(1)} %project_own.1.refs_0_, bf16[256,1024]{1,0:T(8,128)(2,1)S(1)} %get-tuple-element.65.refs_1_, bf16[256,1024]{1,0:T(8,128)(2,1)S(1)} %get-tuple-element.69.refs_2_, bf16[256,1024]{1,0:T(8,128)(2,1)S(1)} %get-tuple-element.78.refs_3_, ...), custom_call_target="tpu_custom_call" | custom-call | flops 20971520 | bytes 131072 | tf_op jit(solution)/shard_map/packet/pallas_call | solution.py:276
  47.1 2.6 %collective-permute-done.11.refs_4_ = bf16[48,1024]{1,0:T(8,128)(2,1)S(1)} collective-permute-done((bf16[48,1024]{1,0:T(8,128)(2,1)S(1)}, bf16[48,1024]{1,0:T(8,128)(2,1)S(1)}, u32[]{:S(2)}, u32[]{:S(2)}) %collective-permute-start.11) | collective-permute-done | bytes 98336 | tf_op jit(solution)/shard_map/ppermute | solution.py:454
  49.7 1.5 %collective-permute-start.12 = (bf16[80,1024]{1,0:T(8,128)(2,1)S(1)}, bf16[80,1024]{1,0:T(8,128)(2,1)S(1)}, u32[]{:S(2)}, u32[]{:S(2)}) collective-permute-start(bf16[80,1024]{1,0:T(8,128)(2,1)S(1)} %get-tuple-element.95), channel_id=1, source_target_pairs={{0,12},{1,13},{4,8},{5,9},{8,4},{9,5},{12,0},{13,1},{2,14},{3,15},... | collective-permute-start | bytes 491528 | tf_op jit(solution)/shard_map/ppermute | solution.py:454
  51.2 1.7 %collective-permute-start.13 = (bf16[80,1024]{1,0:T(8,128)(2,1)S(1)}, bf16[80,1024]{1,0:T(8,128)(2,1)S(1)}, u32[]{:S(2)}, u32[]{:S(2)}) collective-permute-start(bf16[80,1024]{1,0:T(8,128)(2,1)S(1)} %get-tuple-element.97), channel_id=1, source_target_pairs={{0,13},{1,12},{4,9},{5,8},{8,5},{9,4},{12,1},{13,0},{2,15},{3,14},... | collective-permute-start | bytes 491528 | tf_op jit(solution)/shard_map/ppermute | solution.py:454
  52.9 0.6 order_of.1
  53.5 0.7 select.3
  54.2 2.5 %all-gather.2 = bf16[256,1024]{1,0:T(8,128)(2,1)S(1)} all-gather(bf16[128,1024]{1,0:T(8,128)(2,1)S(1)} %get-tuple-element.100), channel_id=4, replica_groups=mesh['groups'=2,'ctx'=4,'enc'=2,'tp'=2] {'tp'}, dimensions={0}, use_global_device_ids=true | all-gather | bytes 786432 | tf_op jit(solution)/shard_map/all_gather | solution.py:458
  56.8 2.6 %collective-permute-start.16 = (bf16[80,1024]{1,0:T(8,128)(2,1)S(1)}, bf16[80,1024]{1,0:T(8,128)(2,1)S(1)}, u32[]{:S(2)}, u32[]{:S(2)}) collective-permute-start(bf16[80,1024]{1,0:T(8,128)(2,1)S(1)} %get-tuple-element.105), channel_id=1, source_target_pairs={{0,9},{1,8},{4,13},{5,12},{8,1},{9,0},{12,5},{13,4},{2,11},{3,10},... | collective-permute-start | bytes 491528 | tf_op jit(solution)/shard_map/ppermute | solution.py:454
  59.4 3.3 %collective-permute-done.12.refs_2_ = bf16[80,1024]{1,0:T(8,128)(2,1)S(1)} collective-permute-done((bf16[80,1024]{1,0:T(8,128)(2,1)S(1)}, bf16[80,1024]{1,0:T(8,128)(2,1)S(1)}, u32[]{:S(2)}, u32[]{:S(2)}) %collective-permute-start.12) | collective-permute-done | bytes 163872 | tf_op jit(solution)/shard_map/ppermute | solution.py:454
  62.7 1.9 %collective-permute-done.13.refs_4_ = bf16[80,1024]{1,0:T(8,128)(2,1)S(1)} collective-permute-done((bf16[80,1024]{1,0:T(8,128)(2,1)S(1)}, bf16[80,1024]{1,0:T(8,128)(2,1)S(1)}, u32[]{:S(2)}, u32[]{:S(2)}) %collective-permute-start.13) | collective-permute-done | bytes 163872 | tf_op jit(solution)/shard_map/ppermute | solution.py:454
  64.6 0.4 place.2
  65.0 0.2 squares.2.refs_0_
  65.2 1.1 %collective-permute-done.14.refs_1_.refs_2_ = bf16[256,1024]{1,0:T(8,128)(2,1)S(1)} collective-permute-done((bf16[256,1024]{1,0:T(8,128)(2,1)S(1)}, bf16[256,1024]{1,0:T(8,128)(2,1)S(1)}, u32[]{:S(2)}, u32[]{:S(2)}) %collective-permute-start.14) | collective-permute-done | bytes 524320 | tf_op jit(solution)/shard_map/ppermute | solution.py:439
  66.3 2.2 %all-gather.3 = bf16[256,1024]{1,0:T(8,128)(2,1)S(1)} all-gather(bf16[128,1024]{1,0:T(8,128)(2,1)S(1)} %slice.4), channel_id=5, replica_groups=mesh['groups'=2,'ctx'=4,'enc'=2,'tp'=2] {'tp'}, dimensions={0}, use_global_device_ids=true | all-gather | bytes 786432 | tf_op jit(solution)/shard_map/all_gather | solution.py:461
  68.6 7.2 %collective-permute-done.15.refs_3_ = bf16[80,1024]{1,0:T(8,128)(2,1)S(1)} collective-permute-done((bf16[80,1024]{1,0:T(8,128)(2,1)S(1)}, bf16[80,1024]{1,0:T(8,128)(2,1)S(1)}, u32[]{:S(2)}, u32[]{:S(2)}) %collective-permute-start.15) | collective-permute-done | bytes 163872 | tf_op jit(solution)/shard_map/ppermute | solution.py:454
  75.8 3.4 %collective-permute-done.16.refs_5_ = bf16[80,1024]{1,0:T(8,128)(2,1)S(1)} collective-permute-done((bf16[80,1024]{1,0:T(8,128)(2,1)S(1)}, bf16[80,1024]{1,0:T(8,128)(2,1)S(1)}, u32[]{:S(2)}, u32[]{:S(2)}) %collective-permute-start.16) | collective-permute-done | bytes 163872 | tf_op jit(solution)/shard_map/ppermute | solution.py:454
  79.2 0.4 place.3
  79.6 1.6 %norm.1 = bf16[128,8192]{1,0:T(8,128)(2,1)} custom-call(bf16[1,8192]{1,0:T(2,128)(2,1)S(1)} %broadcast_in_dim.30.gain, f32[128,1]{1,0:T(8,128)S(1)} %get-tuple-element.106.before, bf16[128,1024]{1,0:T(8,128)(2,1)S(1)} %get-tuple-element.107.refs_0_, bf16[128,1024]{1,0:T(8,128)(2,1)S(1)} %get-tuple-element.108.refs_1_, ...), custom_call_target="tpu_custom_call" | custom-call | flops 262144 | bytes 262144 | tf_op jit(solution)/shard_map/norm/pallas_call | solution.py:416
  (29 shorter events, 0.3 us)
Async XLA Ops:
  2.3 20.6 %collective-permute-start = (bf16[1296,128]{1,0:T(8,128)(2,1)}, bf16[1296,128]{1,0:T(8,128)(2,1)S(1)}, u32[]{:S(2)}, u32[]{:S(2)}) collective-permute-start(bf16[1296,128]{1,0:T(8,128)(2,1)} %get-tuple-element.59), channel_id=1, source_target_pairs={{0,4},{4,0},{8,12},{12,8},{1,5},{5,1},{9,13},{13,9},{2,6},{6,2},{1... | collective-permute-start | bytes 995336 | tf_op jit(solution)/shard_map/ppermute | solution.py:439
  5.4 12.2 %collective-permute-start.1 = (bf16[656,128]{1,0:T(8,128)(2,1)}, bf16[656,128]{1,0:T(8,128)(2,1)S(1)}, u32[]{:S(2)}, u32[]{:S(2)}) collective-permute-start(bf16[656,128]{1,0:T(8,128)(2,1)} %get-tuple-element.60), channel_id=1, source_target_pairs={{0,8},{4,12},{8,0},{12,4},{1,9},{5,13},{9,1},{13,5},{2,10},{6,14},... | collective-permute-start | bytes 503816 | tf_op jit(solution)/shard_map/ppermute | solution.py:439
  8.0 14.9 %collective-permute-start.2 = (bf16[656,128]{1,0:T(8,128)(2,1)}, bf16[656,128]{1,0:T(8,128)(2,1)S(1)}, u32[]{:S(2)}, u32[]{:S(2)}) collective-permute-start(bf16[656,128]{1,0:T(8,128)(2,1)} %get-tuple-element.61), channel_id=1, source_target_pairs={{0,12},{4,8},{8,4},{12,0},{1,13},{5,9},{9,5},{13,1},{2,14},{6,10},... | collective-permute-start | bytes 503816 | tf_op jit(solution)/shard_map/ppermute | solution.py:439
  9.4 1.7 %copy-start = (bf16[1280,1024]{1,0:T(8,128)(2,1)S(1)}, bf16[1280,1024]{1,0:T(8,128)(2,1)}, u32[]{:S(2)}) copy-start(bf16[1280,1024]{1,0:T(8,128)(2,1)} %wa.7) | copy-start | bytes 7864324
  11.1 1.7 %copy-start.2 = (bf16[1280,1024]{1,0:T(8,128)(2,1)S(1)}, bf16[1280,1024]{1,0:T(8,128)(2,1)}, u32[]{:S(2)}) copy-start(bf16[1280,1024]{1,0:T(8,128)(2,1)} %wf.7) | copy-start | bytes 7864324
  12.9 1.1 %copy-start.4 = (bf16[1,256,1280]{2,1,0:T(8,128)(2,1)S(1)}, bf16[1,256,1280]{2,1,0:T(8,128)(2,1)}, u32[]{:S(2)}) copy-start(bf16[1,256,1280]{2,1,0:T(8,128)(2,1)} %param.8) | copy-start | bytes 1966084
  13.9 0.7 copy-start.6
  14.6 10.8 %copy-start.8 = (bf16[8192]{0:T(1024)(128)(2,1)S(1)}, bf16[8192]{0:T(1024)(128)(2,1)}, u32[]{:S(2)}) copy-start(bf16[8192]{0:T(1024)(128)(2,1)} %param.15) | copy-start | bytes 49156
  14.6 10.9 %copy-start.1 = (bf16[1280,1024]{1,0:T(8,128)(2,1)S(1)}, bf16[1280,1024]{1,0:T(8,128)(2,1)}, u32[]{:S(2)}) copy-start(bf16[1280,1024]{1,0:T(8,128)(2,1)} %wa.7) | copy-start | bytes 7864324
  14.6 10.9 %copy-start.3 = (bf16[1280,1024]{1,0:T(8,128)(2,1)S(1)}, bf16[1280,1024]{1,0:T(8,128)(2,1)}, u32[]{:S(2)}) copy-start(bf16[1280,1024]{1,0:T(8,128)(2,1)} %wf.7) | copy-start | bytes 7864324
  22.9 4.2 %collective-permute-start.3 = (bf16[1296,128]{1,0:T(8,128)(2,1)S(1)}, bf16[1296,128]{1,0:T(8,128)(2,1)S(1)}, u32[]{:S(2)}, u32[]{:S(2)}) collective-permute-start(bf16[1296,128]{1,0:T(8,128)(2,1)S(1)} %collective-permute-done), channel_id=1, source_target_pairs={{0,1},{1,0},{2,3},{3,2},{4,5},{5,4},{6,7},{7,6},{8,9},{9,8},{10,11... | collective-permute-start | bytes 995336 | tf_op jit(solution)/shard_map/ppermute | solution.py:442
  22.9 4.2 %collective-permute-start.4 = (bf16[656,128]{1,0:T(8,128)(2,1)S(1)}, bf16[656,128]{1,0:T(8,128)(2,1)S(1)}, u32[]{:S(2)}, u32[]{:S(2)}) collective-permute-start(bf16[656,128]{1,0:T(8,128)(2,1)S(1)} %collective-permute-done.1), channel_id=1, source_target_pairs={{0,1},{1,0},{2,3},{3,2},{4,5},{5,4},{6,7},{7,6},{8,9},{9,8},{10,11... | collective-permute-start | bytes 503816 | tf_op jit(solution)/shard_map/ppermute | solution.py:442
  23.4 3.7 %collective-permute-start.5 = (bf16[656,128]{1,0:T(8,128)(2,1)S(1)}, bf16[656,128]{1,0:T(8,128)(2,1)S(1)}, u32[]{:S(2)}, u32[]{:S(2)}) collective-permute-start(bf16[656,128]{1,0:T(8,128)(2,1)S(1)} %collective-permute-done.2), channel_id=1, source_target_pairs={{0,1},{1,0},{2,3},{3,2},{4,5},{5,4},{6,7},{7,6},{8,9},{9,8},{10,11... | collective-permute-start | bytes 503816 | tf_op jit(solution)/shard_map/ppermute | solution.py:442
  23.4 9.8 %collective-permute-start.6 = (bf16[656,128]{1,0:T(8,128)(2,1)S(1)}, bf16[656,128]{1,0:T(8,128)(2,1)S(1)}, u32[]{:S(2)}, u32[]{:S(2)}) collective-permute-start(bf16[656,128]{1,0:T(8,128)(2,1)S(1)} %collective-permute-done.1), channel_id=1, source_target_pairs={{0,4},{4,0},{8,12},{12,8},{1,5},{5,1},{9,13},{13,9},{2,6},{6,2},{1... | collective-permute-start | bytes 503816 | tf_op jit(solution)/shard_map/ppermute | solution.py:439
  24.2 9.5 %collective-permute-start.7 = (bf16[656,128]{1,0:T(8,128)(2,1)S(1)}, bf16[656,128]{1,0:T(8,128)(2,1)S(1)}, u32[]{:S(2)}, u32[]{:S(2)}) collective-permute-start(bf16[656,128]{1,0:T(8,128)(2,1)S(1)} %collective-permute-done.2), channel_id=1, source_target_pairs={{0,4},{4,0},{8,12},{12,8},{1,5},{5,1},{9,13},{13,9},{2,6},{6,2},{1... | collective-permute-start | bytes 503816 | tf_op jit(solution)/shard_map/ppermute | solution.py:439
  27.1 1.6 %copy-start.5 = (s32[1,256]{1,0:T(1,128)S(1)}, s32[1,256]{1,0:T(1,128)}, u32[]{:S(2)}) copy-start(s32[1,256]{1,0:T(1,128)} %refs_4_.3) | copy-start | bytes 3076
  29.8 17.3 %collective-permute-start.8 = (bf16[48,1024]{1,0:T(8,128)(2,1)S(1)}, bf16[48,1024]{1,0:T(8,128)(2,1)S(1)}, u32[]{:S(2)}, u32[]{:S(2)}) collective-permute-start(bf16[48,1024]{1,0:T(8,128)(2,1)S(1)} %get-tuple-element.72), channel_id=1, source_target_pairs={{0,12},{1,13},{4,8},{5,9},{8,4},{9,5},{12,0},{13,1},{2,14},{3,15},... | collective-permute-start | bytes 294920 | tf_op jit(solution)/shard_map/ppermute | solution.py:454
  32.4 17.3 %collective-permute-start.10 = (bf16[48,1024]{1,0:T(8,128)(2,1)S(1)}, bf16[48,1024]{1,0:T(8,128)(2,1)S(1)}, u32[]{:S(2)}, u32[]{:S(2)}) collective-permute-start(bf16[48,1024]{1,0:T(8,128)(2,1)S(1)} %get-tuple-element.74), channel_id=1, source_target_pairs={{0,8},{1,9},{4,12},{5,13},{8,0},{9,1},{12,4},{13,5},{2,10},{3,11},... | collective-permute-start | bytes 294920 | tf_op jit(solution)/shard_map/ppermute | solution.py:454
  35.8 11.3 %collective-permute-start.9 = (bf16[48,1024]{1,0:T(8,128)(2,1)S(1)}, bf16[48,1024]{1,0:T(8,128)(2,1)S(1)}, u32[]{:S(2)}, u32[]{:S(2)}) collective-permute-start(bf16[48,1024]{1,0:T(8,128)(2,1)S(1)} %get-tuple-element.88), channel_id=1, source_target_pairs={{0,13},{1,12},{4,9},{5,8},{8,5},{9,4},{12,1},{13,0},{2,15},{3,14},... | collective-permute-start | bytes 294920 | tf_op jit(solution)/shard_map/ppermute | solution.py:454
  37.5 12.2 %collective-permute-start.11 = (bf16[48,1024]{1,0:T(8,128)(2,1)S(1)}, bf16[48,1024]{1,0:T(8,128)(2,1)S(1)}, u32[]{:S(2)}, u32[]{:S(2)}) collective-permute-start(bf16[48,1024]{1,0:T(8,128)(2,1)S(1)} %get-tuple-element.89), channel_id=1, source_target_pairs={{0,9},{1,8},{4,13},{5,12},{8,1},{9,0},{12,5},{13,4},{2,11},{3,10},... | collective-permute-start | bytes 294920 | tf_op jit(solution)/shard_map/ppermute | solution.py:454
  42.9 10.0 %copy-start.7 = (s32[1,256]{1,0:T(1,128)S(1)}, s32[1,256]{1,0:T(1,128)}, u32[]{:S(2)}) copy-start(s32[1,256]{1,0:T(1,128)} %get-tuple-element.58.parity) | copy-start | bytes 3076
  43.0 23.3 %collective-permute-start.14 = (bf16[256,1024]{1,0:T(8,128)(2,1)S(1)}, bf16[256,1024]{1,0:T(8,128)(2,1)S(1)}, u32[]{:S(2)}, u32[]{:S(2)}) collective-permute-start(bf16[256,1024]{1,0:T(8,128)(2,1)S(1)} %select.2), channel_id=1, source_target_pairs={{0,4},{4,0},{8,12},{12,8},{1,5},{5,1},{9,13},{13,9},{2,6},{6,2},{1... | collective-permute-start | bytes 1572872 | tf_op jit(solution)/shard_map/ppermute | solution.py:439
  49.7 13.0 %collective-permute-start.12 = (bf16[80,1024]{1,0:T(8,128)(2,1)S(1)}, bf16[80,1024]{1,0:T(8,128)(2,1)S(1)}, u32[]{:S(2)}, u32[]{:S(2)}) collective-permute-start(bf16[80,1024]{1,0:T(8,128)(2,1)S(1)} %get-tuple-element.95), channel_id=1, source_target_pairs={{0,12},{1,13},{4,8},{5,9},{8,4},{9,5},{12,0},{13,1},{2,14},{3,15},... | collective-permute-start | bytes 491528 | tf_op jit(solution)/shard_map/ppermute | solution.py:454
  51.2 13.4 %collective-permute-start.13 = (bf16[80,1024]{1,0:T(8,128)(2,1)S(1)}, bf16[80,1024]{1,0:T(8,128)(2,1)S(1)}, u32[]{:S(2)}, u32[]{:S(2)}) collective-permute-start(bf16[80,1024]{1,0:T(8,128)(2,1)S(1)} %get-tuple-element.97), channel_id=1, source_target_pairs={{0,13},{1,12},{4,9},{5,8},{8,5},{9,4},{12,1},{13,0},{2,15},{3,14},... | collective-permute-start | bytes 491528 | tf_op jit(solution)/shard_map/ppermute | solution.py:454
  56.8 19.1 %collective-permute-start.15 = (bf16[80,1024]{1,0:T(8,128)(2,1)S(1)}, bf16[80,1024]{1,0:T(8,128)(2,1)S(1)}, u32[]{:S(2)}, u32[]{:S(2)}) collective-permute-start(bf16[80,1024]{1,0:T(8,128)(2,1)S(1)} %get-tuple-element.103), channel_id=1, source_target_pairs={{0,8},{1,9},{4,12},{5,13},{8,0},{9,1},{12,4},{13,5},{2,10},{3,11},... | collective-permute-start | bytes 491528 | tf_op jit(solution)/shard_map/ppermute | solution.py:454
  56.8 22.4 %collective-permute-start.16 = (bf16[80,1024]{1,0:T(8,128)(2,1)S(1)}, bf16[80,1024]{1,0:T(8,128)(2,1)S(1)}, u32[]{:S(2)}, u32[]{:S(2)}) collective-permute-start(bf16[80,1024]{1,0:T(8,128)(2,1)S(1)} %get-tuple-element.105), channel_id=1, source_target_pairs={{0,9},{1,8},{4,13},{5,12},{8,1},{9,0},{12,5},{13,4},{2,11},{3,10},... | collective-permute-start | bytes 491528 | tf_op jit(solution)/shard_map/ppermute | solution.py:454

commit v13 on v12

--- a/solution.py
+++ b/solution.py
@@ -425,6 +425,44 @@
     )(gain, before, *pieces)
 
 
+def last_kernel(far, whole, gain, before, order, *refs):
+    packets, pieces, (out, scaled, sems) = refs[:4], refs[4:10], refs[10:]
+    places, cols = scaled.shape[1:]
+    z, t = lax.axis_index("ctx"), lax.axis_index("tp")
+    total = before[...]
+    for k in range(2):
+        both = jnp.concatenate([packets[2 * k][...], packets[2 * k + 1][...]], axis=0)
+        wide = jnp.dot(order[...], both, preferred_element_type=F32)
+        scaled[k] = wide.astype(BF16)
+        total = total + jnp.sum(wide * wide, axis=1, keepdims=True)
+    scale = lax.rsqrt(total / (8 * cols) + 1e-06)
+    copies = []
+    for k, (m, d) in enumerate(far + whole):
+        block = jnp.bitwise_xor(z, m) * 2 + jnp.bitwise_xor(t, d)
+        at = pl.ds(pl.multiple_of(block * cols, cols), cols)
+        piece = scaled[k] if k < 2 else view(pieces[k - 2], places)[...]
+        scaled[k] = (piece.astype(F32) * scale * gain[:, at].astype(F32)).astype(BF16)
+        copies.append(pltpu.make_async_copy(scaled.at[k], out.at[:, at], sems.at[k]))
+        copies[k].start()
+    for copy in copies:
+        copy.wait()
+
+
+def place_and_norm(far, whole, gain, before, order, packets, pieces):
+    places, cols = before.shape[0], packets[0].shape[1]
+    operands = [gain, before, order, *packets, *pieces]
+    return pl.pallas_call(
+        functools.partial(last_kernel, far, whole),
+        out_shape=jax.ShapeDtypeStruct((places, 8 * cols), BF16),
+        in_specs=[VMEM] * len(operands),
+        out_specs=HBM,
+        scratch_shapes=[pltpu.VMEM((8, places, cols), BF16), pltpu.SemaphoreType.DMA((8,))],
+        compiler_params=PARAMS,
+        cost_estimate=cost(32 * places * cols, 32 * places * cols),
+        name="place_and_norm",
+    )(*operands)
+
+
 def after(x, *others):
     return lax.optimization_barrier((x, *others))[0]
 
@@ -485,7 +523,7 @@
         slots[0] = after(slots[0], chosen)
         pieces[1] = over_ctx(chosen, 1)
         rest = {}
-        for m in (3, 2):
+        for m in (2, 3):
             chosen = packet(m, early, blocks, slots, half - size, True)
             slots[0] = after(slots[0], chosen[0])
             joined = lax.optimization_barrier((*chosen, *sent[3], *sent[2]))
@@ -493,12 +531,14 @@
             rest[m] = [to_core(piece, m, d) for d, piece in enumerate(chosen)]
 
         order3, order2 = order_of(size, parity, slots, half)
+        packets = [sent[2][0], rest[2][0], sent[2][1], rest[2][1]]
+        pieces[2, 0], pieces[2, 1], total = place(None, order2, packets)
+        total = own_and_near(total)
         packets = [sent[3][0], rest[3][0], sent[3][1], rest[3][1]]
-        pieces[3, 0], pieces[3, 1], total = place(None, order3, packets)
-        total = own_and_near(total)
-        packets = [sent[2][0], rest[2][0], sent[2][1], rest[2][1]]
-        pieces[2, 0], pieces[2, 1], total = place(total, order2, packets)
-        order, fresh = [3, 1, 0, 2], ()
+        far, whole = ((3, 0), (3, 1)), ((2, 0), (2, 1), (1, 0), (1, 1), (0, 0), (0, 1))
+        whole_pieces = [pieces[at] for at in whole]
+        gain = norm_gain[None, :]
+        return place_and_norm(far, whole, gain, total, order3, packets, whole_pieces)[None]
     else:
         (mine,) = to_send((None,), rows, row_slot, row_kind)
         arrived = [over_ctx(mine, m) for m in range(1, n)]

time: 81.6 us -> 81.5 us (level); the launches traced: 81.2 us -> 79.9 us
  waiting for transfers between devices: 26.7 us -> 23.9 us
  blocking collectives: 8.79 us -> 10 us
    ppermute x8, waiting for transfers between devices: 18.4 us -> 16.7 us  [to_core(): return lax.ppermute(x, ('ctx', 'tp'), pairs)]
    all_gather x1, blocking collectives: 2.18 us -> 3.41 us  [own_and_near(): lax.all_gather(pair[half:], 'tp', axis=0)]
    ppermute x6, waiting for transfers between devices: 8.29 us -> 7.22 us  [over_ctx(): return lax.ppermute(x, 'ctx', [(i, i ^ m) for i in range(n)])]
  transfers between devices with their start and end apart: 17 -> 17, of which waited for: 9 -> 6; matrix products, arithmetic and copies ran while one was open for 2% -> 2% of each run, Pallas kernels for 17% -> 17%
where the time goes in v13:
time: 81.5 us; the launch traced here: 79.9 us
  waiting for transfers between devices  23.9 us (29%)
  starting transfers between devices  20.6 us (25%)
  Pallas kernels  18.5 us (23%)
  blocking collectives  10 us (12%)
  local copies, waits for them, and re-layouts  6.68 us (8%)
    ppermute x8, waiting for transfers between devices, to_core(): return lax.ppermute(x, ('ctx', 'tp'), pairs)  16.7 us
    ppermute x8, starting transfers between devices, to_core(): return lax.ppermute(x, ('ctx', 'tp'), pairs)  11 us
    ppermute x6, starting transfers between devices, over_ctx(): return lax.ppermute(x, 'ctx', [(i, i ^ m) for i in range(n)])  9.05 us
    ppermute x6, waiting for transfers between devices, over_ctx(): return lax.ppermute(x, 'ctx', [(i, i ^ m) for i in range(n)])  7.22 us
    unnamed x18, local copies, waits for them, and re-layouts  5.27 us
    pallas_call x4, Pallas kernels, packet(): pl.pallas_call(functools.partial(packet_kernel, m, early, len(blocks), se...  4.84 us
    pallas_call x3, Pallas kernels, project_parts(): pl.pallas_call(project_parts_kernel, out_shape=[jax.ShapeDtypeStruct((row...  4.77 us
    all_gather x2, blocking collectives, body(): take([lax.all_gather(part, 'tp', axis=0) for part in shared])  4.07 us
  transfers between devices with their start and end apart: 17, of which 6 were waited for; matrix products, arithmetic and copies ran while one was open for 2% of the time, Pallas kernels for 17%

profile of v13, /device:TPU:0, one launch (start us, length us, event | category | flops | bytes accessed | tf_op | source)
XLA Modules:
  0.0 79.9 jit_solution(15535664366864047978)
XLA Ops:
  0.0 2.3 %to_send.1 = (bf16[1296,128]{1,0:T(8,128)(2,1)}, bf16[656,128]{1,0:T(8,128)(2,1)}, bf16[656,128]{1,0:T(8,128)(2,1)}, s32[1,256]{1,0:T(1,128)}) custom-call(bf16[256,1280]{1,0:T(8,128)(2,1)} %bitcast.12, s32[1,256]{1,0:T(1,128)} %refs_4_.3, s32[1,256]{1,0:T(1,128)} %kind.3), custom_call_target="tpu_custom_call" | custom-call | bytes 40960 | tf_op jit(solution)/shard_map/to_send/pallas_call | solution.py:109
  2.3 3.1 %collective-permute-start = (bf16[1296,128]{1,0:T(8,128)(2,1)}, bf16[1296,128]{1,0:T(8,128)(2,1)S(1)}, u32[]{:S(2)}, u32[]{:S(2)}) collective-permute-start(bf16[1296,128]{1,0:T(8,128)(2,1)} %get-tuple-element.56), channel_id=1, source_target_pairs={{0,4},{4,0},{8,12},{12,8},{1,5},{5,1},{9,13},{13,9},{2,6},{6,2},{1... | collective-permute-start | bytes 995336 | tf_op jit(solution)/shard_map/ppermute | solution.py:477
  5.4 2.6 %collective-permute-start.1 = (bf16[656,128]{1,0:T(8,128)(2,1)}, bf16[656,128]{1,0:T(8,128)(2,1)S(1)}, u32[]{:S(2)}, u32[]{:S(2)}) collective-permute-start(bf16[656,128]{1,0:T(8,128)(2,1)} %get-tuple-element.57), channel_id=1, source_target_pairs={{0,8},{4,12},{8,0},{12,4},{1,9},{5,13},{9,1},{13,5},{2,10},{6,14},... | collective-permute-start | bytes 503816 | tf_op jit(solution)/shard_map/ppermute | solution.py:477
  8.0 0.0 collective-permute-start.2
  8.0 0.7 broadcast_in_dim.31.ba
  8.7 0.7 broadcast_in_dim.32.bf
  9.4 1.7 %copy-done = bf16[1280,1024]{1,0:T(8,128)(2,1)S(1)} copy-done((bf16[1280,1024]{1,0:T(8,128)(2,1)S(1)}, bf16[1280,1024]{1,0:T(8,128)(2,1)}, u32[]{:S(2)}) %copy-start) | copy-done | bytes 2621464
  11.1 1.7 %copy-done.2 = bf16[1280,1024]{1,0:T(8,128)(2,1)S(1)} copy-done((bf16[1280,1024]{1,0:T(8,128)(2,1)S(1)}, bf16[1280,1024]{1,0:T(8,128)(2,1)}, u32[]{:S(2)}) %copy-start.2) | copy-done | bytes 2621464
  12.9 1.1 %copy-done.4 = bf16[1,256,1280]{2,1,0:T(8,128)(2,1)S(1)} copy-done((bf16[1,256,1280]{2,1,0:T(8,128)(2,1)S(1)}, bf16[1,256,1280]{2,1,0:T(8,128)(2,1)}, u32[]{:S(2)}) %copy-start.4) | copy-done | bytes 655384
  13.9 0.7 copy-done.6
  14.6 1.6 %project_own.1.refs_0_ = bf16[256,1024]{1,0:T(8,128)(2,1)S(1)} custom-call(s32[1,256]{1,0:T(1,128)S(1)} %copy-done.6, bf16[256,1280]{1,0:T(8,128)(2,1)S(1)} %bitcast.13, bf16[1280,1024]{1,0:T(8,128)(2,1)S(1)} %copy-done, bf16[1280,1024]{1,0:T(8,128)(2,1)S(1)} %copy-done.2, bf16[1,1024]{1,0:T(2,128)(2,1)S(1)} %broadcast_in_dim.31.ba, ...), custom_call_target="tpu_custom_call" | custom-call | flops 83886080 | bytes 327680 | tf_op jit(solution)/shard_map/project_own/pallas_call | solution.py:147
  16.2 1.3 %collective-permute-done.1 = bf16[656,128]{1,0:T(8,128)(2,1)S(1)} collective-permute-done((bf16[656,128]{1,0:T(8,128)(2,1)}, bf16[656,128]{1,0:T(8,128)(2,1)S(1)}, u32[]{:S(2)}, u32[]{:S(2)}) %collective-permute-start.1) | collective-permute-done | bytes 167968 | tf_op jit(solution)/shard_map/ppermute | solution.py:477
  17.6 5.3 %collective-permute-done.2 = bf16[656,128]{1,0:T(8,128)(2,1)S(1)} collective-permute-done((bf16[656,128]{1,0:T(8,128)(2,1)}, bf16[656,128]{1,0:T(8,128)(2,1)S(1)}, u32[]{:S(2)}, u32[]{:S(2)}) %collective-permute-start.2) | collective-permute-done | bytes 167968 | tf_op jit(solution)/shard_map/ppermute | solution.py:477
  22.9 0.5 collective-permute-start.4
  23.4 0.0 collective-permute-start.5
  23.4 0.8 collective-permute-start.6
  24.2 1.3 %collective-permute-start.7 = (bf16[656,128]{1,0:T(8,128)(2,1)S(1)}, bf16[656,128]{1,0:T(8,128)(2,1)S(1)}, u32[]{:S(2)}, u32[]{:S(2)}) collective-permute-start(bf16[656,128]{1,0:T(8,128)(2,1)S(1)} %collective-permute-done.2), channel_id=1, source_target_pairs={{0,4},{4,0},{8,12},{12,8},{1,5},{5,1},{9,13},{13,9},{2,6},{6,2},{1... | collective-permute-start | bytes 503816 | tf_op jit(solution)/shard_map/ppermute | solution.py:477
  25.5 1.6 %project_parts.3 = (bf16[256,1024]{1,0:T(8,128)(2,1)S(1)}, s32[1,256]{1,0:T(1,128)S(1)}) custom-call(bf16[1280,1024]{1,0:T(8,128)(2,1)S(1)} %copy-done.1, bf16[1280,1024]{1,0:T(8,128)(2,1)S(1)} %copy-done.3, bf16[1,1024]{1,0:T(2,128)(2,1)S(1)} %broadcast_in_dim.31.ba, bf16[1,1024]{1,0:T(2,128)(2,1)S(1)} %broadcast_in_dim.32.bf, ...), custom_call_target="tpu_custom_call" | custom-call | flops 83886080 | bytes 327680 | tf_op jit(solution)/shard_map/project_parts/pallas_call | solution.py:177
  27.1 0.0 copy-start.5
  27.1 1.6 %project_parts.4 = (bf16[256,1024]{1,0:T(8,128)(2,1)S(1)}, s32[1,256]{1,0:T(1,128)S(1)}) custom-call(bf16[1280,1024]{1,0:T(8,128)(2,1)S(1)} %copy-done.1, bf16[1280,1024]{1,0:T(8,128)(2,1)S(1)} %copy-done.3, bf16[1,1024]{1,0:T(2,128)(2,1)S(1)} %broadcast_in_dim.31.ba, bf16[1,1024]{1,0:T(2,128)(2,1)S(1)} %broadcast_in_dim.32.bf, ...), custom_call_target="tpu_custom_call" | custom-call | flops 83886080 | bytes 327680 | tf_op jit(solution)/shard_map/project_parts/pallas_call | solution.py:177
  28.8 1.0 %packet.4 = (bf16[48,1024]{1,0:T(8,128)(2,1)S(1)}, bf16[48,1024]{1,0:T(8,128)(2,1)S(1)}) custom-call(bf16[256,1024]{1,0:T(8,128)(2,1)S(1)} %project_own.1.refs_0_, bf16[256,1024]{1,0:T(8,128)(2,1)S(1)} %get-tuple-element.62.refs_1_, bf16[256,1024]{1,0:T(8,128)(2,1)S(1)} %get-tuple-element.66.refs_2_, s32[1,256]{1,0:T(1,128)S(1)} %copy-done.5, ...), custom_call_target="tpu_custom_call" | custom-call | flops 9437184 | bytes 98304 | tf_op jit(solution)/shard_map/packet/pallas_call | solution.py:276
  29.8 1.5 %collective-permute-start.8 = (bf16[48,1024]{1,0:T(8,128)(2,1)S(1)}, bf16[48,1024]{1,0:T(8,128)(2,1)S(1)}, u32[]{:S(2)}, u32[]{:S(2)}) collective-permute-start(bf16[48,1024]{1,0:T(8,128)(2,1)S(1)} %get-tuple-element.69), channel_id=1, source_target_pairs={{0,12},{1,13},{4,8},{5,9},{8,4},{9,5},{12,0},{13,1},{2,14},{3,15},... | collective-permute-start | bytes 294920 | tf_op jit(solution)/shard_map/ppermute | solution.py:492
  31.3 1.0 %packet.5 = (bf16[48,1024]{1,0:T(8,128)(2,1)S(1)}, bf16[48,1024]{1,0:T(8,128)(2,1)S(1)}) custom-call(bf16[256,1024]{1,0:T(8,128)(2,1)S(1)} %project_own.1.refs_0_, bf16[256,1024]{1,0:T(8,128)(2,1)S(1)} %get-tuple-element.62.refs_1_, bf16[256,1024]{1,0:T(8,128)(2,1)S(1)} %get-tuple-element.66.refs_2_, s32[1,256]{1,0:T(1,128)S(1)} %copy-done.5, ...), custom_call_target="tpu_custom_call" | custom-call | flops 9437184 | bytes 98304 | tf_op jit(solution)/shard_map/packet/pallas_call | solution.py:276
  32.4 0.8 %collective-permute-start.10 = (bf16[48,1024]{1,0:T(8,128)(2,1)S(1)}, bf16[48,1024]{1,0:T(8,128)(2,1)S(1)}, u32[]{:S(2)}, u32[]{:S(2)}) collective-permute-start(bf16[48,1024]{1,0:T(8,128)(2,1)S(1)} %get-tuple-element.71), channel_id=1, source_target_pairs={{0,8},{1,9},{4,12},{5,13},{8,0},{9,1},{12,4},{13,5},{2,10},{3,11},... | collective-permute-start | bytes 294920 | tf_op jit(solution)/shard_map/ppermute | solution.py:492
  33.2 0.5 collective-permute-done.7
  33.7 2.0 %all-gather = bf16[1312,128]{1,0:T(8,128)(2,1)S(1)} all-gather(bf16[656,128]{1,0:T(8,128)(2,1)S(1)} %collective-permute-done.6), channel_id=2, replica_groups=mesh['groups'=2,'ctx'=4,'enc'=2,'tp'=2] {'tp'}, dimensions={0}, use_global_device_ids=true | all-gather | bytes 503808 | tf_op jit(solution)/shard_map/all_gather | solution.py:520
  35.8 1.7 %collective-permute-start.9 = (bf16[48,1024]{1,0:T(8,128)(2,1)S(1)}, bf16[48,1024]{1,0:T(8,128)(2,1)S(1)}, u32[]{:S(2)}, u32[]{:S(2)}) collective-permute-start(bf16[48,1024]{1,0:T(8,128)(2,1)S(1)} %get-tuple-element.85), channel_id=1, source_target_pairs={{0,13},{1,12},{4,9},{5,8},{8,5},{9,4},{12,1},{13,0},{2,15},{3,14},... | collective-permute-start | bytes 294920 | tf_op jit(solution)/shard_map/ppermute | solution.py:492
  37.5 1.1 %collective-permute-start.11 = (bf16[48,1024]{1,0:T(8,128)(2,1)S(1)}, bf16[48,1024]{1,0:T(8,128)(2,1)S(1)}, u32[]{:S(2)}, u32[]{:S(2)}) collective-permute-start(bf16[48,1024]{1,0:T(8,128)(2,1)S(1)} %get-tuple-element.86), channel_id=1, source_target_pairs={{0,9},{1,8},{4,13},{5,12},{8,1},{9,0},{12,5},{13,4},{2,11},{3,10},... | collective-permute-start | bytes 294920 | tf_op jit(solution)/shard_map/ppermute | solution.py:492
  38.6 2.0 %all-gather.1 = bf16[1312,128]{1,0:T(8,128)(2,1)S(1)} all-gather(bf16[656,128]{1,0:T(8,128)(2,1)S(1)} %collective-permute-done.7), channel_id=3, replica_groups=mesh['groups'=2,'ctx'=4,'enc'=2,'tp'=2] {'tp'}, dimensions={0}, use_global_device_ids=true | all-gather | bytes 503808 | tf_op jit(solution)/shard_map/all_gather | solution.py:520
  40.6 1.6 %project_parts.5 = (bf16[256,1024]{1,0:T(8,128)(2,1)S(1)}, s32[1,256]{1,0:T(1,128)S(1)}) custom-call(bf16[1280,1024]{1,0:T(8,128)(2,1)S(1)} %copy-done.1, bf16[1280,1024]{1,0:T(8,128)(2,1)S(1)} %copy-done.3, bf16[1,1024]{1,0:T(2,128)(2,1)S(1)} %broadcast_in_dim.31.ba, bf16[1,1024]{1,0:T(2,128)(2,1)S(1)} %broadcast_in_dim.32.bf, ...), custom_call_target="tpu_custom_call" | custom-call | flops 83886080 | bytes 327680 | tf_op jit(solution)/shard_map/project_parts/pallas_call | solution.py:177
  42.2 0.7 select.2
  43.0 1.3 %collective-permute-start.14 = (bf16[256,1024]{1,0:T(8,128)(2,1)S(1)}, bf16[256,1024]{1,0:T(8,128)(2,1)S(1)}, u32[]{:S(2)}, u32[]{:S(2)}) collective-permute-start(bf16[256,1024]{1,0:T(8,128)(2,1)S(1)} %select.2), channel_id=1, source_target_pairs={{0,4},{4,0},{8,12},{12,8},{1,5},{5,1},{9,13},{13,9},{2,6},{6,2},{1... | collective-permute-start | bytes 1572872 | tf_op jit(solution)/shard_map/ppermute | solution.py:477
  44.3 1.4 %packet.6 = (bf16[80,1024]{1,0:T(8,128)(2,1)S(1)}, bf16[80,1024]{1,0:T(8,128)(2,1)S(1)}) custom-call(bf16[256,1024]{1,0:T(8,128)(2,1)S(1)} %project_own.1.refs_0_, bf16[256,1024]{1,0:T(8,128)(2,1)S(1)} %get-tuple-element.62.refs_1_, bf16[256,1024]{1,0:T(8,128)(2,1)S(1)} %get-tuple-element.66.refs_2_, bf16[256,1024]{1,0:T(8,128)(2,1)S(1)} %get-tuple-element.75.refs_3_, ...), custom_call_target="tpu_custom_call" | custom-call | flops 20971520 | bytes 131072 | tf_op jit(solution)/shard_map/packet/pallas_call | solution.py:276
  45.7 1.4 %packet.7 = (bf16[80,1024]{1,0:T(8,128)(2,1)S(1)}, bf16[80,1024]{1,0:T(8,128)(2,1)S(1)}) custom-call(bf16[256,1024]{1,0:T(8,128)(2,1)S(1)} %project_own.1.refs_0_, bf16[256,1024]{1,0:T(8,128)(2,1)S(1)} %get-tuple-element.62.refs_1_, bf16[256,1024]{1,0:T(8,128)(2,1)S(1)} %get-tuple-element.66.refs_2_, bf16[256,1024]{1,0:T(8,128)(2,1)S(1)} %get-tuple-element.75.refs_3_, ...), custom_call_target="tpu_custom_call" | custom-call | flops 20971520 | bytes 131072 | tf_op jit(solution)/shard_map/packet/pallas_call | solution.py:276
  47.1 2.6 %collective-permute-done.11.refs_3_ = bf16[48,1024]{1,0:T(8,128)(2,1)S(1)} collective-permute-done((bf16[48,1024]{1,0:T(8,128)(2,1)S(1)}, bf16[48,1024]{1,0:T(8,128)(2,1)S(1)}, u32[]{:S(2)}, u32[]{:S(2)}) %collective-permute-start.11) | collective-permute-done | bytes 98336 | tf_op jit(solution)/shard_map/ppermute | solution.py:492
  49.7 2.3 %collective-permute-start.13 = (bf16[80,1024]{1,0:T(8,128)(2,1)S(1)}, bf16[80,1024]{1,0:T(8,128)(2,1)S(1)}, u32[]{:S(2)}, u32[]{:S(2)}) collective-permute-start(bf16[80,1024]{1,0:T(8,128)(2,1)S(1)} %get-tuple-element.94), channel_id=1, source_target_pairs={{0,9},{1,8},{4,13},{5,12},{8,1},{9,0},{12,5},{13,4},{2,11},{3,10},... | collective-permute-start | bytes 491528 | tf_op jit(solution)/shard_map/ppermute | solution.py:492
  52.0 0.6 order_of.1
  52.6 0.7 select.3
  53.3 2.5 %all-gather.2 = bf16[256,1024]{1,0:T(8,128)(2,1)S(1)} all-gather(bf16[128,1024]{1,0:T(8,128)(2,1)S(1)} %get-tuple-element.97), channel_id=4, replica_groups=mesh['groups'=2,'ctx'=4,'enc'=2,'tp'=2] {'tp'}, dimensions={0}, use_global_device_ids=true | all-gather | bytes 786432 | tf_op jit(solution)/shard_map/all_gather | solution.py:496
  55.9 1.8 %collective-permute-start.15 = (bf16[80,1024]{1,0:T(8,128)(2,1)S(1)}, bf16[80,1024]{1,0:T(8,128)(2,1)S(1)}, u32[]{:S(2)}, u32[]{:S(2)}) collective-permute-start(bf16[80,1024]{1,0:T(8,128)(2,1)S(1)} %get-tuple-element.100), channel_id=1, source_target_pairs={{0,12},{1,13},{4,8},{5,9},{8,4},{9,5},{12,0},{13,1},{2,14},{3,15},... | collective-permute-start | bytes 491528 | tf_op jit(solution)/shard_map/ppermute | solution.py:492
  57.6 1.8 %collective-permute-start.16 = (bf16[80,1024]{1,0:T(8,128)(2,1)S(1)}, bf16[80,1024]{1,0:T(8,128)(2,1)S(1)}, u32[]{:S(2)}, u32[]{:S(2)}) collective-permute-start(bf16[80,1024]{1,0:T(8,128)(2,1)S(1)} %get-tuple-element.102), channel_id=1, source_target_pairs={{0,13},{1,12},{4,9},{5,8},{8,5},{9,4},{12,1},{13,0},{2,15},{3,14},... | collective-permute-start | bytes 491528 | tf_op jit(solution)/shard_map/ppermute | solution.py:492
  59.4 0.7 collective-permute-done.12.refs_2_
  60.1 13.3 %collective-permute-done.13.refs_4_ = bf16[80,1024]{1,0:T(8,128)(2,1)S(1)} collective-permute-done((bf16[80,1024]{1,0:T(8,128)(2,1)S(1)}, bf16[80,1024]{1,0:T(8,128)(2,1)S(1)}, u32[]{:S(2)}, u32[]{:S(2)}) %collective-permute-start.13) | collective-permute-done | bytes 163872 | tf_op jit(solution)/shard_map/ppermute | solution.py:492
  73.5 0.4 place.1
  73.8 0.2 squares.2.refs_0_
  74.0 3.4 %all-gather.3 = bf16[256,1024]{1,0:T(8,128)(2,1)S(1)} all-gather(bf16[128,1024]{1,0:T(8,128)(2,1)S(1)} %slice.4), channel_id=5, replica_groups=mesh['groups'=2,'ctx'=4,'enc'=2,'tp'=2] {'tp'}, dimensions={0}, use_global_device_ids=true | all-gather | bytes 786432 | tf_op jit(solution)/shard_map/all_gather | solution.py:499
  77.4 0.2 squares.3.before
  77.6 2.3 %place_and_norm.1 = bf16[128,8192]{1,0:T(8,128)(2,1)} custom-call(bf16[1,8192]{1,0:T(2,128)(2,1)S(1)} %broadcast_in_dim.30.gain, f32[128,1]{1,0:T(8,128)S(1)} %squares.3.before, bf16[128,128]{1,0:T(8,128)(2,1)S(1)} %get-tuple-element.98.order, bf16[48,1024]{1,0:T(8,128)(2,1)S(1)} %collective-permute-done.8.refs_0_, ...), custom_call_target="tpu_custom_call" | custom-call | flops 262144 | bytes 262144 | tf_op jit(solution)/shard_map/place_and_norm/pallas_call | solution.py:454
  (28 shorter events, 0.1 us)
Async XLA Ops:
  2.3 20.6 %collective-permute-start = (bf16[1296,128]{1,0:T(8,128)(2,1)}, bf16[1296,128]{1,0:T(8,128)(2,1)S(1)}, u32[]{:S(2)}, u32[]{:S(2)}) collective-permute-start(bf16[1296,128]{1,0:T(8,128)(2,1)} %get-tuple-element.56), channel_id=1, source_target_pairs={{0,4},{4,0},{8,12},{12,8},{1,5},{5,1},{9,13},{13,9},{2,6},{6,2},{1... | collective-permute-start | bytes 995336 | tf_op jit(solution)/shard_map/ppermute | solution.py:477
  5.4 12.2 %collective-permute-start.1 = (bf16[656,128]{1,0:T(8,128)(2,1)}, bf16[656,128]{1,0:T(8,128)(2,1)S(1)}, u32[]{:S(2)}, u32[]{:S(2)}) collective-permute-start(bf16[656,128]{1,0:T(8,128)(2,1)} %get-tuple-element.57), channel_id=1, source_target_pairs={{0,8},{4,12},{8,0},{12,4},{1,9},{5,13},{9,1},{13,5},{2,10},{6,14},... | collective-permute-start | bytes 503816 | tf_op jit(solution)/shard_map/ppermute | solution.py:477
  8.0 14.9 %collective-permute-start.2 = (bf16[656,128]{1,0:T(8,128)(2,1)}, bf16[656,128]{1,0:T(8,128)(2,1)S(1)}, u32[]{:S(2)}, u32[]{:S(2)}) collective-permute-start(bf16[656,128]{1,0:T(8,128)(2,1)} %get-tuple-element.58), channel_id=1, source_target_pairs={{0,12},{4,8},{8,4},{12,0},{1,13},{5,9},{9,5},{13,1},{2,14},{6,10},... | collective-permute-start | bytes 503816 | tf_op jit(solution)/shard_map/ppermute | solution.py:477
  9.4 1.7 %copy-start = (bf16[1280,1024]{1,0:T(8,128)(2,1)S(1)}, bf16[1280,1024]{1,0:T(8,128)(2,1)}, u32[]{:S(2)}) copy-start(bf16[1280,1024]{1,0:T(8,128)(2,1)} %wa.7) | copy-start | bytes 7864324
  11.1 1.7 %copy-start.2 = (bf16[1280,1024]{1,0:T(8,128)(2,1)S(1)}, bf16[1280,1024]{1,0:T(8,128)(2,1)}, u32[]{:S(2)}) copy-start(bf16[1280,1024]{1,0:T(8,128)(2,1)} %wf.7) | copy-start | bytes 7864324
  12.9 1.1 %copy-start.4 = (bf16[1,256,1280]{2,1,0:T(8,128)(2,1)S(1)}, bf16[1,256,1280]{2,1,0:T(8,128)(2,1)}, u32[]{:S(2)}) copy-start(bf16[1,256,1280]{2,1,0:T(8,128)(2,1)} %param.8) | copy-start | bytes 1966084
  13.9 0.7 copy-start.6
  14.6 10.8 %copy-start.8 = (bf16[8192]{0:T(1024)(128)(2,1)S(1)}, bf16[8192]{0:T(1024)(128)(2,1)}, u32[]{:S(2)}) copy-start(bf16[8192]{0:T(1024)(128)(2,1)} %param.15) | copy-start | bytes 49156
  14.6 10.9 %copy-start.1 = (bf16[1280,1024]{1,0:T(8,128)(2,1)S(1)}, bf16[1280,1024]{1,0:T(8,128)(2,1)}, u32[]{:S(2)}) copy-start(bf16[1280,1024]{1,0:T(8,128)(2,1)} %wa.7) | copy-start | bytes 7864324
  14.6 10.9 %copy-start.3 = (bf16[1280,1024]{1,0:T(8,128)(2,1)S(1)}, bf16[1280,1024]{1,0:T(8,128)(2,1)}, u32[]{:S(2)}) copy-start(bf16[1280,1024]{1,0:T(8,128)(2,1)} %wf.7) | copy-start | bytes 7864324
  22.9 4.2 %collective-permute-start.3 = (bf16[1296,128]{1,0:T(8,128)(2,1)S(1)}, bf16[1296,128]{1,0:T(8,128)(2,1)S(1)}, u32[]{:S(2)}, u32[]{:S(2)}) collective-permute-start(bf16[1296,128]{1,0:T(8,128)(2,1)S(1)} %collective-permute-done), channel_id=1, source_target_pairs={{0,1},{1,0},{2,3},{3,2},{4,5},{5,4},{6,7},{7,6},{8,9},{9,8},{10,11... | collective-permute-start | bytes 995336 | tf_op jit(solution)/shard_map/ppermute | solution.py:480
  22.9 4.2 %collective-permute-start.4 = (bf16[656,128]{1,0:T(8,128)(2,1)S(1)}, bf16[656,128]{1,0:T(8,128)(2,1)S(1)}, u32[]{:S(2)}, u32[]{:S(2)}) collective-permute-start(bf16[656,128]{1,0:T(8,128)(2,1)S(1)} %collective-permute-done.1), channel_id=1, source_target_pairs={{0,1},{1,0},{2,3},{3,2},{4,5},{5,4},{6,7},{7,6},{8,9},{9,8},{10,11... | collective-permute-start | bytes 503816 | tf_op jit(solution)/shard_map/ppermute | solution.py:480
  23.4 3.7 %collective-permute-start.5 = (bf16[656,128]{1,0:T(8,128)(2,1)S(1)}, bf16[656,128]{1,0:T(8,128)(2,1)S(1)}, u32[]{:S(2)}, u32[]{:S(2)}) collective-permute-start(bf16[656,128]{1,0:T(8,128)(2,1)S(1)} %collective-permute-done.2), channel_id=1, source_target_pairs={{0,1},{1,0},{2,3},{3,2},{4,5},{5,4},{6,7},{7,6},{8,9},{9,8},{10,11... | collective-permute-start | bytes 503816 | tf_op jit(solution)/shard_map/ppermute | solution.py:480
  23.4 9.8 %collective-permute-start.6 = (bf16[656,128]{1,0:T(8,128)(2,1)S(1)}, bf16[656,128]{1,0:T(8,128)(2,1)S(1)}, u32[]{:S(2)}, u32[]{:S(2)}) collective-permute-start(bf16[656,128]{1,0:T(8,128)(2,1)S(1)} %collective-permute-done.1), channel_id=1, source_target_pairs={{0,4},{4,0},{8,12},{12,8},{1,5},{5,1},{9,13},{13,9},{2,6},{6,2},{1... | collective-permute-start | bytes 503816 | tf_op jit(solution)/shard_map/ppermute | solution.py:477
  24.2 9.5 %collective-permute-start.7 = (bf16[656,128]{1,0:T(8,128)(2,1)S(1)}, bf16[656,128]{1,0:T(8,128)(2,1)S(1)}, u32[]{:S(2)}, u32[]{:S(2)}) collective-permute-start(bf16[656,128]{1,0:T(8,128)(2,1)S(1)} %collective-permute-done.2), channel_id=1, source_target_pairs={{0,4},{4,0},{8,12},{12,8},{1,5},{5,1},{9,13},{13,9},{2,6},{6,2},{1... | collective-permute-start | bytes 503816 | tf_op jit(solution)/shard_map/ppermute | solution.py:477
  27.1 1.6 %copy-start.5 = (s32[1,256]{1,0:T(1,128)S(1)}, s32[1,256]{1,0:T(1,128)}, u32[]{:S(2)}) copy-start(s32[1,256]{1,0:T(1,128)} %refs_4_.3) | copy-start | bytes 3076
  29.8 17.3 %collective-permute-start.8 = (bf16[48,1024]{1,0:T(8,128)(2,1)S(1)}, bf16[48,1024]{1,0:T(8,128)(2,1)S(1)}, u32[]{:S(2)}, u32[]{:S(2)}) collective-permute-start(bf16[48,1024]{1,0:T(8,128)(2,1)S(1)} %get-tuple-element.69), channel_id=1, source_target_pairs={{0,12},{1,13},{4,8},{5,9},{8,4},{9,5},{12,0},{13,1},{2,14},{3,15},... | collective-permute-start | bytes 294920 | tf_op jit(solution)/shard_map/ppermute | solution.py:492
  32.4 17.3 %collective-permute-start.10 = (bf16[48,1024]{1,0:T(8,128)(2,1)S(1)}, bf16[48,1024]{1,0:T(8,128)(2,1)S(1)}, u32[]{:S(2)}, u32[]{:S(2)}) collective-permute-start(bf16[48,1024]{1,0:T(8,128)(2,1)S(1)} %get-tuple-element.71), channel_id=1, source_target_pairs={{0,8},{1,9},{4,12},{5,13},{8,0},{9,1},{12,4},{13,5},{2,10},{3,11},... | collective-permute-start | bytes 294920 | tf_op jit(solution)/shard_map/ppermute | solution.py:492
  35.8 11.3 %collective-permute-start.9 = (bf16[48,1024]{1,0:T(8,128)(2,1)S(1)}, bf16[48,1024]{1,0:T(8,128)(2,1)S(1)}, u32[]{:S(2)}, u32[]{:S(2)}) collective-permute-start(bf16[48,1024]{1,0:T(8,128)(2,1)S(1)} %get-tuple-element.85), channel_id=1, source_target_pairs={{0,13},{1,12},{4,9},{5,8},{8,5},{9,4},{12,1},{13,0},{2,15},{3,14},... | collective-permute-start | bytes 294920 | tf_op jit(solution)/shard_map/ppermute | solution.py:492
  37.5 12.2 %collective-permute-start.11 = (bf16[48,1024]{1,0:T(8,128)(2,1)S(1)}, bf16[48,1024]{1,0:T(8,128)(2,1)S(1)}, u32[]{:S(2)}, u32[]{:S(2)}) collective-permute-start(bf16[48,1024]{1,0:T(8,128)(2,1)S(1)} %get-tuple-element.86), channel_id=1, source_target_pairs={{0,9},{1,8},{4,13},{5,12},{8,1},{9,0},{12,5},{13,4},{2,11},{3,10},... | collective-permute-start | bytes 294920 | tf_op jit(solution)/shard_map/ppermute | solution.py:492
  42.9 9.1 %copy-start.7 = (s32[1,256]{1,0:T(1,128)S(1)}, s32[1,256]{1,0:T(1,128)}, u32[]{:S(2)}) copy-start(s32[1,256]{1,0:T(1,128)} %get-tuple-element.55.parity) | copy-start | bytes 3076
  43.0 31.1 %collective-permute-start.14 = (bf16[256,1024]{1,0:T(8,128)(2,1)S(1)}, bf16[256,1024]{1,0:T(8,128)(2,1)S(1)}, u32[]{:S(2)}, u32[]{:S(2)}) collective-permute-start(bf16[256,1024]{1,0:T(8,128)(2,1)S(1)} %select.2), channel_id=1, source_target_pairs={{0,4},{4,0},{8,12},{12,8},{1,5},{5,1},{9,13},{13,9},{2,6},{6,2},{1... | collective-permute-start | bytes 1572872 | tf_op jit(solution)/shard_map/ppermute | solution.py:477
  49.7 10.4 %collective-permute-start.12 = (bf16[80,1024]{1,0:T(8,128)(2,1)S(1)}, bf16[80,1024]{1,0:T(8,128)(2,1)S(1)}, u32[]{:S(2)}, u32[]{:S(2)}) collective-permute-start(bf16[80,1024]{1,0:T(8,128)(2,1)S(1)} %get-tuple-element.92), channel_id=1, source_target_pairs={{0,8},{1,9},{4,12},{5,13},{8,0},{9,1},{12,4},{13,5},{2,10},{3,11},... | collective-permute-start | bytes 491528 | tf_op jit(solution)/shard_map/ppermute | solution.py:492
  49.7 23.8 %collective-permute-start.13 = (bf16[80,1024]{1,0:T(8,128)(2,1)S(1)}, bf16[80,1024]{1,0:T(8,128)(2,1)S(1)}, u32[]{:S(2)}, u32[]{:S(2)}) collective-permute-start(bf16[80,1024]{1,0:T(8,128)(2,1)S(1)} %get-tuple-element.94), channel_id=1, source_target_pairs={{0,9},{1,8},{4,13},{5,12},{8,1},{9,0},{12,5},{13,4},{2,11},{3,10},... | collective-permute-start | bytes 491528 | tf_op jit(solution)/shard_map/ppermute | solution.py:492
  55.9 21.8 %collective-permute-start.15 = (bf16[80,1024]{1,0:T(8,128)(2,1)S(1)}, bf16[80,1024]{1,0:T(8,128)(2,1)S(1)}, u32[]{:S(2)}, u32[]{:S(2)}) collective-permute-start(bf16[80,1024]{1,0:T(8,128)(2,1)S(1)} %get-tuple-element.100), channel_id=1, source_target_pairs={{0,12},{1,13},{4,8},{5,9},{8,4},{9,5},{12,0},{13,1},{2,14},{3,15},... | collective-permute-start | bytes 491528 | tf_op jit(solution)/shard_map/ppermute | solution.py:492
  57.6 20.0 %collective-permute-start.16 = (bf16[80,1024]{1,0:T(8,128)(2,1)S(1)}, bf16[80,1024]{1,0:T(8,128)(2,1)S(1)}, u32[]{:S(2)}, u32[]{:S(2)}) collective-permute-start(bf16[80,1024]{1,0:T(8,128)(2,1)S(1)} %get-tuple-element.102), channel_id=1, source_target_pairs={{0,13},{1,12},{4,9},{5,8},{8,5},{9,4},{12,1},{13,0},{2,15},{3,14},... | collective-permute-start | bytes 491528 | tf_op jit(solution)/shard_map/ppermute | solution.py:492

commit v14 on v13

--- a/solution.py
+++ b/solution.py
@@ -10,7 +10,7 @@
 VMEM = pl.BlockSpec(memory_space=pltpu.VMEM)
 HBM = pl.BlockSpec(memory_space=pltpu.HBM)
 PARAMS = pltpu.CompilerParams(vmem_limit_bytes=12 << 20)
-SUM_FLOPS = 1 << 35
+OWN_FLOPS, NEAR_FLOPS = 1 << 35, 0
 BF16, F32, I32 = jnp.bfloat16, jnp.float32, jnp.int32
 
 
@@ -239,7 +239,7 @@
 
 def packet_kernel(m, early, count, second, *refs):
     blocks, slots, outs = refs[:count], refs[count : 2 * count], refs[2 * count :]
-    size = outs[0].shape[0]
+    size = sum(out.shape[0] for out in outs) // 2
     places = blocks[0].shape[0] // 2
     first_size = places - size if second else size
     z, t = lax.axis_index("ctx"), lax.axis_index("tp")
@@ -267,17 +267,20 @@
         chosen = jnp.dot(pick, hold, preferred_element_type=F32).astype(BF16)
         part = jnp.dot(chosen, block[...], preferred_element_type=F32)
         total = part if total is None else total + part
-    outs[0][...] = total[:size].astype(BF16)
-    outs[1][...] = total[size:].astype(BF16)
+    if second:
+        outs[0][...] = total[:size].astype(BF16)
+        outs[1][...] = total[size:].astype(BF16)
+    else:
+        outs[0][...] = total.astype(BF16)
 
 
 def packet(m, early, blocks, slots, size, second):
     rows, cols = sum(b.shape[0] for b in blocks), blocks[0].shape[1]
     return pl.pallas_call(
         functools.partial(packet_kernel, m, early, len(blocks), second),
-        out_shape=[jax.ShapeDtypeStruct((size, cols), BF16)] * 2,
+        out_shape=[jax.ShapeDtypeStruct((size if second else 2 * size, cols), BF16)] * (1 + second),
         in_specs=[VMEM] * (2 * len(blocks)),
-        out_specs=[VMEM] * 2,
+        out_specs=[VMEM] * (1 + second),
         compiler_params=PARAMS,
         cost_estimate=cost(4 * size * rows * cols, 2 * rows * cols),
         name="packet",
@@ -325,36 +328,9 @@
         in_specs=[VMEM] * (1 + len(slots)),
         out_specs=[VMEM] * 2,
         compiler_params=PARAMS,
-        cost_estimate=cost(SUM_FLOPS, 0),
+        cost_estimate=cost(1 << 34, 0),
         name="order_of",
     )(parity, *slots)
-
-
-def place_kernel(has_total, *refs):
-    total = refs[0][...] if has_total else None
-    order, packets, outs = refs[has_total], refs[has_total + 1 : has_total + 5], refs[-3:]
-    for d in range(2):
-        both = jnp.concatenate([packets[2 * d][...], packets[2 * d + 1][...]], axis=0)
-        wide = jnp.dot(order[...], both, preferred_element_type=F32)
-        outs[d][...] = wide.astype(BF16)
-        part = jnp.sum(wide * wide, axis=1, keepdims=True)
-        total = part if total is None else total + part
-    outs[2][...] = total
-
-
-def place(total, order, packets):
-    places, cols = order.shape[0], packets[0].shape[1]
-    operands = ([] if total is None else [total]) + [order] + packets
-    return pl.pallas_call(
-        functools.partial(place_kernel, len(operands) - 5),
-        out_shape=[jax.ShapeDtypeStruct((places, cols), BF16)] * 2
-        + [jax.ShapeDtypeStruct((places, 1), F32)],
-        in_specs=[VMEM] * len(operands),
-        out_specs=[VMEM] * 3,
-        compiler_params=PARAMS,
-        cost_estimate=cost(SUM_FLOPS, 0),
-        name="place",
-    )(*operands)
 
 
 def view(ref, places):
@@ -377,7 +353,7 @@
     out[...] = total
 
 
-def squares(total, pieces, places):
+def squares(total, pieces, places, flops=0):
     operands = pieces if total is None else [total] + pieces
     return pl.pallas_call(
         squares_kernel,
@@ -385,7 +361,7 @@
         in_specs=[VMEM] * len(operands),
         out_specs=VMEM,
         compiler_params=PARAMS,
-        cost_estimate=cost(SUM_FLOPS, 0),
+        cost_estimate=cost(flops, 0),
         name="squares",
     )(*operands)
 
@@ -425,14 +401,17 @@
     )(gain, before, *pieces)
 
 
-def last_kernel(far, whole, gain, before, order, *refs):
-    packets, pieces, (out, scaled, sems) = refs[:4], refs[4:10], refs[10:]
+def last_kernel(far, whole, gain, before, before_too, *refs):
+    orders, packets, pieces = refs[:2], refs[2:10], refs[10:14]
+    out, scaled, sems = refs[14:]
     places, cols = scaled.shape[1:]
     z, t = lax.axis_index("ctx"), lax.axis_index("tp")
-    total = before[...]
-    for k in range(2):
-        both = jnp.concatenate([packets[2 * k][...], packets[2 * k + 1][...]], axis=0)
-        wide = jnp.dot(order[...], both, preferred_element_type=F32)
+    total = before[...] + before_too[...]
+    for k in range(4):
+        later = packets[2 * k + 1][...]
+        early = view(packets[2 * k], places - later.shape[0])[...]
+        both = jnp.concatenate([early, later], axis=0)
+        wide = jnp.dot(orders[k // 2][...], both, preferred_element_type=F32)
         scaled[k] = wide.astype(BF16)
         total = total + jnp.sum(wide * wide, axis=1, keepdims=True)
     scale = lax.rsqrt(total / (8 * cols) + 1e-06)
@@ -440,7 +419,7 @@
     for k, (m, d) in enumerate(far + whole):
         block = jnp.bitwise_xor(z, m) * 2 + jnp.bitwise_xor(t, d)
         at = pl.ds(pl.multiple_of(block * cols, cols), cols)
-        piece = scaled[k] if k < 2 else view(pieces[k - 2], places)[...]
+        piece = scaled[k] if k < 4 else view(pieces[k - 4], places)[...]
         scaled[k] = (piece.astype(F32) * scale * gain[:, at].astype(F32)).astype(BF16)
         copies.append(pltpu.make_async_copy(scaled.at[k], out.at[:, at], sems.at[k]))
         copies[k].start()
@@ -448,9 +427,9 @@
         copy.wait()
 
 
-def place_and_norm(far, whole, gain, before, order, packets, pieces):
-    places, cols = before.shape[0], packets[0].shape[1]
-    operands = [gain, before, order, *packets, *pieces]
+def place_and_norm(far, whole, gain, before, orders, packets, pieces):
+    places, cols = before[0].shape[0], packets[0].shape[1]
+    operands = [gain, *before, *orders, *packets, *pieces]
     return pl.pallas_call(
         functools.partial(last_kernel, far, whole),
         out_shape=jax.ShapeDtypeStruct((places, 8 * cols), BF16),
@@ -491,13 +470,15 @@
         pairs = [(i * 2 + c, (i ^ m) * 2 + (c ^ d)) for i in range(n) for c in range(2)]
         return lax.ppermute(x, ("ctx", "tp"), pairs)
 
-    def own_and_near(total):
+    def own_piece():
         pieces[0, 0], other = select(0, blocks, slots, [half, half])
         pieces[0, 1] = lax.all_gather(other, "tp", axis=0)
-        total = squares(total, [pieces[0, 0], pieces[0, 1]], half)
+        return squares(None, [pieces[0, 0], pieces[0, 1]], half, OWN_FLOPS)
+
+    def near_piece(total):
         pair = pieces[1]
         pieces[1, 0], pieces[1, 1] = pair, lax.all_gather(pair[half:], "tp", axis=0)
-        return squares(total, [pieces[1, 0], pieces[1, 1]], half)
+        return squares(total, [pieces[1, 0], pieces[1, 1]], half, NEAR_FLOPS)
 
     pieces = {}
     if n == 4:
@@ -515,7 +496,7 @@
         for m in (3, 2):
             chosen = packet(m, early, blocks, slots, size, False)
             slots[0] = after(slots[0], chosen[0])
-            sent[m] = [to_core(piece, m, d) for d, piece in enumerate(chosen)]
+            sent[m] = over_ctx(chosen[0], m)
         shared = lax.optimization_barrier((*shared, blocks[-1]))[:2]
         take([lax.all_gather(part, "tp", axis=0) for part in shared])
 
@@ -523,22 +504,24 @@
         slots[0] = after(slots[0], chosen)
         pieces[1] = over_ctx(chosen, 1)
         rest = {}
-        for m in (2, 3):
+        for m in (3, 2):
             chosen = packet(m, early, blocks, slots, half - size, True)
             slots[0] = after(slots[0], chosen[0])
-            joined = lax.optimization_barrier((*chosen, *sent[3], *sent[2]))
-            chosen, sent[3], sent[2] = joined[:2], list(joined[2:4]), list(joined[4:])
+            if m == 3:
+                joined = lax.optimization_barrier((*chosen, sent[3], sent[2]))
+                chosen, sent[3], sent[2] = joined[:2], joined[2], joined[3]
             rest[m] = [to_core(piece, m, d) for d, piece in enumerate(chosen)]
 
-        order3, order2 = order_of(size, parity, slots, half)
-        packets = [sent[2][0], rest[2][0], sent[2][1], rest[2][1]]
-        pieces[2, 0], pieces[2, 1], total = place(None, order2, packets)
-        total = own_and_near(total)
-        packets = [sent[3][0], rest[3][0], sent[3][1], rest[3][1]]
-        far, whole = ((3, 0), (3, 1)), ((2, 0), (2, 1), (1, 0), (1, 1), (0, 0), (0, 1))
+        orders = order_of(size, parity, slots, half)
+        total = [own_piece(), near_piece(None)]
+        for m in (3, 2):
+            whole_packet = sent[m]
+            sent[m] = [whole_packet, lax.all_gather(whole_packet[size:], "tp", axis=0)]
+        far, whole = ((3, 0), (3, 1), (2, 0), (2, 1)), ((1, 0), (1, 1), (0, 0), (0, 1))
+        packets = [part for m, d in far for part in (sent[m][d], rest[m][d])]
         whole_pieces = [pieces[at] for at in whole]
         gain = norm_gain[None, :]
-        return place_and_norm(far, whole, gain, total, order3, packets, whole_pieces)[None]
+        return place_and_norm(far, whole, gain, total, orders, packets, whole_pieces)[None]
     else:
         (mine,) = to_send((None,), rows, row_slot, row_kind)
         arrived = [over_ctx(mine, m) for m in range(1, n)]
@@ -560,7 +543,7 @@
             for d, piece in enumerate(chosen):
                 pieces[m, d] = to_core(piece, m, d)
         total = squares(None, [pieces[n - 1, 0], pieces[n - 1, 1]], half)
-        total = own_and_near(total)
+        total = squares(near_piece(total), [own_piece()], half)
         for m in order[2:-1]:
             late = [after(pieces[m, d], total) for d in range(2)]
             total = squares(total, late, half)

time: 81.5 us -> 79.7 us (0.978)
  the two profiles are of different devices: /device:TPU:0 before, /device:TPU:11 now
where the time goes in v14:
time: 79.7 us; the launch traced here: 79.3 us
  blocking collectives  21.2 us (27%)
  starting transfers between devices  20.3 us (25%)
  Pallas kernels  18.2 us (23%)
  waiting for transfers between devices  12.6 us (16%)
  local copies, waits for them, and re-layouts  6.69 us (8%)
    all_gather x1, blocking collectives, near_piece(): lax.all_gather(pair[half:], 'tp', axis=0)  10.7 us
    ppermute x8, waiting for transfers between devices, over_ctx(): return lax.ppermute(x, 'ctx', [(i, i ^ m) for i in range(n)])  7.91 us
    ppermute x4, starting transfers between devices, to_core(): return lax.ppermute(x, ('ctx', 'tp'), pairs)  7.61 us
    ppermute x8, starting transfers between devices, over_ctx(): return lax.ppermute(x, 'ctx', [(i, i ^ m) for i in range(n)])  6.83 us
    ppermute x3, starting transfers between devices, over_tp(): return lax.ppermute(x, 'tp', [(0, 1), (1, 0)])  5.92 us
    unnamed x18, local copies, waits for them, and re-layouts  5.27 us
    pallas_call x4, Pallas kernels, packet(): pl.pallas_call(functools.partial(packet_kernel, m, early, len(blocks), se...  4.86 us
    pallas_call x3, Pallas kernels, project_parts(): pl.pallas_call(project_parts_kernel, out_shape=[jax.ShapeDtypeStruct((row...  4.77 us
  transfers between devices with their start and end apart: 15, of which 6 were waited for; matrix products, arithmetic and copies ran while one was open for 2% of the time, Pallas kernels for 17%

profile of v14, /device:TPU:11, one launch (start us, length us, event | category | flops | bytes accessed | tf_op | source)
XLA Modules:
  0.0 79.3 jit_solution(13705914677871131018)
XLA Ops:
  0.0 2.3 %to_send.1 = (bf16[1296,128]{1,0:T(8,128)(2,1)}, bf16[656,128]{1,0:T(8,128)(2,1)}, bf16[656,128]{1,0:T(8,128)(2,1)}, s32[1,256]{1,0:T(1,128)}) custom-call(bf16[256,1280]{1,0:T(8,128)(2,1)} %bitcast.16, s32[1,256]{1,0:T(1,128)} %refs_0_, s32[1,256]{1,0:T(1,128)} %kind.3), custom_call_target="tpu_custom_call" | custom-call | bytes 40960 | tf_op jit(solution)/shard_map/to_send/pallas_call | solution.py:109
  2.3 0.2 collective-permute-start
  2.5 2.3 %collective-permute-start.1 = (bf16[656,128]{1,0:T(8,128)(2,1)}, bf16[656,128]{1,0:T(8,128)(2,1)S(1)}, u32[]{:S(2)}, u32[]{:S(2)}) collective-permute-start(bf16[656,128]{1,0:T(8,128)(2,1)} %get-tuple-element.41), channel_id=1, source_target_pairs={{0,8},{4,12},{8,0},{12,4},{1,9},{5,13},{9,1},{13,5},{2,10},{6,14},... | collective-permute-start | bytes 503816 | tf_op jit(solution)/shard_map/ppermute | solution.py:456
  4.9 0.2 collective-permute-start.2
  5.0 0.7 broadcast_in_dim.31.ba
  5.7 0.7 broadcast_in_dim.32.bf
  6.4 1.7 %copy-done = bf16[1280,1024]{1,0:T(8,128)(2,1)S(1)} copy-done((bf16[1280,1024]{1,0:T(8,128)(2,1)S(1)}, bf16[1280,1024]{1,0:T(8,128)(2,1)}, u32[]{:S(2)}) %copy-start) | copy-done | bytes 2621464
  8.1 1.7 %copy-done.2 = bf16[1280,1024]{1,0:T(8,128)(2,1)S(1)} copy-done((bf16[1280,1024]{1,0:T(8,128)(2,1)S(1)}, bf16[1280,1024]{1,0:T(8,128)(2,1)}, u32[]{:S(2)}) %copy-start.2) | copy-done | bytes 2621464
  9.9 1.1 %copy-done.4 = bf16[1,256,1280]{2,1,0:T(8,128)(2,1)S(1)} copy-done((bf16[1,256,1280]{2,1,0:T(8,128)(2,1)S(1)}, bf16[1,256,1280]{2,1,0:T(8,128)(2,1)}, u32[]{:S(2)}) %copy-start.4) | copy-done | bytes 655384
  11.0 0.7 copy-done.6
  11.7 1.6 %project_own.1.refs_0_ = bf16[256,1024]{1,0:T(8,128)(2,1)S(1)} custom-call(s32[1,256]{1,0:T(1,128)S(1)} %copy-done.6, bf16[256,1280]{1,0:T(8,128)(2,1)S(1)} %bitcast.17, bf16[1280,1024]{1,0:T(8,128)(2,1)S(1)} %copy-done, bf16[1280,1024]{1,0:T(8,128)(2,1)S(1)} %copy-done.2, bf16[1,1024]{1,0:T(2,128)(2,1)S(1)} %broadcast_in_dim.31.ba, ...), custom_call_target="tpu_custom_call" | custom-call | flops 83886080 | bytes 327680 | tf_op jit(solution)/shard_map/project_own/pallas_call | solution.py:147
  13.2 2.7 %collective-permute-done.1 = bf16[656,128]{1,0:T(8,128)(2,1)S(1)} collective-permute-done((bf16[656,128]{1,0:T(8,128)(2,1)}, bf16[656,128]{1,0:T(8,128)(2,1)S(1)}, u32[]{:S(2)}, u32[]{:S(2)}) %collective-permute-start.1) | collective-permute-done | bytes 167968 | tf_op jit(solution)/shard_map/ppermute | solution.py:456
  15.9 5.4 %collective-permute-start.3 = (bf16[1296,128]{1,0:T(8,128)(2,1)S(1)}, bf16[1296,128]{1,0:T(8,128)(2,1)S(1)}, u32[]{:S(2)}, u32[]{:S(2)}) collective-permute-start(bf16[1296,128]{1,0:T(8,128)(2,1)S(1)} %collective-permute-done), channel_id=1, source_target_pairs={{0,1},{1,0},{2,3},{3,2},{4,5},{5,4},{6,7},{7,6},{8,9},{9,8},{10,11... | collective-permute-start | bytes 995336 | tf_op jit(solution)/shard_map/ppermute | solution.py:459
  21.3 0.5 collective-permute-start.5
  21.8 1.0 %collective-permute-start.6 = (bf16[656,128]{1,0:T(8,128)(2,1)S(1)}, bf16[656,128]{1,0:T(8,128)(2,1)S(1)}, u32[]{:S(2)}, u32[]{:S(2)}) collective-permute-start(bf16[656,128]{1,0:T(8,128)(2,1)S(1)} %collective-permute-done.1), channel_id=1, source_target_pairs={{0,4},{4,0},{8,12},{12,8},{1,5},{5,1},{9,13},{13,9},{2,6},{6,2},{1... | collective-permute-start | bytes 503816 | tf_op jit(solution)/shard_map/ppermute | solution.py:456
  22.8 0.5 collective-permute-start.7
  23.3 1.6 %project_parts.3 = (bf16[256,1024]{1,0:T(8,128)(2,1)S(1)}, s32[1,256]{1,0:T(1,128)S(1)}) custom-call(bf16[1280,1024]{1,0:T(8,128)(2,1)S(1)} %copy-done.1, bf16[1280,1024]{1,0:T(8,128)(2,1)S(1)} %copy-done.3, bf16[1,1024]{1,0:T(2,128)(2,1)S(1)} %broadcast_in_dim.31.ba, bf16[1,1024]{1,0:T(2,128)(2,1)S(1)} %broadcast_in_dim.32.bf, ...), custom_call_target="tpu_custom_call" | custom-call | flops 83886080 | bytes 327680 | tf_op jit(solution)/shard_map/project_parts/pallas_call | solution.py:177
  25.0 0.0 copy-start.5
  25.0 1.6 %project_parts.4 = (bf16[256,1024]{1,0:T(8,128)(2,1)S(1)}, s32[1,256]{1,0:T(1,128)S(1)}) custom-call(bf16[1280,1024]{1,0:T(8,128)(2,1)S(1)} %copy-done.1, bf16[1280,1024]{1,0:T(8,128)(2,1)S(1)} %copy-done.3, bf16[1,1024]{1,0:T(2,128)(2,1)S(1)} %broadcast_in_dim.31.ba, bf16[1,1024]{1,0:T(2,128)(2,1)S(1)} %broadcast_in_dim.32.bf, ...), custom_call_target="tpu_custom_call" | custom-call | flops 83886080 | bytes 327680 | tf_op jit(solution)/shard_map/project_parts/pallas_call | solution.py:177
  26.6 1.0 %packet.4 = bf16[96,1024]{1,0:T(8,128)(2,1)S(1)} custom-call(bf16[256,1024]{1,0:T(8,128)(2,1)S(1)} %project_own.1.refs_0_, bf16[256,1024]{1,0:T(8,128)(2,1)S(1)} %get-tuple-element.46.refs_1_, bf16[256,1024]{1,0:T(8,128)(2,1)S(1)} %get-tuple-element.50.refs_2_, s32[1,256]{1,0:T(1,128)S(1)} %copy-done.5, ...), custom_call_target="tpu_custom_call" | custom-call | flops 9437184 | bytes 98304 | tf_op jit(solution)/shard_map/packet/pallas_call | solution.py:279
  27.7 1.0 %packet.5 = bf16[96,1024]{1,0:T(8,128)(2,1)S(1)} custom-call(bf16[256,1024]{1,0:T(8,128)(2,1)S(1)} %project_own.1.refs_0_, bf16[256,1024]{1,0:T(8,128)(2,1)S(1)} %get-tuple-element.46.refs_1_, bf16[256,1024]{1,0:T(8,128)(2,1)S(1)} %get-tuple-element.50.refs_2_, s32[1,256]{1,0:T(1,128)S(1)} %copy-done.5, ...), custom_call_target="tpu_custom_call" | custom-call | flops 9437184 | bytes 98304 | tf_op jit(solution)/shard_map/packet/pallas_call | solution.py:279
  28.7 1.1 %collective-permute-start.10 = (bf16[96,1024]{1,0:T(8,128)(2,1)S(1)}, bf16[96,1024]{1,0:T(8,128)(2,1)S(1)}, u32[]{:S(2)}, u32[]{:S(2)}) collective-permute-start(bf16[96,1024]{1,0:T(8,128)(2,1)S(1)} %packet.5), channel_id=1, source_target_pairs={{0,8},{4,12},{8,0},{12,4},{1,9},{5,13},{9,1},{13,5},{2,10},{6,14},... | collective-permute-start | bytes 589832 | tf_op jit(solution)/shard_map/ppermute | solution.py:456
  29.8 1.1 %collective-permute-start.9 = (bf16[96,1024]{1,0:T(8,128)(2,1)S(1)}, bf16[96,1024]{1,0:T(8,128)(2,1)S(1)}, u32[]{:S(2)}, u32[]{:S(2)}) collective-permute-start(bf16[96,1024]{1,0:T(8,128)(2,1)S(1)} %packet.4), channel_id=1, source_target_pairs={{0,12},{4,8},{8,4},{12,0},{1,13},{5,9},{9,5},{13,1},{2,14},{6,10},... | collective-permute-start | bytes 589832 | tf_op jit(solution)/shard_map/ppermute | solution.py:456
  30.9 0.4 collective-permute-done.7
  31.3 2.5 %all-gather = bf16[1312,128]{1,0:T(8,128)(2,1)S(1)} all-gather(bf16[656,128]{1,0:T(8,128)(2,1)S(1)} %collective-permute-done.6), channel_id=2, replica_groups=mesh['groups'=2,'ctx'=4,'enc'=2,'tp'=2] {'tp'}, dimensions={0}, use_global_device_ids=true | all-gather | bytes 503808 | tf_op jit(solution)/shard_map/all_gather | solution.py:501
  33.8 2.0 %all-gather.1 = bf16[1312,128]{1,0:T(8,128)(2,1)S(1)} all-gather(bf16[656,128]{1,0:T(8,128)(2,1)S(1)} %collective-permute-done.7), channel_id=3, replica_groups=mesh['groups'=2,'ctx'=4,'enc'=2,'tp'=2] {'tp'}, dimensions={0}, use_global_device_ids=true | all-gather | bytes 503808 | tf_op jit(solution)/shard_map/all_gather | solution.py:501
  35.8 1.6 %project_parts.5 = (bf16[256,1024]{1,0:T(8,128)(2,1)S(1)}, s32[1,256]{1,0:T(1,128)S(1)}) custom-call(bf16[1280,1024]{1,0:T(8,128)(2,1)S(1)} %copy-done.1, bf16[1280,1024]{1,0:T(8,128)(2,1)S(1)} %copy-done.3, bf16[1,1024]{1,0:T(2,128)(2,1)S(1)} %broadcast_in_dim.31.ba, bf16[1,1024]{1,0:T(2,128)(2,1)S(1)} %broadcast_in_dim.32.bf, ...), custom_call_target="tpu_custom_call" | custom-call | flops 83886080 | bytes 327680 | tf_op jit(solution)/shard_map/project_parts/pallas_call | solution.py:177
  37.4 0.7 select.2
  38.1 1.4 %packet.6 = (bf16[80,1024]{1,0:T(8,128)(2,1)S(1)}, bf16[80,1024]{1,0:T(8,128)(2,1)S(1)}) custom-call(bf16[256,1024]{1,0:T(8,128)(2,1)S(1)} %project_own.1.refs_0_, bf16[256,1024]{1,0:T(8,128)(2,1)S(1)} %get-tuple-element.46.refs_1_, bf16[256,1024]{1,0:T(8,128)(2,1)S(1)} %get-tuple-element.50.refs_2_, bf16[256,1024]{1,0:T(8,128)(2,1)S(1)} %get-tuple-element.53.refs_3_, ...), custom_call_target="tpu_custom_call" | custom-call | flops 20971520 | bytes 131072 | tf_op jit(solution)/shard_map/packet/pallas_call | solution.py:279
  39.5 1.4 %packet.7 = (bf16[80,1024]{1,0:T(8,128)(2,1)S(1)}, bf16[80,1024]{1,0:T(8,128)(2,1)S(1)}) custom-call(bf16[256,1024]{1,0:T(8,128)(2,1)S(1)} %project_own.1.refs_0_, bf16[256,1024]{1,0:T(8,128)(2,1)S(1)} %get-tuple-element.46.refs_1_, bf16[256,1024]{1,0:T(8,128)(2,1)S(1)} %get-tuple-element.50.refs_2_, bf16[256,1024]{1,0:T(8,128)(2,1)S(1)} %get-tuple-element.53.refs_3_, ...), custom_call_target="tpu_custom_call" | custom-call | flops 20971520 | bytes 131072 | tf_op jit(solution)/shard_map/packet/pallas_call | solution.py:279
  40.9 2.4 %collective-permute-start.13 = (bf16[80,1024]{1,0:T(8,128)(2,1)S(1)}, bf16[80,1024]{1,0:T(8,128)(2,1)S(1)}, u32[]{:S(2)}, u32[]{:S(2)}) collective-permute-start(bf16[80,1024]{1,0:T(8,128)(2,1)S(1)} %get-tuple-element.62), channel_id=1, source_target_pairs={{0,8},{1,9},{4,12},{5,13},{8,0},{9,1},{12,4},{13,5},{2,10},{3,11},... | collective-permute-start | bytes 491528 | tf_op jit(solution)/shard_map/ppermute | solution.py:471
  43.3 0.4 collective-permute-start.8
  43.7 0.7 select.3
  44.5 1.8 %collective-permute-start.14 = (bf16[80,1024]{1,0:T(8,128)(2,1)S(1)}, bf16[80,1024]{1,0:T(8,128)(2,1)S(1)}, u32[]{:S(2)}, u32[]{:S(2)}) collective-permute-start(bf16[80,1024]{1,0:T(8,128)(2,1)S(1)} %get-tuple-element.74), channel_id=1, source_target_pairs={{0,9},{1,8},{4,13},{5,12},{8,1},{9,0},{12,5},{13,4},{2,11},{3,10},... | collective-permute-start | bytes 491528 | tf_op jit(solution)/shard_map/ppermute | solution.py:471
  46.3 0.6 order_of.1
  46.9 2.2 %all-gather.2 = bf16[256,1024]{1,0:T(8,128)(2,1)S(1)} all-gather(bf16[128,1024]{1,0:T(8,128)(2,1)S(1)} %get-tuple-element.65), channel_id=4, replica_groups=mesh['groups'=2,'ctx'=4,'enc'=2,'tp'=2] {'tp'}, dimensions={0}, use_global_device_ids=true | all-gather | bytes 786432 | tf_op jit(solution)/shard_map/all_gather | solution.py:475
  49.1 0.2 squares.2.before
  49.3 2.6 %collective-permute-done.9.refs_2_ = bf16[96,1024]{1,0:T(8,128)(2,1)S(1)} collective-permute-done((bf16[96,1024]{1,0:T(8,128)(2,1)S(1)}, bf16[96,1024]{1,0:T(8,128)(2,1)S(1)}, u32[]{:S(2)}, u32[]{:S(2)}) %collective-permute-start.9) | collective-permute-done | bytes 196640 | tf_op jit(solution)/shard_map/ppermute | solution.py:456
  51.9 0.1 collective-permute-start.11
  52.0 3.3 %collective-permute-start.12 = (bf16[80,1024]{1,0:T(8,128)(2,1)S(1)}, bf16[80,1024]{1,0:T(8,128)(2,1)S(1)}, u32[]{:S(2)}, u32[]{:S(2)}) collective-permute-start(bf16[80,1024]{1,0:T(8,128)(2,1)S(1)} %get-tuple-element.72), channel_id=1, source_target_pairs={{0,13},{1,12},{4,9},{5,8},{8,5},{9,4},{12,1},{13,0},{2,15},{3,14},... | collective-permute-start | bytes 491528 | tf_op jit(solution)/shard_map/ppermute | solution.py:471
  55.3 1.9 %all-gather.4 = bf16[96,1024]{1,0:T(8,128)(2,1)S(1)} all-gather(bf16[48,1024]{1,0:T(8,128)(2,1)S(1)} %slice.10), channel_id=6, replica_groups=mesh['groups'=2,'ctx'=4,'enc'=2,'tp'=2] {'tp'}, dimensions={0}, use_global_device_ids=true | all-gather | bytes 294912 | tf_op jit(solution)/shard_map/all_gather | solution.py:519
  57.3 1.9 %all-gather.5 = bf16[96,1024]{1,0:T(8,128)(2,1)S(1)} all-gather(bf16[48,1024]{1,0:T(8,128)(2,1)S(1)} %slice.11), channel_id=7, replica_groups=mesh['groups'=2,'ctx'=4,'enc'=2,'tp'=2] {'tp'}, dimensions={0}, use_global_device_ids=true | all-gather | bytes 294912 | tf_op jit(solution)/shard_map/all_gather | solution.py:519
  59.2 2.2 %collective-permute-done.8.refs_0_.refs_10_ = bf16[256,1024]{1,0:T(8,128)(2,1)S(1)} collective-permute-done((bf16[256,1024]{1,0:T(8,128)(2,1)S(1)}, bf16[256,1024]{1,0:T(8,128)(2,1)S(1)}, u32[]{:S(2)}, u32[]{:S(2)}) %collective-permute-start.8) | collective-permute-done | bytes 524320 | tf_op jit(solution)/shard_map/ppermute | solution.py:456
  61.4 10.7 %all-gather.3 = bf16[256,1024]{1,0:T(8,128)(2,1)S(1)} all-gather(bf16[128,1024]{1,0:T(8,128)(2,1)S(1)} %slice.12), channel_id=5, replica_groups=mesh['groups'=2,'ctx'=4,'enc'=2,'tp'=2] {'tp'}, dimensions={0}, use_global_device_ids=true | all-gather | bytes 786432 | tf_op jit(solution)/shard_map/all_gather | solution.py:480
  72.1 0.2 squares.3.before_too
  72.3 0.8 collective-permute-done.11.refs_3_
  73.0 3.9 %collective-permute-done.12.refs_5_ = bf16[80,1024]{1,0:T(8,128)(2,1)S(1)} collective-permute-done((bf16[80,1024]{1,0:T(8,128)(2,1)S(1)}, bf16[80,1024]{1,0:T(8,128)(2,1)S(1)}, u32[]{:S(2)}, u32[]{:S(2)}) %collective-permute-start.12) | collective-permute-done | bytes 163872 | tf_op jit(solution)/shard_map/ppermute | solution.py:471
  76.9 2.4 %place_and_norm.1 = bf16[128,8192]{1,0:T(8,128)(2,1)} custom-call(bf16[1,8192]{1,0:T(2,128)(2,1)S(1)} %broadcast_in_dim.30.gain, f32[128,1]{1,0:T(8,128)S(1)} %squares.2.before, f32[128,1]{1,0:T(8,128)S(1)} %squares.3.before_too, bf16[128,128]{1,0:T(8,128)(2,1)S(1)} %get-tuple-element.67.refs_0_, bf16[128,128]{1,0:T(8,128)(2,1)S(1)} %get-tuple-element.68.refs_1_, ...), custom_call_target="tpu_custom_call" | custom-call | flops 262144 | bytes 262144 | tf_op jit(solution)/shard_map/place_and_norm/pallas_call | solution.py:433
  (27 shorter events, 0.1 us)
Async XLA Ops:
  2.3 13.6 %collective-permute-start = (bf16[1296,128]{1,0:T(8,128)(2,1)}, bf16[1296,128]{1,0:T(8,128)(2,1)S(1)}, u32[]{:S(2)}, u32[]{:S(2)}) collective-permute-start(bf16[1296,128]{1,0:T(8,128)(2,1)} %get-tuple-element.40), channel_id=1, source_target_pairs={{0,4},{4,0},{8,12},{12,8},{1,5},{5,1},{9,13},{13,9},{2,6},{6,2},{1... | collective-permute-start | bytes 995336 | tf_op jit(solution)/shard_map/ppermute | solution.py:456
  2.5 13.4 %collective-permute-start.1 = (bf16[656,128]{1,0:T(8,128)(2,1)}, bf16[656,128]{1,0:T(8,128)(2,1)S(1)}, u32[]{:S(2)}, u32[]{:S(2)}) collective-permute-start(bf16[656,128]{1,0:T(8,128)(2,1)} %get-tuple-element.41), channel_id=1, source_target_pairs={{0,8},{4,12},{8,0},{12,4},{1,9},{5,13},{9,1},{13,5},{2,10},{6,14},... | collective-permute-start | bytes 503816 | tf_op jit(solution)/shard_map/ppermute | solution.py:456
  4.9 11.1 %collective-permute-start.2 = (bf16[656,128]{1,0:T(8,128)(2,1)}, bf16[656,128]{1,0:T(8,128)(2,1)S(1)}, u32[]{:S(2)}, u32[]{:S(2)}) collective-permute-start(bf16[656,128]{1,0:T(8,128)(2,1)} %get-tuple-element.42), channel_id=1, source_target_pairs={{0,12},{4,8},{8,4},{12,0},{1,13},{5,9},{9,5},{13,1},{2,14},{6,10},... | collective-permute-start | bytes 503816 | tf_op jit(solution)/shard_map/ppermute | solution.py:456
  6.4 1.7 %copy-start = (bf16[1280,1024]{1,0:T(8,128)(2,1)S(1)}, bf16[1280,1024]{1,0:T(8,128)(2,1)}, u32[]{:S(2)}) copy-start(bf16[1280,1024]{1,0:T(8,128)(2,1)} %wa.7) | copy-start | bytes 7864324
  8.1 1.7 %copy-start.2 = (bf16[1280,1024]{1,0:T(8,128)(2,1)S(1)}, bf16[1280,1024]{1,0:T(8,128)(2,1)}, u32[]{:S(2)}) copy-start(bf16[1280,1024]{1,0:T(8,128)(2,1)} %wf.7) | copy-start | bytes 7864324
  9.9 1.1 %copy-start.4 = (bf16[1,256,1280]{2,1,0:T(8,128)(2,1)S(1)}, bf16[1,256,1280]{2,1,0:T(8,128)(2,1)}, u32[]{:S(2)}) copy-start(bf16[1,256,1280]{2,1,0:T(8,128)(2,1)} %param.8) | copy-start | bytes 1966084
  11.0 0.7 copy-start.6
  11.6 11.7 %copy-start.8 = (bf16[8192]{0:T(1024)(128)(2,1)S(1)}, bf16[8192]{0:T(1024)(128)(2,1)}, u32[]{:S(2)}) copy-start(bf16[8192]{0:T(1024)(128)(2,1)} %param.15) | copy-start | bytes 49156
  11.6 11.7 %copy-start.1 = (bf16[1280,1024]{1,0:T(8,128)(2,1)S(1)}, bf16[1280,1024]{1,0:T(8,128)(2,1)}, u32[]{:S(2)}) copy-start(bf16[1280,1024]{1,0:T(8,128)(2,1)} %wa.7) | copy-start | bytes 7864324
  11.6 11.7 %copy-start.3 = (bf16[1280,1024]{1,0:T(8,128)(2,1)S(1)}, bf16[1280,1024]{1,0:T(8,128)(2,1)}, u32[]{:S(2)}) copy-start(bf16[1280,1024]{1,0:T(8,128)(2,1)} %wf.7) | copy-start | bytes 7864324
  15.9 9.1 %collective-permute-start.3 = (bf16[1296,128]{1,0:T(8,128)(2,1)S(1)}, bf16[1296,128]{1,0:T(8,128)(2,1)S(1)}, u32[]{:S(2)}, u32[]{:S(2)}) collective-permute-start(bf16[1296,128]{1,0:T(8,128)(2,1)S(1)} %collective-permute-done), channel_id=1, source_target_pairs={{0,1},{1,0},{2,3},{3,2},{4,5},{5,4},{6,7},{7,6},{8,9},{9,8},{10,11... | collective-permute-start | bytes 995336 | tf_op jit(solution)/shard_map/ppermute | solution.py:459
  21.3 3.6 %collective-permute-start.4 = (bf16[656,128]{1,0:T(8,128)(2,1)S(1)}, bf16[656,128]{1,0:T(8,128)(2,1)S(1)}, u32[]{:S(2)}, u32[]{:S(2)}) collective-permute-start(bf16[656,128]{1,0:T(8,128)(2,1)S(1)} %collective-permute-done.1), channel_id=1, source_target_pairs={{0,1},{1,0},{2,3},{3,2},{4,5},{5,4},{6,7},{7,6},{8,9},{9,8},{10,11... | collective-permute-start | bytes 503816 | tf_op jit(solution)/shard_map/ppermute | solution.py:459
  21.3 3.6 %collective-permute-start.5 = (bf16[656,128]{1,0:T(8,128)(2,1)S(1)}, bf16[656,128]{1,0:T(8,128)(2,1)S(1)}, u32[]{:S(2)}, u32[]{:S(2)}) collective-permute-start(bf16[656,128]{1,0:T(8,128)(2,1)S(1)} %collective-permute-done.2), channel_id=1, source_target_pairs={{0,1},{1,0},{2,3},{3,2},{4,5},{5,4},{6,7},{7,6},{8,9},{9,8},{10,11... | collective-permute-start | bytes 503816 | tf_op jit(solution)/shard_map/ppermute | solution.py:459
  21.8 9.1 %collective-permute-start.6 = (bf16[656,128]{1,0:T(8,128)(2,1)S(1)}, bf16[656,128]{1,0:T(8,128)(2,1)S(1)}, u32[]{:S(2)}, u32[]{:S(2)}) collective-permute-start(bf16[656,128]{1,0:T(8,128)(2,1)S(1)} %collective-permute-done.1), channel_id=1, source_target_pairs={{0,4},{4,0},{8,12},{12,8},{1,5},{5,1},{9,13},{13,9},{2,6},{6,2},{1... | collective-permute-start | bytes 503816 | tf_op jit(solution)/shard_map/ppermute | solution.py:456
  22.8 8.5 %collective-permute-start.7 = (bf16[656,128]{1,0:T(8,128)(2,1)S(1)}, bf16[656,128]{1,0:T(8,128)(2,1)S(1)}, u32[]{:S(2)}, u32[]{:S(2)}) collective-permute-start(bf16[656,128]{1,0:T(8,128)(2,1)S(1)} %collective-permute-done.2), channel_id=1, source_target_pairs={{0,4},{4,0},{8,12},{12,8},{1,5},{5,1},{9,13},{13,9},{2,6},{6,2},{1... | collective-permute-start | bytes 503816 | tf_op jit(solution)/shard_map/ppermute | solution.py:456
  25.0 1.6 %copy-start.5 = (s32[1,256]{1,0:T(1,128)S(1)}, s32[1,256]{1,0:T(1,128)}, u32[]{:S(2)}) copy-start(s32[1,256]{1,0:T(1,128)} %refs_0_) | copy-start | bytes 3076
  28.7 20.5 %collective-permute-start.10 = (bf16[96,1024]{1,0:T(8,128)(2,1)S(1)}, bf16[96,1024]{1,0:T(8,128)(2,1)S(1)}, u32[]{:S(2)}, u32[]{:S(2)}) collective-permute-start(bf16[96,1024]{1,0:T(8,128)(2,1)S(1)} %packet.5), channel_id=1, source_target_pairs={{0,8},{4,12},{8,0},{12,4},{1,9},{5,13},{9,1},{13,5},{2,10},{6,14},... | collective-permute-start | bytes 589832 | tf_op jit(solution)/shard_map/ppermute | solution.py:456
  29.8 22.1 %collective-permute-start.9 = (bf16[96,1024]{1,0:T(8,128)(2,1)S(1)}, bf16[96,1024]{1,0:T(8,128)(2,1)S(1)}, u32[]{:S(2)}, u32[]{:S(2)}) collective-permute-start(bf16[96,1024]{1,0:T(8,128)(2,1)S(1)} %packet.4), channel_id=1, source_target_pairs={{0,12},{4,8},{8,4},{12,0},{1,13},{5,9},{9,5},{13,1},{2,14},{6,10},... | collective-permute-start | bytes 589832 | tf_op jit(solution)/shard_map/ppermute | solution.py:456
  39.5 6.7 %copy-start.7 = (s32[1,256]{1,0:T(1,128)S(1)}, s32[1,256]{1,0:T(1,128)}, u32[]{:S(2)}) copy-start(s32[1,256]{1,0:T(1,128)} %get-tuple-element.66.parity) | copy-start | bytes 3076
  40.9 31.4 %collective-permute-start.13 = (bf16[80,1024]{1,0:T(8,128)(2,1)S(1)}, bf16[80,1024]{1,0:T(8,128)(2,1)S(1)}, u32[]{:S(2)}, u32[]{:S(2)}) collective-permute-start(bf16[80,1024]{1,0:T(8,128)(2,1)S(1)} %get-tuple-element.62), channel_id=1, source_target_pairs={{0,8},{1,9},{4,12},{5,13},{8,0},{9,1},{12,4},{13,5},{2,10},{3,11},... | collective-permute-start | bytes 491528 | tf_op jit(solution)/shard_map/ppermute | solution.py:471
  43.3 18.0 %collective-permute-start.8 = (bf16[256,1024]{1,0:T(8,128)(2,1)S(1)}, bf16[256,1024]{1,0:T(8,128)(2,1)S(1)}, u32[]{:S(2)}, u32[]{:S(2)}) collective-permute-start(bf16[256,1024]{1,0:T(8,128)(2,1)S(1)} %select.2), channel_id=1, source_target_pairs={{0,4},{4,0},{8,12},{12,8},{1,5},{5,1},{9,13},{13,9},{2,6},{6,2},{1... | collective-permute-start | bytes 1572872 | tf_op jit(solution)/shard_map/ppermute | solution.py:456
  44.5 27.8 %collective-permute-start.14 = (bf16[80,1024]{1,0:T(8,128)(2,1)S(1)}, bf16[80,1024]{1,0:T(8,128)(2,1)S(1)}, u32[]{:S(2)}, u32[]{:S(2)}) collective-permute-start(bf16[80,1024]{1,0:T(8,128)(2,1)S(1)} %get-tuple-element.74), channel_id=1, source_target_pairs={{0,9},{1,8},{4,13},{5,12},{8,1},{9,0},{12,5},{13,4},{2,11},{3,10},... | collective-permute-start | bytes 491528 | tf_op jit(solution)/shard_map/ppermute | solution.py:471
  51.9 21.1 %collective-permute-start.11 = (bf16[80,1024]{1,0:T(8,128)(2,1)S(1)}, bf16[80,1024]{1,0:T(8,128)(2,1)S(1)}, u32[]{:S(2)}, u32[]{:S(2)}) collective-permute-start(bf16[80,1024]{1,0:T(8,128)(2,1)S(1)} %get-tuple-element.71), channel_id=1, source_target_pairs={{0,12},{1,13},{4,8},{5,9},{8,4},{9,5},{12,0},{13,1},{2,14},{3,15},... | collective-permute-start | bytes 491528 | tf_op jit(solution)/shard_map/ppermute | solution.py:471
  52.0 24.9 %collective-permute-start.12 = (bf16[80,1024]{1,0:T(8,128)(2,1)S(1)}, bf16[80,1024]{1,0:T(8,128)(2,1)S(1)}, u32[]{:S(2)}, u32[]{:S(2)}) collective-permute-start(bf16[80,1024]{1,0:T(8,128)(2,1)S(1)} %get-tuple-element.72), channel_id=1, source_target_pairs={{0,13},{1,12},{4,9},{5,8},{8,5},{9,4},{12,1},{13,0},{2,15},{3,14},... | collective-permute-start | bytes 491528 | tf_op jit(solution)/shard_map/ppermute | solution.py:471

commit v15 on v14

--- a/solution.py
+++ b/solution.py
@@ -504,15 +504,16 @@
         slots[0] = after(slots[0], chosen)
         pieces[1] = over_ctx(chosen, 1)
         rest = {}
-        for m in (3, 2):
+        for m in (2, 3):
             chosen = packet(m, early, blocks, slots, half - size, True)
             slots[0] = after(slots[0], chosen[0])
-            if m == 3:
-                joined = lax.optimization_barrier((*chosen, sent[3], sent[2]))
-                chosen, sent[3], sent[2] = joined[:2], joined[2], joined[3]
+            waited = 3 if m == 2 else 2
+            joined = lax.optimization_barrier((*chosen, sent[waited]))
+            chosen, sent[waited] = joined[:2], joined[2]
             rest[m] = [to_core(piece, m, d) for d, piece in enumerate(chosen)]
 
         orders = order_of(size, parity, slots, half)
+        slots[0] = after(slots[0], rest[2][0])
         total = [own_piece(), near_piece(None)]
         for m in (3, 2):
             whole_packet = sent[m]

time: 79.7 us -> 77.9 us (0.977)
  the two profiles are of different devices: /device:TPU:11 before, /device:TPU:0 now
where the time goes in v15:
time: 77.9 us; the launch traced here: 77.2 us
  waiting for transfers between devices  20.6 us (26%)
  Pallas kernels  18.2 us (23%)
  starting transfers between devices  17.9 us (23%)
  blocking collectives  13.5 us (17%)
  local copies, waits for them, and re-layouts  6.69 us (9%)
    ppermute x8, waiting for transfers between devices, over_ctx(): return lax.ppermute(x, 'ctx', [(i, i ^ m) for i in range(n)])  20.6 us
    ppermute x8, starting transfers between devices, over_ctx(): return lax.ppermute(x, 'ctx', [(i, i ^ m) for i in range(n)])  11.8 us
    ppermute x4, starting transfers between devices, to_core(): return lax.ppermute(x, ('ctx', 'tp'), pairs)  5.61 us
    unnamed x18, local copies, waits for them, and re-layouts  5.27 us
    all_gather x2, blocking collectives, body(): sent[m] = [whole_packet, lax.all_gather(whole_packet[size:], 'tp', axis=0)]  5.07 us
    pallas_call x4, Pallas kernels, packet(): pl.pallas_call(functools.partial(packet_kernel, m, early, len(blocks), se...  4.84 us
    pallas_call x3, Pallas kernels, project_parts(): pl.pallas_call(project_parts_kernel, out_shape=[jax.ShapeDtypeStruct((row...  4.78 us
    all_gather x2, blocking collectives, body(): take([lax.all_gather(part, 'tp', axis=0) for part in shared])  4.07 us
  transfers between devices with their start and end apart: 15, of which 5 were waited for; matrix products, arithmetic and copies ran while one was open for 2% of the time, Pallas kernels for 18%

profile of v15, /device:TPU:0, one launch (start us, length us, event | category | flops | bytes accessed | tf_op | source)
XLA Modules:
  0.0 77.2 jit_solution(18375521359419383349)
XLA Ops:
  0.0 2.3 %to_send.1 = (bf16[1296,128]{1,0:T(8,128)(2,1)}, bf16[656,128]{1,0:T(8,128)(2,1)}, bf16[656,128]{1,0:T(8,128)(2,1)}, s32[1,256]{1,0:T(1,128)}) custom-call(bf16[256,1280]{1,0:T(8,128)(2,1)} %bitcast.16, s32[1,256]{1,0:T(1,128)} %refs_0_, s32[1,256]{1,0:T(1,128)} %kind.3), custom_call_target="tpu_custom_call" | custom-call | bytes 40960 | tf_op jit(solution)/shard_map/to_send/pallas_call | solution.py:109
  2.3 3.1 %collective-permute-start = (bf16[1296,128]{1,0:T(8,128)(2,1)}, bf16[1296,128]{1,0:T(8,128)(2,1)S(1)}, u32[]{:S(2)}, u32[]{:S(2)}) collective-permute-start(bf16[1296,128]{1,0:T(8,128)(2,1)} %get-tuple-element.43), channel_id=1, source_target_pairs={{0,4},{4,0},{8,12},{12,8},{1,5},{5,1},{9,13},{13,9},{2,6},{6,2},{1... | collective-permute-start | bytes 995336 | tf_op jit(solution)/shard_map/ppermute | solution.py:456
  5.4 2.6 %collective-permute-start.1 = (bf16[656,128]{1,0:T(8,128)(2,1)}, bf16[656,128]{1,0:T(8,128)(2,1)S(1)}, u32[]{:S(2)}, u32[]{:S(2)}) collective-permute-start(bf16[656,128]{1,0:T(8,128)(2,1)} %get-tuple-element.44), channel_id=1, source_target_pairs={{0,8},{4,12},{8,0},{12,4},{1,9},{5,13},{9,1},{13,5},{2,10},{6,14},... | collective-permute-start | bytes 503816 | tf_op jit(solution)/shard_map/ppermute | solution.py:456
  8.0 0.0 collective-permute-start.2
  8.0 0.7 broadcast_in_dim.31.ba
  8.7 0.7 broadcast_in_dim.32.bf
  9.4 1.7 %copy-done = bf16[1280,1024]{1,0:T(8,128)(2,1)S(1)} copy-done((bf16[1280,1024]{1,0:T(8,128)(2,1)S(1)}, bf16[1280,1024]{1,0:T(8,128)(2,1)}, u32[]{:S(2)}) %copy-start) | copy-done | bytes 2621464
  11.1 1.7 %copy-done.2 = bf16[1280,1024]{1,0:T(8,128)(2,1)S(1)} copy-done((bf16[1280,1024]{1,0:T(8,128)(2,1)S(1)}, bf16[1280,1024]{1,0:T(8,128)(2,1)}, u32[]{:S(2)}) %copy-start.2) | copy-done | bytes 2621464
  12.8 1.1 %copy-done.4 = bf16[1,256,1280]{2,1,0:T(8,128)(2,1)S(1)} copy-done((bf16[1,256,1280]{2,1,0:T(8,128)(2,1)S(1)}, bf16[1,256,1280]{2,1,0:T(8,128)(2,1)}, u32[]{:S(2)}) %copy-start.4) | copy-done | bytes 655384
  13.9 0.7 copy-done.6
  14.6 1.6 %project_own.1.refs_0_ = bf16[256,1024]{1,0:T(8,128)(2,1)S(1)} custom-call(s32[1,256]{1,0:T(1,128)S(1)} %copy-done.6, bf16[256,1280]{1,0:T(8,128)(2,1)S(1)} %bitcast.17, bf16[1280,1024]{1,0:T(8,128)(2,1)S(1)} %copy-done, bf16[1280,1024]{1,0:T(8,128)(2,1)S(1)} %copy-done.2, bf16[1,1024]{1,0:T(2,128)(2,1)S(1)} %broadcast_in_dim.31.ba, ...), custom_call_target="tpu_custom_call" | custom-call | flops 83886080 | bytes 327680 | tf_op jit(solution)/shard_map/project_own/pallas_call | solution.py:147
  16.2 1.4 %collective-permute-done.1 = bf16[656,128]{1,0:T(8,128)(2,1)S(1)} collective-permute-done((bf16[656,128]{1,0:T(8,128)(2,1)}, bf16[656,128]{1,0:T(8,128)(2,1)S(1)}, u32[]{:S(2)}, u32[]{:S(2)}) %collective-permute-start.1) | collective-permute-done | bytes 167968 | tf_op jit(solution)/shard_map/ppermute | solution.py:456
  17.6 5.3 %collective-permute-done.2 = bf16[656,128]{1,0:T(8,128)(2,1)S(1)} collective-permute-done((bf16[656,128]{1,0:T(8,128)(2,1)}, bf16[656,128]{1,0:T(8,128)(2,1)S(1)}, u32[]{:S(2)}, u32[]{:S(2)}) %collective-permute-start.2) | collective-permute-done | bytes 167968 | tf_op jit(solution)/shard_map/ppermute | solution.py:456
  22.9 0.5 collective-permute-start.4
  23.4 0.0 collective-permute-start.5
  23.4 0.8 collective-permute-start.6
  24.2 1.3 %collective-permute-start.7 = (bf16[656,128]{1,0:T(8,128)(2,1)S(1)}, bf16[656,128]{1,0:T(8,128)(2,1)S(1)}, u32[]{:S(2)}, u32[]{:S(2)}) collective-permute-start(bf16[656,128]{1,0:T(8,128)(2,1)S(1)} %collective-permute-done.2), channel_id=1, source_target_pairs={{0,4},{4,0},{8,12},{12,8},{1,5},{5,1},{9,13},{13,9},{2,6},{6,2},{1... | collective-permute-start | bytes 503816 | tf_op jit(solution)/shard_map/ppermute | solution.py:456
  25.5 1.6 %project_parts.3 = (bf16[256,1024]{1,0:T(8,128)(2,1)S(1)}, s32[1,256]{1,0:T(1,128)S(1)}) custom-call(bf16[1280,1024]{1,0:T(8,128)(2,1)S(1)} %copy-done.1, bf16[1280,1024]{1,0:T(8,128)(2,1)S(1)} %copy-done.3, bf16[1,1024]{1,0:T(2,128)(2,1)S(1)} %broadcast_in_dim.31.ba, bf16[1,1024]{1,0:T(2,128)(2,1)S(1)} %broadcast_in_dim.32.bf, ...), custom_call_target="tpu_custom_call" | custom-call | flops 83886080 | bytes 327680 | tf_op jit(solution)/shard_map/project_parts/pallas_call | solution.py:177
  27.1 0.0 collective-permute-done.4
  27.1 0.0 copy-start.5
  27.1 0.0 copy-start.8
  27.1 1.6 %project_parts.4 = (bf16[256,1024]{1,0:T(8,128)(2,1)S(1)}, s32[1,256]{1,0:T(1,128)S(1)}) custom-call(bf16[1280,1024]{1,0:T(8,128)(2,1)S(1)} %copy-done.1, bf16[1280,1024]{1,0:T(8,128)(2,1)S(1)} %copy-done.3, bf16[1,1024]{1,0:T(2,128)(2,1)S(1)} %broadcast_in_dim.31.ba, bf16[1,1024]{1,0:T(2,128)(2,1)S(1)} %broadcast_in_dim.32.bf, ...), custom_call_target="tpu_custom_call" | custom-call | flops 83886080 | bytes 327680 | tf_op jit(solution)/shard_map/project_parts/pallas_call | solution.py:177
  28.7 1.0 %packet.4 = bf16[96,1024]{1,0:T(8,128)(2,1)S(1)} custom-call(bf16[256,1024]{1,0:T(8,128)(2,1)S(1)} %project_own.1.refs_0_, bf16[256,1024]{1,0:T(8,128)(2,1)S(1)} %get-tuple-element.49.refs_1_, bf16[256,1024]{1,0:T(8,128)(2,1)S(1)} %get-tuple-element.53.refs_2_, s32[1,256]{1,0:T(1,128)S(1)} %copy-done.5, ...), custom_call_target="tpu_custom_call" | custom-call | flops 9437184 | bytes 98304 | tf_op jit(solution)/shard_map/packet/pallas_call | solution.py:279
  29.8 1.5 %collective-permute-start.8 = (bf16[96,1024]{1,0:T(8,128)(2,1)S(1)}, bf16[96,1024]{1,0:T(8,128)(2,1)S(1)}, u32[]{:S(2)}, u32[]{:S(2)}) collective-permute-start(bf16[96,1024]{1,0:T(8,128)(2,1)S(1)} %packet.4), channel_id=1, source_target_pairs={{0,12},{4,8},{8,4},{12,0},{1,13},{5,9},{9,5},{13,1},{2,14},{6,10},... | collective-permute-start | bytes 589832 | tf_op jit(solution)/shard_map/ppermute | solution.py:456
  31.3 1.0 %packet.5 = bf16[96,1024]{1,0:T(8,128)(2,1)S(1)} custom-call(bf16[256,1024]{1,0:T(8,128)(2,1)S(1)} %project_own.1.refs_0_, bf16[256,1024]{1,0:T(8,128)(2,1)S(1)} %get-tuple-element.49.refs_1_, bf16[256,1024]{1,0:T(8,128)(2,1)S(1)} %get-tuple-element.53.refs_2_, s32[1,256]{1,0:T(1,128)S(1)} %copy-done.5, ...), custom_call_target="tpu_custom_call" | custom-call | flops 9437184 | bytes 98304 | tf_op jit(solution)/shard_map/packet/pallas_call | solution.py:279
  32.4 0.8 %collective-permute-start.11 = (bf16[96,1024]{1,0:T(8,128)(2,1)S(1)}, bf16[96,1024]{1,0:T(8,128)(2,1)S(1)}, u32[]{:S(2)}, u32[]{:S(2)}) collective-permute-start(bf16[96,1024]{1,0:T(8,128)(2,1)S(1)} %packet.5), channel_id=1, source_target_pairs={{0,8},{4,12},{8,0},{12,4},{1,9},{5,13},{9,1},{13,5},{2,10},{6,14},... | collective-permute-start | bytes 589832 | tf_op jit(solution)/shard_map/ppermute | solution.py:456
  33.2 0.5 collective-permute-done.7
  33.7 2.0 %all-gather = bf16[1312,128]{1,0:T(8,128)(2,1)S(1)} all-gather(bf16[656,128]{1,0:T(8,128)(2,1)S(1)} %collective-permute-done.6), channel_id=2, replica_groups=mesh['groups'=2,'ctx'=4,'enc'=2,'tp'=2] {'tp'}, dimensions={0}, use_global_device_ids=true | all-gather | bytes 503808 | tf_op jit(solution)/shard_map/all_gather | solution.py:501
  35.8 2.0 %all-gather.1 = bf16[1312,128]{1,0:T(8,128)(2,1)S(1)} all-gather(bf16[656,128]{1,0:T(8,128)(2,1)S(1)} %collective-permute-done.7), channel_id=3, replica_groups=mesh['groups'=2,'ctx'=4,'enc'=2,'tp'=2] {'tp'}, dimensions={0}, use_global_device_ids=true | all-gather | bytes 503808 | tf_op jit(solution)/shard_map/all_gather | solution.py:501
  37.8 1.6 %project_parts.5 = (bf16[256,1024]{1,0:T(8,128)(2,1)S(1)}, s32[1,256]{1,0:T(1,128)S(1)}) custom-call(bf16[1280,1024]{1,0:T(8,128)(2,1)S(1)} %copy-done.1, bf16[1280,1024]{1,0:T(8,128)(2,1)S(1)} %copy-done.3, bf16[1,1024]{1,0:T(2,128)(2,1)S(1)} %broadcast_in_dim.31.ba, bf16[1,1024]{1,0:T(2,128)(2,1)S(1)} %broadcast_in_dim.32.bf, ...), custom_call_target="tpu_custom_call" | custom-call | flops 83886080 | bytes 327680 | tf_op jit(solution)/shard_map/project_parts/pallas_call | solution.py:177
  39.4 0.7 select.2
  40.1 1.7 %collective-permute-start.10 = (bf16[256,1024]{1,0:T(8,128)(2,1)S(1)}, bf16[256,1024]{1,0:T(8,128)(2,1)S(1)}, u32[]{:S(2)}, u32[]{:S(2)}) collective-permute-start(bf16[256,1024]{1,0:T(8,128)(2,1)S(1)} %select.2), channel_id=1, source_target_pairs={{0,4},{4,0},{8,12},{12,8},{1,5},{5,1},{9,13},{13,9},{2,6},{6,2},{1... | collective-permute-start | bytes 1572872 | tf_op jit(solution)/shard_map/ppermute | solution.py:456
  41.9 1.4 %packet.6 = (bf16[80,1024]{1,0:T(8,128)(2,1)S(1)}, bf16[80,1024]{1,0:T(8,128)(2,1)S(1)}) custom-call(bf16[256,1024]{1,0:T(8,128)(2,1)S(1)} %project_own.1.refs_0_, bf16[256,1024]{1,0:T(8,128)(2,1)S(1)} %get-tuple-element.49.refs_1_, bf16[256,1024]{1,0:T(8,128)(2,1)S(1)} %get-tuple-element.53.refs_2_, bf16[256,1024]{1,0:T(8,128)(2,1)S(1)} %get-tuple-element.56.refs_3_, ...), custom_call_target="tpu_custom_call" | custom-call | flops 20971520 | bytes 131072 | tf_op jit(solution)/shard_map/packet/pallas_call | solution.py:279
  43.2 1.4 %packet.7 = (bf16[80,1024]{1,0:T(8,128)(2,1)S(1)}, bf16[80,1024]{1,0:T(8,128)(2,1)S(1)}) custom-call(bf16[256,1024]{1,0:T(8,128)(2,1)S(1)} %project_own.1.refs_0_, bf16[256,1024]{1,0:T(8,128)(2,1)S(1)} %get-tuple-element.49.refs_1_, bf16[256,1024]{1,0:T(8,128)(2,1)S(1)} %get-tuple-element.53.refs_2_, bf16[256,1024]{1,0:T(8,128)(2,1)S(1)} %get-tuple-element.56.refs_3_, ...), custom_call_target="tpu_custom_call" | custom-call | flops 20971520 | bytes 131072 | tf_op jit(solution)/shard_map/packet/pallas_call | solution.py:279
  44.6 3.1 %collective-permute-start.9 = (bf16[80,1024]{1,0:T(8,128)(2,1)S(1)}, bf16[80,1024]{1,0:T(8,128)(2,1)S(1)}, u32[]{:S(2)}, u32[]{:S(2)}) collective-permute-start(bf16[80,1024]{1,0:T(8,128)(2,1)S(1)} %get-tuple-element.68), channel_id=1, source_target_pairs={{0,8},{1,9},{4,12},{5,13},{8,0},{9,1},{12,4},{13,5},{2,10},{3,11},... | collective-permute-start | bytes 491528 | tf_op jit(solution)/shard_map/ppermute | solution.py:471
  47.7 0.6 order_of.1
  48.4 0.1 collective-permute-start.14
  48.4 2.1 %collective-permute-done.11.refs_6_ = bf16[96,1024]{1,0:T(8,128)(2,1)S(1)} collective-permute-done((bf16[96,1024]{1,0:T(8,128)(2,1)S(1)}, bf16[96,1024]{1,0:T(8,128)(2,1)S(1)}, u32[]{:S(2)}, u32[]{:S(2)}) %collective-permute-start.11) | collective-permute-done | bytes 196640 | tf_op jit(solution)/shard_map/ppermute | solution.py:456
  50.6 2.4 %collective-permute-start.12 = (bf16[80,1024]{1,0:T(8,128)(2,1)S(1)}, bf16[80,1024]{1,0:T(8,128)(2,1)S(1)}, u32[]{:S(2)}, u32[]{:S(2)}) collective-permute-start(bf16[80,1024]{1,0:T(8,128)(2,1)S(1)} %get-tuple-element.77), channel_id=1, source_target_pairs={{0,12},{1,13},{4,8},{5,9},{8,4},{9,5},{12,0},{13,1},{2,14},{3,15},... | collective-permute-start | bytes 491528 | tf_op jit(solution)/shard_map/ppermute | solution.py:471
  53.0 3.1 %all-gather.4 = bf16[96,1024]{1,0:T(8,128)(2,1)S(1)} all-gather(bf16[48,1024]{1,0:T(8,128)(2,1)S(1)} %slice.10), channel_id=6, replica_groups=mesh['groups'=2,'ctx'=4,'enc'=2,'tp'=2] {'tp'}, dimensions={0}, use_global_device_ids=true | all-gather | bytes 294912 | tf_op jit(solution)/shard_map/all_gather | solution.py:520
  56.2 1.9 %all-gather.5 = bf16[96,1024]{1,0:T(8,128)(2,1)S(1)} all-gather(bf16[48,1024]{1,0:T(8,128)(2,1)S(1)} %slice.11), channel_id=7, replica_groups=mesh['groups'=2,'ctx'=4,'enc'=2,'tp'=2] {'tp'}, dimensions={0}, use_global_device_ids=true | all-gather | bytes 294912 | tf_op jit(solution)/shard_map/all_gather | solution.py:520
  58.1 0.7 select.3
  58.8 2.2 %all-gather.2 = bf16[256,1024]{1,0:T(8,128)(2,1)S(1)} all-gather(bf16[128,1024]{1,0:T(8,128)(2,1)S(1)} %get-tuple-element.71), channel_id=4, replica_groups=mesh['groups'=2,'ctx'=4,'enc'=2,'tp'=2] {'tp'}, dimensions={0}, use_global_device_ids=true | all-gather | bytes 786432 | tf_op jit(solution)/shard_map/all_gather | solution.py:475
  61.0 0.2 squares.2.before
  61.2 11.2 %collective-permute-done.10.refs_0_.refs_10_ = bf16[256,1024]{1,0:T(8,128)(2,1)S(1)} collective-permute-done((bf16[256,1024]{1,0:T(8,128)(2,1)S(1)}, bf16[256,1024]{1,0:T(8,128)(2,1)S(1)}, u32[]{:S(2)}, u32[]{:S(2)}) %collective-permute-start.10) | collective-permute-done | bytes 524320 | tf_op jit(solution)/shard_map/ppermute | solution.py:456
  72.4 2.2 %all-gather.3 = bf16[256,1024]{1,0:T(8,128)(2,1)S(1)} all-gather(bf16[128,1024]{1,0:T(8,128)(2,1)S(1)} %slice.12), channel_id=5, replica_groups=mesh['groups'=2,'ctx'=4,'enc'=2,'tp'=2] {'tp'}, dimensions={0}, use_global_device_ids=true | all-gather | bytes 786432 | tf_op jit(solution)/shard_map/all_gather | solution.py:480
  74.6 0.2 squares.3.before_too
  74.8 2.4 %place_and_norm.1 = bf16[128,8192]{1,0:T(8,128)(2,1)} custom-call(bf16[1,8192]{1,0:T(2,128)(2,1)S(1)} %broadcast_in_dim.30.gain, f32[128,1]{1,0:T(8,128)S(1)} %squares.2.before, f32[128,1]{1,0:T(8,128)S(1)} %squares.3.before_too, bf16[128,128]{1,0:T(8,128)(2,1)S(1)} %get-tuple-element.73.refs_0_, bf16[128,128]{1,0:T(8,128)(2,1)S(1)} %get-tuple-element.74.refs_1_, ...), custom_call_target="tpu_custom_call" | custom-call | flops 262144 | bytes 262144 | tf_op jit(solution)/shard_map/place_and_norm/pallas_call | solution.py:433
  (27 shorter events, 0.1 us)
Async XLA Ops:
  2.3 20.6 %collective-permute-start = (bf16[1296,128]{1,0:T(8,128)(2,1)}, bf16[1296,128]{1,0:T(8,128)(2,1)S(1)}, u32[]{:S(2)}, u32[]{:S(2)}) collective-permute-start(bf16[1296,128]{1,0:T(8,128)(2,1)} %get-tuple-element.43), channel_id=1, source_target_pairs={{0,4},{4,0},{8,12},{12,8},{1,5},{5,1},{9,13},{13,9},{2,6},{6,2},{1... | collective-permute-start | bytes 995336 | tf_op jit(solution)/shard_map/ppermute | solution.py:456
  5.4 12.2 %collective-permute-start.1 = (bf16[656,128]{1,0:T(8,128)(2,1)}, bf16[656,128]{1,0:T(8,128)(2,1)S(1)}, u32[]{:S(2)}, u32[]{:S(2)}) collective-permute-start(bf16[656,128]{1,0:T(8,128)(2,1)} %get-tuple-element.44), channel_id=1, source_target_pairs={{0,8},{4,12},{8,0},{12,4},{1,9},{5,13},{9,1},{13,5},{2,10},{6,14},... | collective-permute-start | bytes 503816 | tf_op jit(solution)/shard_map/ppermute | solution.py:456
  8.0 14.9 %collective-permute-start.2 = (bf16[656,128]{1,0:T(8,128)(2,1)}, bf16[656,128]{1,0:T(8,128)(2,1)S(1)}, u32[]{:S(2)}, u32[]{:S(2)}) collective-permute-start(bf16[656,128]{1,0:T(8,128)(2,1)} %get-tuple-element.45), channel_id=1, source_target_pairs={{0,12},{4,8},{8,4},{12,0},{1,13},{5,9},{9,5},{13,1},{2,14},{6,10},... | collective-permute-start | bytes 503816 | tf_op jit(solution)/shard_map/ppermute | solution.py:456
  9.4 1.7 %copy-start = (bf16[1280,1024]{1,0:T(8,128)(2,1)S(1)}, bf16[1280,1024]{1,0:T(8,128)(2,1)}, u32[]{:S(2)}) copy-start(bf16[1280,1024]{1,0:T(8,128)(2,1)} %wa.7) | copy-start | bytes 7864324
  11.1 1.7 %copy-start.2 = (bf16[1280,1024]{1,0:T(8,128)(2,1)S(1)}, bf16[1280,1024]{1,0:T(8,128)(2,1)}, u32[]{:S(2)}) copy-start(bf16[1280,1024]{1,0:T(8,128)(2,1)} %wf.7) | copy-start | bytes 7864324
  12.8 1.1 %copy-start.4 = (bf16[1,256,1280]{2,1,0:T(8,128)(2,1)S(1)}, bf16[1,256,1280]{2,1,0:T(8,128)(2,1)}, u32[]{:S(2)}) copy-start(bf16[1,256,1280]{2,1,0:T(8,128)(2,1)} %param.8) | copy-start | bytes 1966084
  13.9 0.7 copy-start.6
  14.6 10.8 %copy-start.1 = (bf16[1280,1024]{1,0:T(8,128)(2,1)S(1)}, bf16[1280,1024]{1,0:T(8,128)(2,1)}, u32[]{:S(2)}) copy-start(bf16[1280,1024]{1,0:T(8,128)(2,1)} %wa.7) | copy-start | bytes 7864324
  14.6 10.8 %copy-start.3 = (bf16[1280,1024]{1,0:T(8,128)(2,1)S(1)}, bf16[1280,1024]{1,0:T(8,128)(2,1)}, u32[]{:S(2)}) copy-start(bf16[1280,1024]{1,0:T(8,128)(2,1)} %wf.7) | copy-start | bytes 7864324
  22.9 4.2 %collective-permute-start.3 = (bf16[1296,128]{1,0:T(8,128)(2,1)S(1)}, bf16[1296,128]{1,0:T(8,128)(2,1)S(1)}, u32[]{:S(2)}, u32[]{:S(2)}) collective-permute-start(bf16[1296,128]{1,0:T(8,128)(2,1)S(1)} %collective-permute-done), channel_id=1, source_target_pairs={{0,1},{1,0},{2,3},{3,2},{4,5},{5,4},{6,7},{7,6},{8,9},{9,8},{10,11... | collective-permute-start | bytes 995336 | tf_op jit(solution)/shard_map/ppermute | solution.py:459
  22.9 4.2 %collective-permute-start.4 = (bf16[656,128]{1,0:T(8,128)(2,1)S(1)}, bf16[656,128]{1,0:T(8,128)(2,1)S(1)}, u32[]{:S(2)}, u32[]{:S(2)}) collective-permute-start(bf16[656,128]{1,0:T(8,128)(2,1)S(1)} %collective-permute-done.1), channel_id=1, source_target_pairs={{0,1},{1,0},{2,3},{3,2},{4,5},{5,4},{6,7},{7,6},{8,9},{9,8},{10,11... | collective-permute-start | bytes 503816 | tf_op jit(solution)/shard_map/ppermute | solution.py:459
  23.4 3.7 %collective-permute-start.5 = (bf16[656,128]{1,0:T(8,128)(2,1)S(1)}, bf16[656,128]{1,0:T(8,128)(2,1)S(1)}, u32[]{:S(2)}, u32[]{:S(2)}) collective-permute-start(bf16[656,128]{1,0:T(8,128)(2,1)S(1)} %collective-permute-done.2), channel_id=1, source_target_pairs={{0,1},{1,0},{2,3},{3,2},{4,5},{5,4},{6,7},{7,6},{8,9},{9,8},{10,11... | collective-permute-start | bytes 503816 | tf_op jit(solution)/shard_map/ppermute | solution.py:459
  23.4 9.8 %collective-permute-start.6 = (bf16[656,128]{1,0:T(8,128)(2,1)S(1)}, bf16[656,128]{1,0:T(8,128)(2,1)S(1)}, u32[]{:S(2)}, u32[]{:S(2)}) collective-permute-start(bf16[656,128]{1,0:T(8,128)(2,1)S(1)} %collective-permute-done.1), channel_id=1, source_target_pairs={{0,4},{4,0},{8,12},{12,8},{1,5},{5,1},{9,13},{13,9},{2,6},{6,2},{1... | collective-permute-start | bytes 503816 | tf_op jit(solution)/shard_map/ppermute | solution.py:456
  24.2 9.5 %collective-permute-start.7 = (bf16[656,128]{1,0:T(8,128)(2,1)S(1)}, bf16[656,128]{1,0:T(8,128)(2,1)S(1)}, u32[]{:S(2)}, u32[]{:S(2)}) collective-permute-start(bf16[656,128]{1,0:T(8,128)(2,1)S(1)} %collective-permute-done.2), channel_id=1, source_target_pairs={{0,4},{4,0},{8,12},{12,8},{1,5},{5,1},{9,13},{13,9},{2,6},{6,2},{1... | collective-permute-start | bytes 503816 | tf_op jit(solution)/shard_map/ppermute | solution.py:456
  27.1 1.6 %copy-start.5 = (s32[1,256]{1,0:T(1,128)S(1)}, s32[1,256]{1,0:T(1,128)}, u32[]{:S(2)}) copy-start(s32[1,256]{1,0:T(1,128)} %refs_0_) | copy-start | bytes 3076
  27.1 4.2 %copy-start.8 = (bf16[8192]{0:T(1024)(128)(2,1)S(1)}, bf16[8192]{0:T(1024)(128)(2,1)}, u32[]{:S(2)}) copy-start(bf16[8192]{0:T(1024)(128)(2,1)} %param.15) | copy-start | bytes 49156
  29.8 14.8 %collective-permute-start.8 = (bf16[96,1024]{1,0:T(8,128)(2,1)S(1)}, bf16[96,1024]{1,0:T(8,128)(2,1)S(1)}, u32[]{:S(2)}, u32[]{:S(2)}) collective-permute-start(bf16[96,1024]{1,0:T(8,128)(2,1)S(1)} %packet.4), channel_id=1, source_target_pairs={{0,12},{4,8},{8,4},{12,0},{1,13},{5,9},{9,5},{13,1},{2,14},{6,10},... | collective-permute-start | bytes 589832 | tf_op jit(solution)/shard_map/ppermute | solution.py:456
  32.4 18.2 %collective-permute-start.11 = (bf16[96,1024]{1,0:T(8,128)(2,1)S(1)}, bf16[96,1024]{1,0:T(8,128)(2,1)S(1)}, u32[]{:S(2)}, u32[]{:S(2)}) collective-permute-start(bf16[96,1024]{1,0:T(8,128)(2,1)S(1)} %packet.5), channel_id=1, source_target_pairs={{0,8},{4,12},{8,0},{12,4},{1,9},{5,13},{9,1},{13,5},{2,10},{6,14},... | collective-permute-start | bytes 589832 | tf_op jit(solution)/shard_map/ppermute | solution.py:456
  40.1 7.6 %copy-start.7 = (s32[1,256]{1,0:T(1,128)S(1)}, s32[1,256]{1,0:T(1,128)}, u32[]{:S(2)}) copy-start(s32[1,256]{1,0:T(1,128)} %get-tuple-element.72.parity) | copy-start | bytes 3076
  40.1 32.3 %collective-permute-start.10 = (bf16[256,1024]{1,0:T(8,128)(2,1)S(1)}, bf16[256,1024]{1,0:T(8,128)(2,1)S(1)}, u32[]{:S(2)}, u32[]{:S(2)}) collective-permute-start(bf16[256,1024]{1,0:T(8,128)(2,1)S(1)} %select.2), channel_id=1, source_target_pairs={{0,4},{4,0},{8,12},{12,8},{1,5},{5,1},{9,13},{13,9},{2,6},{6,2},{1... | collective-permute-start | bytes 1572872 | tf_op jit(solution)/shard_map/ppermute | solution.py:456
  44.6 13.5 %collective-permute-start.9 = (bf16[80,1024]{1,0:T(8,128)(2,1)S(1)}, bf16[80,1024]{1,0:T(8,128)(2,1)S(1)}, u32[]{:S(2)}, u32[]{:S(2)}) collective-permute-start(bf16[80,1024]{1,0:T(8,128)(2,1)S(1)} %get-tuple-element.68), channel_id=1, source_target_pairs={{0,8},{1,9},{4,12},{5,13},{8,0},{9,1},{12,4},{13,5},{2,10},{3,11},... | collective-permute-start | bytes 491528 | tf_op jit(solution)/shard_map/ppermute | solution.py:471
  48.4 26.4 %collective-permute-start.14 = (bf16[80,1024]{1,0:T(8,128)(2,1)S(1)}, bf16[80,1024]{1,0:T(8,128)(2,1)S(1)}, u32[]{:S(2)}, u32[]{:S(2)}) collective-permute-start(bf16[80,1024]{1,0:T(8,128)(2,1)S(1)} %get-tuple-element.80), channel_id=1, source_target_pairs={{0,9},{1,8},{4,13},{5,12},{8,1},{9,0},{12,5},{13,4},{2,11},{3,10},... | collective-permute-start | bytes 491528 | tf_op jit(solution)/shard_map/ppermute | solution.py:471
  50.6 24.2 %collective-permute-start.12 = (bf16[80,1024]{1,0:T(8,128)(2,1)S(1)}, bf16[80,1024]{1,0:T(8,128)(2,1)S(1)}, u32[]{:S(2)}, u32[]{:S(2)}) collective-permute-start(bf16[80,1024]{1,0:T(8,128)(2,1)S(1)} %get-tuple-element.77), channel_id=1, source_target_pairs={{0,12},{1,13},{4,8},{5,9},{8,4},{9,5},{12,0},{13,1},{2,14},{3,15},... | collective-permute-start | bytes 491528 | tf_op jit(solution)/shard_map/ppermute | solution.py:471
  53.0 21.8 %collective-permute-start.13 = (bf16[80,1024]{1,0:T(8,128)(2,1)S(1)}, bf16[80,1024]{1,0:T(8,128)(2,1)S(1)}, u32[]{:S(2)}, u32[]{:S(2)}) collective-permute-start(bf16[80,1024]{1,0:T(8,128)(2,1)S(1)} %get-tuple-element.78), channel_id=1, source_target_pairs={{0,13},{1,12},{4,9},{5,8},{8,5},{9,4},{12,1},{13,0},{2,15},{3,14},... | collective-permute-start | bytes 491528 | tf_op jit(solution)/shard_map/ppermute | solution.py:471

commit v16 on v15

--- a/solution.py
+++ b/solution.py
@@ -117,10 +117,10 @@
             pltpu.VMEM(slot.shape, I32),
             pltpu.SemaphoreType.DMA((3,)),
         ],
-        compiler_params=pltpu.CompilerParams(vmem_limit_bytes=60 << 20),
+        compiler_params=pltpu.CompilerParams(vmem_limit_bytes=16 << 20),
         cost_estimate=cost(0, 4 * half * width),
         name="to_send",
-    )(rows, slot, kind)
+    )(*[pltpu.with_memory_space_constraint(x, pltpu.HBM) for x in (rows, slot, kind)])
 
 
 def column_of(row_vector):

time: 77.9 us -> 76.9 us (0.987)
    pallas_call x1, Pallas kernels: 2.3 us -> 1.51 us  [to_send(): pl.pallas_call(functools.partial(send_kernel, cuts), out_shape=out_shape,...]
    unnamed x18 -> x16, local copies, waits for them, and re-layouts: 5.27 us -> 5.26 us
where the time goes in v16:
time: 76.9 us; the launch traced here: 76.2 us
  waiting for transfers between devices  20.4 us (27%)
  starting transfers between devices  17.9 us (23%)
  Pallas kernels  17.5 us (23%)
  blocking collectives  13.5 us (18%)
  local copies, waits for them, and re-layouts  6.69 us (9%)
    ppermute x8, waiting for transfers between devices, over_ctx(): return lax.ppermute(x, 'ctx', [(i, i ^ m) for i in range(n)])  20.4 us
    ppermute x8, starting transfers between devices, over_ctx(): return lax.ppermute(x, 'ctx', [(i, i ^ m) for i in range(n)])  11.8 us
    ppermute x4, starting transfers between devices, to_core(): return lax.ppermute(x, ('ctx', 'tp'), pairs)  5.61 us
    unnamed x16, local copies, waits for them, and re-layouts  5.26 us
    all_gather x2, blocking collectives, body(): sent[m] = [whole_packet, lax.all_gather(whole_packet[size:], 'tp', axis=0)]  5.08 us
    pallas_call x4, Pallas kernels, packet(): pl.pallas_call(functools.partial(packet_kernel, m, early, len(blocks), se...  4.84 us
    pallas_call x3, Pallas kernels, project_parts(): pl.pallas_call(project_parts_kernel, out_shape=[jax.ShapeDtypeStruct((row...  4.8 us
    all_gather x2, blocking collectives, body(): take([lax.all_gather(part, 'tp', axis=0) for part in shared])  4.07 us
  transfers between devices with their start and end apart: 15, of which 5 were waited for; matrix products, arithmetic and copies ran while one was open for 2% of the time, Pallas kernels for 18%

profile of v16, /device:TPU:0, one launch (start us, length us, event | category | flops | bytes accessed | tf_op | source)
XLA Modules:
  0.0 76.2 jit_solution(7173288168867057169)
XLA Ops:
  0.0 1.5 %to_send.1 = (bf16[1296,128]{1,0:T(8,128)(2,1)S(1)}, bf16[656,128]{1,0:T(8,128)(2,1)S(1)}, bf16[656,128]{1,0:T(8,128)(2,1)S(1)}, s32[1,256]{1,0:T(1,128)S(1)}) custom-call(bf16[256,1280]{1,0:T(8,128)(2,1)} %bitcast.16, s32[1,256]{1,0:T(1,128)} %refs_0_, s32[1,256]{1,0:T(1,128)} %kind.3), custom_call_target="tpu_custom_call" | custom-call | bytes 40960 | tf_op jit(solution)/shard_map/to_send/pallas_call | solution.py:109
  1.5 3.1 %collective-permute-start = (bf16[1296,128]{1,0:T(8,128)(2,1)S(1)}, bf16[1296,128]{1,0:T(8,128)(2,1)S(1)}, u32[]{:S(2)}, u32[]{:S(2)}) collective-permute-start(bf16[1296,128]{1,0:T(8,128)(2,1)S(1)} %get-tuple-element.43), channel_id=1, source_target_pairs={{0,4},{4,0},{8,12},{12,8},{1,5},{5,1},{9,13},{13,9},{2,6},{6,2},{1... | collective-permute-start | bytes 995336 | tf_op jit(solution)/shard_map/ppermute | solution.py:456
  4.6 2.6 %collective-permute-start.1 = (bf16[656,128]{1,0:T(8,128)(2,1)S(1)}, bf16[656,128]{1,0:T(8,128)(2,1)S(1)}, u32[]{:S(2)}, u32[]{:S(2)}) collective-permute-start(bf16[656,128]{1,0:T(8,128)(2,1)S(1)} %get-tuple-element.44), channel_id=1, source_target_pairs={{0,8},{4,12},{8,0},{12,4},{1,9},{5,13},{9,1},{13,5},{2,10},{6,14},... | collective-permute-start | bytes 503816 | tf_op jit(solution)/shard_map/ppermute | solution.py:456
  7.2 0.7 broadcast_in_dim.31.ba
  7.9 0.7 broadcast_in_dim.32.bf
  8.6 1.7 %copy-done = bf16[1280,1024]{1,0:T(8,128)(2,1)S(1)} copy-done((bf16[1280,1024]{1,0:T(8,128)(2,1)S(1)}, bf16[1280,1024]{1,0:T(8,128)(2,1)}, u32[]{:S(2)}) %copy-start) | copy-done | bytes 2621464
  10.3 1.7 %copy-done.2 = bf16[1280,1024]{1,0:T(8,128)(2,1)S(1)} copy-done((bf16[1280,1024]{1,0:T(8,128)(2,1)S(1)}, bf16[1280,1024]{1,0:T(8,128)(2,1)}, u32[]{:S(2)}) %copy-start.2) | copy-done | bytes 2621464
  12.1 1.1 %copy-done.4 = bf16[1,256,1280]{2,1,0:T(8,128)(2,1)S(1)} copy-done((bf16[1,256,1280]{2,1,0:T(8,128)(2,1)S(1)}, bf16[1,256,1280]{2,1,0:T(8,128)(2,1)}, u32[]{:S(2)}) %copy-start.4) | copy-done | bytes 655384
  13.1 0.7 copy-done.6
  13.8 1.6 %project_own.1.refs_0_ = bf16[256,1024]{1,0:T(8,128)(2,1)S(1)} custom-call(s32[1,256]{1,0:T(1,128)S(1)} %copy-done.6, bf16[256,1280]{1,0:T(8,128)(2,1)S(1)} %bitcast.17, bf16[1280,1024]{1,0:T(8,128)(2,1)S(1)} %copy-done, bf16[1280,1024]{1,0:T(8,128)(2,1)S(1)} %copy-done.2, bf16[1,1024]{1,0:T(2,128)(2,1)S(1)} %broadcast_in_dim.31.ba, ...), custom_call_target="tpu_custom_call" | custom-call | flops 83886080 | bytes 327680 | tf_op jit(solution)/shard_map/project_own/pallas_call | solution.py:147
  15.4 1.1 %collective-permute-done.1 = bf16[656,128]{1,0:T(8,128)(2,1)S(1)} collective-permute-done((bf16[656,128]{1,0:T(8,128)(2,1)S(1)}, bf16[656,128]{1,0:T(8,128)(2,1)S(1)}, u32[]{:S(2)}, u32[]{:S(2)}) %collective-permute-start.1) | collective-permute-done | bytes 167968 | tf_op jit(solution)/shard_map/ppermute | solution.py:456
  16.5 5.4 %collective-permute-done.2 = bf16[656,128]{1,0:T(8,128)(2,1)S(1)} collective-permute-done((bf16[656,128]{1,0:T(8,128)(2,1)S(1)}, bf16[656,128]{1,0:T(8,128)(2,1)S(1)}, u32[]{:S(2)}, u32[]{:S(2)}) %collective-permute-start.2) | collective-permute-done | bytes 167968 | tf_op jit(solution)/shard_map/ppermute | solution.py:456
  21.9 0.0 collective-permute-done
  21.9 0.0 collective-permute-start.3
  21.9 0.5 collective-permute-start.4
  22.4 0.0 collective-permute-start.5
  22.4 0.8 collective-permute-start.6
  23.2 1.3 %collective-permute-start.7 = (bf16[656,128]{1,0:T(8,128)(2,1)S(1)}, bf16[656,128]{1,0:T(8,128)(2,1)S(1)}, u32[]{:S(2)}, u32[]{:S(2)}) collective-permute-start(bf16[656,128]{1,0:T(8,128)(2,1)S(1)} %collective-permute-done.2), channel_id=1, source_target_pairs={{0,4},{4,0},{8,12},{12,8},{1,5},{5,1},{9,13},{13,9},{2,6},{6,2},{1... | collective-permute-start | bytes 503816 | tf_op jit(solution)/shard_map/ppermute | solution.py:456
  24.5 1.6 %project_parts.3 = (bf16[256,1024]{1,0:T(8,128)(2,1)S(1)}, s32[1,256]{1,0:T(1,128)S(1)}) custom-call(bf16[1280,1024]{1,0:T(8,128)(2,1)S(1)} %copy-done.1, bf16[1280,1024]{1,0:T(8,128)(2,1)S(1)} %copy-done.3, bf16[1,1024]{1,0:T(2,128)(2,1)S(1)} %broadcast_in_dim.31.ba, bf16[1,1024]{1,0:T(2,128)(2,1)S(1)} %broadcast_in_dim.32.bf, ...), custom_call_target="tpu_custom_call" | custom-call | flops 83886080 | bytes 327680 | tf_op jit(solution)/shard_map/project_parts/pallas_call | solution.py:177
  26.1 0.0 copy-start.5
  26.1 0.0 copy-start.7
  26.1 1.6 %project_parts.4 = (bf16[256,1024]{1,0:T(8,128)(2,1)S(1)}, s32[1,256]{1,0:T(1,128)S(1)}) custom-call(bf16[1280,1024]{1,0:T(8,128)(2,1)S(1)} %copy-done.1, bf16[1280,1024]{1,0:T(8,128)(2,1)S(1)} %copy-done.3, bf16[1,1024]{1,0:T(2,128)(2,1)S(1)} %broadcast_in_dim.31.ba, bf16[1,1024]{1,0:T(2,128)(2,1)S(1)} %broadcast_in_dim.32.bf, ...), custom_call_target="tpu_custom_call" | custom-call | flops 83886080 | bytes 327680 | tf_op jit(solution)/shard_map/project_parts/pallas_call | solution.py:177
  27.7 1.0 %packet.4 = bf16[96,1024]{1,0:T(8,128)(2,1)S(1)} custom-call(bf16[256,1024]{1,0:T(8,128)(2,1)S(1)} %project_own.1.refs_0_, bf16[256,1024]{1,0:T(8,128)(2,1)S(1)} %get-tuple-element.49.refs_1_, bf16[256,1024]{1,0:T(8,128)(2,1)S(1)} %get-tuple-element.53.refs_2_, s32[1,256]{1,0:T(1,128)S(1)} %copy-done.5, ...), custom_call_target="tpu_custom_call" | custom-call | flops 9437184 | bytes 98304 | tf_op jit(solution)/shard_map/packet/pallas_call | solution.py:279
  28.8 1.5 %collective-permute-start.8 = (bf16[96,1024]{1,0:T(8,128)(2,1)S(1)}, bf16[96,1024]{1,0:T(8,128)(2,1)S(1)}, u32[]{:S(2)}, u32[]{:S(2)}) collective-permute-start(bf16[96,1024]{1,0:T(8,128)(2,1)S(1)} %packet.4), channel_id=1, source_target_pairs={{0,12},{4,8},{8,4},{12,0},{1,13},{5,9},{9,5},{13,1},{2,14},{6,10},... | collective-permute-start | bytes 589832 | tf_op jit(solution)/shard_map/ppermute | solution.py:456
  30.3 1.0 %packet.5 = bf16[96,1024]{1,0:T(8,128)(2,1)S(1)} custom-call(bf16[256,1024]{1,0:T(8,128)(2,1)S(1)} %project_own.1.refs_0_, bf16[256,1024]{1,0:T(8,128)(2,1)S(1)} %get-tuple-element.49.refs_1_, bf16[256,1024]{1,0:T(8,128)(2,1)S(1)} %get-tuple-element.53.refs_2_, s32[1,256]{1,0:T(1,128)S(1)} %copy-done.5, ...), custom_call_target="tpu_custom_call" | custom-call | flops 9437184 | bytes 98304 | tf_op jit(solution)/shard_map/packet/pallas_call | solution.py:279
  31.4 0.8 %collective-permute-start.11 = (bf16[96,1024]{1,0:T(8,128)(2,1)S(1)}, bf16[96,1024]{1,0:T(8,128)(2,1)S(1)}, u32[]{:S(2)}, u32[]{:S(2)}) collective-permute-start(bf16[96,1024]{1,0:T(8,128)(2,1)S(1)} %packet.5), channel_id=1, source_target_pairs={{0,8},{4,12},{8,0},{12,4},{1,9},{5,13},{9,1},{13,5},{2,10},{6,14},... | collective-permute-start | bytes 589832 | tf_op jit(solution)/shard_map/ppermute | solution.py:456
  32.2 0.5 collective-permute-done.7
  32.7 2.0 %all-gather = bf16[1312,128]{1,0:T(8,128)(2,1)S(1)} all-gather(bf16[656,128]{1,0:T(8,128)(2,1)S(1)} %collective-permute-done.6), channel_id=2, replica_groups=mesh['groups'=2,'ctx'=4,'enc'=2,'tp'=2] {'tp'}, dimensions={0}, use_global_device_ids=true | all-gather | bytes 503808 | tf_op jit(solution)/shard_map/all_gather | solution.py:501
  34.8 2.0 %all-gather.1 = bf16[1312,128]{1,0:T(8,128)(2,1)S(1)} all-gather(bf16[656,128]{1,0:T(8,128)(2,1)S(1)} %collective-permute-done.7), channel_id=3, replica_groups=mesh['groups'=2,'ctx'=4,'enc'=2,'tp'=2] {'tp'}, dimensions={0}, use_global_device_ids=true | all-gather | bytes 503808 | tf_op jit(solution)/shard_map/all_gather | solution.py:501
  36.8 1.6 %project_parts.5 = (bf16[256,1024]{1,0:T(8,128)(2,1)S(1)}, s32[1,256]{1,0:T(1,128)S(1)}) custom-call(bf16[1280,1024]{1,0:T(8,128)(2,1)S(1)} %copy-done.1, bf16[1280,1024]{1,0:T(8,128)(2,1)S(1)} %copy-done.3, bf16[1,1024]{1,0:T(2,128)(2,1)S(1)} %broadcast_in_dim.31.ba, bf16[1,1024]{1,0:T(2,128)(2,1)S(1)} %broadcast_in_dim.32.bf, ...), custom_call_target="tpu_custom_call" | custom-call | flops 83886080 | bytes 327680 | tf_op jit(solution)/shard_map/project_parts/pallas_call | solution.py:177
  38.4 0.7 select.2
  39.1 1.7 %collective-permute-start.10 = (bf16[256,1024]{1,0:T(8,128)(2,1)S(1)}, bf16[256,1024]{1,0:T(8,128)(2,1)S(1)}, u32[]{:S(2)}, u32[]{:S(2)}) collective-permute-start(bf16[256,1024]{1,0:T(8,128)(2,1)S(1)} %select.2), channel_id=1, source_target_pairs={{0,4},{4,0},{8,12},{12,8},{1,5},{5,1},{9,13},{13,9},{2,6},{6,2},{1... | collective-permute-start | bytes 1572872 | tf_op jit(solution)/shard_map/ppermute | solution.py:456
  40.8 1.4 %packet.6 = (bf16[80,1024]{1,0:T(8,128)(2,1)S(1)}, bf16[80,1024]{1,0:T(8,128)(2,1)S(1)}) custom-call(bf16[256,1024]{1,0:T(8,128)(2,1)S(1)} %project_own.1.refs_0_, bf16[256,1024]{1,0:T(8,128)(2,1)S(1)} %get-tuple-element.49.refs_1_, bf16[256,1024]{1,0:T(8,128)(2,1)S(1)} %get-tuple-element.53.refs_2_, bf16[256,1024]{1,0:T(8,128)(2,1)S(1)} %get-tuple-element.56.refs_3_, ...), custom_call_target="tpu_custom_call" | custom-call | flops 20971520 | bytes 131072 | tf_op jit(solution)/shard_map/packet/pallas_call | solution.py:279
  42.2 1.4 %packet.7 = (bf16[80,1024]{1,0:T(8,128)(2,1)S(1)}, bf16[80,1024]{1,0:T(8,128)(2,1)S(1)}) custom-call(bf16[256,1024]{1,0:T(8,128)(2,1)S(1)} %project_own.1.refs_0_, bf16[256,1024]{1,0:T(8,128)(2,1)S(1)} %get-tuple-element.49.refs_1_, bf16[256,1024]{1,0:T(8,128)(2,1)S(1)} %get-tuple-element.53.refs_2_, bf16[256,1024]{1,0:T(8,128)(2,1)S(1)} %get-tuple-element.56.refs_3_, ...), custom_call_target="tpu_custom_call" | custom-call | flops 20971520 | bytes 131072 | tf_op jit(solution)/shard_map/packet/pallas_call | solution.py:279
  43.6 3.1 %collective-permute-start.9 = (bf16[80,1024]{1,0:T(8,128)(2,1)S(1)}, bf16[80,1024]{1,0:T(8,128)(2,1)S(1)}, u32[]{:S(2)}, u32[]{:S(2)}) collective-permute-start(bf16[80,1024]{1,0:T(8,128)(2,1)S(1)} %get-tuple-element.68), channel_id=1, source_target_pairs={{0,8},{1,9},{4,12},{5,13},{8,0},{9,1},{12,4},{13,5},{2,10},{3,11},... | collective-permute-start | bytes 491528 | tf_op jit(solution)/shard_map/ppermute | solution.py:471
  46.7 0.6 order_of.1
  47.3 0.1 collective-permute-start.14
  47.4 2.1 %collective-permute-done.11.refs_6_ = bf16[96,1024]{1,0:T(8,128)(2,1)S(1)} collective-permute-done((bf16[96,1024]{1,0:T(8,128)(2,1)S(1)}, bf16[96,1024]{1,0:T(8,128)(2,1)S(1)}, u32[]{:S(2)}, u32[]{:S(2)}) %collective-permute-start.11) | collective-permute-done | bytes 196640 | tf_op jit(solution)/shard_map/ppermute | solution.py:456
  49.6 2.4 %collective-permute-start.12 = (bf16[80,1024]{1,0:T(8,128)(2,1)S(1)}, bf16[80,1024]{1,0:T(8,128)(2,1)S(1)}, u32[]{:S(2)}, u32[]{:S(2)}) collective-permute-start(bf16[80,1024]{1,0:T(8,128)(2,1)S(1)} %get-tuple-element.77), channel_id=1, source_target_pairs={{0,12},{1,13},{4,8},{5,9},{8,4},{9,5},{12,0},{13,1},{2,14},{3,15},... | collective-permute-start | bytes 491528 | tf_op jit(solution)/shard_map/ppermute | solution.py:471
  52.0 3.1 %all-gather.4 = bf16[96,1024]{1,0:T(8,128)(2,1)S(1)} all-gather(bf16[48,1024]{1,0:T(8,128)(2,1)S(1)} %slice.10), channel_id=6, replica_groups=mesh['groups'=2,'ctx'=4,'enc'=2,'tp'=2] {'tp'}, dimensions={0}, use_global_device_ids=true | all-gather | bytes 294912 | tf_op jit(solution)/shard_map/all_gather | solution.py:520
  55.1 1.9 %all-gather.5 = bf16[96,1024]{1,0:T(8,128)(2,1)S(1)} all-gather(bf16[48,1024]{1,0:T(8,128)(2,1)S(1)} %slice.11), channel_id=7, replica_groups=mesh['groups'=2,'ctx'=4,'enc'=2,'tp'=2] {'tp'}, dimensions={0}, use_global_device_ids=true | all-gather | bytes 294912 | tf_op jit(solution)/shard_map/all_gather | solution.py:520
  57.1 0.7 select.3
  57.8 2.2 %all-gather.2 = bf16[256,1024]{1,0:T(8,128)(2,1)S(1)} all-gather(bf16[128,1024]{1,0:T(8,128)(2,1)S(1)} %get-tuple-element.71), channel_id=4, replica_groups=mesh['groups'=2,'ctx'=4,'enc'=2,'tp'=2] {'tp'}, dimensions={0}, use_global_device_ids=true | all-gather | bytes 786432 | tf_op jit(solution)/shard_map/all_gather | solution.py:475
  60.0 0.2 squares.2.before
  60.2 11.2 %collective-permute-done.10.refs_0_.refs_10_ = bf16[256,1024]{1,0:T(8,128)(2,1)S(1)} collective-permute-done((bf16[256,1024]{1,0:T(8,128)(2,1)S(1)}, bf16[256,1024]{1,0:T(8,128)(2,1)S(1)}, u32[]{:S(2)}, u32[]{:S(2)}) %collective-permute-start.10) | collective-permute-done | bytes 524320 | tf_op jit(solution)/shard_map/ppermute | solution.py:456
  71.4 2.2 %all-gather.3 = bf16[256,1024]{1,0:T(8,128)(2,1)S(1)} all-gather(bf16[128,1024]{1,0:T(8,128)(2,1)S(1)} %slice.12), channel_id=5, replica_groups=mesh['groups'=2,'ctx'=4,'enc'=2,'tp'=2] {'tp'}, dimensions={0}, use_global_device_ids=true | all-gather | bytes 786432 | tf_op jit(solution)/shard_map/all_gather | solution.py:480
  73.6 0.2 squares.3.before_too
  73.8 2.4 %place_and_norm.1 = bf16[128,8192]{1,0:T(8,128)(2,1)} custom-call(bf16[1,8192]{1,0:T(2,128)(2,1)S(1)} %broadcast_in_dim.30.gain, f32[128,1]{1,0:T(8,128)S(1)} %squares.2.before, f32[128,1]{1,0:T(8,128)S(1)} %squares.3.before_too, bf16[128,128]{1,0:T(8,128)(2,1)S(1)} %get-tuple-element.73.refs_0_, bf16[128,128]{1,0:T(8,128)(2,1)S(1)} %get-tuple-element.74.refs_1_, ...), custom_call_target="tpu_custom_call" | custom-call | flops 262144 | bytes 262144 | tf_op jit(solution)/shard_map/place_and_norm/pallas_call | solution.py:433
  (25 shorter events, 0.1 us)
Async XLA Ops:
  1.5 20.4 %collective-permute-start = (bf16[1296,128]{1,0:T(8,128)(2,1)S(1)}, bf16[1296,128]{1,0:T(8,128)(2,1)S(1)}, u32[]{:S(2)}, u32[]{:S(2)}) collective-permute-start(bf16[1296,128]{1,0:T(8,128)(2,1)S(1)} %get-tuple-element.43), channel_id=1, source_target_pairs={{0,4},{4,0},{8,12},{12,8},{1,5},{5,1},{9,13},{13,9},{2,6},{6,2},{1... | collective-permute-start | bytes 995336 | tf_op jit(solution)/shard_map/ppermute | solution.py:456
  4.6 11.8 %collective-permute-start.1 = (bf16[656,128]{1,0:T(8,128)(2,1)S(1)}, bf16[656,128]{1,0:T(8,128)(2,1)S(1)}, u32[]{:S(2)}, u32[]{:S(2)}) collective-permute-start(bf16[656,128]{1,0:T(8,128)(2,1)S(1)} %get-tuple-element.44), channel_id=1, source_target_pairs={{0,8},{4,12},{8,0},{12,4},{1,9},{5,13},{9,1},{13,5},{2,10},{6,14},... | collective-permute-start | bytes 503816 | tf_op jit(solution)/shard_map/ppermute | solution.py:456
  7.2 14.7 %collective-permute-start.2 = (bf16[656,128]{1,0:T(8,128)(2,1)S(1)}, bf16[656,128]{1,0:T(8,128)(2,1)S(1)}, u32[]{:S(2)}, u32[]{:S(2)}) collective-permute-start(bf16[656,128]{1,0:T(8,128)(2,1)S(1)} %get-tuple-element.45), channel_id=1, source_target_pairs={{0,12},{4,8},{8,4},{12,0},{1,13},{5,9},{9,5},{13,1},{2,14},{6,10},... | collective-permute-start | bytes 503816 | tf_op jit(solution)/shard_map/ppermute | solution.py:456
  8.6 1.7 %copy-start = (bf16[1280,1024]{1,0:T(8,128)(2,1)S(1)}, bf16[1280,1024]{1,0:T(8,128)(2,1)}, u32[]{:S(2)}) copy-start(bf16[1280,1024]{1,0:T(8,128)(2,1)} %wa.7) | copy-start | bytes 7864324
  10.3 1.7 %copy-start.2 = (bf16[1280,1024]{1,0:T(8,128)(2,1)S(1)}, bf16[1280,1024]{1,0:T(8,128)(2,1)}, u32[]{:S(2)}) copy-start(bf16[1280,1024]{1,0:T(8,128)(2,1)} %wf.7) | copy-start | bytes 7864324
  12.1 1.1 %copy-start.4 = (bf16[1,256,1280]{2,1,0:T(8,128)(2,1)S(1)}, bf16[1,256,1280]{2,1,0:T(8,128)(2,1)}, u32[]{:S(2)}) copy-start(bf16[1,256,1280]{2,1,0:T(8,128)(2,1)} %param.8) | copy-start | bytes 1966084
  13.1 0.7 copy-start.6
  13.8 10.6 %copy-start.1 = (bf16[1280,1024]{1,0:T(8,128)(2,1)S(1)}, bf16[1280,1024]{1,0:T(8,128)(2,1)}, u32[]{:S(2)}) copy-start(bf16[1280,1024]{1,0:T(8,128)(2,1)} %wa.7) | copy-start | bytes 7864324
  13.8 10.6 %copy-start.3 = (bf16[1280,1024]{1,0:T(8,128)(2,1)S(1)}, bf16[1280,1024]{1,0:T(8,128)(2,1)}, u32[]{:S(2)}) copy-start(bf16[1280,1024]{1,0:T(8,128)(2,1)} %wf.7) | copy-start | bytes 7864324
  21.9 4.2 %collective-permute-start.3 = (bf16[1296,128]{1,0:T(8,128)(2,1)S(1)}, bf16[1296,128]{1,0:T(8,128)(2,1)S(1)}, u32[]{:S(2)}, u32[]{:S(2)}) collective-permute-start(bf16[1296,128]{1,0:T(8,128)(2,1)S(1)} %collective-permute-done), channel_id=1, source_target_pairs={{0,1},{1,0},{2,3},{3,2},{4,5},{5,4},{6,7},{7,6},{8,9},{9,8},{10,11... | collective-permute-start | bytes 995336 | tf_op jit(solution)/shard_map/ppermute | solution.py:459
  21.9 4.1 %collective-permute-start.4 = (bf16[656,128]{1,0:T(8,128)(2,1)S(1)}, bf16[656,128]{1,0:T(8,128)(2,1)S(1)}, u32[]{:S(2)}, u32[]{:S(2)}) collective-permute-start(bf16[656,128]{1,0:T(8,128)(2,1)S(1)} %collective-permute-done.1), channel_id=1, source_target_pairs={{0,1},{1,0},{2,3},{3,2},{4,5},{5,4},{6,7},{7,6},{8,9},{9,8},{10,11... | collective-permute-start | bytes 503816 | tf_op jit(solution)/shard_map/ppermute | solution.py:459
  22.4 3.7 %collective-permute-start.5 = (bf16[656,128]{1,0:T(8,128)(2,1)S(1)}, bf16[656,128]{1,0:T(8,128)(2,1)S(1)}, u32[]{:S(2)}, u32[]{:S(2)}) collective-permute-start(bf16[656,128]{1,0:T(8,128)(2,1)S(1)} %collective-permute-done.2), channel_id=1, source_target_pairs={{0,1},{1,0},{2,3},{3,2},{4,5},{5,4},{6,7},{7,6},{8,9},{9,8},{10,11... | collective-permute-start | bytes 503816 | tf_op jit(solution)/shard_map/ppermute | solution.py:459
  22.4 9.8 %collective-permute-start.6 = (bf16[656,128]{1,0:T(8,128)(2,1)S(1)}, bf16[656,128]{1,0:T(8,128)(2,1)S(1)}, u32[]{:S(2)}, u32[]{:S(2)}) collective-permute-start(bf16[656,128]{1,0:T(8,128)(2,1)S(1)} %collective-permute-done.1), channel_id=1, source_target_pairs={{0,4},{4,0},{8,12},{12,8},{1,5},{5,1},{9,13},{13,9},{2,6},{6,2},{1... | collective-permute-start | bytes 503816 | tf_op jit(solution)/shard_map/ppermute | solution.py:456
  23.2 9.5 %collective-permute-start.7 = (bf16[656,128]{1,0:T(8,128)(2,1)S(1)}, bf16[656,128]{1,0:T(8,128)(2,1)S(1)}, u32[]{:S(2)}, u32[]{:S(2)}) collective-permute-start(bf16[656,128]{1,0:T(8,128)(2,1)S(1)} %collective-permute-done.2), channel_id=1, source_target_pairs={{0,4},{4,0},{8,12},{12,8},{1,5},{5,1},{9,13},{13,9},{2,6},{6,2},{1... | collective-permute-start | bytes 503816 | tf_op jit(solution)/shard_map/ppermute | solution.py:456
  26.1 1.6 %copy-start.5 = (s32[1,256]{1,0:T(1,128)S(1)}, s32[1,256]{1,0:T(1,128)}, u32[]{:S(2)}) copy-start(s32[1,256]{1,0:T(1,128)} %refs_0_) | copy-start | bytes 3076
  26.1 4.2 %copy-start.7 = (bf16[8192]{0:T(1024)(128)(2,1)S(1)}, bf16[8192]{0:T(1024)(128)(2,1)}, u32[]{:S(2)}) copy-start(bf16[8192]{0:T(1024)(128)(2,1)} %param.15) | copy-start | bytes 49156
  28.8 14.8 %collective-permute-start.8 = (bf16[96,1024]{1,0:T(8,128)(2,1)S(1)}, bf16[96,1024]{1,0:T(8,128)(2,1)S(1)}, u32[]{:S(2)}, u32[]{:S(2)}) collective-permute-start(bf16[96,1024]{1,0:T(8,128)(2,1)S(1)} %packet.4), channel_id=1, source_target_pairs={{0,12},{4,8},{8,4},{12,0},{1,13},{5,9},{9,5},{13,1},{2,14},{6,10},... | collective-permute-start | bytes 589832 | tf_op jit(solution)/shard_map/ppermute | solution.py:456
  31.4 18.2 %collective-permute-start.11 = (bf16[96,1024]{1,0:T(8,128)(2,1)S(1)}, bf16[96,1024]{1,0:T(8,128)(2,1)S(1)}, u32[]{:S(2)}, u32[]{:S(2)}) collective-permute-start(bf16[96,1024]{1,0:T(8,128)(2,1)S(1)} %packet.5), channel_id=1, source_target_pairs={{0,8},{4,12},{8,0},{12,4},{1,9},{5,13},{9,1},{13,5},{2,10},{6,14},... | collective-permute-start | bytes 589832 | tf_op jit(solution)/shard_map/ppermute | solution.py:456
  39.1 32.3 %collective-permute-start.10 = (bf16[256,1024]{1,0:T(8,128)(2,1)S(1)}, bf16[256,1024]{1,0:T(8,128)(2,1)S(1)}, u32[]{:S(2)}, u32[]{:S(2)}) collective-permute-start(bf16[256,1024]{1,0:T(8,128)(2,1)S(1)} %select.2), channel_id=1, source_target_pairs={{0,4},{4,0},{8,12},{12,8},{1,5},{5,1},{9,13},{13,9},{2,6},{6,2},{1... | collective-permute-start | bytes 1572872 | tf_op jit(solution)/shard_map/ppermute | solution.py:456
  43.6 13.5 %collective-permute-start.9 = (bf16[80,1024]{1,0:T(8,128)(2,1)S(1)}, bf16[80,1024]{1,0:T(8,128)(2,1)S(1)}, u32[]{:S(2)}, u32[]{:S(2)}) collective-permute-start(bf16[80,1024]{1,0:T(8,128)(2,1)S(1)} %get-tuple-element.68), channel_id=1, source_target_pairs={{0,8},{1,9},{4,12},{5,13},{8,0},{9,1},{12,4},{13,5},{2,10},{3,11},... | collective-permute-start | bytes 491528 | tf_op jit(solution)/shard_map/ppermute | solution.py:471
  47.3 26.4 %collective-permute-start.14 = (bf16[80,1024]{1,0:T(8,128)(2,1)S(1)}, bf16[80,1024]{1,0:T(8,128)(2,1)S(1)}, u32[]{:S(2)}, u32[]{:S(2)}) collective-permute-start(bf16[80,1024]{1,0:T(8,128)(2,1)S(1)} %get-tuple-element.80), channel_id=1, source_target_pairs={{0,9},{1,8},{4,13},{5,12},{8,1},{9,0},{12,5},{13,4},{2,11},{3,10},... | collective-permute-start | bytes 491528 | tf_op jit(solution)/shard_map/ppermute | solution.py:471
  49.6 24.2 %collective-permute-start.12 = (bf16[80,1024]{1,0:T(8,128)(2,1)S(1)}, bf16[80,1024]{1,0:T(8,128)(2,1)S(1)}, u32[]{:S(2)}, u32[]{:S(2)}) collective-permute-start(bf16[80,1024]{1,0:T(8,128)(2,1)S(1)} %get-tuple-element.77), channel_id=1, source_target_pairs={{0,12},{1,13},{4,8},{5,9},{8,4},{9,5},{12,0},{13,1},{2,14},{3,15},... | collective-permute-start | bytes 491528 | tf_op jit(solution)/shard_map/ppermute | solution.py:471
  52.0 21.8 %collective-permute-start.13 = (bf16[80,1024]{1,0:T(8,128)(2,1)S(1)}, bf16[80,1024]{1,0:T(8,128)(2,1)S(1)}, u32[]{:S(2)}, u32[]{:S(2)}) collective-permute-start(bf16[80,1024]{1,0:T(8,128)(2,1)S(1)} %get-tuple-element.78), channel_id=1, source_target_pairs={{0,13},{1,12},{4,9},{5,8},{8,5},{9,4},{12,1},{13,0},{2,15},{3,14},... | collective-permute-start | bytes 491528 | tf_op jit(solution)/shard_map/ppermute | solution.py:471

commit v17 on v16

--- a/solution.py
+++ b/solution.py
@@ -401,17 +401,45 @@
     )(gain, before, *pieces)
 
 
-def last_kernel(far, whole, gain, before, before_too, *refs):
-    orders, packets, pieces = refs[:2], refs[2:10], refs[10:14]
+def placed(order, early, later):
+    early = view(early, order.shape[0] - later.shape[0])[...]
+    both = jnp.concatenate([early, later[...]], axis=0)
+    return jnp.dot(order[...], both, preferred_element_type=F32)
+
+
+def place_kernel(order, *refs):
+    packets, outs = refs[:4], refs[4:]
+    total = None
+    for d in range(2):
+        wide = placed(order, packets[2 * d], packets[2 * d + 1])
+        outs[d][...] = wide.astype(BF16)
+        part = jnp.sum(wide * wide, axis=1, keepdims=True)
+        total = part if total is None else total + part
+    outs[2][...] = total
+
+
+def place(order, packets):
+    places, cols = order.shape[0], packets[0].shape[-1]
+    piece = jax.ShapeDtypeStruct((places, cols), BF16)
+    return pl.pallas_call(
+        place_kernel,
+        out_shape=[piece, piece, jax.ShapeDtypeStruct((places, 1), F32)],
+        in_specs=[VMEM] * 5,
+        out_specs=[VMEM] * 3,
+        compiler_params=PARAMS,
+        cost_estimate=cost(0, 0),
+        name="place",
+    )(order, *packets)
+
+
+def last_kernel(far, whole, gain, *refs):
+    before, order, packets, pieces = refs[:3], refs[3], refs[4:8], refs[8:14]
     out, scaled, sems = refs[14:]
     places, cols = scaled.shape[1:]
     z, t = lax.axis_index("ctx"), lax.axis_index("tp")
-    total = before[...] + before_too[...]
-    for k in range(4):
-        later = packets[2 * k + 1][...]
-        early = view(packets[2 * k], places - later.shape[0])[...]
-        both = jnp.concatenate([early, later], axis=0)
-        wide = jnp.dot(orders[k // 2][...], both, preferred_element_type=F32)
+    total = before[0][...] + before[1][...] + before[2][...]
+    for k in range(2):
+        wide = placed(order, packets[2 * k], packets[2 * k + 1])
         scaled[k] = wide.astype(BF16)
         total = total + jnp.sum(wide * wide, axis=1, keepdims=True)
     scale = lax.rsqrt(total / (8 * cols) + 1e-06)
@@ -419,7 +447,7 @@
     for k, (m, d) in enumerate(far + whole):
         block = jnp.bitwise_xor(z, m) * 2 + jnp.bitwise_xor(t, d)
         at = pl.ds(pl.multiple_of(block * cols, cols), cols)
-        piece = scaled[k] if k < 4 else view(pieces[k - 4], places)[...]
+        piece = scaled[k] if k < 2 else view(pieces[k - 2], places)[...]
         scaled[k] = (piece.astype(F32) * scale * gain[:, at].astype(F32)).astype(BF16)
         copies.append(pltpu.make_async_copy(scaled.at[k], out.at[:, at], sems.at[k]))
         copies[k].start()
@@ -427,9 +455,9 @@
         copy.wait()
 
 
-def place_and_norm(far, whole, gain, before, orders, packets, pieces):
+def place_and_norm(far, whole, gain, before, order, packets, pieces):
     places, cols = before[0].shape[0], packets[0].shape[1]
-    operands = [gain, *before, *orders, *packets, *pieces]
+    operands = [gain, *before, order, *packets, *pieces]
     return pl.pallas_call(
         functools.partial(last_kernel, far, whole),
         out_shape=jax.ShapeDtypeStruct((places, 8 * cols), BF16),
@@ -518,11 +546,13 @@
         for m in (3, 2):
             whole_packet = sent[m]
             sent[m] = [whole_packet, lax.all_gather(whole_packet[size:], "tp", axis=0)]
-        far, whole = ((3, 0), (3, 1), (2, 0), (2, 1)), ((1, 0), (1, 1), (0, 0), (0, 1))
-        packets = [part for m, d in far for part in (sent[m][d], rest[m][d])]
+        packets = {m: [part for d in range(2) for part in (sent[m][d], rest[m][d])] for m in (3, 2)}
+        order3, order2 = orders
+        pieces[2, 0], pieces[2, 1], squared = place(order2, packets[2])
+        far, whole = ((3, 0), (3, 1)), ((2, 0), (2, 1), (1, 0), (1, 1), (0, 0), (0, 1))
         whole_pieces = [pieces[at] for at in whole]
-        gain = norm_gain[None, :]
-        return place_and_norm(far, whole, gain, total, orders, packets, whole_pieces)[None]
+        gain, total = norm_gain[None, :], [*total, squared]
+        return place_and_norm(far, whole, gain, total, order3, packets[3], whole_pieces)[None]
     else:
         (mine,) = to_send((None,), rows, row_slot, row_kind)
         arrived = [over_ctx(mine, m) for m in range(1, n)]

time: 76.9 us -> 76.7 us (level)
    ppermute x8, waiting for transfers between devices: 20.4 us -> 11.2 us  [over_ctx(): return lax.ppermute(x, 'ctx', [(i, i ^ m) for i in range(n)])]
    ppermute x4, waiting for transfers between devices: 0.01 us -> 8.86 us  [to_core(): return lax.ppermute(x, ('ctx', 'tp'), pairs)]
  transfers between devices with their start and end apart: 15 -> 15, of which waited for: 5 -> 6; matrix products, arithmetic and copies ran while one was open for 2% -> 2% of each run, Pallas kernels for 18% -> 18%
where the time goes in v17:
time: 76.7 us; the launch traced here: 76 us
  waiting for transfers between devices  20 us (26%)
  starting transfers between devices  17.9 us (23%)
  Pallas kernels  17.7 us (23%)
  blocking collectives  13.5 us (18%)
  local copies, waits for them, and re-layouts  6.69 us (9%)
    ppermute x8, starting transfers between devices, over_ctx(): return lax.ppermute(x, 'ctx', [(i, i ^ m) for i in range(n)])  11.8 us
    ppermute x8, waiting for transfers between devices, over_ctx(): return lax.ppermute(x, 'ctx', [(i, i ^ m) for i in range(n)])  11.2 us
    ppermute x4, waiting for transfers between devices, to_core(): return lax.ppermute(x, ('ctx', 'tp'), pairs)  8.86 us
    ppermute x4, starting transfers between devices, to_core(): return lax.ppermute(x, ('ctx', 'tp'), pairs)  5.61 us
    unnamed x16, local copies, waits for them, and re-layouts  5.26 us
    all_gather x2, blocking collectives, body(): sent[m] = [whole_packet, lax.all_gather(whole_packet[size:], 'tp', axis=0)]  5.08 us
    pallas_call x4, Pallas kernels, packet(): pl.pallas_call(functools.partial(packet_kernel, m, early, len(blocks), se...  4.84 us
    pallas_call x3, Pallas kernels, project_parts(): pl.pallas_call(project_parts_kernel, out_shape=[jax.ShapeDtypeStruct((row...  4.8 us
  transfers between devices with their start and end apart: 15, of which 6 were waited for; matrix products, arithmetic and copies ran while one was open for 2% of the time, Pallas kernels for 18%

profile of v17, /device:TPU:0, one launch (start us, length us, event | category | flops | bytes accessed | tf_op | source)
XLA Modules:
  0.0 76.0 jit_solution(3652811711256745673)
XLA Ops:
  0.0 1.5 %to_send.1 = (bf16[1296,128]{1,0:T(8,128)(2,1)S(1)}, bf16[656,128]{1,0:T(8,128)(2,1)S(1)}, bf16[656,128]{1,0:T(8,128)(2,1)S(1)}, s32[1,256]{1,0:T(1,128)S(1)}) custom-call(bf16[256,1280]{1,0:T(8,128)(2,1)} %bitcast.16, s32[1,256]{1,0:T(1,128)} %refs_0_, s32[1,256]{1,0:T(1,128)} %kind.3), custom_call_target="tpu_custom_call" | custom-call | bytes 40960 | tf_op jit(solution)/shard_map/to_send/pallas_call | solution.py:109
  1.5 3.1 %collective-permute-start = (bf16[1296,128]{1,0:T(8,128)(2,1)S(1)}, bf16[1296,128]{1,0:T(8,128)(2,1)S(1)}, u32[]{:S(2)}, u32[]{:S(2)}) collective-permute-start(bf16[1296,128]{1,0:T(8,128)(2,1)S(1)} %get-tuple-element.46), channel_id=1, source_target_pairs={{0,4},{4,0},{8,12},{12,8},{1,5},{5,1},{9,13},{13,9},{2,6},{6,2},{1... | collective-permute-start | bytes 995336 | tf_op jit(solution)/shard_map/ppermute | solution.py:484
  4.6 2.6 %collective-permute-start.1 = (bf16[656,128]{1,0:T(8,128)(2,1)S(1)}, bf16[656,128]{1,0:T(8,128)(2,1)S(1)}, u32[]{:S(2)}, u32[]{:S(2)}) collective-permute-start(bf16[656,128]{1,0:T(8,128)(2,1)S(1)} %get-tuple-element.47), channel_id=1, source_target_pairs={{0,8},{4,12},{8,0},{12,4},{1,9},{5,13},{9,1},{13,5},{2,10},{6,14},... | collective-permute-start | bytes 503816 | tf_op jit(solution)/shard_map/ppermute | solution.py:484
  7.2 0.7 broadcast_in_dim.31.ba
  7.9 0.7 broadcast_in_dim.32.bf
  8.6 1.7 %copy-done = bf16[1280,1024]{1,0:T(8,128)(2,1)S(1)} copy-done((bf16[1280,1024]{1,0:T(8,128)(2,1)S(1)}, bf16[1280,1024]{1,0:T(8,128)(2,1)}, u32[]{:S(2)}) %copy-start) | copy-done | bytes 2621464
  10.3 1.7 %copy-done.2 = bf16[1280,1024]{1,0:T(8,128)(2,1)S(1)} copy-done((bf16[1280,1024]{1,0:T(8,128)(2,1)S(1)}, bf16[1280,1024]{1,0:T(8,128)(2,1)}, u32[]{:S(2)}) %copy-start.2) | copy-done | bytes 2621464
  12.1 1.1 %copy-done.4 = bf16[1,256,1280]{2,1,0:T(8,128)(2,1)S(1)} copy-done((bf16[1,256,1280]{2,1,0:T(8,128)(2,1)S(1)}, bf16[1,256,1280]{2,1,0:T(8,128)(2,1)}, u32[]{:S(2)}) %copy-start.4) | copy-done | bytes 655384
  13.1 0.7 copy-done.6
  13.8 1.6 %project_own.1.refs_0_ = bf16[256,1024]{1,0:T(8,128)(2,1)S(1)} custom-call(s32[1,256]{1,0:T(1,128)S(1)} %copy-done.6, bf16[256,1280]{1,0:T(8,128)(2,1)S(1)} %bitcast.17, bf16[1280,1024]{1,0:T(8,128)(2,1)S(1)} %copy-done, bf16[1280,1024]{1,0:T(8,128)(2,1)S(1)} %copy-done.2, bf16[1,1024]{1,0:T(2,128)(2,1)S(1)} %broadcast_in_dim.31.ba, ...), custom_call_target="tpu_custom_call" | custom-call | flops 83886080 | bytes 327680 | tf_op jit(solution)/shard_map/project_own/pallas_call | solution.py:147
  15.4 1.1 %collective-permute-done.1 = bf16[656,128]{1,0:T(8,128)(2,1)S(1)} collective-permute-done((bf16[656,128]{1,0:T(8,128)(2,1)S(1)}, bf16[656,128]{1,0:T(8,128)(2,1)S(1)}, u32[]{:S(2)}, u32[]{:S(2)}) %collective-permute-start.1) | collective-permute-done | bytes 167968 | tf_op jit(solution)/shard_map/ppermute | solution.py:484
  16.5 5.4 %collective-permute-done.2 = bf16[656,128]{1,0:T(8,128)(2,1)S(1)} collective-permute-done((bf16[656,128]{1,0:T(8,128)(2,1)S(1)}, bf16[656,128]{1,0:T(8,128)(2,1)S(1)}, u32[]{:S(2)}, u32[]{:S(2)}) %collective-permute-start.2) | collective-permute-done | bytes 167968 | tf_op jit(solution)/shard_map/ppermute | solution.py:484
  21.9 0.5 collective-permute-start.4
  22.4 0.0 collective-permute-start.5
  22.4 0.8 %collective-permute-start.6 = (bf16[656,128]{1,0:T(8,128)(2,1)S(1)}, bf16[656,128]{1,0:T(8,128)(2,1)S(1)}, u32[]{:S(2)}, u32[]{:S(2)}) collective-permute-start(bf16[656,128]{1,0:T(8,128)(2,1)S(1)} %collective-permute-done.1), channel_id=1, source_target_pairs={{0,4},{4,0},{8,12},{12,8},{1,5},{5,1},{9,13},{13,9},{2,6},{6,2},{1... | collective-permute-start | bytes 503816 | tf_op jit(solution)/shard_map/ppermute | solution.py:484
  23.2 1.3 %collective-permute-start.7 = (bf16[656,128]{1,0:T(8,128)(2,1)S(1)}, bf16[656,128]{1,0:T(8,128)(2,1)S(1)}, u32[]{:S(2)}, u32[]{:S(2)}) collective-permute-start(bf16[656,128]{1,0:T(8,128)(2,1)S(1)} %collective-permute-done.2), channel_id=1, source_target_pairs={{0,4},{4,0},{8,12},{12,8},{1,5},{5,1},{9,13},{13,9},{2,6},{6,2},{1... | collective-permute-start | bytes 503816 | tf_op jit(solution)/shard_map/ppermute | solution.py:484
  24.5 1.6 %project_parts.3 = (bf16[256,1024]{1,0:T(8,128)(2,1)S(1)}, s32[1,256]{1,0:T(1,128)S(1)}) custom-call(bf16[1280,1024]{1,0:T(8,128)(2,1)S(1)} %copy-done.1, bf16[1280,1024]{1,0:T(8,128)(2,1)S(1)} %copy-done.3, bf16[1,1024]{1,0:T(2,128)(2,1)S(1)} %broadcast_in_dim.31.ba, bf16[1,1024]{1,0:T(2,128)(2,1)S(1)} %broadcast_in_dim.32.bf, ...), custom_call_target="tpu_custom_call" | custom-call | flops 83886080 | bytes 327680 | tf_op jit(solution)/shard_map/project_parts/pallas_call | solution.py:177
  26.1 0.0 copy-start.5
  26.1 0.0 copy-start.7
  26.1 1.6 %project_parts.4 = (bf16[256,1024]{1,0:T(8,128)(2,1)S(1)}, s32[1,256]{1,0:T(1,128)S(1)}) custom-call(bf16[1280,1024]{1,0:T(8,128)(2,1)S(1)} %copy-done.1, bf16[1280,1024]{1,0:T(8,128)(2,1)S(1)} %copy-done.3, bf16[1,1024]{1,0:T(2,128)(2,1)S(1)} %broadcast_in_dim.31.ba, bf16[1,1024]{1,0:T(2,128)(2,1)S(1)} %broadcast_in_dim.32.bf, ...), custom_call_target="tpu_custom_call" | custom-call | flops 83886080 | bytes 327680 | tf_op jit(solution)/shard_map/project_parts/pallas_call | solution.py:177
  27.7 1.0 %packet.4 = bf16[96,1024]{1,0:T(8,128)(2,1)S(1)} custom-call(bf16[256,1024]{1,0:T(8,128)(2,1)S(1)} %project_own.1.refs_0_, bf16[256,1024]{1,0:T(8,128)(2,1)S(1)} %get-tuple-element.52.refs_1_, bf16[256,1024]{1,0:T(8,128)(2,1)S(1)} %get-tuple-element.56.refs_2_, s32[1,256]{1,0:T(1,128)S(1)} %copy-done.5, ...), custom_call_target="tpu_custom_call" | custom-call | flops 9437184 | bytes 98304 | tf_op jit(solution)/shard_map/packet/pallas_call | solution.py:279
  28.8 1.5 %collective-permute-start.8 = (bf16[96,1024]{1,0:T(8,128)(2,1)S(1)}, bf16[96,1024]{1,0:T(8,128)(2,1)S(1)}, u32[]{:S(2)}, u32[]{:S(2)}) collective-permute-start(bf16[96,1024]{1,0:T(8,128)(2,1)S(1)} %packet.4), channel_id=1, source_target_pairs={{0,12},{4,8},{8,4},{12,0},{1,13},{5,9},{9,5},{13,1},{2,14},{6,10},... | collective-permute-start | bytes 589832 | tf_op jit(solution)/shard_map/ppermute | solution.py:484
  30.3 1.0 %packet.5 = bf16[96,1024]{1,0:T(8,128)(2,1)S(1)} custom-call(bf16[256,1024]{1,0:T(8,128)(2,1)S(1)} %project_own.1.refs_0_, bf16[256,1024]{1,0:T(8,128)(2,1)S(1)} %get-tuple-element.52.refs_1_, bf16[256,1024]{1,0:T(8,128)(2,1)S(1)} %get-tuple-element.56.refs_2_, s32[1,256]{1,0:T(1,128)S(1)} %copy-done.5, ...), custom_call_target="tpu_custom_call" | custom-call | flops 9437184 | bytes 98304 | tf_op jit(solution)/shard_map/packet/pallas_call | solution.py:279
  31.4 0.8 %collective-permute-start.11 = (bf16[96,1024]{1,0:T(8,128)(2,1)S(1)}, bf16[96,1024]{1,0:T(8,128)(2,1)S(1)}, u32[]{:S(2)}, u32[]{:S(2)}) collective-permute-start(bf16[96,1024]{1,0:T(8,128)(2,1)S(1)} %packet.5), channel_id=1, source_target_pairs={{0,8},{4,12},{8,0},{12,4},{1,9},{5,13},{9,1},{13,5},{2,10},{6,14},... | collective-permute-start | bytes 589832 | tf_op jit(solution)/shard_map/ppermute | solution.py:484
  32.2 0.5 collective-permute-done.7
  32.7 2.0 %all-gather = bf16[1312,128]{1,0:T(8,128)(2,1)S(1)} all-gather(bf16[656,128]{1,0:T(8,128)(2,1)S(1)} %collective-permute-done.6), channel_id=2, replica_groups=mesh['groups'=2,'ctx'=4,'enc'=2,'tp'=2] {'tp'}, dimensions={0}, use_global_device_ids=true | all-gather | bytes 503808 | tf_op jit(solution)/shard_map/all_gather | solution.py:529
  34.8 2.0 %all-gather.1 = bf16[1312,128]{1,0:T(8,128)(2,1)S(1)} all-gather(bf16[656,128]{1,0:T(8,128)(2,1)S(1)} %collective-permute-done.7), channel_id=3, replica_groups=mesh['groups'=2,'ctx'=4,'enc'=2,'tp'=2] {'tp'}, dimensions={0}, use_global_device_ids=true | all-gather | bytes 503808 | tf_op jit(solution)/shard_map/all_gather | solution.py:529
  36.8 1.6 %project_parts.5 = (bf16[256,1024]{1,0:T(8,128)(2,1)S(1)}, s32[1,256]{1,0:T(1,128)S(1)}) custom-call(bf16[1280,1024]{1,0:T(8,128)(2,1)S(1)} %copy-done.1, bf16[1280,1024]{1,0:T(8,128)(2,1)S(1)} %copy-done.3, bf16[1,1024]{1,0:T(2,128)(2,1)S(1)} %broadcast_in_dim.31.ba, bf16[1,1024]{1,0:T(2,128)(2,1)S(1)} %broadcast_in_dim.32.bf, ...), custom_call_target="tpu_custom_call" | custom-call | flops 83886080 | bytes 327680 | tf_op jit(solution)/shard_map/project_parts/pallas_call | solution.py:177
  38.4 0.7 select.2
  39.1 1.7 %collective-permute-start.10 = (bf16[256,1024]{1,0:T(8,128)(2,1)S(1)}, bf16[256,1024]{1,0:T(8,128)(2,1)S(1)}, u32[]{:S(2)}, u32[]{:S(2)}) collective-permute-start(bf16[256,1024]{1,0:T(8,128)(2,1)S(1)} %select.2), channel_id=1, source_target_pairs={{0,4},{4,0},{8,12},{12,8},{1,5},{5,1},{9,13},{13,9},{2,6},{6,2},{1... | collective-permute-start | bytes 1572872 | tf_op jit(solution)/shard_map/ppermute | solution.py:484
  40.8 1.4 %packet.6 = (bf16[80,1024]{1,0:T(8,128)(2,1)S(1)}, bf16[80,1024]{1,0:T(8,128)(2,1)S(1)}) custom-call(bf16[256,1024]{1,0:T(8,128)(2,1)S(1)} %project_own.1.refs_0_, bf16[256,1024]{1,0:T(8,128)(2,1)S(1)} %get-tuple-element.52.refs_1_, bf16[256,1024]{1,0:T(8,128)(2,1)S(1)} %get-tuple-element.56.refs_2_, bf16[256,1024]{1,0:T(8,128)(2,1)S(1)} %get-tuple-element.59.refs_3_, ...), custom_call_target="tpu_custom_call" | custom-call | flops 20971520 | bytes 131072 | tf_op jit(solution)/shard_map/packet/pallas_call | solution.py:279
  42.2 1.4 %packet.7 = (bf16[80,1024]{1,0:T(8,128)(2,1)S(1)}, bf16[80,1024]{1,0:T(8,128)(2,1)S(1)}) custom-call(bf16[256,1024]{1,0:T(8,128)(2,1)S(1)} %project_own.1.refs_0_, bf16[256,1024]{1,0:T(8,128)(2,1)S(1)} %get-tuple-element.52.refs_1_, bf16[256,1024]{1,0:T(8,128)(2,1)S(1)} %get-tuple-element.56.refs_2_, bf16[256,1024]{1,0:T(8,128)(2,1)S(1)} %get-tuple-element.59.refs_3_, ...), custom_call_target="tpu_custom_call" | custom-call | flops 20971520 | bytes 131072 | tf_op jit(solution)/shard_map/packet/pallas_call | solution.py:279
  43.6 3.1 %collective-permute-start.9 = (bf16[80,1024]{1,0:T(8,128)(2,1)S(1)}, bf16[80,1024]{1,0:T(8,128)(2,1)S(1)}, u32[]{:S(2)}, u32[]{:S(2)}) collective-permute-start(bf16[80,1024]{1,0:T(8,128)(2,1)S(1)} %get-tuple-element.71), channel_id=1, source_target_pairs={{0,8},{1,9},{4,12},{5,13},{8,0},{9,1},{12,4},{13,5},{2,10},{3,11},... | collective-permute-start | bytes 491528 | tf_op jit(solution)/shard_map/ppermute | solution.py:499
  46.7 0.6 order_of.1
  47.3 0.1 collective-permute-start.12
  47.4 2.1 %collective-permute-done.11.refs_0_ = bf16[96,1024]{1,0:T(8,128)(2,1)S(1)} collective-permute-done((bf16[96,1024]{1,0:T(8,128)(2,1)S(1)}, bf16[96,1024]{1,0:T(8,128)(2,1)S(1)}, u32[]{:S(2)}, u32[]{:S(2)}) %collective-permute-start.11) | collective-permute-done | bytes 196640 | tf_op jit(solution)/shard_map/ppermute | solution.py:484
  49.6 2.4 %collective-permute-start.13 = (bf16[80,1024]{1,0:T(8,128)(2,1)S(1)}, bf16[80,1024]{1,0:T(8,128)(2,1)S(1)}, u32[]{:S(2)}, u32[]{:S(2)}) collective-permute-start(bf16[80,1024]{1,0:T(8,128)(2,1)S(1)} %get-tuple-element.83), channel_id=1, source_target_pairs={{0,12},{1,13},{4,8},{5,9},{8,4},{9,5},{12,0},{13,1},{2,14},{3,15},... | collective-permute-start | bytes 491528 | tf_op jit(solution)/shard_map/ppermute | solution.py:499
  52.0 3.1 %all-gather.5 = bf16[96,1024]{1,0:T(8,128)(2,1)S(1)} all-gather(bf16[48,1024]{1,0:T(8,128)(2,1)S(1)} %slice.11), channel_id=7, replica_groups=mesh['groups'=2,'ctx'=4,'enc'=2,'tp'=2] {'tp'}, dimensions={0}, use_global_device_ids=true | all-gather | bytes 294912 | tf_op jit(solution)/shard_map/all_gather | solution.py:548
  55.1 1.9 %all-gather.4 = bf16[96,1024]{1,0:T(8,128)(2,1)S(1)} all-gather(bf16[48,1024]{1,0:T(8,128)(2,1)S(1)} %slice.10), channel_id=6, replica_groups=mesh['groups'=2,'ctx'=4,'enc'=2,'tp'=2] {'tp'}, dimensions={0}, use_global_device_ids=true | all-gather | bytes 294912 | tf_op jit(solution)/shard_map/all_gather | solution.py:548
  57.1 0.7 select.3
  57.8 2.2 %all-gather.2 = bf16[256,1024]{1,0:T(8,128)(2,1)S(1)} all-gather(bf16[128,1024]{1,0:T(8,128)(2,1)S(1)} %get-tuple-element.74), channel_id=4, replica_groups=mesh['groups'=2,'ctx'=4,'enc'=2,'tp'=2] {'tp'}, dimensions={0}, use_global_device_ids=true | all-gather | bytes 786432 | tf_op jit(solution)/shard_map/all_gather | solution.py:503
  60.0 0.2 squares.2.refs_0_
  60.2 8.9 %collective-permute-done.12.refs_3_ = bf16[80,1024]{1,0:T(8,128)(2,1)S(1)} collective-permute-done((bf16[80,1024]{1,0:T(8,128)(2,1)S(1)}, bf16[80,1024]{1,0:T(8,128)(2,1)S(1)}, u32[]{:S(2)}, u32[]{:S(2)}) %collective-permute-start.12) | collective-permute-done | bytes 163872 | tf_op jit(solution)/shard_map/ppermute | solution.py:499
  69.0 0.4 place.1
  69.4 2.0 %collective-permute-done.10.refs_0_.refs_10_ = bf16[256,1024]{1,0:T(8,128)(2,1)S(1)} collective-permute-done((bf16[256,1024]{1,0:T(8,128)(2,1)S(1)}, bf16[256,1024]{1,0:T(8,128)(2,1)S(1)}, u32[]{:S(2)}, u32[]{:S(2)}) %collective-permute-start.10) | collective-permute-done | bytes 524320 | tf_op jit(solution)/shard_map/ppermute | solution.py:484
  71.4 2.2 %all-gather.3 = bf16[256,1024]{1,0:T(8,128)(2,1)S(1)} all-gather(bf16[128,1024]{1,0:T(8,128)(2,1)S(1)} %slice.12), channel_id=5, replica_groups=mesh['groups'=2,'ctx'=4,'enc'=2,'tp'=2] {'tp'}, dimensions={0}, use_global_device_ids=true | all-gather | bytes 786432 | tf_op jit(solution)/shard_map/all_gather | solution.py:508
  73.6 0.2 squares.3.refs_1_
  73.8 2.2 %place_and_norm.1 = bf16[128,8192]{1,0:T(8,128)(2,1)} custom-call(bf16[1,8192]{1,0:T(2,128)(2,1)S(1)} %broadcast_in_dim.30.gain, f32[128,1]{1,0:T(8,128)S(1)} %squares.2.refs_0_, f32[128,1]{1,0:T(8,128)S(1)} %squares.3.refs_1_, f32[128,1]{1,0:T(8,128)S(1)} %get-tuple-element.80.refs_2_, bf16[128,128]{1,0:T(8,128)(2,1)S(1)} %get-tuple-element.81.refs_3_, ...), custom_call_target="tpu_custom_call" | custom-call | flops 262144 | bytes 262144 | tf_op jit(solution)/shard_map/place_and_norm/pallas_call | solution.py:461
  (26 shorter events, 0.1 us)
Async XLA Ops:
  1.5 20.4 %collective-permute-start = (bf16[1296,128]{1,0:T(8,128)(2,1)S(1)}, bf16[1296,128]{1,0:T(8,128)(2,1)S(1)}, u32[]{:S(2)}, u32[]{:S(2)}) collective-permute-start(bf16[1296,128]{1,0:T(8,128)(2,1)S(1)} %get-tuple-element.46), channel_id=1, source_target_pairs={{0,4},{4,0},{8,12},{12,8},{1,5},{5,1},{9,13},{13,9},{2,6},{6,2},{1... | collective-permute-start | bytes 995336 | tf_op jit(solution)/shard_map/ppermute | solution.py:484
  4.6 11.8 %collective-permute-start.1 = (bf16[656,128]{1,0:T(8,128)(2,1)S(1)}, bf16[656,128]{1,0:T(8,128)(2,1)S(1)}, u32[]{:S(2)}, u32[]{:S(2)}) collective-permute-start(bf16[656,128]{1,0:T(8,128)(2,1)S(1)} %get-tuple-element.47), channel_id=1, source_target_pairs={{0,8},{4,12},{8,0},{12,4},{1,9},{5,13},{9,1},{13,5},{2,10},{6,14},... | collective-permute-start | bytes 503816 | tf_op jit(solution)/shard_map/ppermute | solution.py:484
  7.2 14.7 %collective-permute-start.2 = (bf16[656,128]{1,0:T(8,128)(2,1)S(1)}, bf16[656,128]{1,0:T(8,128)(2,1)S(1)}, u32[]{:S(2)}, u32[]{:S(2)}) collective-permute-start(bf16[656,128]{1,0:T(8,128)(2,1)S(1)} %get-tuple-element.48), channel_id=1, source_target_pairs={{0,12},{4,8},{8,4},{12,0},{1,13},{5,9},{9,5},{13,1},{2,14},{6,10},... | collective-permute-start | bytes 503816 | tf_op jit(solution)/shard_map/ppermute | solution.py:484
  8.6 1.7 %copy-start = (bf16[1280,1024]{1,0:T(8,128)(2,1)S(1)}, bf16[1280,1024]{1,0:T(8,128)(2,1)}, u32[]{:S(2)}) copy-start(bf16[1280,1024]{1,0:T(8,128)(2,1)} %wa.7) | copy-start | bytes 7864324
  10.3 1.7 %copy-start.2 = (bf16[1280,1024]{1,0:T(8,128)(2,1)S(1)}, bf16[1280,1024]{1,0:T(8,128)(2,1)}, u32[]{:S(2)}) copy-start(bf16[1280,1024]{1,0:T(8,128)(2,1)} %wf.7) | copy-start | bytes 7864324
  12.1 1.1 %copy-start.4 = (bf16[1,256,1280]{2,1,0:T(8,128)(2,1)S(1)}, bf16[1,256,1280]{2,1,0:T(8,128)(2,1)}, u32[]{:S(2)}) copy-start(bf16[1,256,1280]{2,1,0:T(8,128)(2,1)} %param.8) | copy-start | bytes 1966084
  13.1 0.7 copy-start.6
  13.8 10.6 %copy-start.1 = (bf16[1280,1024]{1,0:T(8,128)(2,1)S(1)}, bf16[1280,1024]{1,0:T(8,128)(2,1)}, u32[]{:S(2)}) copy-start(bf16[1280,1024]{1,0:T(8,128)(2,1)} %wa.7) | copy-start | bytes 7864324
  13.8 10.6 %copy-start.3 = (bf16[1280,1024]{1,0:T(8,128)(2,1)S(1)}, bf16[1280,1024]{1,0:T(8,128)(2,1)}, u32[]{:S(2)}) copy-start(bf16[1280,1024]{1,0:T(8,128)(2,1)} %wf.7) | copy-start | bytes 7864324
  21.9 4.2 %collective-permute-start.3 = (bf16[1296,128]{1,0:T(8,128)(2,1)S(1)}, bf16[1296,128]{1,0:T(8,128)(2,1)S(1)}, u32[]{:S(2)}, u32[]{:S(2)}) collective-permute-start(bf16[1296,128]{1,0:T(8,128)(2,1)S(1)} %collective-permute-done), channel_id=1, source_target_pairs={{0,1},{1,0},{2,3},{3,2},{4,5},{5,4},{6,7},{7,6},{8,9},{9,8},{10,11... | collective-permute-start | bytes 995336 | tf_op jit(solution)/shard_map/ppermute | solution.py:487
  21.9 4.1 %collective-permute-start.4 = (bf16[656,128]{1,0:T(8,128)(2,1)S(1)}, bf16[656,128]{1,0:T(8,128)(2,1)S(1)}, u32[]{:S(2)}, u32[]{:S(2)}) collective-permute-start(bf16[656,128]{1,0:T(8,128)(2,1)S(1)} %collective-permute-done.1), channel_id=1, source_target_pairs={{0,1},{1,0},{2,3},{3,2},{4,5},{5,4},{6,7},{7,6},{8,9},{9,8},{10,11... | collective-permute-start | bytes 503816 | tf_op jit(solution)/shard_map/ppermute | solution.py:487
  22.4 3.7 %collective-permute-start.5 = (bf16[656,128]{1,0:T(8,128)(2,1)S(1)}, bf16[656,128]{1,0:T(8,128)(2,1)S(1)}, u32[]{:S(2)}, u32[]{:S(2)}) collective-permute-start(bf16[656,128]{1,0:T(8,128)(2,1)S(1)} %collective-permute-done.2), channel_id=1, source_target_pairs={{0,1},{1,0},{2,3},{3,2},{4,5},{5,4},{6,7},{7,6},{8,9},{9,8},{10,11... | collective-permute-start | bytes 503816 | tf_op jit(solution)/shard_map/ppermute | solution.py:487
  22.4 9.8 %collective-permute-start.6 = (bf16[656,128]{1,0:T(8,128)(2,1)S(1)}, bf16[656,128]{1,0:T(8,128)(2,1)S(1)}, u32[]{:S(2)}, u32[]{:S(2)}) collective-permute-start(bf16[656,128]{1,0:T(8,128)(2,1)S(1)} %collective-permute-done.1), channel_id=1, source_target_pairs={{0,4},{4,0},{8,12},{12,8},{1,5},{5,1},{9,13},{13,9},{2,6},{6,2},{1... | collective-permute-start | bytes 503816 | tf_op jit(solution)/shard_map/ppermute | solution.py:484
  23.2 9.5 %collective-permute-start.7 = (bf16[656,128]{1,0:T(8,128)(2,1)S(1)}, bf16[656,128]{1,0:T(8,128)(2,1)S(1)}, u32[]{:S(2)}, u32[]{:S(2)}) collective-permute-start(bf16[656,128]{1,0:T(8,128)(2,1)S(1)} %collective-permute-done.2), channel_id=1, source_target_pairs={{0,4},{4,0},{8,12},{12,8},{1,5},{5,1},{9,13},{13,9},{2,6},{6,2},{1... | collective-permute-start | bytes 503816 | tf_op jit(solution)/shard_map/ppermute | solution.py:484
  26.1 1.6 %copy-start.5 = (s32[1,256]{1,0:T(1,128)S(1)}, s32[1,256]{1,0:T(1,128)}, u32[]{:S(2)}) copy-start(s32[1,256]{1,0:T(1,128)} %refs_0_) | copy-start | bytes 3076
  26.1 4.2 %copy-start.7 = (bf16[8192]{0:T(1024)(128)(2,1)S(1)}, bf16[8192]{0:T(1024)(128)(2,1)}, u32[]{:S(2)}) copy-start(bf16[8192]{0:T(1024)(128)(2,1)} %param.15) | copy-start | bytes 49156
  28.8 14.8 %collective-permute-start.8 = (bf16[96,1024]{1,0:T(8,128)(2,1)S(1)}, bf16[96,1024]{1,0:T(8,128)(2,1)S(1)}, u32[]{:S(2)}, u32[]{:S(2)}) collective-permute-start(bf16[96,1024]{1,0:T(8,128)(2,1)S(1)} %packet.4), channel_id=1, source_target_pairs={{0,12},{4,8},{8,4},{12,0},{1,13},{5,9},{9,5},{13,1},{2,14},{6,10},... | collective-permute-start | bytes 589832 | tf_op jit(solution)/shard_map/ppermute | solution.py:484
  31.4 18.2 %collective-permute-start.11 = (bf16[96,1024]{1,0:T(8,128)(2,1)S(1)}, bf16[96,1024]{1,0:T(8,128)(2,1)S(1)}, u32[]{:S(2)}, u32[]{:S(2)}) collective-permute-start(bf16[96,1024]{1,0:T(8,128)(2,1)S(1)} %packet.5), channel_id=1, source_target_pairs={{0,8},{4,12},{8,0},{12,4},{1,9},{5,13},{9,1},{13,5},{2,10},{6,14},... | collective-permute-start | bytes 589832 | tf_op jit(solution)/shard_map/ppermute | solution.py:484
  39.1 32.3 %collective-permute-start.10 = (bf16[256,1024]{1,0:T(8,128)(2,1)S(1)}, bf16[256,1024]{1,0:T(8,128)(2,1)S(1)}, u32[]{:S(2)}, u32[]{:S(2)}) collective-permute-start(bf16[256,1024]{1,0:T(8,128)(2,1)S(1)} %select.2), channel_id=1, source_target_pairs={{0,4},{4,0},{8,12},{12,8},{1,5},{5,1},{9,13},{13,9},{2,6},{6,2},{1... | collective-permute-start | bytes 1572872 | tf_op jit(solution)/shard_map/ppermute | solution.py:484
  43.6 13.5 %collective-permute-start.9 = (bf16[80,1024]{1,0:T(8,128)(2,1)S(1)}, bf16[80,1024]{1,0:T(8,128)(2,1)S(1)}, u32[]{:S(2)}, u32[]{:S(2)}) collective-permute-start(bf16[80,1024]{1,0:T(8,128)(2,1)S(1)} %get-tuple-element.71), channel_id=1, source_target_pairs={{0,8},{1,9},{4,12},{5,13},{8,0},{9,1},{12,4},{13,5},{2,10},{3,11},... | collective-permute-start | bytes 491528 | tf_op jit(solution)/shard_map/ppermute | solution.py:499
  47.3 21.7 %collective-permute-start.12 = (bf16[80,1024]{1,0:T(8,128)(2,1)S(1)}, bf16[80,1024]{1,0:T(8,128)(2,1)S(1)}, u32[]{:S(2)}, u32[]{:S(2)}) collective-permute-start(bf16[80,1024]{1,0:T(8,128)(2,1)S(1)} %get-tuple-element.79), channel_id=1, source_target_pairs={{0,9},{1,8},{4,13},{5,12},{8,1},{9,0},{12,5},{13,4},{2,11},{3,10},... | collective-permute-start | bytes 491528 | tf_op jit(solution)/shard_map/ppermute | solution.py:499
  49.6 24.2 %collective-permute-start.13 = (bf16[80,1024]{1,0:T(8,128)(2,1)S(1)}, bf16[80,1024]{1,0:T(8,128)(2,1)S(1)}, u32[]{:S(2)}, u32[]{:S(2)}) collective-permute-start(bf16[80,1024]{1,0:T(8,128)(2,1)S(1)} %get-tuple-element.83), channel_id=1, source_target_pairs={{0,12},{1,13},{4,8},{5,9},{8,4},{9,5},{12,0},{13,1},{2,14},{3,15},... | collective-permute-start | bytes 491528 | tf_op jit(solution)/shard_map/ppermute | solution.py:499
  52.0 21.8 %collective-permute-start.14 = (bf16[80,1024]{1,0:T(8,128)(2,1)S(1)}, bf16[80,1024]{1,0:T(8,128)(2,1)S(1)}, u32[]{:S(2)}, u32[]{:S(2)}) collective-permute-start(bf16[80,1024]{1,0:T(8,128)(2,1)S(1)} %get-tuple-element.84), channel_id=1, source_target_pairs={{0,13},{1,12},{4,9},{5,8},{8,5},{9,4},{12,1},{13,0},{2,15},{3,14},... | collective-permute-start | bytes 491528 | tf_op jit(solution)/shard_map/ppermute | solution.py:499

commit v18 on v17

--- a/solution.py
+++ b/solution.py
@@ -287,6 +287,33 @@
     )(*blocks, *slots)
 
 
+def parts_and_packet_kernel(m, early, n_parts, *refs):
+    weights, parts = refs[:4], refs[4 : 4 + n_parts]
+    blocks, slots = refs[4 + n_parts : 3 + n_parts + early], refs[3 + n_parts + early : -3]
+    block, slot, out = refs[-3:]
+    project_parts_kernel(*weights, *parts, block, slot)
+    packet_kernel(m, early, early, False, *blocks, block, *slots, slot, out)
+
+
+def parts_and_packet(m, parts, weights, blocks, slots, size):
+    ew, cols = weights[0].shape
+    rows = sum(p.shape[0] * (p.shape[1] - 16) * 128 // ew for p in parts)
+    operands = [*weights, *parts, *blocks, *slots]
+    return pl.pallas_call(
+        functools.partial(parts_and_packet_kernel, m, len(blocks) + 1, len(parts)),
+        out_shape=[
+            jax.ShapeDtypeStruct((rows, cols), BF16),
+            jax.ShapeDtypeStruct((1, rows), I32),
+            jax.ShapeDtypeStruct((2 * size, cols), BF16),
+        ],
+        in_specs=[VMEM] * len(operands),
+        out_specs=[VMEM] * 3,
+        compiler_params=PARAMS,
+        cost_estimate=cost(4 * rows * ew * cols, 4 * ew * cols),
+        name="parts_and_packet",
+    )(*operands)
+
+
 def order_kernel(first_size, parity, *refs):
     slots, outs = refs[:-2], refs[-2:]
     places = outs[0].shape[0]
@@ -517,14 +544,16 @@
         other = [over_tp(part)[None] for part in first]
         take([part[None] for part in first])
         other = lax.optimization_barrier((*other, blocks[-1]))[:3]
-        take(other)
-
-        early, size = len(blocks), 3 * half // 8
+        early, size = len(blocks) + 1, 3 * half // 8
         sent = {}
-        for m in (3, 2):
-            chosen = packet(m, early, blocks, slots, size, False)
-            slots[0] = after(slots[0], chosen[0])
-            sent[m] = over_ctx(chosen[0], m)
+        block, slot, chosen = parts_and_packet(3, other, weights, blocks, slots, size)
+        blocks.append(block)
+        slots.append(slot)
+        sent[3] = over_ctx(chosen, 3)
+        slots[0] = after(slots[0], chosen)
+        (chosen,) = packet(2, early, blocks, slots, size, False)
+        slots[0] = after(slots[0], chosen)
+        sent[2] = over_ctx(chosen, 2)
         shared = lax.optimization_barrier((*shared, blocks[-1]))[:2]
         take([lax.all_gather(part, "tp", axis=0) for part in shared])
 

time: 76.7 us -> 76.6 us (level)
    ppermute x8, waiting for transfers between devices: 11.2 us -> 20.2 us  [over_ctx(): return lax.ppermute(x, 'ctx', [(i, i ^ m) for i in range(n)])]
    ppermute x4, waiting for transfers between devices: 8.86 us -> 0.01 us  [to_core(): return lax.ppermute(x, ('ctx', 'tp'), pairs)]
    pallas_call x0 -> x1, Pallas kernels: none -> 2.51 us  [parts_and_packet(): pl.pallas_call(functools.partial(parts_and_packet_kernel, m, len(blocks)...]
    pallas_call x3 -> x2, Pallas kernels: 4.8 us -> 3.17 us  [project_parts(): pl.pallas_call(project_parts_kernel, out_shape=[jax.ShapeDtypeStruct((row...]
    pallas_call x4 -> x3, Pallas kernels: 4.84 us -> 3.78 us  [packet(): pl.pallas_call(functools.partial(packet_kernel, m, early, len(blocks), se...]
  transfers between devices with their start and end apart: 15 -> 15, of which waited for: 6 -> 5; matrix products, arithmetic and copies ran while one was open for 2% -> 2% of each run, Pallas kernels for 18% -> 18%
where the time goes in v18:
time: 76.6 us; the launch traced here: 76 us
  waiting for transfers between devices  20.2 us (26%)
  starting transfers between devices  18 us (23%)
  Pallas kernels  17.5 us (23%)
  blocking collectives  13.5 us (18%)
  local copies, waits for them, and re-layouts  6.69 us (9%)
    ppermute x8, waiting for transfers between devices, over_ctx(): return lax.ppermute(x, 'ctx', [(i, i ^ m) for i in range(n)])  20.2 us
    ppermute x8, starting transfers between devices, over_ctx(): return lax.ppermute(x, 'ctx', [(i, i ^ m) for i in range(n)])  11.6 us
    ppermute x4, starting transfers between devices, to_core(): return lax.ppermute(x, ('ctx', 'tp'), pairs)  5.79 us
    unnamed x16, local copies, waits for them, and re-layouts  5.26 us
    all_gather x2, blocking collectives, body(): sent[m] = [whole_packet, lax.all_gather(whole_packet[size:], 'tp', axis=0)]  5.02 us
    all_gather x2, blocking collectives, body(): take([lax.all_gather(part, 'tp', axis=0) for part in shared])  4.07 us
    pallas_call x3, Pallas kernels, packet(): pl.pallas_call(functools.partial(packet_kernel, m, early, len(blocks), se...  3.78 us
    pallas_call x2, Pallas kernels, project_parts(): pl.pallas_call(project_parts_kernel, out_shape=[jax.ShapeDtypeStruct((row...  3.17 us
  transfers between devices with their start and end apart: 15, of which 5 were waited for; matrix products, arithmetic and copies ran while one was open for 2% of the time, Pallas kernels for 18%

profile of v18, /device:TPU:0, one launch (start us, length us, event | category | flops | bytes accessed | tf_op | source)
XLA Modules:
  0.0 76.0 jit_solution(12913094392628876333)
XLA Ops:
  0.0 1.5 %to_send.1 = (bf16[1296,128]{1,0:T(8,128)(2,1)S(1)}, bf16[656,128]{1,0:T(8,128)(2,1)S(1)}, bf16[656,128]{1,0:T(8,128)(2,1)S(1)}, s32[1,256]{1,0:T(1,128)S(1)}) custom-call(bf16[256,1280]{1,0:T(8,128)(2,1)} %bitcast.16, s32[1,256]{1,0:T(1,128)} %refs_0_.2, s32[1,256]{1,0:T(1,128)} %kind.3), custom_call_target="tpu_custom_call" | custom-call | bytes 40960 | tf_op jit(solution)/shard_map/to_send/pallas_call | solution.py:109
  1.5 3.1 %collective-permute-start = (bf16[1296,128]{1,0:T(8,128)(2,1)S(1)}, bf16[1296,128]{1,0:T(8,128)(2,1)S(1)}, u32[]{:S(2)}, u32[]{:S(2)}) collective-permute-start(bf16[1296,128]{1,0:T(8,128)(2,1)S(1)} %get-tuple-element.47), channel_id=1, source_target_pairs={{0,4},{4,0},{8,12},{12,8},{1,5},{5,1},{9,13},{13,9},{2,6},{6,2},{1... | collective-permute-start | bytes 995336 | tf_op jit(solution)/shard_map/ppermute | solution.py:511
  4.6 2.6 %collective-permute-start.1 = (bf16[656,128]{1,0:T(8,128)(2,1)S(1)}, bf16[656,128]{1,0:T(8,128)(2,1)S(1)}, u32[]{:S(2)}, u32[]{:S(2)}) collective-permute-start(bf16[656,128]{1,0:T(8,128)(2,1)S(1)} %get-tuple-element.48), channel_id=1, source_target_pairs={{0,8},{4,12},{8,0},{12,4},{1,9},{5,13},{9,1},{13,5},{2,10},{6,14},... | collective-permute-start | bytes 503816 | tf_op jit(solution)/shard_map/ppermute | solution.py:511
  7.2 0.0 collective-permute-start.2
  7.2 0.7 broadcast_in_dim.31.ba.refs_2_
  7.9 0.7 broadcast_in_dim.32.bf.refs_3_
  8.6 1.7 %copy-done = bf16[1280,1024]{1,0:T(8,128)(2,1)S(1)} copy-done((bf16[1280,1024]{1,0:T(8,128)(2,1)S(1)}, bf16[1280,1024]{1,0:T(8,128)(2,1)}, u32[]{:S(2)}) %copy-start) | copy-done | bytes 2621464
  10.3 1.7 %copy-done.2 = bf16[1280,1024]{1,0:T(8,128)(2,1)S(1)} copy-done((bf16[1280,1024]{1,0:T(8,128)(2,1)S(1)}, bf16[1280,1024]{1,0:T(8,128)(2,1)}, u32[]{:S(2)}) %copy-start.2) | copy-done | bytes 2621464
  12.1 1.1 %copy-done.4 = bf16[1,256,1280]{2,1,0:T(8,128)(2,1)S(1)} copy-done((bf16[1,256,1280]{2,1,0:T(8,128)(2,1)S(1)}, bf16[1,256,1280]{2,1,0:T(8,128)(2,1)}, u32[]{:S(2)}) %copy-start.4) | copy-done | bytes 655384
  13.1 0.7 copy-done.6
  13.8 1.6 %project_own.1.refs_7_.refs_0_ = bf16[256,1024]{1,0:T(8,128)(2,1)S(1)} custom-call(s32[1,256]{1,0:T(1,128)S(1)} %copy-done.6, bf16[256,1280]{1,0:T(8,128)(2,1)S(1)} %bitcast.17, bf16[1280,1024]{1,0:T(8,128)(2,1)S(1)} %copy-done, bf16[1280,1024]{1,0:T(8,128)(2,1)S(1)} %copy-done.2, bf16[1,1024]{1,0:T(2,128)(2,1)S(1)} %broadcast_in_dim.31.ba.refs_2_, ...), custom_call_target="tpu_custom_call" | custom-call | flops 83886080 | bytes 327680 | tf_op jit(solution)/shard_map/project_own/pallas_call | solution.py:147
  15.4 1.1 %collective-permute-done.1 = bf16[656,128]{1,0:T(8,128)(2,1)S(1)} collective-permute-done((bf16[656,128]{1,0:T(8,128)(2,1)S(1)}, bf16[656,128]{1,0:T(8,128)(2,1)S(1)}, u32[]{:S(2)}, u32[]{:S(2)}) %collective-permute-start.1) | collective-permute-done | bytes 167968 | tf_op jit(solution)/shard_map/ppermute | solution.py:511
  16.5 5.4 %collective-permute-done.2 = bf16[656,128]{1,0:T(8,128)(2,1)S(1)} collective-permute-done((bf16[656,128]{1,0:T(8,128)(2,1)S(1)}, bf16[656,128]{1,0:T(8,128)(2,1)S(1)}, u32[]{:S(2)}, u32[]{:S(2)}) %collective-permute-start.2) | collective-permute-done | bytes 167968 | tf_op jit(solution)/shard_map/ppermute | solution.py:511
  21.9 0.5 collective-permute-start.4
  22.4 0.0 collective-permute-start.5
  22.4 0.8 %collective-permute-start.6 = (bf16[656,128]{1,0:T(8,128)(2,1)S(1)}, bf16[656,128]{1,0:T(8,128)(2,1)S(1)}, u32[]{:S(2)}, u32[]{:S(2)}) collective-permute-start(bf16[656,128]{1,0:T(8,128)(2,1)S(1)} %collective-permute-done.1), channel_id=1, source_target_pairs={{0,4},{4,0},{8,12},{12,8},{1,5},{5,1},{9,13},{13,9},{2,6},{6,2},{1... | collective-permute-start | bytes 503816 | tf_op jit(solution)/shard_map/ppermute | solution.py:511
  23.2 1.3 %collective-permute-start.7 = (bf16[656,128]{1,0:T(8,128)(2,1)S(1)}, bf16[656,128]{1,0:T(8,128)(2,1)S(1)}, u32[]{:S(2)}, u32[]{:S(2)}) collective-permute-start(bf16[656,128]{1,0:T(8,128)(2,1)S(1)} %collective-permute-done.2), channel_id=1, source_target_pairs={{0,4},{4,0},{8,12},{12,8},{1,5},{5,1},{9,13},{13,9},{2,6},{6,2},{1... | collective-permute-start | bytes 503816 | tf_op jit(solution)/shard_map/ppermute | solution.py:511
  24.5 1.6 %project_parts.2 = (bf16[256,1024]{1,0:T(8,128)(2,1)S(1)}, s32[1,256]{1,0:T(1,128)S(1)}) custom-call(bf16[1280,1024]{1,0:T(8,128)(2,1)S(1)} %copy-done.1, bf16[1280,1024]{1,0:T(8,128)(2,1)S(1)} %copy-done.3, bf16[1,1024]{1,0:T(2,128)(2,1)S(1)} %broadcast_in_dim.31.ba.refs_2_, bf16[1,1024]{1,0:T(2,128)(2,1)S(1)} %broadcast_in_dim.32.bf.refs_3_, ...), custom_call_target="tpu_custom_call" | custom-call | flops 83886080 | bytes 327680 | tf_op jit(solution)/shard_map/project_parts/pallas_call | solution.py:177
  26.1 0.0 collective-permute-done.4
  26.1 0.0 collective-permute-done.5
  26.1 0.0 copy-start.7
  26.1 2.5 %parts_and_packet.1 = (bf16[256,1024]{1,0:T(8,128)(2,1)S(1)}, s32[1,256]{1,0:T(1,128)S(1)}, bf16[96,1024]{1,0:T(8,128)(2,1)S(1)}) custom-call(bf16[1280,1024]{1,0:T(8,128)(2,1)S(1)} %copy-done.1, bf16[1280,1024]{1,0:T(8,128)(2,1)S(1)} %copy-done.3, bf16[1,1024]{1,0:T(2,128)(2,1)S(1)} %broadcast_in_dim.31.ba.refs_2_, ...), custom_call_target="tpu_custom_call" | custom-call | flops 83886080 | bytes 327680 | tf_op jit(solution)/shard_map/parts_and_packet/pallas_call | solution.py:302
  28.6 1.5 %collective-permute-start.8 = (bf16[96,1024]{1,0:T(8,128)(2,1)S(1)}, bf16[96,1024]{1,0:T(8,128)(2,1)S(1)}, u32[]{:S(2)}, u32[]{:S(2)}) collective-permute-start(bf16[96,1024]{1,0:T(8,128)(2,1)S(1)} %get-tuple-element.62), channel_id=1, source_target_pairs={{0,12},{4,8},{8,4},{12,0},{1,13},{5,9},{9,5},{13,1},{2,14},{6,10},... | collective-permute-start | bytes 589832 | tf_op jit(solution)/shard_map/ppermute | solution.py:511
  30.2 1.0 %packet.3 = bf16[96,1024]{1,0:T(8,128)(2,1)S(1)} custom-call(bf16[256,1024]{1,0:T(8,128)(2,1)S(1)} %project_own.1.refs_7_.refs_0_, bf16[256,1024]{1,0:T(8,128)(2,1)S(1)} %get-tuple-element.53.refs_8_.refs_1_, bf16[256,1024]{1,0:T(8,128)(2,1)S(1)} %get-tuple-element.58.refs_2_, s32[1,256]{1,0:T(1,128)S(1)} %copy-done.5, ...), custom_call_target="tpu_custom_call" | custom-call | flops 9437184 | bytes 98304 | tf_op jit(solution)/shard_map/packet/pallas_call | solution.py:279
  31.2 0.8 %collective-permute-start.11 = (bf16[96,1024]{1,0:T(8,128)(2,1)S(1)}, bf16[96,1024]{1,0:T(8,128)(2,1)S(1)}, u32[]{:S(2)}, u32[]{:S(2)}) collective-permute-start(bf16[96,1024]{1,0:T(8,128)(2,1)S(1)} %packet.3), channel_id=1, source_target_pairs={{0,8},{4,12},{8,0},{12,4},{1,9},{5,13},{9,1},{13,5},{2,10},{6,14},... | collective-permute-start | bytes 589832 | tf_op jit(solution)/shard_map/ppermute | solution.py:511
  32.1 0.6 collective-permute-done.7
  32.7 2.0 %all-gather = bf16[1312,128]{1,0:T(8,128)(2,1)S(1)} all-gather(bf16[656,128]{1,0:T(8,128)(2,1)S(1)} %collective-permute-done.6), channel_id=2, replica_groups=mesh['groups'=2,'ctx'=4,'enc'=2,'tp'=2] {'tp'}, dimensions={0}, use_global_device_ids=true | all-gather | bytes 503808 | tf_op jit(solution)/shard_map/all_gather | solution.py:558
  34.7 2.0 %all-gather.1 = bf16[1312,128]{1,0:T(8,128)(2,1)S(1)} all-gather(bf16[656,128]{1,0:T(8,128)(2,1)S(1)} %collective-permute-done.7), channel_id=3, replica_groups=mesh['groups'=2,'ctx'=4,'enc'=2,'tp'=2] {'tp'}, dimensions={0}, use_global_device_ids=true | all-gather | bytes 503808 | tf_op jit(solution)/shard_map/all_gather | solution.py:558
  36.8 1.6 %project_parts.3 = (bf16[256,1024]{1,0:T(8,128)(2,1)S(1)}, s32[1,256]{1,0:T(1,128)S(1)}) custom-call(bf16[1280,1024]{1,0:T(8,128)(2,1)S(1)} %copy-done.1, bf16[1280,1024]{1,0:T(8,128)(2,1)S(1)} %copy-done.3, bf16[1,1024]{1,0:T(2,128)(2,1)S(1)} %broadcast_in_dim.31.ba.refs_2_, bf16[1,1024]{1,0:T(2,128)(2,1)S(1)} %broadcast_in_dim.32.bf.refs_3_, ...), custom_call_target="tpu_custom_call" | custom-call | flops 83886080 | bytes 327680 | tf_op jit(solution)/shard_map/project_parts/pallas_call | solution.py:177
  38.4 0.7 select.2
  39.1 1.6 %collective-permute-start.10 = (bf16[256,1024]{1,0:T(8,128)(2,1)S(1)}, bf16[256,1024]{1,0:T(8,128)(2,1)S(1)}, u32[]{:S(2)}, u32[]{:S(2)}) collective-permute-start(bf16[256,1024]{1,0:T(8,128)(2,1)S(1)} %select.2), channel_id=1, source_target_pairs={{0,4},{4,0},{8,12},{12,8},{1,5},{5,1},{9,13},{13,9},{2,6},{6,2},{1... | collective-permute-start | bytes 1572872 | tf_op jit(solution)/shard_map/ppermute | solution.py:511
  40.7 1.4 %packet.4 = (bf16[80,1024]{1,0:T(8,128)(2,1)S(1)}, bf16[80,1024]{1,0:T(8,128)(2,1)S(1)}) custom-call(bf16[256,1024]{1,0:T(8,128)(2,1)S(1)} %project_own.1.refs_7_.refs_0_, bf16[256,1024]{1,0:T(8,128)(2,1)S(1)} %get-tuple-element.53.refs_8_.refs_1_, bf16[256,1024]{1,0:T(8,128)(2,1)S(1)} %get-tuple-element.58.refs_2_, ...), custom_call_target="tpu_custom_call" | custom-call | flops 20971520 | bytes 131072 | tf_op jit(solution)/shard_map/packet/pallas_call | solution.py:279
  42.0 1.4 %packet.5 = (bf16[80,1024]{1,0:T(8,128)(2,1)S(1)}, bf16[80,1024]{1,0:T(8,128)(2,1)S(1)}) custom-call(bf16[256,1024]{1,0:T(8,128)(2,1)S(1)} %project_own.1.refs_7_.refs_0_, bf16[256,1024]{1,0:T(8,128)(2,1)S(1)} %get-tuple-element.53.refs_8_.refs_1_, bf16[256,1024]{1,0:T(8,128)(2,1)S(1)} %get-tuple-element.58.refs_2_, ...), custom_call_target="tpu_custom_call" | custom-call | flops 20971520 | bytes 131072 | tf_op jit(solution)/shard_map/packet/pallas_call | solution.py:279
  43.4 3.2 %collective-permute-start.9 = (bf16[80,1024]{1,0:T(8,128)(2,1)S(1)}, bf16[80,1024]{1,0:T(8,128)(2,1)S(1)}, u32[]{:S(2)}, u32[]{:S(2)}) collective-permute-start(bf16[80,1024]{1,0:T(8,128)(2,1)S(1)} %get-tuple-element.73), channel_id=1, source_target_pairs={{0,8},{1,9},{4,12},{5,13},{8,0},{9,1},{12,4},{13,5},{2,10},{3,11},... | collective-permute-start | bytes 491528 | tf_op jit(solution)/shard_map/ppermute | solution.py:526
  46.6 0.6 order_of.1
  47.3 0.1 collective-permute-start.12
  47.3 2.1 %collective-permute-done.11.refs_0_ = bf16[96,1024]{1,0:T(8,128)(2,1)S(1)} collective-permute-done((bf16[96,1024]{1,0:T(8,128)(2,1)S(1)}, bf16[96,1024]{1,0:T(8,128)(2,1)S(1)}, u32[]{:S(2)}, u32[]{:S(2)}) %collective-permute-start.11) | collective-permute-done | bytes 196640 | tf_op jit(solution)/shard_map/ppermute | solution.py:511
  49.4 2.5 %collective-permute-start.13 = (bf16[80,1024]{1,0:T(8,128)(2,1)S(1)}, bf16[80,1024]{1,0:T(8,128)(2,1)S(1)}, u32[]{:S(2)}, u32[]{:S(2)}) collective-permute-start(bf16[80,1024]{1,0:T(8,128)(2,1)S(1)} %get-tuple-element.85), channel_id=1, source_target_pairs={{0,12},{1,13},{4,8},{5,9},{8,4},{9,5},{12,0},{13,1},{2,14},{3,15},... | collective-permute-start | bytes 491528 | tf_op jit(solution)/shard_map/ppermute | solution.py:526
  51.9 3.1 %all-gather.5 = bf16[96,1024]{1,0:T(8,128)(2,1)S(1)} all-gather(bf16[48,1024]{1,0:T(8,128)(2,1)S(1)} %slice.11), channel_id=7, replica_groups=mesh['groups'=2,'ctx'=4,'enc'=2,'tp'=2] {'tp'}, dimensions={0}, use_global_device_ids=true | all-gather | bytes 294912 | tf_op jit(solution)/shard_map/all_gather | solution.py:577
  55.0 1.9 %all-gather.4 = bf16[96,1024]{1,0:T(8,128)(2,1)S(1)} all-gather(bf16[48,1024]{1,0:T(8,128)(2,1)S(1)} %slice.10), channel_id=6, replica_groups=mesh['groups'=2,'ctx'=4,'enc'=2,'tp'=2] {'tp'}, dimensions={0}, use_global_device_ids=true | all-gather | bytes 294912 | tf_op jit(solution)/shard_map/all_gather | solution.py:577
  57.0 0.7 select.3
  57.7 2.2 %all-gather.2 = bf16[256,1024]{1,0:T(8,128)(2,1)S(1)} all-gather(bf16[128,1024]{1,0:T(8,128)(2,1)S(1)} %get-tuple-element.76), channel_id=4, replica_groups=mesh['groups'=2,'ctx'=4,'enc'=2,'tp'=2] {'tp'}, dimensions={0}, use_global_device_ids=true | all-gather | bytes 786432 | tf_op jit(solution)/shard_map/all_gather | solution.py:530
  59.9 0.2 squares.2.refs_0_
  60.0 0.4 place.1
  60.4 11.0 %collective-permute-done.10.refs_0_.refs_10_ = bf16[256,1024]{1,0:T(8,128)(2,1)S(1)} collective-permute-done((bf16[256,1024]{1,0:T(8,128)(2,1)S(1)}, bf16[256,1024]{1,0:T(8,128)(2,1)S(1)}, u32[]{:S(2)}, u32[]{:S(2)}) %collective-permute-start.10) | collective-permute-done | bytes 524320 | tf_op jit(solution)/shard_map/ppermute | solution.py:511
  71.4 2.2 %all-gather.3 = bf16[256,1024]{1,0:T(8,128)(2,1)S(1)} all-gather(bf16[128,1024]{1,0:T(8,128)(2,1)S(1)} %slice.12), channel_id=5, replica_groups=mesh['groups'=2,'ctx'=4,'enc'=2,'tp'=2] {'tp'}, dimensions={0}, use_global_device_ids=true | all-gather | bytes 786432 | tf_op jit(solution)/shard_map/all_gather | solution.py:535
  73.6 0.2 squares.3.refs_1_
  73.8 2.2 %place_and_norm.1 = bf16[128,8192]{1,0:T(8,128)(2,1)} custom-call(bf16[1,8192]{1,0:T(2,128)(2,1)S(1)} %broadcast_in_dim.30.gain, f32[128,1]{1,0:T(8,128)S(1)} %squares.2.refs_0_, f32[128,1]{1,0:T(8,128)S(1)} %squares.3.refs_1_, f32[128,1]{1,0:T(8,128)S(1)} %get-tuple-element.82.refs_2_, bf16[128,128]{1,0:T(8,128)(2,1)S(1)} %get-tuple-element.83.refs_3_, ...), custom_call_target="tpu_custom_call" | custom-call | flops 262144 | bytes 262144 | tf_op jit(solution)/shard_map/place_and_norm/pallas_call | solution.py:488
  (25 shorter events, 0.1 us)
Async XLA Ops:
  1.5 20.4 %collective-permute-start = (bf16[1296,128]{1,0:T(8,128)(2,1)S(1)}, bf16[1296,128]{1,0:T(8,128)(2,1)S(1)}, u32[]{:S(2)}, u32[]{:S(2)}) collective-permute-start(bf16[1296,128]{1,0:T(8,128)(2,1)S(1)} %get-tuple-element.47), channel_id=1, source_target_pairs={{0,4},{4,0},{8,12},{12,8},{1,5},{5,1},{9,13},{13,9},{2,6},{6,2},{1... | collective-permute-start | bytes 995336 | tf_op jit(solution)/shard_map/ppermute | solution.py:511
  4.6 11.8 %collective-permute-start.1 = (bf16[656,128]{1,0:T(8,128)(2,1)S(1)}, bf16[656,128]{1,0:T(8,128)(2,1)S(1)}, u32[]{:S(2)}, u32[]{:S(2)}) collective-permute-start(bf16[656,128]{1,0:T(8,128)(2,1)S(1)} %get-tuple-element.48), channel_id=1, source_target_pairs={{0,8},{4,12},{8,0},{12,4},{1,9},{5,13},{9,1},{13,5},{2,10},{6,14},... | collective-permute-start | bytes 503816 | tf_op jit(solution)/shard_map/ppermute | solution.py:511
  7.2 14.7 %collective-permute-start.2 = (bf16[656,128]{1,0:T(8,128)(2,1)S(1)}, bf16[656,128]{1,0:T(8,128)(2,1)S(1)}, u32[]{:S(2)}, u32[]{:S(2)}) collective-permute-start(bf16[656,128]{1,0:T(8,128)(2,1)S(1)} %get-tuple-element.49), channel_id=1, source_target_pairs={{0,12},{4,8},{8,4},{12,0},{1,13},{5,9},{9,5},{13,1},{2,14},{6,10},... | collective-permute-start | bytes 503816 | tf_op jit(solution)/shard_map/ppermute | solution.py:511
  8.6 1.7 %copy-start = (bf16[1280,1024]{1,0:T(8,128)(2,1)S(1)}, bf16[1280,1024]{1,0:T(8,128)(2,1)}, u32[]{:S(2)}) copy-start(bf16[1280,1024]{1,0:T(8,128)(2,1)} %wa.5) | copy-start | bytes 7864324
  10.3 1.7 %copy-start.2 = (bf16[1280,1024]{1,0:T(8,128)(2,1)S(1)}, bf16[1280,1024]{1,0:T(8,128)(2,1)}, u32[]{:S(2)}) copy-start(bf16[1280,1024]{1,0:T(8,128)(2,1)} %wf.5) | copy-start | bytes 7864324
  12.0 1.1 %copy-start.4 = (bf16[1,256,1280]{2,1,0:T(8,128)(2,1)S(1)}, bf16[1,256,1280]{2,1,0:T(8,128)(2,1)}, u32[]{:S(2)}) copy-start(bf16[1,256,1280]{2,1,0:T(8,128)(2,1)} %param.8) | copy-start | bytes 1966084
  13.1 0.7 copy-start.6
  13.8 10.6 %copy-start.1 = (bf16[1280,1024]{1,0:T(8,128)(2,1)S(1)}, bf16[1280,1024]{1,0:T(8,128)(2,1)}, u32[]{:S(2)}) copy-start(bf16[1280,1024]{1,0:T(8,128)(2,1)} %wa.5) | copy-start | bytes 7864324
  13.8 10.6 %copy-start.3 = (bf16[1280,1024]{1,0:T(8,128)(2,1)S(1)}, bf16[1280,1024]{1,0:T(8,128)(2,1)}, u32[]{:S(2)}) copy-start(bf16[1280,1024]{1,0:T(8,128)(2,1)} %wf.5) | copy-start | bytes 7864324
  21.9 4.2 %collective-permute-start.3 = (bf16[1296,128]{1,0:T(8,128)(2,1)S(1)}, bf16[1296,128]{1,0:T(8,128)(2,1)S(1)}, u32[]{:S(2)}, u32[]{:S(2)}) collective-permute-start(bf16[1296,128]{1,0:T(8,128)(2,1)S(1)} %collective-permute-done), channel_id=1, source_target_pairs={{0,1},{1,0},{2,3},{3,2},{4,5},{5,4},{6,7},{7,6},{8,9},{9,8},{10,11... | collective-permute-start | bytes 995336 | tf_op jit(solution)/shard_map/ppermute | solution.py:514
  21.9 4.2 %collective-permute-start.4 = (bf16[656,128]{1,0:T(8,128)(2,1)S(1)}, bf16[656,128]{1,0:T(8,128)(2,1)S(1)}, u32[]{:S(2)}, u32[]{:S(2)}) collective-permute-start(bf16[656,128]{1,0:T(8,128)(2,1)S(1)} %collective-permute-done.1), channel_id=1, source_target_pairs={{0,1},{1,0},{2,3},{3,2},{4,5},{5,4},{6,7},{7,6},{8,9},{9,8},{10,11... | collective-permute-start | bytes 503816 | tf_op jit(solution)/shard_map/ppermute | solution.py:514
  22.4 3.7 %collective-permute-start.5 = (bf16[656,128]{1,0:T(8,128)(2,1)S(1)}, bf16[656,128]{1,0:T(8,128)(2,1)S(1)}, u32[]{:S(2)}, u32[]{:S(2)}) collective-permute-start(bf16[656,128]{1,0:T(8,128)(2,1)S(1)} %collective-permute-done.2), channel_id=1, source_target_pairs={{0,1},{1,0},{2,3},{3,2},{4,5},{5,4},{6,7},{7,6},{8,9},{9,8},{10,11... | collective-permute-start | bytes 503816 | tf_op jit(solution)/shard_map/ppermute | solution.py:514
  22.4 9.7 %collective-permute-start.6 = (bf16[656,128]{1,0:T(8,128)(2,1)S(1)}, bf16[656,128]{1,0:T(8,128)(2,1)S(1)}, u32[]{:S(2)}, u32[]{:S(2)}) collective-permute-start(bf16[656,128]{1,0:T(8,128)(2,1)S(1)} %collective-permute-done.1), channel_id=1, source_target_pairs={{0,4},{4,0},{8,12},{12,8},{1,5},{5,1},{9,13},{13,9},{2,6},{6,2},{1... | collective-permute-start | bytes 503816 | tf_op jit(solution)/shard_map/ppermute | solution.py:511
  23.2 9.5 %collective-permute-start.7 = (bf16[656,128]{1,0:T(8,128)(2,1)S(1)}, bf16[656,128]{1,0:T(8,128)(2,1)S(1)}, u32[]{:S(2)}, u32[]{:S(2)}) collective-permute-start(bf16[656,128]{1,0:T(8,128)(2,1)S(1)} %collective-permute-done.2), channel_id=1, source_target_pairs={{0,4},{4,0},{8,12},{12,8},{1,5},{5,1},{9,13},{13,9},{2,6},{6,2},{1... | collective-permute-start | bytes 503816 | tf_op jit(solution)/shard_map/ppermute | solution.py:511
  24.4 1.6 %copy-start.5 = (s32[1,256]{1,0:T(1,128)S(1)}, s32[1,256]{1,0:T(1,128)}, u32[]{:S(2)}) copy-start(s32[1,256]{1,0:T(1,128)} %refs_0_.2) | copy-start | bytes 3076
  26.1 4.1 %copy-start.7 = (bf16[8192]{0:T(1024)(128)(2,1)S(1)}, bf16[8192]{0:T(1024)(128)(2,1)}, u32[]{:S(2)}) copy-start(bf16[8192]{0:T(1024)(128)(2,1)} %param.15) | copy-start | bytes 49156
  28.6 14.8 %collective-permute-start.8 = (bf16[96,1024]{1,0:T(8,128)(2,1)S(1)}, bf16[96,1024]{1,0:T(8,128)(2,1)S(1)}, u32[]{:S(2)}, u32[]{:S(2)}) collective-permute-start(bf16[96,1024]{1,0:T(8,128)(2,1)S(1)} %get-tuple-element.62), channel_id=1, source_target_pairs={{0,12},{4,8},{8,4},{12,0},{1,13},{5,9},{9,5},{13,1},{2,14},{6,10},... | collective-permute-start | bytes 589832 | tf_op jit(solution)/shard_map/ppermute | solution.py:511
  31.2 18.2 %collective-permute-start.11 = (bf16[96,1024]{1,0:T(8,128)(2,1)S(1)}, bf16[96,1024]{1,0:T(8,128)(2,1)S(1)}, u32[]{:S(2)}, u32[]{:S(2)}) collective-permute-start(bf16[96,1024]{1,0:T(8,128)(2,1)S(1)} %packet.3), channel_id=1, source_target_pairs={{0,8},{4,12},{8,0},{12,4},{1,9},{5,13},{9,1},{13,5},{2,10},{6,14},... | collective-permute-start | bytes 589832 | tf_op jit(solution)/shard_map/ppermute | solution.py:511
  39.1 32.3 %collective-permute-start.10 = (bf16[256,1024]{1,0:T(8,128)(2,1)S(1)}, bf16[256,1024]{1,0:T(8,128)(2,1)S(1)}, u32[]{:S(2)}, u32[]{:S(2)}) collective-permute-start(bf16[256,1024]{1,0:T(8,128)(2,1)S(1)} %select.2), channel_id=1, source_target_pairs={{0,4},{4,0},{8,12},{12,8},{1,5},{5,1},{9,13},{13,9},{2,6},{6,2},{1... | collective-permute-start | bytes 1572872 | tf_op jit(solution)/shard_map/ppermute | solution.py:511
  43.4 13.5 %collective-permute-start.9 = (bf16[80,1024]{1,0:T(8,128)(2,1)S(1)}, bf16[80,1024]{1,0:T(8,128)(2,1)S(1)}, u32[]{:S(2)}, u32[]{:S(2)}) collective-permute-start(bf16[80,1024]{1,0:T(8,128)(2,1)S(1)} %get-tuple-element.73), channel_id=1, source_target_pairs={{0,8},{1,9},{4,12},{5,13},{8,0},{9,1},{12,4},{13,5},{2,10},{3,11},... | collective-permute-start | bytes 491528 | tf_op jit(solution)/shard_map/ppermute | solution.py:526
  47.3 12.8 %collective-permute-start.12 = (bf16[80,1024]{1,0:T(8,128)(2,1)S(1)}, bf16[80,1024]{1,0:T(8,128)(2,1)S(1)}, u32[]{:S(2)}, u32[]{:S(2)}) collective-permute-start(bf16[80,1024]{1,0:T(8,128)(2,1)S(1)} %get-tuple-element.81), channel_id=1, source_target_pairs={{0,9},{1,8},{4,13},{5,12},{8,1},{9,0},{12,5},{13,4},{2,11},{3,10},... | collective-permute-start | bytes 491528 | tf_op jit(solution)/shard_map/ppermute | solution.py:526
  49.4 24.3 %collective-permute-start.13 = (bf16[80,1024]{1,0:T(8,128)(2,1)S(1)}, bf16[80,1024]{1,0:T(8,128)(2,1)S(1)}, u32[]{:S(2)}, u32[]{:S(2)}) collective-permute-start(bf16[80,1024]{1,0:T(8,128)(2,1)S(1)} %get-tuple-element.85), channel_id=1, source_target_pairs={{0,12},{1,13},{4,8},{5,9},{8,4},{9,5},{12,0},{13,1},{2,14},{3,15},... | collective-permute-start | bytes 491528 | tf_op jit(solution)/shard_map/ppermute | solution.py:526
  51.9 21.8 %collective-permute-start.14 = (bf16[80,1024]{1,0:T(8,128)(2,1)S(1)}, bf16[80,1024]{1,0:T(8,128)(2,1)S(1)}, u32[]{:S(2)}, u32[]{:S(2)}) collective-permute-start(bf16[80,1024]{1,0:T(8,128)(2,1)S(1)} %get-tuple-element.86), channel_id=1, source_target_pairs={{0,13},{1,12},{4,9},{5,8},{8,5},{9,4},{12,1},{13,0},{2,15},{3,14},... | collective-permute-start | bytes 491528 | tf_op jit(solution)/shard_map/ppermute | solution.py:526

commit v19 on v17

--- a/solution.py
+++ b/solution.py
@@ -47,8 +47,13 @@
     copies = [
         pltpu.make_async_copy(slot, slot_here, sems.at[0]),
         pltpu.make_async_copy(kind, kind_here, sems.at[1]),
-        pltpu.make_async_copy(source, rows_here, sems.at[2]),
     ]
+    cut = rows_here.shape[0] // 2
+    for k in range(2):
+        at = pl.ds(k * cut, cut)
+        copies.append(
+            pltpu.make_async_copy(source.at[at, :], rows_here.at[at, :], sems.at[2 + k])
+        )
     for copy in copies:
         copy.start()
     copies[0].wait()
@@ -68,15 +73,23 @@
         slots = jnp.sum(jnp.where(here, slot_col, 0), axis=0, keepdims=True)
         kinds = jnp.sum(jnp.where(here, kind_col, 0), axis=0, keepdims=True)
         deal = rank_row == rank_at(lax.broadcasted_iota(I32, (half, 1), 0))
-        copies[2].wait()
+        deal = deal.astype(F32).astype(BF16)
+        dealt_rows = None
+        for k in range(2):
+            copies[2 + k].wait()
+            part = jnp.dot(
+                deal[:, k * cut : (k + 1) * cut],
+                rows_here[k * cut : (k + 1) * cut, :],
+                preferred_element_type=F32,
+            )
+            dealt_rows = part if dealt_rows is None else dealt_rows + part
         rows_out = refs[-5]
-        rows_out[...] = jnp.dot(
-            deal.astype(F32).astype(BF16), rows_here[...], preferred_element_type=F32
-        ).astype(BF16)
+        rows_out[...] = dealt_rows.astype(BF16)
     else:
         slots = jnp.where(t == 0, slot_here[:, :half], slot_here[:, half:])
         kinds = jnp.where(t == 0, kind_here[:, :half], kind_here[:, half:])
         copies[2].wait()
+        copies[3].wait()
         rows_out = rows_here
     for out, parity in zip(outs, cuts):
         x, s, k = rows_out, slots, kinds
@@ -115,7 +128,7 @@
         + [
             pltpu.VMEM(slot.shape, I32),
             pltpu.VMEM(slot.shape, I32),
-            pltpu.SemaphoreType.DMA((3,)),
+            pltpu.SemaphoreType.DMA((4,)),
         ],
         compiler_params=pltpu.CompilerParams(vmem_limit_bytes=16 << 20),
         cost_estimate=cost(0, 4 * half * width),

time: 76.7 us -> 76.8 us (level)
  no operation moved by 1% of the time
where the time goes in v19:
time: 76.8 us; the launch traced here: 76.1 us
  waiting for transfers between devices  20 us (26%)
  starting transfers between devices  17.9 us (23%)
  Pallas kernels  17.8 us (23%)
  blocking collectives  13.5 us (18%)
  local copies, waits for them, and re-layouts  6.69 us (9%)
    ppermute x8, starting transfers between devices, over_ctx(): return lax.ppermute(x, 'ctx', [(i, i ^ m) for i in range(n)])  11.8 us
    ppermute x8, waiting for transfers between devices, over_ctx(): return lax.ppermute(x, 'ctx', [(i, i ^ m) for i in range(n)])  11.1 us
    ppermute x4, waiting for transfers between devices, to_core(): return lax.ppermute(x, ('ctx', 'tp'), pairs)  8.86 us
    ppermute x4, starting transfers between devices, to_core(): return lax.ppermute(x, ('ctx', 'tp'), pairs)  5.63 us
    unnamed x16, local copies, waits for them, and re-layouts  5.26 us
    all_gather x2, blocking collectives, body(): sent[m] = [whole_packet, lax.all_gather(whole_packet[size:], 'tp', axis=0)]  5.07 us
    pallas_call x4, Pallas kernels, packet(): pl.pallas_call(functools.partial(packet_kernel, m, early, len(blocks), se...  4.84 us
    pallas_call x3, Pallas kernels, project_parts(): pl.pallas_call(project_parts_kernel, out_shape=[jax.ShapeDtypeStruct((row...  4.8 us
  transfers between devices with their start and end apart: 15, of which 6 were waited for; matrix products, arithmetic and copies ran while one was open for 2% of the time, Pallas kernels for 18%

profile of v19, /device:TPU:0, one launch (start us, length us, event | category | flops | bytes accessed | tf_op | source)
XLA Modules:
  0.0 76.1 jit_solution(7121062712747543748)
XLA Ops:
  0.0 1.6 %to_send.1 = (bf16[1296,128]{1,0:T(8,128)(2,1)S(1)}, bf16[656,128]{1,0:T(8,128)(2,1)S(1)}, bf16[656,128]{1,0:T(8,128)(2,1)S(1)}, s32[1,256]{1,0:T(1,128)S(1)}) custom-call(bf16[256,1280]{1,0:T(8,128)(2,1)} %bitcast.16, s32[1,256]{1,0:T(1,128)} %refs_0_, s32[1,256]{1,0:T(1,128)} %kind.3), custom_call_target="tpu_custom_call" | custom-call | bytes 40960 | tf_op jit(solution)/shard_map/to_send/pallas_call | solution.py:122
  1.6 3.1 %collective-permute-start = (bf16[1296,128]{1,0:T(8,128)(2,1)S(1)}, bf16[1296,128]{1,0:T(8,128)(2,1)S(1)}, u32[]{:S(2)}, u32[]{:S(2)}) collective-permute-start(bf16[1296,128]{1,0:T(8,128)(2,1)S(1)} %get-tuple-element.46), channel_id=1, source_target_pairs={{0,4},{4,0},{8,12},{12,8},{1,5},{5,1},{9,13},{13,9},{2,6},{6,2},{1... | collective-permute-start | bytes 995336 | tf_op jit(solution)/shard_map/ppermute | solution.py:497
  4.7 2.6 %collective-permute-start.1 = (bf16[656,128]{1,0:T(8,128)(2,1)S(1)}, bf16[656,128]{1,0:T(8,128)(2,1)S(1)}, u32[]{:S(2)}, u32[]{:S(2)}) collective-permute-start(bf16[656,128]{1,0:T(8,128)(2,1)S(1)} %get-tuple-element.47), channel_id=1, source_target_pairs={{0,8},{4,12},{8,0},{12,4},{1,9},{5,13},{9,1},{13,5},{2,10},{6,14},... | collective-permute-start | bytes 503816 | tf_op jit(solution)/shard_map/ppermute | solution.py:497
  7.3 0.7 broadcast_in_dim.31.ba
  8.0 0.7 broadcast_in_dim.32.bf
  8.6 1.7 %copy-done = bf16[1280,1024]{1,0:T(8,128)(2,1)S(1)} copy-done((bf16[1280,1024]{1,0:T(8,128)(2,1)S(1)}, bf16[1280,1024]{1,0:T(8,128)(2,1)}, u32[]{:S(2)}) %copy-start) | copy-done | bytes 2621464
  10.4 1.7 %copy-done.2 = bf16[1280,1024]{1,0:T(8,128)(2,1)S(1)} copy-done((bf16[1280,1024]{1,0:T(8,128)(2,1)S(1)}, bf16[1280,1024]{1,0:T(8,128)(2,1)}, u32[]{:S(2)}) %copy-start.2) | copy-done | bytes 2621464
  12.1 1.1 %copy-done.4 = bf16[1,256,1280]{2,1,0:T(8,128)(2,1)S(1)} copy-done((bf16[1,256,1280]{2,1,0:T(8,128)(2,1)S(1)}, bf16[1,256,1280]{2,1,0:T(8,128)(2,1)}, u32[]{:S(2)}) %copy-start.4) | copy-done | bytes 655384
  13.2 0.7 copy-done.6
  13.9 1.6 %project_own.1.refs_0_ = bf16[256,1024]{1,0:T(8,128)(2,1)S(1)} custom-call(s32[1,256]{1,0:T(1,128)S(1)} %copy-done.6, bf16[256,1280]{1,0:T(8,128)(2,1)S(1)} %bitcast.17, bf16[1280,1024]{1,0:T(8,128)(2,1)S(1)} %copy-done, bf16[1280,1024]{1,0:T(8,128)(2,1)S(1)} %copy-done.2, bf16[1,1024]{1,0:T(2,128)(2,1)S(1)} %broadcast_in_dim.31.ba, ...), custom_call_target="tpu_custom_call" | custom-call | flops 83886080 | bytes 327680 | tf_op jit(solution)/shard_map/project_own/pallas_call | solution.py:160
  15.5 1.1 %collective-permute-done.1 = bf16[656,128]{1,0:T(8,128)(2,1)S(1)} collective-permute-done((bf16[656,128]{1,0:T(8,128)(2,1)S(1)}, bf16[656,128]{1,0:T(8,128)(2,1)S(1)}, u32[]{:S(2)}, u32[]{:S(2)}) %collective-permute-start.1) | collective-permute-done | bytes 167968 | tf_op jit(solution)/shard_map/ppermute | solution.py:497
  16.5 5.4 %collective-permute-done.2 = bf16[656,128]{1,0:T(8,128)(2,1)S(1)} collective-permute-done((bf16[656,128]{1,0:T(8,128)(2,1)S(1)}, bf16[656,128]{1,0:T(8,128)(2,1)S(1)}, u32[]{:S(2)}, u32[]{:S(2)}) %collective-permute-start.2) | collective-permute-done | bytes 167968 | tf_op jit(solution)/shard_map/ppermute | solution.py:497
  22.0 0.5 collective-permute-start.4
  22.5 0.0 collective-permute-start.5
  22.5 0.8 %collective-permute-start.6 = (bf16[656,128]{1,0:T(8,128)(2,1)S(1)}, bf16[656,128]{1,0:T(8,128)(2,1)S(1)}, u32[]{:S(2)}, u32[]{:S(2)}) collective-permute-start(bf16[656,128]{1,0:T(8,128)(2,1)S(1)} %collective-permute-done.1), channel_id=1, source_target_pairs={{0,4},{4,0},{8,12},{12,8},{1,5},{5,1},{9,13},{13,9},{2,6},{6,2},{1... | collective-permute-start | bytes 503816 | tf_op jit(solution)/shard_map/ppermute | solution.py:497
  23.3 1.3 %collective-permute-start.7 = (bf16[656,128]{1,0:T(8,128)(2,1)S(1)}, bf16[656,128]{1,0:T(8,128)(2,1)S(1)}, u32[]{:S(2)}, u32[]{:S(2)}) collective-permute-start(bf16[656,128]{1,0:T(8,128)(2,1)S(1)} %collective-permute-done.2), channel_id=1, source_target_pairs={{0,4},{4,0},{8,12},{12,8},{1,5},{5,1},{9,13},{13,9},{2,6},{6,2},{1... | collective-permute-start | bytes 503816 | tf_op jit(solution)/shard_map/ppermute | solution.py:497
  24.5 1.6 %project_parts.3 = (bf16[256,1024]{1,0:T(8,128)(2,1)S(1)}, s32[1,256]{1,0:T(1,128)S(1)}) custom-call(bf16[1280,1024]{1,0:T(8,128)(2,1)S(1)} %copy-done.1, bf16[1280,1024]{1,0:T(8,128)(2,1)S(1)} %copy-done.3, bf16[1,1024]{1,0:T(2,128)(2,1)S(1)} %broadcast_in_dim.31.ba, bf16[1,1024]{1,0:T(2,128)(2,1)S(1)} %broadcast_in_dim.32.bf, ...), custom_call_target="tpu_custom_call" | custom-call | flops 83886080 | bytes 327680 | tf_op jit(solution)/shard_map/project_parts/pallas_call | solution.py:190
  26.2 0.0 copy-start.5
  26.2 0.0 copy-start.7
  26.2 1.6 %project_parts.4 = (bf16[256,1024]{1,0:T(8,128)(2,1)S(1)}, s32[1,256]{1,0:T(1,128)S(1)}) custom-call(bf16[1280,1024]{1,0:T(8,128)(2,1)S(1)} %copy-done.1, bf16[1280,1024]{1,0:T(8,128)(2,1)S(1)} %copy-done.3, bf16[1,1024]{1,0:T(2,128)(2,1)S(1)} %broadcast_in_dim.31.ba, bf16[1,1024]{1,0:T(2,128)(2,1)S(1)} %broadcast_in_dim.32.bf, ...), custom_call_target="tpu_custom_call" | custom-call | flops 83886080 | bytes 327680 | tf_op jit(solution)/shard_map/project_parts/pallas_call | solution.py:190
  27.8 1.0 %packet.4 = bf16[96,1024]{1,0:T(8,128)(2,1)S(1)} custom-call(bf16[256,1024]{1,0:T(8,128)(2,1)S(1)} %project_own.1.refs_0_, bf16[256,1024]{1,0:T(8,128)(2,1)S(1)} %get-tuple-element.52.refs_1_, bf16[256,1024]{1,0:T(8,128)(2,1)S(1)} %get-tuple-element.56.refs_2_, s32[1,256]{1,0:T(1,128)S(1)} %copy-done.5, ...), custom_call_target="tpu_custom_call" | custom-call | flops 9437184 | bytes 98304 | tf_op jit(solution)/shard_map/packet/pallas_call | solution.py:292
  28.9 1.5 %collective-permute-start.8 = (bf16[96,1024]{1,0:T(8,128)(2,1)S(1)}, bf16[96,1024]{1,0:T(8,128)(2,1)S(1)}, u32[]{:S(2)}, u32[]{:S(2)}) collective-permute-start(bf16[96,1024]{1,0:T(8,128)(2,1)S(1)} %packet.4), channel_id=1, source_target_pairs={{0,12},{4,8},{8,4},{12,0},{1,13},{5,9},{9,5},{13,1},{2,14},{6,10},... | collective-permute-start | bytes 589832 | tf_op jit(solution)/shard_map/ppermute | solution.py:497
  30.4 1.0 %packet.5 = bf16[96,1024]{1,0:T(8,128)(2,1)S(1)} custom-call(bf16[256,1024]{1,0:T(8,128)(2,1)S(1)} %project_own.1.refs_0_, bf16[256,1024]{1,0:T(8,128)(2,1)S(1)} %get-tuple-element.52.refs_1_, bf16[256,1024]{1,0:T(8,128)(2,1)S(1)} %get-tuple-element.56.refs_2_, s32[1,256]{1,0:T(1,128)S(1)} %copy-done.5, ...), custom_call_target="tpu_custom_call" | custom-call | flops 9437184 | bytes 98304 | tf_op jit(solution)/shard_map/packet/pallas_call | solution.py:292
  31.4 0.8 %collective-permute-start.11 = (bf16[96,1024]{1,0:T(8,128)(2,1)S(1)}, bf16[96,1024]{1,0:T(8,128)(2,1)S(1)}, u32[]{:S(2)}, u32[]{:S(2)}) collective-permute-start(bf16[96,1024]{1,0:T(8,128)(2,1)S(1)} %packet.5), channel_id=1, source_target_pairs={{0,8},{4,12},{8,0},{12,4},{1,9},{5,13},{9,1},{13,5},{2,10},{6,14},... | collective-permute-start | bytes 589832 | tf_op jit(solution)/shard_map/ppermute | solution.py:497
  32.3 0.5 collective-permute-done.7
  32.8 2.0 %all-gather = bf16[1312,128]{1,0:T(8,128)(2,1)S(1)} all-gather(bf16[656,128]{1,0:T(8,128)(2,1)S(1)} %collective-permute-done.6), channel_id=2, replica_groups=mesh['groups'=2,'ctx'=4,'enc'=2,'tp'=2] {'tp'}, dimensions={0}, use_global_device_ids=true | all-gather | bytes 503808 | tf_op jit(solution)/shard_map/all_gather | solution.py:542
  34.8 2.0 %all-gather.1 = bf16[1312,128]{1,0:T(8,128)(2,1)S(1)} all-gather(bf16[656,128]{1,0:T(8,128)(2,1)S(1)} %collective-permute-done.7), channel_id=3, replica_groups=mesh['groups'=2,'ctx'=4,'enc'=2,'tp'=2] {'tp'}, dimensions={0}, use_global_device_ids=true | all-gather | bytes 503808 | tf_op jit(solution)/shard_map/all_gather | solution.py:542
  36.9 1.6 %project_parts.5 = (bf16[256,1024]{1,0:T(8,128)(2,1)S(1)}, s32[1,256]{1,0:T(1,128)S(1)}) custom-call(bf16[1280,1024]{1,0:T(8,128)(2,1)S(1)} %copy-done.1, bf16[1280,1024]{1,0:T(8,128)(2,1)S(1)} %copy-done.3, bf16[1,1024]{1,0:T(2,128)(2,1)S(1)} %broadcast_in_dim.31.ba, bf16[1,1024]{1,0:T(2,128)(2,1)S(1)} %broadcast_in_dim.32.bf, ...), custom_call_target="tpu_custom_call" | custom-call | flops 83886080 | bytes 327680 | tf_op jit(solution)/shard_map/project_parts/pallas_call | solution.py:190
  38.5 0.7 select.2
  39.2 1.7 %collective-permute-start.10 = (bf16[256,1024]{1,0:T(8,128)(2,1)S(1)}, bf16[256,1024]{1,0:T(8,128)(2,1)S(1)}, u32[]{:S(2)}, u32[]{:S(2)}) collective-permute-start(bf16[256,1024]{1,0:T(8,128)(2,1)S(1)} %select.2), channel_id=1, source_target_pairs={{0,4},{4,0},{8,12},{12,8},{1,5},{5,1},{9,13},{13,9},{2,6},{6,2},{1... | collective-permute-start | bytes 1572872 | tf_op jit(solution)/shard_map/ppermute | solution.py:497
  40.9 1.4 %packet.6 = (bf16[80,1024]{1,0:T(8,128)(2,1)S(1)}, bf16[80,1024]{1,0:T(8,128)(2,1)S(1)}) custom-call(bf16[256,1024]{1,0:T(8,128)(2,1)S(1)} %project_own.1.refs_0_, bf16[256,1024]{1,0:T(8,128)(2,1)S(1)} %get-tuple-element.52.refs_1_, bf16[256,1024]{1,0:T(8,128)(2,1)S(1)} %get-tuple-element.56.refs_2_, bf16[256,1024]{1,0:T(8,128)(2,1)S(1)} %get-tuple-element.59.refs_3_, ...), custom_call_target="tpu_custom_call" | custom-call | flops 20971520 | bytes 131072 | tf_op jit(solution)/shard_map/packet/pallas_call | solution.py:292
  42.3 1.4 %packet.7 = (bf16[80,1024]{1,0:T(8,128)(2,1)S(1)}, bf16[80,1024]{1,0:T(8,128)(2,1)S(1)}) custom-call(bf16[256,1024]{1,0:T(8,128)(2,1)S(1)} %project_own.1.refs_0_, bf16[256,1024]{1,0:T(8,128)(2,1)S(1)} %get-tuple-element.52.refs_1_, bf16[256,1024]{1,0:T(8,128)(2,1)S(1)} %get-tuple-element.56.refs_2_, bf16[256,1024]{1,0:T(8,128)(2,1)S(1)} %get-tuple-element.59.refs_3_, ...), custom_call_target="tpu_custom_call" | custom-call | flops 20971520 | bytes 131072 | tf_op jit(solution)/shard_map/packet/pallas_call | solution.py:292
  43.7 3.1 %collective-permute-start.9 = (bf16[80,1024]{1,0:T(8,128)(2,1)S(1)}, bf16[80,1024]{1,0:T(8,128)(2,1)S(1)}, u32[]{:S(2)}, u32[]{:S(2)}) collective-permute-start(bf16[80,1024]{1,0:T(8,128)(2,1)S(1)} %get-tuple-element.71), channel_id=1, source_target_pairs={{0,8},{1,9},{4,12},{5,13},{8,0},{9,1},{12,4},{13,5},{2,10},{3,11},... | collective-permute-start | bytes 491528 | tf_op jit(solution)/shard_map/ppermute | solution.py:512
  46.8 0.6 order_of.1
  47.4 0.1 collective-permute-start.12
  47.5 2.1 %collective-permute-done.11.refs_0_ = bf16[96,1024]{1,0:T(8,128)(2,1)S(1)} collective-permute-done((bf16[96,1024]{1,0:T(8,128)(2,1)S(1)}, bf16[96,1024]{1,0:T(8,128)(2,1)S(1)}, u32[]{:S(2)}, u32[]{:S(2)}) %collective-permute-start.11) | collective-permute-done | bytes 196640 | tf_op jit(solution)/shard_map/ppermute | solution.py:497
  49.6 2.4 %collective-permute-start.13 = (bf16[80,1024]{1,0:T(8,128)(2,1)S(1)}, bf16[80,1024]{1,0:T(8,128)(2,1)S(1)}, u32[]{:S(2)}, u32[]{:S(2)}) collective-permute-start(bf16[80,1024]{1,0:T(8,128)(2,1)S(1)} %get-tuple-element.83), channel_id=1, source_target_pairs={{0,12},{1,13},{4,8},{5,9},{8,4},{9,5},{12,0},{13,1},{2,14},{3,15},... | collective-permute-start | bytes 491528 | tf_op jit(solution)/shard_map/ppermute | solution.py:512
  52.1 3.1 %all-gather.5 = bf16[96,1024]{1,0:T(8,128)(2,1)S(1)} all-gather(bf16[48,1024]{1,0:T(8,128)(2,1)S(1)} %slice.11), channel_id=7, replica_groups=mesh['groups'=2,'ctx'=4,'enc'=2,'tp'=2] {'tp'}, dimensions={0}, use_global_device_ids=true | all-gather | bytes 294912 | tf_op jit(solution)/shard_map/all_gather | solution.py:561
  55.2 1.9 %all-gather.4 = bf16[96,1024]{1,0:T(8,128)(2,1)S(1)} all-gather(bf16[48,1024]{1,0:T(8,128)(2,1)S(1)} %slice.10), channel_id=6, replica_groups=mesh['groups'=2,'ctx'=4,'enc'=2,'tp'=2] {'tp'}, dimensions={0}, use_global_device_ids=true | all-gather | bytes 294912 | tf_op jit(solution)/shard_map/all_gather | solution.py:561
  57.2 0.7 select.3
  57.9 2.2 %all-gather.2 = bf16[256,1024]{1,0:T(8,128)(2,1)S(1)} all-gather(bf16[128,1024]{1,0:T(8,128)(2,1)S(1)} %get-tuple-element.74), channel_id=4, replica_groups=mesh['groups'=2,'ctx'=4,'enc'=2,'tp'=2] {'tp'}, dimensions={0}, use_global_device_ids=true | all-gather | bytes 786432 | tf_op jit(solution)/shard_map/all_gather | solution.py:516
  60.1 0.2 squares.2.refs_0_
  60.2 8.9 %collective-permute-done.12.refs_3_ = bf16[80,1024]{1,0:T(8,128)(2,1)S(1)} collective-permute-done((bf16[80,1024]{1,0:T(8,128)(2,1)S(1)}, bf16[80,1024]{1,0:T(8,128)(2,1)S(1)}, u32[]{:S(2)}, u32[]{:S(2)}) %collective-permute-start.12) | collective-permute-done | bytes 163872 | tf_op jit(solution)/shard_map/ppermute | solution.py:512
  69.1 0.4 place.1
  69.5 2.0 %collective-permute-done.10.refs_0_.refs_10_ = bf16[256,1024]{1,0:T(8,128)(2,1)S(1)} collective-permute-done((bf16[256,1024]{1,0:T(8,128)(2,1)S(1)}, bf16[256,1024]{1,0:T(8,128)(2,1)S(1)}, u32[]{:S(2)}, u32[]{:S(2)}) %collective-permute-start.10) | collective-permute-done | bytes 524320 | tf_op jit(solution)/shard_map/ppermute | solution.py:497
  71.5 2.2 %all-gather.3 = bf16[256,1024]{1,0:T(8,128)(2,1)S(1)} all-gather(bf16[128,1024]{1,0:T(8,128)(2,1)S(1)} %slice.12), channel_id=5, replica_groups=mesh['groups'=2,'ctx'=4,'enc'=2,'tp'=2] {'tp'}, dimensions={0}, use_global_device_ids=true | all-gather | bytes 786432 | tf_op jit(solution)/shard_map/all_gather | solution.py:521
  73.7 0.2 squares.3.refs_1_
  73.9 2.2 %place_and_norm.1 = bf16[128,8192]{1,0:T(8,128)(2,1)} custom-call(bf16[1,8192]{1,0:T(2,128)(2,1)S(1)} %broadcast_in_dim.30.gain, f32[128,1]{1,0:T(8,128)S(1)} %squares.2.refs_0_, f32[128,1]{1,0:T(8,128)S(1)} %squares.3.refs_1_, f32[128,1]{1,0:T(8,128)S(1)} %get-tuple-element.80.refs_2_, bf16[128,128]{1,0:T(8,128)(2,1)S(1)} %get-tuple-element.81.refs_3_, ...), custom_call_target="tpu_custom_call" | custom-call | flops 262144 | bytes 262144 | tf_op jit(solution)/shard_map/place_and_norm/pallas_call | solution.py:474
  (26 shorter events, 0.1 us)
Async XLA Ops:
  1.6 20.4 %collective-permute-start = (bf16[1296,128]{1,0:T(8,128)(2,1)S(1)}, bf16[1296,128]{1,0:T(8,128)(2,1)S(1)}, u32[]{:S(2)}, u32[]{:S(2)}) collective-permute-start(bf16[1296,128]{1,0:T(8,128)(2,1)S(1)} %get-tuple-element.46), channel_id=1, source_target_pairs={{0,4},{4,0},{8,12},{12,8},{1,5},{5,1},{9,13},{13,9},{2,6},{6,2},{1... | collective-permute-start | bytes 995336 | tf_op jit(solution)/shard_map/ppermute | solution.py:497
  4.7 11.8 %collective-permute-start.1 = (bf16[656,128]{1,0:T(8,128)(2,1)S(1)}, bf16[656,128]{1,0:T(8,128)(2,1)S(1)}, u32[]{:S(2)}, u32[]{:S(2)}) collective-permute-start(bf16[656,128]{1,0:T(8,128)(2,1)S(1)} %get-tuple-element.47), channel_id=1, source_target_pairs={{0,8},{4,12},{8,0},{12,4},{1,9},{5,13},{9,1},{13,5},{2,10},{6,14},... | collective-permute-start | bytes 503816 | tf_op jit(solution)/shard_map/ppermute | solution.py:497
  7.3 14.7 %collective-permute-start.2 = (bf16[656,128]{1,0:T(8,128)(2,1)S(1)}, bf16[656,128]{1,0:T(8,128)(2,1)S(1)}, u32[]{:S(2)}, u32[]{:S(2)}) collective-permute-start(bf16[656,128]{1,0:T(8,128)(2,1)S(1)} %get-tuple-element.48), channel_id=1, source_target_pairs={{0,12},{4,8},{8,4},{12,0},{1,13},{5,9},{9,5},{13,1},{2,14},{6,10},... | collective-permute-start | bytes 503816 | tf_op jit(solution)/shard_map/ppermute | solution.py:497
  8.6 1.7 %copy-start = (bf16[1280,1024]{1,0:T(8,128)(2,1)S(1)}, bf16[1280,1024]{1,0:T(8,128)(2,1)}, u32[]{:S(2)}) copy-start(bf16[1280,1024]{1,0:T(8,128)(2,1)} %wa.7) | copy-start | bytes 7864324
  10.4 1.7 %copy-start.2 = (bf16[1280,1024]{1,0:T(8,128)(2,1)S(1)}, bf16[1280,1024]{1,0:T(8,128)(2,1)}, u32[]{:S(2)}) copy-start(bf16[1280,1024]{1,0:T(8,128)(2,1)} %wf.7) | copy-start | bytes 7864324
  12.1 1.1 %copy-start.4 = (bf16[1,256,1280]{2,1,0:T(8,128)(2,1)S(1)}, bf16[1,256,1280]{2,1,0:T(8,128)(2,1)}, u32[]{:S(2)}) copy-start(bf16[1,256,1280]{2,1,0:T(8,128)(2,1)} %param.8) | copy-start | bytes 1966084
  13.2 0.7 copy-start.6
  13.9 10.6 %copy-start.1 = (bf16[1280,1024]{1,0:T(8,128)(2,1)S(1)}, bf16[1280,1024]{1,0:T(8,128)(2,1)}, u32[]{:S(2)}) copy-start(bf16[1280,1024]{1,0:T(8,128)(2,1)} %wa.7) | copy-start | bytes 7864324
  13.9 10.6 %copy-start.3 = (bf16[1280,1024]{1,0:T(8,128)(2,1)S(1)}, bf16[1280,1024]{1,0:T(8,128)(2,1)}, u32[]{:S(2)}) copy-start(bf16[1280,1024]{1,0:T(8,128)(2,1)} %wf.7) | copy-start | bytes 7864324
  22.0 4.2 %collective-permute-start.3 = (bf16[1296,128]{1,0:T(8,128)(2,1)S(1)}, bf16[1296,128]{1,0:T(8,128)(2,1)S(1)}, u32[]{:S(2)}, u32[]{:S(2)}) collective-permute-start(bf16[1296,128]{1,0:T(8,128)(2,1)S(1)} %collective-permute-done), channel_id=1, source_target_pairs={{0,1},{1,0},{2,3},{3,2},{4,5},{5,4},{6,7},{7,6},{8,9},{9,8},{10,11... | collective-permute-start | bytes 995336 | tf_op jit(solution)/shard_map/ppermute | solution.py:500
  22.0 4.1 %collective-permute-start.4 = (bf16[656,128]{1,0:T(8,128)(2,1)S(1)}, bf16[656,128]{1,0:T(8,128)(2,1)S(1)}, u32[]{:S(2)}, u32[]{:S(2)}) collective-permute-start(bf16[656,128]{1,0:T(8,128)(2,1)S(1)} %collective-permute-done.1), channel_id=1, source_target_pairs={{0,1},{1,0},{2,3},{3,2},{4,5},{5,4},{6,7},{7,6},{8,9},{9,8},{10,11... | collective-permute-start | bytes 503816 | tf_op jit(solution)/shard_map/ppermute | solution.py:500
  22.5 3.7 %collective-permute-start.5 = (bf16[656,128]{1,0:T(8,128)(2,1)S(1)}, bf16[656,128]{1,0:T(8,128)(2,1)S(1)}, u32[]{:S(2)}, u32[]{:S(2)}) collective-permute-start(bf16[656,128]{1,0:T(8,128)(2,1)S(1)} %collective-permute-done.2), channel_id=1, source_target_pairs={{0,1},{1,0},{2,3},{3,2},{4,5},{5,4},{6,7},{7,6},{8,9},{9,8},{10,11... | collective-permute-start | bytes 503816 | tf_op jit(solution)/shard_map/ppermute | solution.py:500
  22.5 9.8 %collective-permute-start.6 = (bf16[656,128]{1,0:T(8,128)(2,1)S(1)}, bf16[656,128]{1,0:T(8,128)(2,1)S(1)}, u32[]{:S(2)}, u32[]{:S(2)}) collective-permute-start(bf16[656,128]{1,0:T(8,128)(2,1)S(1)} %collective-permute-done.1), channel_id=1, source_target_pairs={{0,4},{4,0},{8,12},{12,8},{1,5},{5,1},{9,13},{13,9},{2,6},{6,2},{1... | collective-permute-start | bytes 503816 | tf_op jit(solution)/shard_map/ppermute | solution.py:497
  23.3 9.5 %collective-permute-start.7 = (bf16[656,128]{1,0:T(8,128)(2,1)S(1)}, bf16[656,128]{1,0:T(8,128)(2,1)S(1)}, u32[]{:S(2)}, u32[]{:S(2)}) collective-permute-start(bf16[656,128]{1,0:T(8,128)(2,1)S(1)} %collective-permute-done.2), channel_id=1, source_target_pairs={{0,4},{4,0},{8,12},{12,8},{1,5},{5,1},{9,13},{13,9},{2,6},{6,2},{1... | collective-permute-start | bytes 503816 | tf_op jit(solution)/shard_map/ppermute | solution.py:497
  26.2 1.6 %copy-start.5 = (s32[1,256]{1,0:T(1,128)S(1)}, s32[1,256]{1,0:T(1,128)}, u32[]{:S(2)}) copy-start(s32[1,256]{1,0:T(1,128)} %refs_0_) | copy-start | bytes 3076
  26.2 4.2 %copy-start.7 = (bf16[8192]{0:T(1024)(128)(2,1)S(1)}, bf16[8192]{0:T(1024)(128)(2,1)}, u32[]{:S(2)}) copy-start(bf16[8192]{0:T(1024)(128)(2,1)} %param.15) | copy-start | bytes 49156
  28.9 14.8 %collective-permute-start.8 = (bf16[96,1024]{1,0:T(8,128)(2,1)S(1)}, bf16[96,1024]{1,0:T(8,128)(2,1)S(1)}, u32[]{:S(2)}, u32[]{:S(2)}) collective-permute-start(bf16[96,1024]{1,0:T(8,128)(2,1)S(1)} %packet.4), channel_id=1, source_target_pairs={{0,12},{4,8},{8,4},{12,0},{1,13},{5,9},{9,5},{13,1},{2,14},{6,10},... | collective-permute-start | bytes 589832 | tf_op jit(solution)/shard_map/ppermute | solution.py:497
  31.4 18.2 %collective-permute-start.11 = (bf16[96,1024]{1,0:T(8,128)(2,1)S(1)}, bf16[96,1024]{1,0:T(8,128)(2,1)S(1)}, u32[]{:S(2)}, u32[]{:S(2)}) collective-permute-start(bf16[96,1024]{1,0:T(8,128)(2,1)S(1)} %packet.5), channel_id=1, source_target_pairs={{0,8},{4,12},{8,0},{12,4},{1,9},{5,13},{9,1},{13,5},{2,10},{6,14},... | collective-permute-start | bytes 589832 | tf_op jit(solution)/shard_map/ppermute | solution.py:497
  39.2 32.3 %collective-permute-start.10 = (bf16[256,1024]{1,0:T(8,128)(2,1)S(1)}, bf16[256,1024]{1,0:T(8,128)(2,1)S(1)}, u32[]{:S(2)}, u32[]{:S(2)}) collective-permute-start(bf16[256,1024]{1,0:T(8,128)(2,1)S(1)} %select.2), channel_id=1, source_target_pairs={{0,4},{4,0},{8,12},{12,8},{1,5},{5,1},{9,13},{13,9},{2,6},{6,2},{1... | collective-permute-start | bytes 1572872 | tf_op jit(solution)/shard_map/ppermute | solution.py:497
  43.7 13.5 %collective-permute-start.9 = (bf16[80,1024]{1,0:T(8,128)(2,1)S(1)}, bf16[80,1024]{1,0:T(8,128)(2,1)S(1)}, u32[]{:S(2)}, u32[]{:S(2)}) collective-permute-start(bf16[80,1024]{1,0:T(8,128)(2,1)S(1)} %get-tuple-element.71), channel_id=1, source_target_pairs={{0,8},{1,9},{4,12},{5,13},{8,0},{9,1},{12,4},{13,5},{2,10},{3,11},... | collective-permute-start | bytes 491528 | tf_op jit(solution)/shard_map/ppermute | solution.py:512
  47.4 21.7 %collective-permute-start.12 = (bf16[80,1024]{1,0:T(8,128)(2,1)S(1)}, bf16[80,1024]{1,0:T(8,128)(2,1)S(1)}, u32[]{:S(2)}, u32[]{:S(2)}) collective-permute-start(bf16[80,1024]{1,0:T(8,128)(2,1)S(1)} %get-tuple-element.79), channel_id=1, source_target_pairs={{0,9},{1,8},{4,13},{5,12},{8,1},{9,0},{12,5},{13,4},{2,11},{3,10},... | collective-permute-start | bytes 491528 | tf_op jit(solution)/shard_map/ppermute | solution.py:512
  49.6 24.2 %collective-permute-start.13 = (bf16[80,1024]{1,0:T(8,128)(2,1)S(1)}, bf16[80,1024]{1,0:T(8,128)(2,1)S(1)}, u32[]{:S(2)}, u32[]{:S(2)}) collective-permute-start(bf16[80,1024]{1,0:T(8,128)(2,1)S(1)} %get-tuple-element.83), channel_id=1, source_target_pairs={{0,12},{1,13},{4,8},{5,9},{8,4},{9,5},{12,0},{13,1},{2,14},{3,15},... | collective-permute-start | bytes 491528 | tf_op jit(solution)/shard_map/ppermute | solution.py:512
  52.1 21.8 %collective-permute-start.14 = (bf16[80,1024]{1,0:T(8,128)(2,1)S(1)}, bf16[80,1024]{1,0:T(8,128)(2,1)S(1)}, u32[]{:S(2)}, u32[]{:S(2)}) collective-permute-start(bf16[80,1024]{1,0:T(8,128)(2,1)S(1)} %get-tuple-element.84), channel_id=1, source_target_pairs={{0,13},{1,12},{4,9},{5,8},{8,5},{9,4},{12,1},{13,0},{2,15},{3,14},... | collective-permute-start | bytes 491528 | tf_op jit(solution)/shard_map/ppermute | solution.py:512
